TPU v7x, 256 devices: a whole 4x4x8 slice. The times are simulated.
256 devices in a mesh: tm: 8 (over y_lo, x), space: 32 (over y_hi, z, core).
Axes of the slice: x: 4, y: 4 (y_hi: 2, y_lo: 2; y = y_hi * 2 + y_lo), z: 8, core: 2. Of those that a mesh axis runs over, the one named last changes fastest.
Arguments:
- hidden_in: bfloat16 [16, 64, 32, 5120], P('tm', 'space'), may hold values from -6 to 6
- queries: bfloat16 [16, 64, 32, 5120], P('tm', 'space'), may hold values from -250 to 250
- keys: bfloat16 [16, 64, 32, 5120], P('tm', 'space'), may hold values from -250 to 250
- values: bfloat16 [16, 64, 32, 5120], P('tm', 'space'), may hold values from -6 to 6
- query_gain: float32 [5120], replicated, may hold values from 0.5 to 3
- key_gain: float32 [5120], replicated, may hold values from 0.5 to 3
- reach_time: int32 [40], replicated, may hold values from 0 to 1
- reach_rows: int32 [40], replicated, may hold values from 0 to 1
- reach_cols: int32 [40], replicated, may hold values from 0 to 2
- out_weight: bfloat16 [5120, 5120], P('space', 'tm'), may hold values from -0.25 to 0.25
- gate: float32 [5120], replicated, may hold values from -1.5 to 1.5
Outputs:
- output: bfloat16 [16, 64, 32, 5120], P('tm', 'space')
All inputs are finite; a program needn't handle non-finite values.
Results may differ from a plain program's by a relative error of at most 0.013.
The roundings to bfloat16 on the way count: a program that leaves them out, or rounds other values in their place, can miss the bound.
Values may be sent and summed in bfloat16 or wider, within the bound.
No kernel may reach another device: no remote copies, remote signals or barrier semaphores. Data moves between devices by JAX's collectives and lax.ppermute only.
A program may use at most 128 MiB of HBM per device.

v0:
```python
import jax
import jax.numpy as jnp
from jax import lax
from jax.sharding import PartitionSpec as P

TW = 8


def passed_along(block, axis, distance):
    devices = range(lax.axis_size(axis))
    route = [(i - distance, i) for i in devices if i - distance in devices]
    return lax.ppermute(block, axis, route)


def normalize(source, gain):
    values_f = source.astype(jnp.float32)
    mean_square = jnp.mean(values_f * values_f, axis=-1, keepdims=True)
    return (values_f * lax.rsqrt(mean_square + 1e-06) * gain).astype(jnp.bfloat16)


def attend(
    query_block,
    key_region,
    value_region,
    first_frame,
    first_row,
    frame_count,
    row_count,
    reach_time,
    reach_rows,
    reach_cols,
):
    frames_here, rows_here, columns, inner = query_block.shape
    head_count = reach_time.shape[0]
    head_width = inner // head_count
    query_flat = query_block.reshape(-1, head_count, head_width)
    key_flat = key_region.reshape(-1, head_count, head_width)
    value_flat = value_region.reshape(-1, head_count, head_width)
    frame_q = first_frame + jnp.arange(frames_here, dtype=jnp.int32)
    frame_k = first_frame - 1 + jnp.arange(frames_here + 2, dtype=jnp.int32)
    row_q = first_row + jnp.arange(rows_here, dtype=jnp.int32)
    row_k = first_row - 1 + jnp.arange(rows_here + 2, dtype=jnp.int32)
    tiles = jnp.arange(columns, dtype=jnp.int32) // TW
    query_shape = (frames_here, rows_here, columns)
    key_shape = (frames_here + 2, rows_here + 2, columns)
    query_frame = jnp.broadcast_to(frame_q[:, None, None], query_shape).reshape(-1)
    query_row = jnp.broadcast_to(row_q[None, :, None], query_shape).reshape(-1)
    query_tile = jnp.broadcast_to(tiles[None, None, :], query_shape).reshape(-1)
    key_frame = jnp.broadcast_to(frame_k[:, None, None], key_shape).reshape(-1)
    key_row = jnp.broadcast_to(row_k[None, :, None], key_shape).reshape(-1)
    key_tile = jnp.broadcast_to(tiles[None, None, :], key_shape).reshape(-1)
    frame_gap = jnp.abs(query_frame[:, None] - key_frame[None, :])
    row_gap = jnp.abs(query_row[:, None] - key_row[None, :])
    tile_gap = jnp.abs(query_tile[:, None] - key_tile[None, :])
    inside = (key_frame >= 0) & (key_frame < frame_count) & (key_row >= 0) & (key_row < row_count)
    allowed = (frame_gap[None] <= reach_time[:, None, None]) & (
        row_gap[None] <= reach_rows[:, None, None]
    )
    allowed = allowed & (tile_gap[None] <= reach_cols[:, None, None]) & inside[None, None, :]
    scores = jnp.einsum(
        "qhd,khd->hqk", query_flat, key_flat, preferred_element_type=jnp.float32
    ) * head_width ** (-0.5)
    masked = jnp.where(allowed, scores, -jnp.inf)
    row_peak = jnp.max(masked, axis=2, keepdims=True)
    weights = jnp.exp(masked - row_peak)
    totals = jnp.sum(weights, axis=2, keepdims=True)
    rounded = weights.astype(jnp.bfloat16)
    mixed = jnp.einsum("hqk,khd->qhd", rounded, value_flat, preferred_element_type=jnp.float32)
    mixed = mixed / jnp.transpose(totals, (1, 0, 2))
    return mixed.reshape(mixed.shape[0], inner).astype(jnp.bfloat16)


def shards(
    hidden_in,
    queries,
    keys,
    values,
    query_gain,
    key_gain,
    reach_time,
    reach_rows,
    reach_cols,
    out_weight,
    gate,
):
    frames_here, rows_here, columns, inner = queries.shape
    width = hidden_in.shape[3]
    query_norm = normalize(queries, query_gain)
    key_norm = normalize(keys, key_gain)
    stacked = jnp.stack([key_norm, values])
    below_frame = passed_along(stacked[:, -1:], "tm", 1)
    above_frame = passed_along(stacked[:, :1], "tm", -1)
    framed = jnp.concatenate([below_frame, stacked, above_frame], axis=1)
    below_rows = passed_along(framed[:, :, -1:], "space", 1)
    above_rows = passed_along(framed[:, :, :1], "space", -1)
    region = jnp.concatenate([below_rows, framed, above_rows], axis=2)
    first_frame = lax.axis_index("tm") * frames_here
    first_row = lax.axis_index("space") * rows_here
    frame_count = frames_here * lax.axis_size("tm")
    row_count = rows_here * lax.axis_size("space")
    attention = attend(
        query_norm,
        region[0],
        region[1],
        first_frame,
        first_row,
        frame_count,
        row_count,
        reach_time,
        reach_rows,
        reach_cols,
    )
    token_count = attention.shape[0]
    gathered_rows = lax.all_gather(out_weight, "space", axis=0, tiled=True)
    group_terms = jnp.dot(
        lax.all_gather(attention, "tm", axis=0, tiled=True),
        gathered_rows,
        preferred_element_type=jnp.float32,
    )
    branch = lax.all_to_all(group_terms, "tm", split_axis=0, concat_axis=1, tiled=True)
    residual = hidden_in.reshape(token_count, width).astype(jnp.float32)
    output = (residual + gate * branch).astype(jnp.bfloat16)
    return output.reshape(frames_here, rows_here, columns, width)


def solution(mesh):
    in_specs = (
        P("tm", "space", None, None),
        P("tm", "space", None, None),
        P("tm", "space", None, None),
        P("tm", "space", None, None),
        P(),
        P(),
        P(),
        P(),
        P(),
        P("space", "tm"),
        P(),
    )
    out_specs = P("tm", "space", None, None)
    return jax.shard_map(shards, mesh=mesh, in_specs=in_specs, out_specs=out_specs, check_vma=False)
```

profile of v0, /device:TPU:1, one launch (start us, length us, event | category | flops | bytes accessed | tf_op | source)
XLA Modules:
  0.0 318.6 jit_solution(1563956579666153965)
XLA Ops:
  9.0 1.7 fusion.22
  10.7 1.7 fusion.21
  12.5 5.0 %collective-permute-start = (bf16[2,1,2,32,5120]{4,3,2,1,0:T(8,128)(2,1)}, bf16[2,1,2,32,5120]{4,3,2,1,0:T(8,128)(2,1)}, u32[]{:S(2)}, u32[]{:S(2)}) collective-permute-start(bf16[2,1,2,32,5120]{4,3,2,1,0:T(8,128)(2,1)} %get-tuple-element.9), channel_id=1, source_target_pairs={{0,32},{32,64},{64,96},{96,128},{128,160},{160,192},{192,224},{1,3... | collective-permute-start | bytes 3932168 | tf_op jit(solution)/shard_map/ppermute | solution.py:12
  19.1 25.0 %collective-permute-done = bf16[2,1,2,32,5120]{4,3,2,1,0:T(8,128)(2,1)} collective-permute-done((bf16[2,1,2,32,5120]{4,3,2,1,0:T(8,128)(2,1)}, bf16[2,1,2,32,5120]{4,3,2,1,0:T(8,128)(2,1)}, u32[]{:S(2)}, u32[]{:S(2)}) %collective-permute-start) | collective-permute-done | bytes 1310752 | tf_op jit(solution)/shard_map/ppermute | solution.py:12
  44.1 4.9 %collective-permute-done.1 = bf16[2,1,2,32,5120]{4,3,2,1,0:T(8,128)(2,1)} collective-permute-done((bf16[2,1,2,32,5120]{4,3,2,1,0:T(8,128)(2,1)}, bf16[2,1,2,32,5120]{4,3,2,1,0:T(8,128)(2,1)}, u32[]{:S(2)}, u32[]{:S(2)}) %collective-permute-start.1) | collective-permute-done | bytes 1310752 | tf_op jit(solution)/shard_map/ppermute | solution.py:12
  49.0 2.8 pad_maximum_fusion.1
  51.8 2.8 fusion.25
  54.6 5.3 %collective-permute-start.2 = (bf16[2,4,1,32,5120]{4,3,2,1,0:T(8,128)(2,1)}, bf16[2,4,1,32,5120]{4,3,2,1,0:T(8,128)(2,1)}, u32[]{:S(2)}, u32[]{:S(2)}) collective-permute-start(bf16[2,4,1,32,5120]{4,3,2,1,0:T(8,128)(2,1)} %get-tuple-element.7), channel_id=1, source_target_pairs={{0,1},{1,2},{2,3},{3,4},{4,5},{5,6},{6,7},{7,8},{8,9},{9,10},{10,1... | collective-permute-start | bytes 7864328 | tf_op jit(solution)/shard_map/ppermute | solution.py:12
  59.9 1.9 collective-permute-start.3
  64.0 1.7 fusion.15
  67.3 29.4 %collective-permute-done.2 = bf16[2,4,1,32,5120]{4,3,2,1,0:T(8,128)(2,1)} collective-permute-done((bf16[2,4,1,32,5120]{4,3,2,1,0:T(8,128)(2,1)}, bf16[2,4,1,32,5120]{4,3,2,1,0:T(8,128)(2,1)}, u32[]{:S(2)}, u32[]{:S(2)}) %collective-permute-start.2) | collective-permute-done | bytes 2621472 | tf_op jit(solution)/shard_map/ppermute | solution.py:12
  96.7 4.0 %collective-permute-done.3 = bf16[2,4,1,32,5120]{4,3,2,1,0:T(8,128)(2,1)} collective-permute-done((bf16[2,4,1,32,5120]{4,3,2,1,0:T(8,128)(2,1)}, bf16[2,4,1,32,5120]{4,3,2,1,0:T(8,128)(2,1)}, u32[]{:S(2)}, u32[]{:S(2)}) %collective-permute-start.3) | collective-permute-done | bytes 2621472 | tf_op jit(solution)/shard_map/ppermute | solution.py:12
  100.7 9.0 %pad_maximum_fusion = bf16[2,4,4,32,5120]{4,3,2,1,0:T(8,128)(2,1)} fusion(bf16[2,4,1,32,5120]{4,3,2,1,0:T(8,128)(2,1)} %collective-permute-done.3, bf16[2,1,2,32,5120]{4,3,2,1,0:T(8,128)(2,1)} %collective-permute-done.1, bf16[1,2,2,32,5120]{4,3,2,1,0:T(8,128)(2,1)S(1)} %bitcast.35, bf16[1,2,2,32,5120]{4,3,2,1,0:T(8,128)(2,1)S(1)} %fusion.22, ...), kind=kLoop, calls=%fused_computation | loop fusion | flops 26214400 | bytes 20971520 | tf_op jit(solution)/shard_map/concatenate | solution.py:96
  109.7 9.3 %fusion.24 = (bf16[1,4,4,32,5120]{4,3,2,1,0:T(8,128)(2,1)}, bf16[1,4,4,32,5120]{4,3,2,1,0:T(8,128)(2,1)}) fusion(bf16[2,4,4,32,5120]{4,3,2,1,0:T(8,128)(2,1)} %pad_maximum_fusion), kind=kLoop, calls=%fused_computation.44 | loop fusion | bytes 20971520 | tf_op jit(solution)/shard_map/slice | solution.py:104
  119.0 4.1 %copy.21 = bf16[64,8,40,128]{3,2,1,0:T(8,128)(2,1)S(1)} copy(bf16[64,8,40,128]{3,1,2,0:T(8,128)(2,1)} %bitcast.32) | data formatting | bytes 10485760
  124.7 4.7 %fusion.26 = (f32[40,128]{1,0:T(8,128)S(1)}, f32[40,128,512]{2,1,0:T(8,128)S(1)}) fusion(bf16[512,40,128]{2,1,0:T(8,128)(2,1)S(1)} %bitcast.38, bf16[128,40,128]{2,1,0:T(8,128)(2,1)S(1)} %bitcast.41, pred[512]{0:T(512)(128)(4,1)S(1)} %compare_and_fusion, s32[40]{0:T(128)S(1)} %copy-done.6, s32[128,512]{1,0:T(8,128)S(1)} %get-tuple-element.13, ...), kind=kOutput, calls=%fused_computation.46 | convolution fusion | flops 694676480 | bytes 17847264 | tf_op jit(solution)/shard_map/qhd,khd->hqk/dot_general | solution.py:60
  129.4 2.4 fusion
  133.4 7.3 %fusion.16 = bf16[128,40,128]{0,2,1:T(8,128)(2,1)} fusion(f32[40,128,512]{2,1,0:T(8,128)} %copy-done.1, f32[40,128]{1,0:T(8,128)S(1)} %get-tuple-element.11, bf16[512,40,128]{2,1,0:T(8,128)(2,1)S(1)} %bitcast.37, f32[128,40]{0,1:T(8,128)S(1)} %bitcast.43), kind=kOutput, calls=%fused_computation.24 | convolution fusion | flops 677642240 | bytes 17080320 | tf_op jit(solution)/shard_map/hqk,khd->qhd/dot_general | solution.py:68
  141.8 115.0 %all-gather.3.cloned.1.call-done = bf16[1024,5120]{0,1:T(8,128)(2,1)} async-done(((bf16[128,5120]{0,1:T(8,128)(2,1)}), bf16[1024,5120]{0,1:T(8,128)(2,1)}) %all-gather.3.cloned.1.call-update) | async-done | bytes 10485776 | tf_op jit(solution)/shard_map/all_gather | solution.py:116
  256.9 12.6 %fusion.27 = f32[1024,640]{1,0:T(8,128)S(1)} fusion(bf16[1024,5120]{0,1:T(8,128)(2,1)} %all-gather.3.cloned.1.call-done, bf16[5120,640]{1,0:T(8,128)(2,1)} %all-gather.5.cloned.1.call-done), kind=kOutput, calls=%fused_computation.47 | convolution fusion | flops 6710886400 | bytes 19660800 | tf_op jit(solution)/shard_map/dot_general | solution.py:115
  269.4 32.6 %all_to_all.19 = f32[8,128,640]{2,1,0:T(8,128)S(1)} all-to-all(f32[8,128,640]{2,1,0:T(8,128)S(1)} %bitcast.40), channel_id=1, replica_groups=mesh['tm'=8,'space'=32] {'tm'}, dimensions={0} | all-to-all | bytes 5242880 | tf_op jit(solution)/shard_map/all_to_all | solution.py:120
  302.1 3.0 copy.18
  305.1 3.6 %all_to_all.17 = f32[2,2,32,5120]{3,2,1,0:T(8,128)} reshape(f32[128,8,640]{2,1,0:T(8,128)} %copy.18) | data formatting | bytes 5242880 | tf_op jit(solution)/shard_map/all_to_all | solution.py:120
  308.7 3.1 add_convert_fusion
  (55 shorter events, 12.0 us)
Async XLA Ops:
  6.5 4.2 %copy-start = (bf16[2,2,32,5120]{3,2,1,0:T(8,128)(2,1)S(1)}, bf16[2,2,32,5120]{3,2,1,0:T(8,128)(2,1)}, u32[]{:S(2)}) copy-start(bf16[2,2,32,5120]{3,2,1,0:T(8,128)(2,1)} %param.14) | copy-start | bytes 3932164
  6.5 135.3 %all-gather.5.cloned.1.call-start = ((), (), s32[]{:S(2)}) async-start(), calls=%async_computation.2 | async-start | bytes 6758400 | tf_op jit(solution)/shard_map/all_gather | solution.py:114
  7.3 249.6 %all-gather.3.cloned.1.call-start = ((), (), s32[]{:S(2)}) async-start(), calls=%async_computation.1 | async-start | bytes 11796480 | tf_op jit(solution)/shard_map/all_gather | solution.py:116
  12.5 31.7 %collective-permute-start = (bf16[2,1,2,32,5120]{4,3,2,1,0:T(8,128)(2,1)}, bf16[2,1,2,32,5120]{4,3,2,1,0:T(8,128)(2,1)}, u32[]{:S(2)}, u32[]{:S(2)}) collective-permute-start(bf16[2,1,2,32,5120]{4,3,2,1,0:T(8,128)(2,1)} %get-tuple-element.9), channel_id=1, source_target_pairs={{0,32},{32,64},{64,96},{96,128},{128,160},{160,192},{192,224},{1,3... | collective-permute-start | bytes 3932168 | tf_op jit(solution)/shard_map/ppermute | solution.py:12
  17.5 31.5 %collective-permute-start.1 = (bf16[2,1,2,32,5120]{4,3,2,1,0:T(8,128)(2,1)}, bf16[2,1,2,32,5120]{4,3,2,1,0:T(8,128)(2,1)}, u32[]{:S(2)}, u32[]{:S(2)}) collective-permute-start(bf16[2,1,2,32,5120]{4,3,2,1,0:T(8,128)(2,1)} %get-tuple-element.10), channel_id=1, source_target_pairs={{32,0},{64,32},{96,64},{128,96},{160,128},{192,160},{224,192},{33,... | collective-permute-start | bytes 3932168 | tf_op jit(solution)/shard_map/ppermute | solution.py:12
  51.8 12.2 %copy-start.4 = (f32[5120]{0:T(1024)S(1)}, f32[5120]{0:T(1024)}, u32[]{:S(2)}) copy-start(f32[5120]{0:T(1024)} %param.15) | copy-start | bytes 61444
  54.6 42.1 %collective-permute-start.2 = (bf16[2,4,1,32,5120]{4,3,2,1,0:T(8,128)(2,1)}, bf16[2,4,1,32,5120]{4,3,2,1,0:T(8,128)(2,1)}, u32[]{:S(2)}, u32[]{:S(2)}) collective-permute-start(bf16[2,4,1,32,5120]{4,3,2,1,0:T(8,128)(2,1)} %get-tuple-element.7), channel_id=1, source_target_pairs={{0,1},{1,2},{2,3},{3,4},{4,5},{5,6},{6,7},{7,8},{8,9},{9,10},{10,1... | collective-permute-start | bytes 7864328 | tf_op jit(solution)/shard_map/ppermute | solution.py:12
  59.9 40.9 %collective-permute-start.3 = (bf16[2,4,1,32,5120]{4,3,2,1,0:T(8,128)(2,1)}, bf16[2,4,1,32,5120]{4,3,2,1,0:T(8,128)(2,1)}, u32[]{:S(2)}, u32[]{:S(2)}) collective-permute-start(bf16[2,4,1,32,5120]{4,3,2,1,0:T(8,128)(2,1)} %get-tuple-element.8), channel_id=1, source_target_pairs={{1,0},{2,1},{3,2},{4,3},{5,4},{6,5},{7,6},{8,7},{9,8},{10,9},{11,1... | collective-permute-start | bytes 7864328 | tf_op jit(solution)/shard_map/ppermute | solution.py:12
  119.0 4.1 %slice-start = ((s8[5242880]{0:T(1024)(128)(4,1)}), s8[4194304]{0:T(1024)(128)(4,1)S(1)}, s32[]{:S(2)}) async-start(s8[5242880]{0:T(1024)(128)(4,1)} %bitcast.29), calls=%async_computation.3 | async-start | bytes 8388608
  119.0 4.1 %slice-start.1 = ((s8[5242880]{0:T(1024)(128)(4,1)}), s8[1048576]{0:T(1024)(128)(4,1)S(1)}, s32[]{:S(2)}) async-start(s8[5242880]{0:T(1024)(128)(4,1)} %bitcast.29), calls=%async_computation.4 | async-start | bytes 2097152
  123.1 1.5 copy-start.2
  123.1 1.5 copy-start.6
  123.2 1.5 copy-start.7
  123.2 1.5 copy-start.8
  129.4 4.0 %copy-start.1 = (f32[40,128,512]{2,1,0:T(8,128)}, f32[40,128,512]{2,1,0:T(8,128)S(1)}, u32[]{:S(2)}) copy-start(f32[40,128,512]{2,1,0:T(8,128)S(1)} %get-tuple-element.12) | copy-start | bytes 31457284
  305.1 3.6 %copy-start.3 = (bf16[2,2,32,5120]{3,2,1,0:T(8,128)(2,1)S(1)}, bf16[2,2,32,5120]{3,2,1,0:T(8,128)(2,1)}, u32[]{:S(2)}) copy-start(bf16[2,2,32,5120]{3,2,1,0:T(8,128)(2,1)} %param.11) | copy-start | bytes 3932164
  305.1 3.6 %copy-start.5 = (f32[5120]{0:T(1024)S(1)}, f32[5120]{0:T(1024)}, u32[]{:S(2)}) copy-start(f32[5120]{0:T(1024)} %param.21) | copy-start | bytes 61444
Sparse Core Ops, SparseCore 0:
  10.1 131.6 all-gather.4
  143.5 113.2 all-gather.2
where the time goes:
time: 322 us; the launch traced here: 319 us
  waiting for transfers between devices  180 us (56%)
  blocking collectives  32.6 us (10%)
  local copies, waits for them, and re-layouts  27.9 us (9%)
  other arithmetic  26.1 us (8%)
  matrix products  24.6 us (8%)
  between operations  13.7 us (4%)
  starting transfers between devices  13.5 us (4%)
    all_gather x1, waiting for transfers between devices, shards(): lax.all_gather(attention, 'tm', axis=0, tiled=True)  115 us
    ppermute x4, waiting for transfers between devices, passed_along(): return lax.ppermute(block, axis, route)  63.3 us
    all_to_all x1, blocking collectives, shards(): lax.all_to_all(group_terms, 'tm', split_axis=0, concat_axis=1, tiled=True)  32.6 us
    ppermute x4, starting transfers between devices, passed_along(): return lax.ppermute(block, axis, route)  13.5 us
    dot_general x1, matrix products, shards(): jnp.dot(lax.all_gather(attention, 'tm', axis=0, tiled=True), gathered_row...  12.6 us
    slice x1, local copies, waits for them, and re-layouts, shards(): region[1]  9.29 us
    concatenate x1, other arithmetic, shards(): region = jnp.concatenate([below_rows, framed, above_rows], axis=2)  8.98 us
    unnamed x25, local copies, waits for them, and re-layouts  8.41 us
  transfers between devices with their start and end apart: 6, of which 6 were waited for; matrix products, arithmetic and copies ran while one was open for 17% of the time, Pallas kernels for 0%

commit v1 on v0

v1 whole, which is shorter than its diff:
```python
import functools

import jax
import jax.numpy as jnp
from jax import lax
from jax.experimental import pallas as pl
from jax.experimental.pallas import tpu as pltpu
from jax.sharding import Mesh, PartitionSpec as P

TW = 8
HEAD = 128
TM = ("y_lo", "x")
SP = ("y_hi", "z", "core")
CHUNKS = 1
COMBOS = 12
F32, BF16 = jnp.float32, jnp.bfloat16


def axis_size(axes):
    n = 1
    for a in axes:
        n *= lax.axis_size(a)
    return n


def passed_along(block, axes, distance):
    n = axis_size(axes)
    route = [(i - distance, i) for i in range(n) if 0 <= i - distance < n]
    return lax.ppermute(block, axes, route)


def shifted(block, axis, distance):
    n = lax.axis_size(axis)
    return lax.ppermute(block, axis, [(i, (i + distance) % n) for i in range(n)])


def params(megabytes=48):
    return pltpu.CompilerParams(vmem_limit_bytes=megabytes << 20)


def prepare_kernel(q_ref, k_ref, v_ref, qg_ref, kg_ref, qn_ref, *outs):
    i = pl.program_id(0)
    f, r = i // 2, i % 2
    inner = q_ref.shape[-1]

    def normed(ref, gain):
        a = ref[0].astype(F32)
        ms = jnp.sum(a * a, axis=-1, keepdims=True) * (1.0 / inner)
        return (a * lax.rsqrt(ms + 1e-06) * gain[...]).astype(BF16)

    qn_ref[0] = normed(q_ref, qg_ref)
    kn = normed(k_ref, kg_ref)
    v = v_ref[0]
    width = inner // (len(outs) // 4)
    for c in range(len(outs) // 4):
        f0, f1, r0, r1 = outs[4 * c : 4 * c + 4]
        lanes = slice(c * width, (c + 1) * width)
        for which, ref in ((0, f0), (1, f1)):

            @pl.when(f == which)
            def _(ref=ref):
                ref[0, 0] = kn[:, lanes]
                ref[1, 0] = v[:, lanes]

        for which, ref in ((0, r0), (1, r1)):

            @pl.when(r == which)
            def _(ref=ref):
                ref[0, 0] = kn[:, lanes]
                ref[0, 1] = v[:, lanes]


def prepare(queries, keys, values, query_gain, key_gain):
    groups, nw, inner = queries.shape
    width = inner // CHUNKS
    token_spec = pl.BlockSpec((1, nw, inner), lambda i: (i, 0, 0))
    gain_spec = pl.BlockSpec((1, inner), lambda i: (0, 0))
    out_shape = [jax.ShapeDtypeStruct(queries.shape, BF16)]
    out_specs = [token_spec]
    for _ in range(CHUNKS):
        out_shape += [jax.ShapeDtypeStruct((2, 2, nw, width), BF16)] * 4
        out_specs += [
            pl.BlockSpec((2, 1, nw, width), lambda i: (0, jnp.minimum(i, 1), 0, 0)),
            pl.BlockSpec((2, 1, nw, width), lambda i: (0, jnp.maximum(i - 2, 0), 0, 0)),
            pl.BlockSpec((1, 2, nw, width), lambda i: (i // 2, 0, 0, 0)),
            pl.BlockSpec((1, 2, nw, width), lambda i: (i // 2, 0, 0, 0)),
        ]
    return pl.pallas_call(
        prepare_kernel,
        grid=(groups,),
        in_specs=[token_spec] * 3 + [gain_spec] * 2,
        out_specs=out_specs,
        out_shape=out_shape,
        compiler_params=params(),
        cost_estimate=pl.CostEstimate(flops=0, bytes_accessed=12 << 20, transcendentals=0),
        name="prepare",
    )(queries, keys, values, query_gain[None], key_gain[None])


def mask_tables(first_frame, first_row, frame_count, row_count, nw):
    i32 = jnp.int32
    shape = (COMBOS, 2, 2 * nw, 3 * 4 * nw)
    t = lax.broadcasted_iota(i32, shape, 0)
    f = lax.broadcasted_iota(i32, shape, 1)
    q = lax.broadcasted_iota(i32, shape, 2)
    k = lax.broadcasted_iota(i32, shape, 3)
    kf, kr, kc = k // (4 * nw), k // nw % 4, k % nw
    frame, row = first_frame - 1 + f + kf, first_row - 1 + kr
    allowed = jnp.abs(kf - 1) <= t // 6
    allowed &= jnp.abs(q // nw + 1 - kr) <= t // 3 % 2
    allowed &= jnp.abs(q % nw // TW - kc // TW) <= t % 3
    allowed &= (frame >= 0) & (frame < frame_count) & (row >= 0) & (row < row_count)
    return jnp.where(allowed, 0.0, -jnp.inf).astype(F32)


def attend_kernel(heads, scale, combo_ref, q_ref, f0, f1, hb, ha, rb, ra, cb, ca, mask_ref, out_ref):
    step = pl.program_id(0)
    for h in range(heads):
        lanes = slice(h * HEAD, (h + 1) * HEAD)
        combo = combo_ref[step * heads + h]

        def region(kv):
            frames = ((cb[0], hb, ca[0]), (rb[0], f0, ra[0]), (rb[1], f1, ra[1]), (cb[1], ha, ca[1]))
            parts = []
            for below, own, above in frames:
                parts += [below[kv, :, lanes], own[kv, 0, :, lanes], own[kv, 1, :, lanes], above[kv, :, lanes]]
            return jnp.concatenate(parts, axis=0)

        keys, values = region(0), region(1)
        span = keys.shape[0] // 4 * 3
        for f in range(2):
            first = f * (span // 3)
            q = q_ref[2 * f : 2 * f + 2, :, lanes].reshape(-1, HEAD)
            s = lax.dot_general(
                q, keys[first : first + span], (((1,), (1,)), ((), ())), preferred_element_type=F32
            )
            s = s + mask_ref[combo, f]
            peak = jnp.max(s, axis=1, keepdims=True)
            w = jnp.exp((s - peak) * scale)
            total = jnp.sum(w, axis=1, keepdims=True)
            o = jnp.dot(w.astype(BF16), values[first : first + span], preferred_element_type=F32)
            out_ref[2 * f : 2 * f + 2, :, lanes] = (o / total).astype(BF16).reshape(2, -1, HEAD)


def attend(combo, chunk, qn, own, halos, masks, heads=4):
    groups, nw, inner = qn.shape
    width = own[0].shape[-1]
    lanes = heads * HEAD
    steps = width // lanes
    kv_spec = pl.BlockSpec((2, 2, nw, lanes), lambda i, *_: (0, 0, 0, i))
    return pl.pallas_call(
        functools.partial(attend_kernel, heads, HEAD**-0.5),
        grid_spec=pltpu.PrefetchScalarGridSpec(
            num_scalar_prefetch=1,
            grid=(steps,),
            in_specs=[pl.BlockSpec((groups, nw, lanes), lambda i, *_: (0, 0, chunk * steps + i))]
            + [kv_spec] * 8
            + [pl.BlockSpec(masks.shape, lambda i, *_: (0, 0, 0, 0))],
            out_specs=pl.BlockSpec((groups, nw, lanes), lambda i, *_: (0, 0, i)),
        ),
        out_shape=jax.ShapeDtypeStruct((groups, nw, width), BF16),
        compiler_params=params(),
        cost_estimate=pl.CostEstimate(flops=4 * 128 * 384 * width, bytes_accessed=32 << 20, transcendentals=0),
        name="attend",
    )(combo, qn, *own, *halos, masks)


def project_kernel(a0, a1, a2, a3, w_ref, o0, o1, o2, o3, acc):
    k = pl.program_id(0)
    a = jnp.concatenate([a0[...], a1[...], a2[...], a3[...]], axis=0)
    half = w_ref.shape[-1]
    for n in range(2):
        cols = slice(n * half, (n + 1) * half)
        term = jnp.dot(a, w_ref[n], preferred_element_type=F32)

        @pl.when(k == 0)
        def _():
            acc[:, cols] = term

        @pl.when(k > 0)
        def _():
            acc[:, cols] += term

    @pl.when(k == pl.num_programs(0) - 1)
    def _():
        rows = a0.shape[0]
        for d, o in enumerate((o0, o1, o2, o3)):
            o[...] = acc[d * rows : (d + 1) * rows, :].astype(BF16)


def project(blocks, weight, step=1024):
    rows, inner = blocks[0].shape
    cols = 2 * weight.shape[-1]
    return pl.pallas_call(
        project_kernel,
        grid=(inner // step,),
        in_specs=[pl.BlockSpec((rows, step), lambda k: (0, k))] * 4
        + [pl.BlockSpec((2, step, cols // 2), lambda k: (0, k, 0))],
        out_specs=[pl.BlockSpec((rows, cols), lambda k: (0, 0))] * 4,
        out_shape=[jax.ShapeDtypeStruct((rows, cols), BF16)] * 4,
        scratch_shapes=[pltpu.VMEM((4 * rows, cols), F32)],
        compiler_params=params(),
        cost_estimate=pl.CostEstimate(flops=8 * rows * inner * cols, bytes_accessed=20 << 20, transcendentals=0),
        name="project",
    )(*blocks, weight)


def finish_kernel(x_ref, hidden, gate, p0, p1, p2, p3, out):
    cols = p0.shape[-1] // 2
    for d, p in enumerate((p0, p1, p2, p3)):
        x = lax.rem(x_ref[0] + d, 4)
        for n in range(2):
            where = pl.ds(pl.multiple_of((n * 4 + x) * cols, HEAD), cols)
            term = gate[:, where] * p[:, n * cols : (n + 1) * cols].astype(F32)
            out[:, where] = (hidden[:, where].astype(F32) + term).astype(BF16)


def finish(x, hidden, gate, pieces, blocks=4):
    rows, width = hidden.shape
    step = rows // blocks
    row_spec = pl.BlockSpec((step, width), lambda i, *_: (i, 0))
    return pl.pallas_call(
        finish_kernel,
        grid_spec=pltpu.PrefetchScalarGridSpec(
            num_scalar_prefetch=1,
            grid=(blocks,),
            in_specs=[row_spec, pl.BlockSpec((1, width), lambda i, *_: (0, 0))]
            + [pl.BlockSpec((step, pieces[0].shape[1]), lambda i, *_: (i, 0))] * 4,
            out_specs=row_spec,
        ),
        out_shape=jax.ShapeDtypeStruct(hidden.shape, BF16),
        compiler_params=params(),
        name="finish",
    )(x, hidden, gate[None], *pieces)


def shards(hidden_in, queries, keys, values, query_gain, key_gain, reach_time, reach_rows, reach_cols, out_weight, gate):
    frames, rows, nw, inner = queries.shape
    width = hidden_in.shape[3]
    weight = lax.all_gather(out_weight, ("y_lo",) + SP, axis=0, tiled=True)
    weight = weight.reshape(2, inner, out_weight.shape[1])

    tokens = [a.reshape(frames * rows, nw, inner) for a in (queries, keys, values)]
    qn, *own = prepare(*tokens, query_gain, key_gain)
    masks = mask_tables(
        lax.axis_index(TM) * frames,
        lax.axis_index(SP) * rows,
        frames * axis_size(TM),
        rows * axis_size(SP),
        nw,
    )
    combo = reach_time * 6 + reach_rows * 3 + reach_cols
    heads = reach_time.shape[0] // CHUNKS
    outs = []
    for c in range(CHUNKS):
        f0, f1, r0, r1 = own[4 * c : 4 * c + 4]
        hb, ha = passed_along(f1, TM, 1), passed_along(f0, TM, -1)
        rb, ra = passed_along(r1, SP, 1), passed_along(r0, SP, -1)
        cb = passed_along(jnp.stack([hb[:, 1], ha[:, 1]]), SP, 1)
        ca = passed_along(jnp.stack([hb[:, 0], ha[:, 0]]), SP, -1)
        a = attend(combo[c * heads : (c + 1) * heads], c, qn, (f0, f1), (hb, ha, rb, ra, cb, ca), masks)
        outs.append(a.reshape(frames * rows * nw, inner // CHUNKS))
    a = outs[0]
    blocks = [a] + [shifted(a, "x", d) for d in (1, 2, 3)]
    terms = project(blocks, weight)
    pieces = [terms[0]] + [shifted(terms[d], "x", -d) for d in (1, 2, 3)]
    x = lax.axis_index("x").astype(jnp.int32)[None]
    out = finish(x, hidden_in.reshape(-1, width), gate, pieces)
    return out.reshape(hidden_in.shape)


def solution(mesh):
    inner_mesh = Mesh(mesh.devices.reshape(2, 4, 2, 8, 2), TM + SP)
    tokens = P(TM, SP, None, None)
    in_specs = (tokens,) * 4 + (P(),) * 5 + (P(SP, TM), P())
    return jax.shard_map(shards, mesh=inner_mesh, in_specs=in_specs, out_specs=tokens, check_vma=False)
```

time: 322 us -> 240 us (0.75)
  waiting for transfers between devices: 180 us -> 107 us
  Pallas kernels: 0 us -> 48 us
  starting transfers between devices: 13.5 us -> 52.4 us
  blocking collectives: 32.6 us -> 0 us
  matrix products: 24.6 us -> 0 us
  other arithmetic: 26.1 us -> 3.02 us
  local copies, waits for them, and re-layouts: 27.9 us -> 15 us
    all_gather x2 -> x1, waiting for transfers between devices: 116 us -> 22.2 us  [shards(): weight = lax.all_gather(out_weight, ('y_lo',) + SP, axis=0, tiled=True)]
    pallas_call x0 -> x4, Pallas kernels: none -> 48 us  [the longest x1 24.7 us: attend(): pl.pallas_call(functools.partial(attend_kernel, heads, HEAD ** (-0.5)), g...]
    ppermute x4 -> x12, starting transfers between devices: 13.5 us -> 52.3 us  [the longest x6 32.5 us: shifted(): lax.ppermute(block, axis, [(i, (i + distance) % n) for i in range(n)])]
    all_to_all x1 -> x0, blocking collectives: 32.6 us -> none  [shards(): lax.all_to_all(group_terms, 'tm', split_axis=0, concat_axis=1, tiled=True)]
    dot_general x3 -> x0, matrix products: 24.6 us -> none  [the longest x1 12.6 us: shards(): jnp.dot(lax.all_gather(attention, 'tm', axis=0, tiled=True), gathered_row...]
    ppermute x4 -> x12, waiting for transfers between devices: 63.3 us -> 84.2 us  [the longest x6 53.2 us: shifted(): lax.ppermute(block, axis, [(i, (i + distance) % n) for i in range(n)])]
    slice x2 -> x0, local copies, waits for them, and re-layouts: 12.1 us -> none  [the longest x1 9.29 us: shards(): region[1]]
    concatenate x2 -> x0, other arithmetic: 11.8 us -> none  [the longest x1 8.98 us: shards(): region = jnp.concatenate([below_rows, framed, above_rows], axis=2)]
  transfers between devices with their start and end apart: 6 -> 13, of which waited for: 6 -> 10; matrix products, arithmetic and copies ran while one was open for 17% -> 6% of each run, Pallas kernels for 0% -> 13%
where the time goes in v1:
time: 240 us; the launch traced here: 239 us
  waiting for transfers between devices  107 us (45%)
  starting transfers between devices  52.4 us (22%)
  Pallas kernels  48 us (20%)
  local copies, waits for them, and re-layouts  15 us (6%)
  between operations  13.7 us (6%)
  other arithmetic  3.02 us (1%)
    ppermute x6, waiting for transfers between devices, shifted(): lax.ppermute(block, axis, [(i, (i + distance) % n) for i in range(n)])  53.2 us
    ppermute x6, starting transfers between devices, shifted(): lax.ppermute(block, axis, [(i, (i + distance) % n) for i in range(n)])  32.5 us
    ppermute x6, waiting for transfers between devices, passed_along(): return lax.ppermute(block, axes, route)  31 us
    pallas_call x1, Pallas kernels, attend(): pl.pallas_call(functools.partial(attend_kernel, heads, HEAD ** (-0.5)), g...  24.7 us
    all_gather x1, waiting for transfers between devices, shards(): weight = lax.all_gather(out_weight, ('y_lo',) + SP, axis=0, tiled=True)  22.2 us
    ppermute x6, starting transfers between devices, passed_along(): return lax.ppermute(block, axes, route)  19.8 us
    pallas_call x1, Pallas kernels, project(): pl.pallas_call(project_kernel, grid=(inner // step,), in_specs=[pl.BlockS...  15.9 us
    pallas_call x1, Pallas kernels, prepare(): pl.pallas_call(prepare_kernel, grid=(groups,), in_specs=[token_spec] * 3...  5.64 us
  transfers between devices with their start and end apart: 13, of which 10 were waited for; matrix products, arithmetic and copies ran while one was open for 6% of the time, Pallas kernels for 13%

profile of v1, /device:TPU:1, one launch (start us, length us, event | category | flops | bytes accessed | tf_op | source)
XLA Modules:
  0.0 239.3 jit_solution(16869139186033247688)
XLA Ops:
  8.7 5.6 %prepare.1 = (bf16[4,32,5120]{2,1,0:T(8,128)(2,1)S(1)}, bf16[2,2,32,5120]{3,2,1,0:T(8,128)(2,1)S(1)}, bf16[2,2,32,5120]{3,2,1,0:T(8,128)(2,1)S(1)}, bf16[2,2,32,...) custom-call(bf16[4,32,5120]{2,1,0:T(8,128)(2,1)} %bitcast.27, bf16[4,32,5120]{2,1,0:T(8,128)(2,1)} %bitcast.28, ...), custom_call_target="tpu_custom_call" | custom-call | bytes 12582912 | tf_op jit(solution)/shard_map/prepare/pallas_call | solution.py:88
  15.5 5.0 %collective-permute-start = (bf16[2,2,32,5120]{3,2,0,1:T(8,128)(2,1)}, bf16[2,2,32,5120]{3,2,0,1:T(8,128)(2,1)}, u32[]{:S(2)}, u32[]{:S(2)}) collective-permute-start(bf16[2,2,32,5120]{3,2,0,1:T(8,128)(2,1)} %copy.12), channel_id=1, source_target_pairs={{0,32},{32,64},{64,96},{96,128},{128,160},{160,192},{192,224},{1,3... | collective-permute-start | bytes 3932168 | tf_op jit(solution)/shard_map/ppermute | solution.py:29
  23.0 4.4 %collective-permute-start.2 = (bf16[2,2,32,5120]{3,2,1,0:T(8,128)(2,1)}, bf16[2,2,32,5120]{3,2,1,0:T(8,128)(2,1)}, u32[]{:S(2)}, u32[]{:S(2)}) collective-permute-start(bf16[2,2,32,5120]{3,2,1,0:T(8,128)(2,1)} %get-tuple-element.17), channel_id=1, source_target_pairs={{0,1},{1,2},{2,3},{3,4},{4,5},{5,6},{6,7},{7,8},{8,9},{9,10},{10,1... | collective-permute-start | bytes 3932168 | tf_op jit(solution)/shard_map/ppermute | solution.py:29
  27.4 1.9 collective-permute-start.3
  29.6 17.6 %collective-permute-done = bf16[2,2,32,5120]{3,2,0,1:T(8,128)(2,1)} collective-permute-done((bf16[2,2,32,5120]{3,2,0,1:T(8,128)(2,1)}, bf16[2,2,32,5120]{3,2,0,1:T(8,128)(2,1)}, u32[]{:S(2)}, u32[]{:S(2)}) %collective-permute-start) | collective-permute-done | bytes 1310752 | tf_op jit(solution)/shard_map/ppermute | solution.py:29
  48.6 4.7 %collective-permute-done.1 = bf16[2,2,32,5120]{3,2,0,1:T(8,128)(2,1)} collective-permute-done((bf16[2,2,32,5120]{3,2,0,1:T(8,128)(2,1)}, bf16[2,2,32,5120]{3,2,0,1:T(8,128)(2,1)}, u32[]{:S(2)}, u32[]{:S(2)}) %collective-permute-start.1) | collective-permute-done | bytes 1310752 | tf_op jit(solution)/shard_map/ppermute | solution.py:29
  54.8 3.8 %collective-permute-start.5 = (bf16[2,2,32,5120]{3,2,1,0:T(8,128)(2,1)S(1)}, bf16[2,2,32,5120]{3,2,1,0:T(8,128)(2,1)S(1)}, u32[]{:S(2)}, u32[]{:S(2)}) collective-permute-start(bf16[2,2,32,5120]{3,2,1,0:T(8,128)(2,1)S(1)} %pad_maximum_fusion.1), channel_id=1, source_target_pairs={{1,0},{2,1},{3,2},{4,3},{5,4},{6,5},{7,6},{8,7},{9,8},{10,9},{11,1... | collective-permute-start | bytes 3932168 | tf_op jit(solution)/shard_map/ppermute | solution.py:29
  58.7 3.4 %collective-permute-start.4 = (bf16[2,2,32,5120]{3,2,1,0:T(8,128)(2,1)S(1)}, bf16[2,2,32,5120]{3,2,1,0:T(8,128)(2,1)S(1)}, u32[]{:S(2)}, u32[]{:S(2)}) collective-permute-start(bf16[2,2,32,5120]{3,2,1,0:T(8,128)(2,1)S(1)} %pad_maximum_fusion), channel_id=1, source_target_pairs={{0,1},{1,2},{2,3},{3,4},{4,5},{5,6},{6,7},{7,8},{8,9},{9,10},{10,1... | collective-permute-start | bytes 3932168 | tf_op jit(solution)/shard_map/ppermute | solution.py:29
  62.1 2.7 %fusion.23.mask_ref = f32[12,2,64,384]{3,2,1,0:T(8,128)} fusion(s32[]{:T(128)S(6)} %sub.68, s32[2]{0:T(128)S(1)} %iota_add_fusion, s32[12]{0:T(128)S(1)} %get-tuple-element.38, s32[12]{0:T(128)S(1)} %get-tuple-element.40, s32[384]{0:T(512)S(1)} %get-tuple-element.28, s32[384]{0:T(512)S(1)} %get-tuple-element.30, s32[64]{0:T(128)S(1)} %get-tuple-element.42, ...), kind=kLoop, calls=%fused_computation.49 | loop fusion | flops 48955392 | bytes 2371152 | tf_op jit(solution)/shard_map/jit(_where)/select_n | solution.py:113
  64.8 2.6 %copy.14.hb = bf16[2,2,32,5120]{3,2,1,0:T(8,128)(2,1)} copy(bf16[2,2,32,5120]{3,2,0,1:T(8,128)(2,1)} %collective-permute-done) | data formatting | bytes 2621440 | tf_op jit(solution)/shard_map/ppermute | solution.py:29
  67.4 2.5 %copy.15.ha = bf16[2,2,32,5120]{3,2,1,0:T(8,128)(2,1)} copy(bf16[2,2,32,5120]{3,2,0,1:T(8,128)(2,1)} %collective-permute-done.1) | data formatting | bytes 2621440 | tf_op jit(solution)/shard_map/ppermute | solution.py:29
  69.9 6.4 %collective-permute-done.5.ca = bf16[2,2,32,5120]{3,2,1,0:T(8,128)(2,1)S(1)} collective-permute-done((bf16[2,2,32,5120]{3,2,1,0:T(8,128)(2,1)S(1)}, bf16[2,2,32,5120]{3,2,1,0:T(8,128)(2,1)S(1)}, u32[]{:S(2)}, u32[]{:S(2)}) %collective-permute-start.5) | collective-permute-done | bytes 1310752 | tf_op jit(solution)/shard_map/ppermute | solution.py:29
  76.3 2.3 collective-permute-done.4.cb
  79.6 24.7 %attend.1 = bf16[4,32,5120]{2,1,0:T(8,128)(2,1)S(1)} custom-call(s32[40]{0:T(128)S(1)} %add_add_fusion.combo_ref, bf16[4,32,5120]{2,1,0:T(8,128)(2,1)S(1)} %copy-done.1, bf16[2,2,32,5120]{3,2,1,0:T(8,128)(2,1)S(1)} %get-tuple-element.15.f0, bf16[2,2,32,5120]{3,2,1,0:T(8,128)(2,1)S(1)} %get-tuple-element.16.f1, bf16[2,2,32,5120]{3,2,1,0:T(8,128)(2,1)} %copy.14.hb, ...), custom_call_target="tpu_custom_call" | custom-call | flops 1006632960 | bytes 33554432 | tf_op jit(solution)/shard_map/attend/pallas_call | solution.py:151
  104.3 9.7 %collective-permute-start.6 = (bf16[128,5120]{1,0:T(8,128)(2,1)S(1)}, bf16[128,5120]{1,0:T(8,128)(2,1)S(1)}, u32[]{:S(2)}, u32[]{:S(2)}) collective-permute-start(bf16[128,5120]{1,0:T(8,128)(2,1)S(1)} %bitcast.19), channel_id=1, source_target_pairs={{0,32},{32,64},{64,96},{96,0},{1,33},{33,65},{65,97},{97,1},{2,34}... | collective-permute-start | bytes 3932168 | tf_op jit(solution)/shard_map/ppermute | solution.py:34
  114.0 18.9 %collective-permute-start.7 = (bf16[128,5120]{1,0:T(8,128)(2,1)S(1)}, bf16[128,5120]{1,0:T(8,128)(2,1)S(1)}, u32[]{:S(2)}, u32[]{:S(2)}) collective-permute-start(bf16[128,5120]{1,0:T(8,128)(2,1)S(1)} %bitcast.20), channel_id=1, source_target_pairs={{0,64},{32,96},{64,0},{96,32},{1,65},{33,97},{65,1},{97,33},{2,66}... | collective-permute-start | bytes 3932168 | tf_op jit(solution)/shard_map/ppermute | solution.py:34
  134.0 24.6 %collective-permute-done.6.a1 = bf16[128,5120]{1,0:T(8,128)(2,1)S(1)} collective-permute-done((bf16[128,5120]{1,0:T(8,128)(2,1)S(1)}, bf16[128,5120]{1,0:T(8,128)(2,1)S(1)}, u32[]{:S(2)}, u32[]{:S(2)}) %collective-permute-start.6) | collective-permute-done | bytes 1310752 | tf_op jit(solution)/shard_map/ppermute | solution.py:34
  158.5 14.0 %collective-permute-done.7.a2 = bf16[128,5120]{1,0:T(8,128)(2,1)S(1)} collective-permute-done((bf16[128,5120]{1,0:T(8,128)(2,1)S(1)}, bf16[128,5120]{1,0:T(8,128)(2,1)S(1)}, u32[]{:S(2)}, u32[]{:S(2)}) %collective-permute-start.7) | collective-permute-done | bytes 1310752 | tf_op jit(solution)/shard_map/ppermute | solution.py:34
  172.6 22.2 %all-gather.2.cloned.1.call-done = bf16[10240,640]{1,0:T(8,128)(2,1)} async-done(((bf16[160,640]{1,0:T(8,128)(2,1)}), bf16[10240,640]{1,0:T(8,128)(2,1)}) %all-gather.2.cloned.1.call-update) | async-done | bytes 13107216 | tf_op jit(solution)/shard_map/all_gather | solution.py:240
  196.1 15.9 %project.1 = (bf16[128,1280]{1,0:T(8,128)(2,1)S(1)}, bf16[128,1280]{1,0:T(8,128)(2,1)S(1)}, bf16[128,1280]{1,0:T(8,128)(2,1)S(1)}, bf16[128,1280]{1,0:T(8,128)(2,1)S(1)}) custom-call(bf16[128,5120]{1,0:T(8,128)(2,1)S(1)} %bitcast.22, bf16[128,5120]{1,0:T(8,128)(2,1)S(1)} %collective-permute-done.6.a1, bf16[128,5120]{1,0:T(8,128)(2,1)S(1)} %collective-permute-done.7.a2, ...), custom_call_target="tpu_custom_call" | custom-call | flops 6710886400 | bytes 20971520 | tf_op jit(solution)/shard_map/project/pallas_call | solution.py:194
  212.1 3.8 %collective-permute-start.11 = (bf16[128,1280]{1,0:T(8,128)(2,1)S(1)}, bf16[128,1280]{1,0:T(8,128)(2,1)S(1)}, u32[]{:S(2)}, u32[]{:S(2)}) collective-permute-start(bf16[128,1280]{1,0:T(8,128)(2,1)S(1)} %get-tuple-element.22), channel_id=1, source_target_pairs={{0,32},{32,64},{64,96},{96,0},{1,33},{33,65},{65,97},{97,1},{2,34}... | collective-permute-start | bytes 983048 | tf_op jit(solution)/shard_map/ppermute | solution.py:34
  216.0 6.7 %collective-permute-done.10.p2 = bf16[128,1280]{1,0:T(8,128)(2,1)S(1)} collective-permute-done((bf16[128,1280]{1,0:T(8,128)(2,1)S(1)}, bf16[128,1280]{1,0:T(8,128)(2,1)S(1)}, u32[]{:S(2)}, u32[]{:S(2)}) %collective-permute-start.10) | collective-permute-done | bytes 327712 | tf_op jit(solution)/shard_map/ppermute | solution.py:34
  222.7 7.6 %collective-permute-done.11.p3 = bf16[128,1280]{1,0:T(8,128)(2,1)S(1)} collective-permute-done((bf16[128,1280]{1,0:T(8,128)(2,1)S(1)}, bf16[128,1280]{1,0:T(8,128)(2,1)S(1)}, u32[]{:S(2)}, u32[]{:S(2)}) %collective-permute-start.11) | collective-permute-done | bytes 327712 | tf_op jit(solution)/shard_map/ppermute | solution.py:34
  230.6 1.8 finish.1
  (57 shorter events, 12.7 us)
Async XLA Ops:
  6.5 188.3 %all-gather.2.cloned.1.call-start = ((), (), s32[]{:S(2)}) async-start(), calls=%async_computation | async-start | bytes 13312000 | tf_op jit(solution)/shard_map/all_gather | solution.py:240
  14.4 7.4 %copy-start = (bf16[4,32,5120]{2,1,0:T(8,128)(2,1)}, bf16[4,32,5120]{2,1,0:T(8,128)(2,1)S(1)}, u32[]{:S(2)}) copy-start(bf16[4,32,5120]{2,1,0:T(8,128)(2,1)S(1)} %get-tuple-element.14.q_ref) | copy-start | bytes 3932164
  14.4 15.2 %copy-start.10 = (s32[40]{0:T(128)S(1)}, s32[40]{0:T(128)}, u32[]{:S(2)}) copy-start(s32[40]{0:T(128)} %param.19) | copy-start | bytes 484
  14.4 15.2 %copy-start.11 = (s32[40]{0:T(128)S(1)}, s32[40]{0:T(128)}, u32[]{:S(2)}) copy-start(s32[40]{0:T(128)} %param.18) | copy-start | bytes 484
  14.4 15.2 %copy-start.12 = (s32[40]{0:T(128)S(1)}, s32[40]{0:T(128)}, u32[]{:S(2)}) copy-start(s32[40]{0:T(128)} %param.17) | copy-start | bytes 484
  15.5 31.7 %collective-permute-start = (bf16[2,2,32,5120]{3,2,0,1:T(8,128)(2,1)}, bf16[2,2,32,5120]{3,2,0,1:T(8,128)(2,1)}, u32[]{:S(2)}, u32[]{:S(2)}) collective-permute-start(bf16[2,2,32,5120]{3,2,0,1:T(8,128)(2,1)} %copy.12), channel_id=1, source_target_pairs={{0,32},{32,64},{64,96},{96,128},{128,160},{160,192},{192,224},{1,3... | collective-permute-start | bytes 3932168 | tf_op jit(solution)/shard_map/ppermute | solution.py:29
  21.7 31.5 %collective-permute-start.1 = (bf16[2,2,32,5120]{3,2,0,1:T(8,128)(2,1)}, bf16[2,2,32,5120]{3,2,0,1:T(8,128)(2,1)}, u32[]{:S(2)}, u32[]{:S(2)}) collective-permute-start(bf16[2,2,32,5120]{3,2,0,1:T(8,128)(2,1)} %copy.13), channel_id=1, source_target_pairs={{32,0},{64,32},{96,64},{128,96},{160,128},{192,160},{224,192},{33,... | collective-permute-start | bytes 3932168 | tf_op jit(solution)/shard_map/ppermute | solution.py:29
  23.0 46.9 %collective-permute-start.2 = (bf16[2,2,32,5120]{3,2,1,0:T(8,128)(2,1)}, bf16[2,2,32,5120]{3,2,1,0:T(8,128)(2,1)}, u32[]{:S(2)}, u32[]{:S(2)}) collective-permute-start(bf16[2,2,32,5120]{3,2,1,0:T(8,128)(2,1)} %get-tuple-element.17), channel_id=1, source_target_pairs={{0,1},{1,2},{2,3},{3,4},{4,5},{5,6},{6,7},{7,8},{8,9},{9,10},{10,1... | collective-permute-start | bytes 3932168 | tf_op jit(solution)/shard_map/ppermute | solution.py:29
  27.4 42.5 %collective-permute-start.3 = (bf16[2,2,32,5120]{3,2,1,0:T(8,128)(2,1)}, bf16[2,2,32,5120]{3,2,1,0:T(8,128)(2,1)}, u32[]{:S(2)}, u32[]{:S(2)}) collective-permute-start(bf16[2,2,32,5120]{3,2,1,0:T(8,128)(2,1)} %get-tuple-element.18), channel_id=1, source_target_pairs={{1,0},{2,1},{3,2},{4,3},{5,4},{6,5},{7,6},{8,7},{9,8},{10,9},{11,1... | collective-permute-start | bytes 3932168 | tf_op jit(solution)/shard_map/ppermute | solution.py:29
  54.8 21.5 %collective-permute-start.5 = (bf16[2,2,32,5120]{3,2,1,0:T(8,128)(2,1)S(1)}, bf16[2,2,32,5120]{3,2,1,0:T(8,128)(2,1)S(1)}, u32[]{:S(2)}, u32[]{:S(2)}) collective-permute-start(bf16[2,2,32,5120]{3,2,1,0:T(8,128)(2,1)S(1)} %pad_maximum_fusion.1), channel_id=1, source_target_pairs={{1,0},{2,1},{3,2},{4,3},{5,4},{6,5},{7,6},{8,7},{9,8},{10,9},{11,1... | collective-permute-start | bytes 3932168 | tf_op jit(solution)/shard_map/ppermute | solution.py:29
  58.7 19.9 %collective-permute-start.4 = (bf16[2,2,32,5120]{3,2,1,0:T(8,128)(2,1)S(1)}, bf16[2,2,32,5120]{3,2,1,0:T(8,128)(2,1)S(1)}, u32[]{:S(2)}, u32[]{:S(2)}) collective-permute-start(bf16[2,2,32,5120]{3,2,1,0:T(8,128)(2,1)S(1)} %pad_maximum_fusion), channel_id=1, source_target_pairs={{0,1},{1,2},{2,3},{3,4},{4,5},{5,6},{6,7},{7,8},{8,9},{9,10},{10,1... | collective-permute-start | bytes 3932168 | tf_op jit(solution)/shard_map/ppermute | solution.py:29
  64.8 14.8 %copy-start.1 = (bf16[4,32,5120]{2,1,0:T(8,128)(2,1)S(1)}, bf16[4,32,5120]{2,1,0:T(8,128)(2,1)}, u32[]{:S(2)}) copy-start(bf16[4,32,5120]{2,1,0:T(8,128)(2,1)} %copy-done) | copy-start | bytes 3932164
  76.3 2.3 copy-start.8
  78.6 1.1 copy-start.9
  104.3 54.2 %collective-permute-start.6 = (bf16[128,5120]{1,0:T(8,128)(2,1)S(1)}, bf16[128,5120]{1,0:T(8,128)(2,1)S(1)}, u32[]{:S(2)}, u32[]{:S(2)}) collective-permute-start(bf16[128,5120]{1,0:T(8,128)(2,1)S(1)} %bitcast.19), channel_id=1, source_target_pairs={{0,32},{32,64},{64,96},{96,0},{1,33},{33,65},{65,97},{97,1},{2,34}... | collective-permute-start | bytes 3932168 | tf_op jit(solution)/shard_map/ppermute | solution.py:34
  114.0 58.6 %collective-permute-start.7 = (bf16[128,5120]{1,0:T(8,128)(2,1)S(1)}, bf16[128,5120]{1,0:T(8,128)(2,1)S(1)}, u32[]{:S(2)}, u32[]{:S(2)}) collective-permute-start(bf16[128,5120]{1,0:T(8,128)(2,1)S(1)} %bitcast.20), channel_id=1, source_target_pairs={{0,64},{32,96},{64,0},{96,32},{1,65},{33,97},{65,1},{97,33},{2,66}... | collective-permute-start | bytes 3932168 | tf_op jit(solution)/shard_map/ppermute | solution.py:34
  132.9 39.7 %collective-permute-start.8 = (bf16[128,5120]{1,0:T(8,128)(2,1)S(1)}, bf16[128,5120]{1,0:T(8,128)(2,1)}, u32[]{:S(2)}, u32[]{:S(2)}) collective-permute-start(bf16[128,5120]{1,0:T(8,128)(2,1)S(1)} %bitcast.21), channel_id=1, source_target_pairs={{0,96},{32,0},{64,32},{96,64},{1,97},{33,1},{65,33},{97,65},{2,98}... | collective-permute-start | bytes 3932168 | tf_op jit(solution)/shard_map/ppermute | solution.py:34
  132.9 1.1 copy-start.2
  194.8 1.3 copy-start.3
  196.1 34.4 %copy-start.4 = (bf16[2,2,32,5120]{3,2,1,0:T(8,128)(2,1)S(1)}, bf16[2,2,32,5120]{3,2,1,0:T(8,128)(2,1)}, u32[]{:S(2)}) copy-start(bf16[2,2,32,5120]{3,2,1,0:T(8,128)(2,1)} %param.11) | copy-start | bytes 3932164
  196.1 34.4 %copy-start.5 = (f32[5120]{0:T(1024)S(1)}, f32[5120]{0:T(1024)}, u32[]{:S(2)}) copy-start(f32[5120]{0:T(1024)} %param.21) | copy-start | bytes 61444
  212.0 10.7 %collective-permute-start.10 = (bf16[128,1280]{1,0:T(8,128)(2,1)S(1)}, bf16[128,1280]{1,0:T(8,128)(2,1)S(1)}, u32[]{:S(2)}, u32[]{:S(2)}) collective-permute-start(bf16[128,1280]{1,0:T(8,128)(2,1)S(1)} %get-tuple-element.21), channel_id=1, source_target_pairs={{0,64},{32,96},{64,0},{96,32},{1,65},{33,97},{65,1},{97,33},{2,66}... | collective-permute-start | bytes 983048 | tf_op jit(solution)/shard_map/ppermute | solution.py:34
  212.1 18.2 %collective-permute-start.11 = (bf16[128,1280]{1,0:T(8,128)(2,1)S(1)}, bf16[128,1280]{1,0:T(8,128)(2,1)S(1)}, u32[]{:S(2)}, u32[]{:S(2)}) collective-permute-start(bf16[128,1280]{1,0:T(8,128)(2,1)S(1)} %get-tuple-element.22), channel_id=1, source_target_pairs={{0,32},{32,64},{64,96},{96,0},{1,33},{33,65},{65,97},{97,1},{2,34}... | collective-permute-start | bytes 983048 | tf_op jit(solution)/shard_map/ppermute | solution.py:34
  216.0 14.6 %collective-permute-start.9 = (bf16[128,1280]{1,0:T(8,128)(2,1)S(1)}, bf16[128,1280]{1,0:T(8,128)(2,1)S(1)}, u32[]{:S(2)}, u32[]{:S(2)}) collective-permute-start(bf16[128,1280]{1,0:T(8,128)(2,1)S(1)} %get-tuple-element.20), channel_id=1, source_target_pairs={{0,96},{32,0},{64,32},{96,64},{1,97},{33,1},{65,33},{97,65},{2,98}... | collective-permute-start | bytes 983048 | tf_op jit(solution)/shard_map/ppermute | solution.py:34
  (2 other events, 1.5 us)
Sparse Core Ops, SparseCore 0:
  9.2 185.5 all-gather.1

commit v2 on v1

--- a/solution.py
+++ b/solution.py
@@ -34,7 +34,7 @@
     return lax.ppermute(block, axis, [(i, (i + distance) % n) for i in range(n)])
 
 
-def params(megabytes=48):
+def params(megabytes=24):
     return pltpu.CompilerParams(vmem_limit_bytes=megabytes << 20)
 
 
@@ -60,7 +60,7 @@
             @pl.when(f == which)
             def _(ref=ref):
                 ref[0, 0] = kn[:, lanes]
-                ref[1, 0] = v[:, lanes]
+                ref[0, 1] = v[:, lanes]
 
         for which, ref in ((0, r0), (1, r1)):
 
@@ -80,8 +80,8 @@
     for _ in range(CHUNKS):
         out_shape += [jax.ShapeDtypeStruct((2, 2, nw, width), BF16)] * 4
         out_specs += [
-            pl.BlockSpec((2, 1, nw, width), lambda i: (0, jnp.minimum(i, 1), 0, 0)),
-            pl.BlockSpec((2, 1, nw, width), lambda i: (0, jnp.maximum(i - 2, 0), 0, 0)),
+            pl.BlockSpec((1, 2, nw, width), lambda i: (jnp.minimum(i, 1), 0, 0, 0)),
+            pl.BlockSpec((1, 2, nw, width), lambda i: (jnp.maximum(i - 2, 0), 0, 0, 0)),
             pl.BlockSpec((1, 2, nw, width), lambda i: (i // 2, 0, 0, 0)),
             pl.BlockSpec((1, 2, nw, width), lambda i: (i // 2, 0, 0, 0)),
         ]
@@ -113,7 +113,7 @@
     return jnp.where(allowed, 0.0, -jnp.inf).astype(F32)
 
 
-def attend_kernel(heads, scale, combo_ref, q_ref, f0, f1, hb, ha, rb, ra, cb, ca, mask_ref, out_ref):
+def attend_kernel(heads, scale, combo_ref, q_ref, f0, f1, hb, ha, rb, ra, cb, ca, mask_ref, *out_refs):
     step = pl.program_id(0)
     for h in range(heads):
         lanes = slice(h * HEAD, (h + 1) * HEAD)
@@ -123,7 +123,7 @@
             frames = ((cb[0], hb, ca[0]), (rb[0], f0, ra[0]), (rb[1], f1, ra[1]), (cb[1], ha, ca[1]))
             parts = []
             for below, own, above in frames:
-                parts += [below[kv, :, lanes], own[kv, 0, :, lanes], own[kv, 1, :, lanes], above[kv, :, lanes]]
+                parts += [below[kv, :, lanes], own[0, kv, :, lanes], own[1, kv, :, lanes], above[kv, :, lanes]]
             return jnp.concatenate(parts, axis=0)
 
         keys, values = region(0), region(1)
@@ -139,7 +139,7 @@
             w = jnp.exp((s - peak) * scale)
             total = jnp.sum(w, axis=1, keepdims=True)
             o = jnp.dot(w.astype(BF16), values[first : first + span], preferred_element_type=F32)
-            out_ref[2 * f : 2 * f + 2, :, lanes] = (o / total).astype(BF16).reshape(2, -1, HEAD)
+            out_refs[f][:, lanes] = (o / total).astype(BF16)
 
 
 def attend(combo, chunk, qn, own, halos, masks, heads=4):
@@ -156,22 +156,23 @@
             in_specs=[pl.BlockSpec((groups, nw, lanes), lambda i, *_: (0, 0, chunk * steps + i))]
             + [kv_spec] * 8
             + [pl.BlockSpec(masks.shape, lambda i, *_: (0, 0, 0, 0))],
-            out_specs=pl.BlockSpec((groups, nw, lanes), lambda i, *_: (0, 0, i)),
+            out_specs=[pl.BlockSpec((2 * nw, lanes), lambda i, *_: (0, i))] * 2,
         ),
-        out_shape=jax.ShapeDtypeStruct((groups, nw, width), BF16),
+        out_shape=[jax.ShapeDtypeStruct((2 * nw, width), BF16)] * 2,
         compiler_params=params(),
         cost_estimate=pl.CostEstimate(flops=4 * 128 * 384 * width, bytes_accessed=32 << 20, transcendentals=0),
         name="attend",
     )(combo, qn, *own, *halos, masks)
 
 
-def project_kernel(a0, a1, a2, a3, w_ref, o0, o1, o2, o3, acc):
+def project_kernel(blocks, *refs):
+    ins, w_ref, outs, acc = refs[:blocks], refs[blocks], refs[blocks + 1 : -1], refs[-1]
     k = pl.program_id(0)
-    a = jnp.concatenate([a0[...], a1[...], a2[...], a3[...]], axis=0)
+    a = jnp.concatenate([i[...] for i in ins], axis=0)
     half = w_ref.shape[-1]
     for n in range(2):
         cols = slice(n * half, (n + 1) * half)
-        term = jnp.dot(a, w_ref[n], preferred_element_type=F32)
+        term = jnp.dot(a, w_ref[0, n], preferred_element_type=F32)
 
         @pl.when(k == 0)
         def _():
@@ -183,24 +184,27 @@
 
     @pl.when(k == pl.num_programs(0) - 1)
     def _():
-        rows = a0.shape[0]
-        for d, o in enumerate((o0, o1, o2, o3)):
+        rows = outs[0].shape[0]
+        for d, o in enumerate(outs):
             o[...] = acc[d * rows : (d + 1) * rows, :].astype(BF16)
 
 
-def project(blocks, weight, step=1024):
+def project(blocks, weight, step=1280):
     rows, inner = blocks[0].shape
-    cols = 2 * weight.shape[-1]
-    return pl.pallas_call(
-        project_kernel,
-        grid=(inner // step,),
-        in_specs=[pl.BlockSpec((rows, step), lambda k: (0, k))] * 4
-        + [pl.BlockSpec((2, step, cols // 2), lambda k: (0, k, 0))],
-        out_specs=[pl.BlockSpec((rows, cols), lambda k: (0, 0))] * 4,
-        out_shape=[jax.ShapeDtypeStruct((rows, cols), BF16)] * 4,
-        scratch_shapes=[pltpu.VMEM((4 * rows, cols), F32)],
-        compiler_params=params(),
-        cost_estimate=pl.CostEstimate(flops=8 * rows * inner * cols, bytes_accessed=20 << 20, transcendentals=0),
+    groups, halves, depth, half = weight.shape
+    cols, devices, inside = halves * half, len(blocks) // 2, depth // step
+    return pl.pallas_call(
+        functools.partial(project_kernel, len(blocks)),
+        grid=(groups * inside,),
+        in_specs=[pl.BlockSpec((rows, step), lambda k: (0, k))] * len(blocks)
+        + [pl.BlockSpec((1, halves, step, half), lambda k: (k // inside, 0, k % inside, 0))],
+        out_specs=[pl.BlockSpec((2 * rows, cols), lambda k: (0, 0))] * devices,
+        out_shape=[jax.ShapeDtypeStruct((2 * rows, cols), BF16)] * devices,
+        scratch_shapes=[pltpu.VMEM((2 * devices * rows, cols), F32)],
+        compiler_params=params(),
+        cost_estimate=pl.CostEstimate(
+            flops=4 * devices * rows * inner * cols, bytes_accessed=2 * inner * cols, transcendentals=0
+        ),
         name="project",
     )(*blocks, weight)
 
@@ -237,8 +241,8 @@
 def shards(hidden_in, queries, keys, values, query_gain, key_gain, reach_time, reach_rows, reach_cols, out_weight, gate):
     frames, rows, nw, inner = queries.shape
     width = hidden_in.shape[3]
-    weight = lax.all_gather(out_weight, ("y_lo",) + SP, axis=0, tiled=True)
-    weight = weight.reshape(2, inner, out_weight.shape[1])
+    weight = lax.all_gather(out_weight, ("y_hi", "y_lo", "z", "core"), axis=0, tiled=True)
+    weight = weight.reshape(2, 2, inner // 2, out_weight.shape[1])
 
     tokens = [a.reshape(frames * rows, nw, inner) for a in (queries, keys, values)]
     qn, *own = prepare(*tokens, query_gain, key_gain)
@@ -256,14 +260,17 @@
         f0, f1, r0, r1 = own[4 * c : 4 * c + 4]
         hb, ha = passed_along(f1, TM, 1), passed_along(f0, TM, -1)
         rb, ra = passed_along(r1, SP, 1), passed_along(r0, SP, -1)
-        cb = passed_along(jnp.stack([hb[:, 1], ha[:, 1]]), SP, 1)
-        ca = passed_along(jnp.stack([hb[:, 0], ha[:, 0]]), SP, -1)
+        cb = passed_along(jnp.stack([hb[1], ha[1]]), SP, 1)
+        ca = passed_along(jnp.stack([hb[0], ha[0]]), SP, -1)
         a = attend(combo[c * heads : (c + 1) * heads], c, qn, (f0, f1), (hb, ha, rb, ra, cb, ca), masks)
-        outs.append(a.reshape(frames * rows * nw, inner // CHUNKS))
-    a = outs[0]
-    blocks = [a] + [shifted(a, "x", d) for d in (1, 2, 3)]
-    terms = project(blocks, weight)
-    pieces = [terms[0]] + [shifted(terms[d], "x", -d) for d in (1, 2, 3)]
+        outs.append(a)
+    a0, a1 = outs[0]
+    left0, right1 = shifted(a0, "x", 1), shifted(a1, "x", -1)
+    left1, right0 = shifted(a1, "x", 1), shifted(a0, "x", -1)
+    far0, far1 = shifted(left0, "x", 1), shifted(right1, "x", -1)
+    mine, near_left, near_right = project([a0, a1, left0, left1, right0, right1], weight)
+    (far,) = project([far0, far1], weight)
+    pieces = [mine, shifted(near_left, "x", -1), shifted(far, "x", 2), shifted(near_right, "x", 1)]
     x = lax.axis_index("x").astype(jnp.int32)[None]
     out = finish(x, hidden_in.reshape(-1, width), gate, pieces)
     return out.reshape(hidden_in.shape)

time: 240 us -> 211 us (0.88)
  waiting for transfers between devices: 107 us -> 76.5 us
  starting transfers between devices: 52.4 us -> 55.2 us
    ppermute x6 -> x9, waiting for transfers between devices: 53.2 us -> 31.7 us  [shifted(): lax.ppermute(block, axis, [(i, (i + distance) % n) for i in range(n)])]
    all_gather x1, waiting for transfers between devices: 22.2 us -> 4.42 us  [shards(): lax.all_gather(out_weight, ('y_hi', 'y_lo', 'z', 'core'), axis=0, tiled=T...]
    unnamed x26 -> x40, local copies, waits for them, and re-layouts: 4.9 us -> 17 us
    ppermute x6, waiting for transfers between devices: 31 us -> 39.6 us  [passed_along(): return lax.ppermute(block, axes, route)]
    ppermute x2 -> x0, local copies, waits for them, and re-layouts: 5.09 us -> none  [passed_along(): return lax.ppermute(block, axes, route)]
    ppermute x6 -> x9, starting transfers between devices: 32.5 us -> 36.2 us  [shifted(): lax.ppermute(block, axis, [(i, (i + distance) % n) for i in range(n)])]
    another operation x2 -> x0, local copies, waits for them, and re-layouts: 2.74 us -> none  [shards(): ca = passed_along(jnp.stack([hb[:, 0], ha[:, 0]]), SP, -1)]
    pallas_call x1 -> x2, Pallas kernels: 15.9 us -> 17 us  [project(): pl.pallas_call(functools.partial(project_kernel, len(blocks)), grid=(grou...]
  transfers between devices with their start and end apart: 13 -> 16, of which waited for: 10 -> 9; matrix products, arithmetic and copies ran while one was open for 6% -> 1% of each run, Pallas kernels for 13% -> 21%
where the time goes in v2:
time: 211 us
  waiting for transfers between devices  76.5 us (36%)
  starting transfers between devices  55.2 us (26%)
  Pallas kernels  46.7 us (22%)
  local copies, waits for them, and re-layouts  17.2 us (8%)
  between operations  13.7 us (6%)
    ppermute x6, waiting for transfers between devices, passed_along(): return lax.ppermute(block, axes, route)  39.6 us
    ppermute x9, starting transfers between devices, shifted(): lax.ppermute(block, axis, [(i, (i + distance) % n) for i in range(n)])  36.2 us
    ppermute x9, waiting for transfers between devices, shifted(): lax.ppermute(block, axis, [(i, (i + distance) % n) for i in range(n)])  31.7 us
    pallas_call x1, Pallas kernels, attend(): pl.pallas_call(functools.partial(attend_kernel, heads, HEAD ** (-0.5)), g...  23.9 us
    ppermute x6, starting transfers between devices, passed_along(): return lax.ppermute(block, axes, route)  19 us
    unnamed x40, local copies, waits for them, and re-layouts  17 us
    pallas_call x2, Pallas kernels, project(): pl.pallas_call(functools.partial(project_kernel, len(blocks)), grid=(grou...  17 us
    all_gather x1, waiting for transfers between devices, shards(): lax.all_gather(out_weight, ('y_hi', 'y_lo', 'z', 'core'), axis=0, tiled=T...  4.42 us
  transfers between devices with their start and end apart: 16, of which 9 were waited for; matrix products, arithmetic and copies ran while one was open for 1% of the time, Pallas kernels for 21%

profile of v2, /device:TPU:1, one launch (start us, length us, event | category | flops | bytes accessed | tf_op | source)
XLA Modules:
  0.0 210.5 jit_solution(7499829902910451399)
XLA Ops:
  8.6 1.3 copy-done.4
  12.7 4.0 %prepare.1 = (bf16[4,32,5120]{2,1,0:T(8,128)(2,1)S(1)}, bf16[2,2,32,5120]{3,2,1,0:T(8,128)(2,1)}, bf16[2,2,32,5120]{3,2,1,0:T(8,128)(2,1)}, bf16[2,2,32,5120]{3,2,1,0:T(8,128)(2,1)}, bf16[2,2,32,5120]{3,2,1,0:T(8,128)(2,1)}) custom-call(bf16[4,32,5120]{2,1,0:T(8,128)(2,1)S(1)} %bitcast.13, bf16[4,32,5120]{2,1,0:T(8,128)(2,1)S(1)} %bitcast.14, ...), custom_call_target="tpu_custom_call" | custom-call | bytes 12582912 | tf_op jit(solution)/shard_map/prepare/pallas_call | solution.py:88
  17.8 4.0 %collective-permute-start = (bf16[2,2,32,5120]{3,2,1,0:T(8,128)(2,1)}, bf16[2,2,32,5120]{3,2,1,0:T(8,128)(2,1)S(1)}, u32[]{:S(2)}, u32[]{:S(2)}) collective-permute-start(bf16[2,2,32,5120]{3,2,1,0:T(8,128)(2,1)} %get-tuple-element.17.f1), channel_id=1, source_target_pairs={{0,32},{32,64},{64,96},{96,128},{128,160},{160,192},{192,224},{1,3... | collective-permute-start | bytes 3932168 | tf_op jit(solution)/shard_map/ppermute | solution.py:29
  23.1 4.4 %collective-permute-start.2 = (bf16[2,2,32,5120]{3,2,1,0:T(8,128)(2,1)}, bf16[2,2,32,5120]{3,2,1,0:T(8,128)(2,1)}, u32[]{:S(2)}, u32[]{:S(2)}) collective-permute-start(bf16[2,2,32,5120]{3,2,1,0:T(8,128)(2,1)} %get-tuple-element.18), channel_id=1, source_target_pairs={{0,1},{1,2},{2,3},{3,4},{4,5},{5,6},{6,7},{7,8},{8,9},{9,10},{10,1... | collective-permute-start | bytes 3932168 | tf_op jit(solution)/shard_map/ppermute | solution.py:29
  27.5 1.9 collective-permute-start.3
  29.7 23.6 %collective-permute-done.1.ha = bf16[2,2,32,5120]{3,2,1,0:T(8,128)(2,1)S(1)} collective-permute-done((bf16[2,2,32,5120]{3,2,1,0:T(8,128)(2,1)}, bf16[2,2,32,5120]{3,2,1,0:T(8,128)(2,1)S(1)}, u32[]{:S(2)}, u32[]{:S(2)}) %collective-permute-start.1) | collective-permute-done | bytes 1310752 | tf_op jit(solution)/shard_map/ppermute | solution.py:29
  53.5 5.3 %collective-permute-start.4 = (bf16[2,2,32,5120]{3,2,1,0:T(8,128)(2,1)S(1)}, bf16[2,2,32,5120]{3,2,1,0:T(8,128)(2,1)S(1)}, u32[]{:S(2)}, u32[]{:S(2)}) collective-permute-start(bf16[2,2,32,5120]{3,2,1,0:T(8,128)(2,1)S(1)} %pad_maximum_fusion), channel_id=1, source_target_pairs={{0,1},{1,2},{2,3},{3,4},{4,5},{5,6},{6,7},{7,8},{8,9},{9,10},{10,1... | collective-permute-start | bytes 3932168 | tf_op jit(solution)/shard_map/ppermute | solution.py:29
  59.0 2.1 collective-permute-start.5
  62.0 11.4 %collective-permute-done.4.cb = bf16[2,2,32,5120]{3,2,1,0:T(8,128)(2,1)S(1)} collective-permute-done((bf16[2,2,32,5120]{3,2,1,0:T(8,128)(2,1)S(1)}, bf16[2,2,32,5120]{3,2,1,0:T(8,128)(2,1)S(1)}, u32[]{:S(2)}, u32[]{:S(2)}) %collective-permute-start.4) | collective-permute-done | bytes 1310752 | tf_op jit(solution)/shard_map/ppermute | solution.py:29
  73.4 4.7 %collective-permute-done.5.ca = bf16[2,2,32,5120]{3,2,1,0:T(8,128)(2,1)S(1)} collective-permute-done((bf16[2,2,32,5120]{3,2,1,0:T(8,128)(2,1)S(1)}, bf16[2,2,32,5120]{3,2,1,0:T(8,128)(2,1)S(1)}, u32[]{:S(2)}, u32[]{:S(2)}) %collective-permute-start.5) | collective-permute-done | bytes 1310752 | tf_op jit(solution)/shard_map/ppermute | solution.py:29
  78.0 23.9 %attend.1 = (bf16[64,5120]{1,0:T(8,128)(2,1)S(1)}, bf16[64,5120]{1,0:T(8,128)(2,1)S(1)}) custom-call(s32[40]{0:T(128)S(1)} %add_add_fusion.combo_ref, bf16[4,32,5120]{2,1,0:T(8,128)(2,1)S(1)} %copy-done.7, bf16[2,2,32,5120]{3,2,1,0:T(8,128)(2,1)} %get-tuple-element.16.f0, bf16[2,2,32,5120]{3,2,1,0:T(8,128)(2,1)} %get-tuple-element.17.f1, ...), custom_call_target="tpu_custom_call" | custom-call | flops 1006632960 | bytes 33554432 | tf_op jit(solution)/shard_map/attend/pallas_call | solution.py:151
  103.1 25.4 %collective-permute-start.9 = (bf16[64,5120]{1,0:T(8,128)(2,1)S(1)}, bf16[64,5120]{1,0:T(8,128)(2,1)S(1)}, u32[]{:S(2)}, u32[]{:S(2)}) collective-permute-start(bf16[64,5120]{1,0:T(8,128)(2,1)S(1)} %get-tuple-element.21.refs_1_), channel_id=1, source_target_pairs={{0,96},{32,0},{64,32},{96,64},{1,97},{33,1},{65,33},{97,65},{2,98}... | collective-permute-start | bytes 1966088 | tf_op jit(solution)/shard_map/ppermute | solution.py:34
  129.4 2.7 %collective-permute-start.8 = (bf16[64,5120]{1,0:T(8,128)(2,1)S(1)}, bf16[64,5120]{1,0:T(8,128)(2,1)S(1)}, u32[]{:S(2)}, u32[]{:S(2)}) collective-permute-start(bf16[64,5120]{1,0:T(8,128)(2,1)S(1)} %get-tuple-element.20.refs_0_), channel_id=1, source_target_pairs={{0,96},{32,0},{64,32},{96,64},{1,97},{33,1},{65,33},{97,65},{2,98}... | collective-permute-start | bytes 1966088 | tf_op jit(solution)/shard_map/ppermute | solution.py:34
  132.0 10.7 %collective-permute-done.6.refs_2_ = bf16[64,5120]{1,0:T(8,128)(2,1)S(1)} collective-permute-done((bf16[64,5120]{1,0:T(8,128)(2,1)S(1)}, bf16[64,5120]{1,0:T(8,128)(2,1)S(1)}, u32[]{:S(2)}, u32[]{:S(2)}) %collective-permute-start.6) | collective-permute-done | bytes 655392 | tf_op jit(solution)/shard_map/ppermute | solution.py:34
  142.7 3.0 %collective-permute-start.12 = (bf16[64,5120]{1,0:T(8,128)(2,1)S(1)}, bf16[64,5120]{1,0:T(8,128)(2,1)S(1)}, u32[]{:S(2)}, u32[]{:S(2)}) collective-permute-start(bf16[64,5120]{1,0:T(8,128)(2,1)S(1)} %collective-permute-done.9.refs_5_), channel_id=1, source_target_pairs={{0,96},{32,0},{64,32},{96,64},{1,97},{33,1},{65,33},{97,65},{2,98}... | collective-permute-start | bytes 1966088 | tf_op jit(solution)/shard_map/ppermute | solution.py:34
  145.8 4.0 %collective-permute-done.7.refs_3_ = bf16[64,5120]{1,0:T(8,128)(2,1)S(1)} collective-permute-done((bf16[64,5120]{1,0:T(8,128)(2,1)S(1)}, bf16[64,5120]{1,0:T(8,128)(2,1)S(1)}, u32[]{:S(2)}, u32[]{:S(2)}) %collective-permute-start.7) | collective-permute-done | bytes 655392 | tf_op jit(solution)/shard_map/ppermute | solution.py:34
  151.5 4.4 %all-gather.2.cloned.1.call-done = bf16[10240,640]{1,0:T(8,128)(2,1)} async-done(((bf16[160,640]{1,0:T(8,128)(2,1)}), bf16[10240,640]{1,0:T(8,128)(2,1)}) %all-gather.2.cloned.1.call-update) | async-done | bytes 13107216 | tf_op jit(solution)/shard_map/all_gather | solution.py:244
  155.9 4.7 %copy-done = bf16[10240,640]{1,0:T(8,128)(2,1)S(1)} copy-done((bf16[10240,640]{1,0:T(8,128)(2,1)S(1)}, bf16[10240,640]{1,0:T(8,128)(2,1)}, u32[]{:S(2)}) %copy-start) | copy-done | bytes 13107224
  163.9 11.8 %project.2 = (bf16[128,1280]{1,0:T(8,128)(2,1)S(1)}, bf16[128,1280]{1,0:T(8,128)(2,1)S(1)}, bf16[128,1280]{1,0:T(8,128)(2,1)S(1)}) custom-call(bf16[64,5120]{1,0:T(8,128)(2,1)S(1)} %get-tuple-element.20.refs_0_, bf16[64,5120]{1,0:T(8,128)(2,1)S(1)} %copy-done.12, bf16[64,5120]{1,0:T(8,128)(2,1)S(1)} %collective-permute-done.6.refs_2_, ...), custom_call_target="tpu_custom_call" | custom-call | flops 5033164800 | bytes 13107200 | tf_op jit(solution)/shard_map/project/pallas_call | solution.py:196
  175.7 2.7 %collective-permute-start.10 = (bf16[128,1280]{1,0:T(8,128)(2,1)S(1)}, bf16[128,1280]{1,0:T(8,128)(2,1)S(1)}, u32[]{:S(2)}, u32[]{:S(2)}) collective-permute-start(bf16[128,1280]{1,0:T(8,128)(2,1)S(1)} %get-tuple-element.23), channel_id=1, source_target_pairs={{0,96},{32,0},{64,32},{96,64},{1,97},{33,1},{65,33},{97,65},{2,98}... | collective-permute-start | bytes 983048 | tf_op jit(solution)/shard_map/ppermute | solution.py:34
  178.4 5.2 %project.3 = bf16[128,1280]{1,0:T(8,128)(2,1)S(1)} custom-call(bf16[64,5120]{1,0:T(8,128)(2,1)S(1)} %collective-permute-done.11.refs_0_, bf16[64,5120]{1,0:T(8,128)(2,1)S(1)} %collective-permute-done.12.refs_1_, bf16[2,2,2560,640]{3,2,1,0:T(8,128)(2,1)S(1)} %bitcast.11), custom_call_target="tpu_custom_call" | custom-call | flops 1677721600 | bytes 13107200 | tf_op jit(solution)/shard_map/project/pallas_call | solution.py:196
  185.2 8.8 %collective-permute-done.13.p2 = bf16[128,1280]{1,0:T(8,128)(2,1)S(1)} collective-permute-done((bf16[128,1280]{1,0:T(8,128)(2,1)S(1)}, bf16[128,1280]{1,0:T(8,128)(2,1)S(1)}, u32[]{:S(2)}, u32[]{:S(2)}) %collective-permute-start.13) | collective-permute-done | bytes 327712 | tf_op jit(solution)/shard_map/ppermute | solution.py:34
  194.0 7.9 %collective-permute-done.14.p3 = bf16[128,1280]{1,0:T(8,128)(2,1)S(1)} collective-permute-done((bf16[128,1280]{1,0:T(8,128)(2,1)S(1)}, bf16[128,1280]{1,0:T(8,128)(2,1)S(1)}, u32[]{:S(2)}, u32[]{:S(2)}) %collective-permute-start.14) | collective-permute-done | bytes 327712 | tf_op jit(solution)/shard_map/ppermute | solution.py:34
  201.8 1.8 finish.1
  (74 shorter events, 17.3 us)
Async XLA Ops:
  6.5 23.0 %copy-start.17 = (s32[40]{0:T(128)S(1)}, s32[40]{0:T(128)}, u32[]{:S(2)}) copy-start(s32[40]{0:T(128)} %param.19) | copy-start | bytes 484
  6.5 23.1 %copy-start.18 = (s32[40]{0:T(128)S(1)}, s32[40]{0:T(128)}, u32[]{:S(2)}) copy-start(s32[40]{0:T(128)} %param.18) | copy-start | bytes 484
  6.5 23.1 %copy-start.19 = (s32[40]{0:T(128)S(1)}, s32[40]{0:T(128)}, u32[]{:S(2)}) copy-start(s32[40]{0:T(128)} %param.17) | copy-start | bytes 484
  6.5 149.3 %all-gather.2.cloned.1.call-start = ((), (), s32[]{:S(2)}) async-start(), calls=%async_computation | async-start | bytes 13312000 | tf_op jit(solution)/shard_map/all_gather | solution.py:244
  17.8 35.5 %collective-permute-start = (bf16[2,2,32,5120]{3,2,1,0:T(8,128)(2,1)}, bf16[2,2,32,5120]{3,2,1,0:T(8,128)(2,1)S(1)}, u32[]{:S(2)}, u32[]{:S(2)}) collective-permute-start(bf16[2,2,32,5120]{3,2,1,0:T(8,128)(2,1)} %get-tuple-element.17.f1), channel_id=1, source_target_pairs={{0,32},{32,64},{64,96},{96,128},{128,160},{160,192},{192,224},{1,3... | collective-permute-start | bytes 3932168 | tf_op jit(solution)/shard_map/ppermute | solution.py:29
  21.8 31.4 %collective-permute-start.1 = (bf16[2,2,32,5120]{3,2,1,0:T(8,128)(2,1)}, bf16[2,2,32,5120]{3,2,1,0:T(8,128)(2,1)S(1)}, u32[]{:S(2)}, u32[]{:S(2)}) collective-permute-start(bf16[2,2,32,5120]{3,2,1,0:T(8,128)(2,1)} %get-tuple-element.16.f0), channel_id=1, source_target_pairs={{32,0},{64,32},{96,64},{128,96},{160,128},{192,160},{224,192},{33,... | collective-permute-start | bytes 3932168 | tf_op jit(solution)/shard_map/ppermute | solution.py:29
  23.1 38.9 %collective-permute-start.2 = (bf16[2,2,32,5120]{3,2,1,0:T(8,128)(2,1)}, bf16[2,2,32,5120]{3,2,1,0:T(8,128)(2,1)}, u32[]{:S(2)}, u32[]{:S(2)}) collective-permute-start(bf16[2,2,32,5120]{3,2,1,0:T(8,128)(2,1)} %get-tuple-element.18), channel_id=1, source_target_pairs={{0,1},{1,2},{2,3},{3,4},{4,5},{5,6},{6,7},{7,8},{8,9},{9,10},{10,1... | collective-permute-start | bytes 3932168 | tf_op jit(solution)/shard_map/ppermute | solution.py:29
  27.5 34.5 %collective-permute-start.3 = (bf16[2,2,32,5120]{3,2,1,0:T(8,128)(2,1)}, bf16[2,2,32,5120]{3,2,1,0:T(8,128)(2,1)}, u32[]{:S(2)}, u32[]{:S(2)}) collective-permute-start(bf16[2,2,32,5120]{3,2,1,0:T(8,128)(2,1)} %get-tuple-element.19), channel_id=1, source_target_pairs={{1,0},{2,1},{3,2},{4,3},{5,4},{6,5},{7,6},{8,7},{9,8},{10,9},{11,1... | collective-permute-start | bytes 3932168 | tf_op jit(solution)/shard_map/ppermute | solution.py:29
  53.5 19.8 %collective-permute-start.4 = (bf16[2,2,32,5120]{3,2,1,0:T(8,128)(2,1)S(1)}, bf16[2,2,32,5120]{3,2,1,0:T(8,128)(2,1)S(1)}, u32[]{:S(2)}, u32[]{:S(2)}) collective-permute-start(bf16[2,2,32,5120]{3,2,1,0:T(8,128)(2,1)S(1)} %pad_maximum_fusion), channel_id=1, source_target_pairs={{0,1},{1,2},{2,3},{3,4},{4,5},{5,6},{6,7},{7,8},{8,9},{9,10},{10,1... | collective-permute-start | bytes 3932168 | tf_op jit(solution)/shard_map/ppermute | solution.py:29
  58.8 19.2 %copy-start.7 = (bf16[4,32,5120]{2,1,0:T(8,128)(2,1)S(1)}, bf16[4,32,5120]{2,1,0:T(8,128)(2,1)}, u32[]{:S(2)}) copy-start(bf16[4,32,5120]{2,1,0:T(8,128)(2,1)} %copy-done.6) | copy-start | bytes 3932164
  59.0 19.1 %collective-permute-start.5 = (bf16[2,2,32,5120]{3,2,1,0:T(8,128)(2,1)S(1)}, bf16[2,2,32,5120]{3,2,1,0:T(8,128)(2,1)S(1)}, u32[]{:S(2)}, u32[]{:S(2)}) collective-permute-start(bf16[2,2,32,5120]{3,2,1,0:T(8,128)(2,1)S(1)} %pad_maximum_fusion.1), channel_id=1, source_target_pairs={{1,0},{2,1},{3,2},{4,3},{5,4},{6,5},{7,6},{8,7},{9,8},{10,9},{11,1... | collective-permute-start | bytes 3932168 | tf_op jit(solution)/shard_map/ppermute | solution.py:29
  101.9 40.8 %collective-permute-start.6 = (bf16[64,5120]{1,0:T(8,128)(2,1)S(1)}, bf16[64,5120]{1,0:T(8,128)(2,1)S(1)}, u32[]{:S(2)}, u32[]{:S(2)}) collective-permute-start(bf16[64,5120]{1,0:T(8,128)(2,1)S(1)} %get-tuple-element.20.refs_0_), channel_id=1, source_target_pairs={{0,32},{32,64},{64,96},{96,0},{1,33},{33,65},{65,97},{97,1},{2,34}... | collective-permute-start | bytes 1966088 | tf_op jit(solution)/shard_map/ppermute | solution.py:34
  103.1 39.6 %collective-permute-start.9 = (bf16[64,5120]{1,0:T(8,128)(2,1)S(1)}, bf16[64,5120]{1,0:T(8,128)(2,1)S(1)}, u32[]{:S(2)}, u32[]{:S(2)}) collective-permute-start(bf16[64,5120]{1,0:T(8,128)(2,1)S(1)} %get-tuple-element.21.refs_1_), channel_id=1, source_target_pairs={{0,96},{32,0},{64,32},{96,64},{1,97},{33,1},{65,33},{97,65},{2,98}... | collective-permute-start | bytes 1966088 | tf_op jit(solution)/shard_map/ppermute | solution.py:34
  128.5 21.2 %collective-permute-start.7 = (bf16[64,5120]{1,0:T(8,128)(2,1)S(1)}, bf16[64,5120]{1,0:T(8,128)(2,1)S(1)}, u32[]{:S(2)}, u32[]{:S(2)}) collective-permute-start(bf16[64,5120]{1,0:T(8,128)(2,1)S(1)} %get-tuple-element.21.refs_1_), channel_id=1, source_target_pairs={{0,32},{32,64},{64,96},{96,0},{1,33},{33,65},{65,97},{97,1},{2,34}... | collective-permute-start | bytes 1966088 | tf_op jit(solution)/shard_map/ppermute | solution.py:34
  129.4 21.2 %collective-permute-start.8 = (bf16[64,5120]{1,0:T(8,128)(2,1)S(1)}, bf16[64,5120]{1,0:T(8,128)(2,1)S(1)}, u32[]{:S(2)}, u32[]{:S(2)}) collective-permute-start(bf16[64,5120]{1,0:T(8,128)(2,1)S(1)} %get-tuple-element.20.refs_0_), channel_id=1, source_target_pairs={{0,96},{32,0},{64,32},{96,64},{1,97},{33,1},{65,33},{97,65},{2,98}... | collective-permute-start | bytes 1966088 | tf_op jit(solution)/shard_map/ppermute | solution.py:34
  142.7 35.6 %collective-permute-start.11 = (bf16[64,5120]{1,0:T(8,128)(2,1)S(1)}, bf16[64,5120]{1,0:T(8,128)(2,1)S(1)}, u32[]{:S(2)}, u32[]{:S(2)}) collective-permute-start(bf16[64,5120]{1,0:T(8,128)(2,1)S(1)} %collective-permute-done.6.refs_2_), channel_id=1, source_target_pairs={{0,32},{32,64},{64,96},{96,0},{1,33},{33,65},{65,97},{97,1},{2,34}... | collective-permute-start | bytes 1966088 | tf_op jit(solution)/shard_map/ppermute | solution.py:34
  142.7 35.6 %collective-permute-start.12 = (bf16[64,5120]{1,0:T(8,128)(2,1)S(1)}, bf16[64,5120]{1,0:T(8,128)(2,1)S(1)}, u32[]{:S(2)}, u32[]{:S(2)}) collective-permute-start(bf16[64,5120]{1,0:T(8,128)(2,1)S(1)} %collective-permute-done.9.refs_5_), channel_id=1, source_target_pairs={{0,96},{32,0},{64,32},{96,64},{1,97},{33,1},{65,33},{97,65},{2,98}... | collective-permute-start | bytes 1966088 | tf_op jit(solution)/shard_map/ppermute | solution.py:34
  155.9 4.7 %copy-start = (bf16[10240,640]{1,0:T(8,128)(2,1)S(1)}, bf16[10240,640]{1,0:T(8,128)(2,1)}, u32[]{:S(2)}) copy-start(bf16[10240,640]{1,0:T(8,128)(2,1)} %all-gather.2.cloned.1.call-done) | copy-start | bytes 39321604
  163.9 14.5 %copy-start.1 = (bf16[10240,640]{1,0:T(8,128)(2,1)S(1)}, bf16[10240,640]{1,0:T(8,128)(2,1)}, u32[]{:S(2)}) copy-start(bf16[10240,640]{1,0:T(8,128)(2,1)} %all-gather.2.cloned.1.call-done) | copy-start | bytes 39321604
  175.7 26.2 %copy-start.2 = (bf16[2,2,32,5120]{3,2,1,0:T(8,128)(2,1)S(1)}, bf16[2,2,32,5120]{3,2,1,0:T(8,128)(2,1)}, u32[]{:S(2)}) copy-start(bf16[2,2,32,5120]{3,2,1,0:T(8,128)(2,1)} %param.11) | copy-start | bytes 3932164
  175.7 26.2 %copy-start.8 = (f32[5120]{0:T(1024)S(1)}, f32[5120]{0:T(1024)}, u32[]{:S(2)}) copy-start(f32[5120]{0:T(1024)} %param.21) | copy-start | bytes 61444
  175.7 9.5 %collective-permute-start.10 = (bf16[128,1280]{1,0:T(8,128)(2,1)S(1)}, bf16[128,1280]{1,0:T(8,128)(2,1)S(1)}, u32[]{:S(2)}, u32[]{:S(2)}) collective-permute-start(bf16[128,1280]{1,0:T(8,128)(2,1)S(1)} %get-tuple-element.23), channel_id=1, source_target_pairs={{0,96},{32,0},{64,32},{96,64},{1,97},{33,1},{65,33},{97,65},{2,98}... | collective-permute-start | bytes 983048 | tf_op jit(solution)/shard_map/ppermute | solution.py:34
  183.6 10.4 %collective-permute-start.13 = (bf16[128,1280]{1,0:T(8,128)(2,1)S(1)}, bf16[128,1280]{1,0:T(8,128)(2,1)S(1)}, u32[]{:S(2)}, u32[]{:S(2)}) collective-permute-start(bf16[128,1280]{1,0:T(8,128)(2,1)S(1)} %project.3), channel_id=1, source_target_pairs={{0,64},{32,96},{64,0},{96,32},{1,65},{33,97},{65,1},{97,33},{2,66}... | collective-permute-start | bytes 983048 | tf_op jit(solution)/shard_map/ppermute | solution.py:34
  184.2 17.6 %collective-permute-start.14 = (bf16[128,1280]{1,0:T(8,128)(2,1)S(1)}, bf16[128,1280]{1,0:T(8,128)(2,1)S(1)}, u32[]{:S(2)}, u32[]{:S(2)}) collective-permute-start(bf16[128,1280]{1,0:T(8,128)(2,1)S(1)} %get-tuple-element.24), channel_id=1, source_target_pairs={{0,32},{32,64},{64,96},{96,0},{1,33},{33,65},{65,97},{97,1},{2,34}... | collective-permute-start | bytes 983048 | tf_op jit(solution)/shard_map/ppermute | solution.py:34
  (12 other events, 12.3 us)
Sparse Core Ops, SparseCore 0:
  10.1 145.7 all-gather.1

commit v3 on v2

--- a/solution.py
+++ b/solution.py
@@ -32,6 +32,10 @@
 def shifted(block, axis, distance):
     n = lax.axis_size(axis)
     return lax.ppermute(block, axis, [(i, (i + distance) % n) for i in range(n)])
+
+
+def in_hbm(array):
+    return pltpu.with_memory_space_constraint(array, pltpu.HBM)
 
 
 def params(megabytes=24):
@@ -94,7 +98,7 @@
         compiler_params=params(),
         cost_estimate=pl.CostEstimate(flops=0, bytes_accessed=12 << 20, transcendentals=0),
         name="prepare",
-    )(queries, keys, values, query_gain[None], key_gain[None])
+    )(*[in_hbm(a) for a in (queries, keys, values)], query_gain[None], key_gain[None])
 
 
 def mask_tables(first_frame, first_row, frame_count, row_count, nw):
@@ -115,34 +119,41 @@
 
 def attend_kernel(heads, scale, combo_ref, q_ref, f0, f1, hb, ha, rb, ra, cb, ca, mask_ref, *out_refs):
     step = pl.program_id(0)
+    frames = ((cb.at[0], hb, ca.at[0]), (rb.at[0], f0, ra.at[0]), (rb.at[1], f1, ra.at[1]), (cb.at[1], ha, ca.at[1]))
+
+    def region(kv, lanes):
+        parts = []
+        for below, own, above in frames:
+            parts += [below[kv, :, lanes], own[0, kv, :, lanes], own[1, kv, :, lanes], above[kv, :, lanes]]
+        return jnp.concatenate(parts, axis=0)
+
+    scores = {}
     for h in range(heads):
         lanes = slice(h * HEAD, (h + 1) * HEAD)
+        keys = region(0, lanes)
+        group = keys.shape[0] // 4
         combo = combo_ref[step * heads + h]
-
-        def region(kv):
-            frames = ((cb[0], hb, ca[0]), (rb[0], f0, ra[0]), (rb[1], f1, ra[1]), (cb[1], ha, ca[1]))
-            parts = []
-            for below, own, above in frames:
-                parts += [below[kv, :, lanes], own[0, kv, :, lanes], own[1, kv, :, lanes], above[kv, :, lanes]]
-            return jnp.concatenate(parts, axis=0)
-
-        keys, values = region(0), region(1)
-        span = keys.shape[0] // 4 * 3
         for f in range(2):
-            first = f * (span // 3)
             q = q_ref[2 * f : 2 * f + 2, :, lanes].reshape(-1, HEAD)
-            s = lax.dot_general(
-                q, keys[first : first + span], (((1,), (1,)), ((), ())), preferred_element_type=F32
-            )
-            s = s + mask_ref[combo, f]
-            peak = jnp.max(s, axis=1, keepdims=True)
-            w = jnp.exp((s - peak) * scale)
-            total = jnp.sum(w, axis=1, keepdims=True)
-            o = jnp.dot(w.astype(BF16), values[first : first + span], preferred_element_type=F32)
+            k = keys[f * group : (f + 3) * group]
+            s = lax.dot_general(q, k, (((1,), (1,)), ((), ())), preferred_element_type=F32)
+            scores[h, f] = s + mask_ref[combo, f]
+    weights = {}
+    for at, s in scores.items():
+        peak = jnp.max(s, axis=1, keepdims=True)
+        w = jnp.exp((s - peak) * scale)
+        weights[at] = w.astype(BF16), jnp.sum(w, axis=1, keepdims=True)
+    for h in range(heads):
+        lanes = slice(h * HEAD, (h + 1) * HEAD)
+        values = region(1, lanes)
+        group = values.shape[0] // 4
+        for f in range(2):
+            w, total = weights[h, f]
+            o = jnp.dot(w, values[f * group : (f + 3) * group], preferred_element_type=F32)
             out_refs[f][:, lanes] = (o / total).astype(BF16)
 
 
-def attend(combo, chunk, qn, own, halos, masks, heads=4):
+def attend(combo, chunk, qn, own, halos, masks, heads=8):
     groups, nw, inner = qn.shape
     width = own[0].shape[-1]
     lanes = heads * HEAD
@@ -169,18 +180,23 @@
     ins, w_ref, outs, acc = refs[:blocks], refs[blocks], refs[blocks + 1 : -1], refs[-1]
     k = pl.program_id(0)
     a = jnp.concatenate([i[...] for i in ins], axis=0)
-    half = w_ref.shape[-1]
-    for n in range(2):
-        cols = slice(n * half, (n + 1) * half)
-        term = jnp.dot(a, w_ref[0, n], preferred_element_type=F32)
-
-        @pl.when(k == 0)
-        def _():
-            acc[:, cols] = term
-
-        @pl.when(k > 0)
-        def _():
-            acc[:, cols] += term
+    _, halves, cores, zs, _, _ = w_ref.shape
+    w = jnp.concatenate(
+        [
+            jnp.concatenate([w_ref[0, n, c, z] for z in range(zs) for c in range(cores)], axis=0)
+            for n in range(halves)
+        ],
+        axis=1,
+    )
+    term = jnp.dot(a, w, preferred_element_type=F32)
+
+    @pl.when(k == 0)
+    def _():
+        acc[...] = term
+
+    @pl.when(k > 0)
+    def _():
+        acc[...] += term
 
     @pl.when(k == pl.num_programs(0) - 1)
     def _():
@@ -189,24 +205,24 @@
             o[...] = acc[d * rows : (d + 1) * rows, :].astype(BF16)
 
 
-def project(blocks, weight, step=1280):
+def project(blocks, weight, zs=4):
     rows, inner = blocks[0].shape
-    groups, halves, depth, half = weight.shape
-    cols, devices, inside = halves * half, len(blocks) // 2, depth // step
+    groups, halves, cores, depth, part, half = weight.shape
+    cols, devices, inside, step = halves * half, len(blocks) // 2, depth // zs, cores * zs * part
     return pl.pallas_call(
         functools.partial(project_kernel, len(blocks)),
         grid=(groups * inside,),
         in_specs=[pl.BlockSpec((rows, step), lambda k: (0, k))] * len(blocks)
-        + [pl.BlockSpec((1, halves, step, half), lambda k: (k // inside, 0, k % inside, 0))],
+        + [pl.BlockSpec((1, halves, cores, zs, part, half), lambda k: (k // inside, 0, 0, k % inside, 0, 0))],
         out_specs=[pl.BlockSpec((2 * rows, cols), lambda k: (0, 0))] * devices,
         out_shape=[jax.ShapeDtypeStruct((2 * rows, cols), BF16)] * devices,
         scratch_shapes=[pltpu.VMEM((2 * devices * rows, cols), F32)],
-        compiler_params=params(),
+        compiler_params=params(40),
         cost_estimate=pl.CostEstimate(
             flops=4 * devices * rows * inner * cols, bytes_accessed=2 * inner * cols, transcendentals=0
         ),
         name="project",
-    )(*blocks, weight)
+    )(*[in_hbm(b) for b in blocks], in_hbm(weight))
 
 
 def finish_kernel(x_ref, hidden, gate, p0, p1, p2, p3, out):
@@ -235,15 +251,13 @@
         out_shape=jax.ShapeDtypeStruct(hidden.shape, BF16),
         compiler_params=params(),
         name="finish",
-    )(x, hidden, gate[None], *pieces)
+    )(x, in_hbm(hidden), gate[None], *pieces)
 
 
 def shards(hidden_in, queries, keys, values, query_gain, key_gain, reach_time, reach_rows, reach_cols, out_weight, gate):
     frames, rows, nw, inner = queries.shape
     width = hidden_in.shape[3]
-    weight = lax.all_gather(out_weight, ("y_hi", "y_lo", "z", "core"), axis=0, tiled=True)
-    weight = weight.reshape(2, 2, inner // 2, out_weight.shape[1])
-
+    weight = lax.all_gather(out_weight, "z", axis=0, tiled=False)
     tokens = [a.reshape(frames * rows, nw, inner) for a in (queries, keys, values)]
     qn, *own = prepare(*tokens, query_gain, key_gain)
     masks = mask_tables(
@@ -262,7 +276,11 @@
         rb, ra = passed_along(r1, SP, 1), passed_along(r0, SP, -1)
         cb = passed_along(jnp.stack([hb[1], ha[1]]), SP, 1)
         ca = passed_along(jnp.stack([hb[0], ha[0]]), SP, -1)
-        a = attend(combo[c * heads : (c + 1) * heads], c, qn, (f0, f1), (hb, ha, rb, ra, cb, ca), masks)
+        if c == 0:
+            hb_in, ha_in, rb, ra, weight = lax.optimization_barrier((hb, ha, rb, ra, weight))
+            weight = lax.all_gather(weight, ("y_hi", "y_lo", "core"), axis=0, tiled=False)
+            weight = weight.reshape((2, 2, 2) + weight.shape[1:])
+        a = attend(combo[c * heads : (c + 1) * heads], c, qn, (f0, f1), (hb_in, ha_in, rb, ra, cb, ca), masks)
         outs.append(a)
     a0, a1 = outs[0]
     left0, right1 = shifted(a0, "x", 1), shifted(a1, "x", -1)

time: 211 us -> 193 us (0.915)
  waiting for transfers between devices: 76.5 us -> 94.3 us
  Pallas kernels: 46.7 us -> 32.8 us
  starting transfers between devices: 55.2 us -> 43.8 us
  local copies, waits for them, and re-layouts: 17.2 us -> 6.97 us
    pallas_call x1, Pallas kernels: 23.9 us -> 8.51 us  [attend(): pl.pallas_call(functools.partial(attend_kernel, heads, HEAD ** (-0.5)), g...]
    all_gather x1 -> x2, waiting for transfers between devices: 4.42 us -> 18.1 us  [the longest x1 18.1 us: shards(): lax.all_gather(weight, ('y_hi', 'y_lo', 'core'), axis=0, tiled=False)]
    unnamed x40 -> x42, local copies, waits for them, and re-layouts: 17 us -> 6.79 us
    ppermute x9, starting transfers between devices: 36.2 us -> 26.2 us  [shifted(): lax.ppermute(block, axis, [(i, (i + distance) % n) for i in range(n)])]
    ppermute x6, waiting for transfers between devices: 39.6 us -> 42 us  [passed_along(): return lax.ppermute(block, axes, route)]
  transfers between devices with their start and end apart: 16 -> 17, of which waited for: 9 -> 11; matrix products, arithmetic and copies ran while one was open for 1% -> 1% of each run, Pallas kernels for 21% -> 15%
where the time goes in v3:
time: 193 us
  waiting for transfers between devices  94.3 us (49%)
  starting transfers between devices  43.8 us (23%)
  Pallas kernels  32.8 us (17%)
  between operations  13.8 us (7%)
  local copies, waits for them, and re-layouts  6.97 us (4%)
    ppermute x6, waiting for transfers between devices, passed_along(): return lax.ppermute(block, axes, route)  42 us
    ppermute x9, waiting for transfers between devices, shifted(): lax.ppermute(block, axis, [(i, (i + distance) % n) for i in range(n)])  33.4 us
    ppermute x9, starting transfers between devices, shifted(): lax.ppermute(block, axis, [(i, (i + distance) % n) for i in range(n)])  26.2 us
    all_gather x1, waiting for transfers between devices, shards(): lax.all_gather(weight, ('y_hi', 'y_lo', 'core'), axis=0, tiled=False)  18.1 us
    ppermute x6, starting transfers between devices, passed_along(): return lax.ppermute(block, axes, route)  17.5 us
    pallas_call x2, Pallas kernels, project(): pl.pallas_call(functools.partial(project_kernel, len(blocks)), grid=(grou...  16.7 us
    pallas_call x1, Pallas kernels, attend(): pl.pallas_call(functools.partial(attend_kernel, heads, HEAD ** (-0.5)), g...  8.51 us
    unnamed x42, local copies, waits for them, and re-layouts  6.79 us
  transfers between devices with their start and end apart: 17, of which 11 were waited for; matrix products, arithmetic and copies ran while one was open for 1% of the time, Pallas kernels for 15%

profile of v3, /device:TPU:1, one launch (start us, length us, event | category | flops | bytes accessed | tf_op | source)
XLA Modules:
  0.0 192.8 jit_solution(2168478755662418120)
XLA Ops:
  8.8 3.9 %prepare.1 = (bf16[4,32,5120]{2,1,0:T(8,128)(2,1)S(1)}, bf16[2,2,32,5120]{3,2,1,0:T(8,128)(2,1)S(1)}, bf16[2,2,32,5120]{3,2,1,0:T(8,128)(2,1)S(1)}, bf16[2,2,32,...) custom-call(bf16[4,32,5120]{2,1,0:T(8,128)(2,1)} %bitcast.18, bf16[4,32,5120]{2,1,0:T(8,128)(2,1)} %bitcast.19, ...), custom_call_target="tpu_custom_call" | custom-call | bytes 12582912 | tf_op jit(solution)/shard_map/prepare/pallas_call | solution.py:92
  13.7 4.0 %collective-permute-start = (bf16[2,2,32,5120]{3,2,1,0:T(8,128)(2,1)S(1)}, bf16[2,2,32,5120]{3,2,1,0:T(8,128)(2,1)S(1)}, u32[]{:S(2)}, u32[]{:S(2)}) collective-permute-start(bf16[2,2,32,5120]{3,2,1,0:T(8,128)(2,1)S(1)} %get-tuple-element.22.f1), channel_id=1, source_target_pairs={{0,32},{32,64},{64,96},{96,128},{128,160},{160,192},{192,224},{1,3... | collective-permute-start | bytes 3932168 | tf_op jit(solution)/shard_map/ppermute | solution.py:29
  21.2 4.4 %collective-permute-start.2 = (bf16[2,2,32,5120]{3,2,1,0:T(8,128)(2,1)S(1)}, bf16[2,2,32,5120]{3,2,1,0:T(8,128)(2,1)S(1)}, u32[]{:S(2)}, u32[]{:S(2)}) collective-permute-start(bf16[2,2,32,5120]{3,2,1,0:T(8,128)(2,1)S(1)} %get-tuple-element.23), channel_id=1, source_target_pairs={{0,1},{1,2},{2,3},{3,4},{4,5},{5,6},{6,7},{7,8},{8,9},{9,10},{10,1... | collective-permute-start | bytes 3932168 | tf_op jit(solution)/shard_map/ppermute | solution.py:29
  25.6 1.9 collective-permute-start.3
  27.5 17.6 %collective-permute-done.hb = bf16[2,2,32,5120]{3,2,1,0:T(8,128)(2,1)S(1)} collective-permute-done((bf16[2,2,32,5120]{3,2,1,0:T(8,128)(2,1)S(1)}, bf16[2,2,32,5120]{3,2,1,0:T(8,128)(2,1)S(1)}, u32[]{:S(2)}, u32[]{:S(2)}) %collective-permute-start) | collective-permute-done | bytes 1310752 | tf_op jit(solution)/shard_map/ppermute | solution.py:29
  45.1 5.0 %collective-permute-done.1.ha = bf16[2,2,32,5120]{3,2,1,0:T(8,128)(2,1)S(1)} collective-permute-done((bf16[2,2,32,5120]{3,2,1,0:T(8,128)(2,1)S(1)}, bf16[2,2,32,5120]{3,2,1,0:T(8,128)(2,1)S(1)}, u32[]{:S(2)}, u32[]{:S(2)}) %collective-permute-start.1) | collective-permute-done | bytes 1310752 | tf_op jit(solution)/shard_map/ppermute | solution.py:29
  50.1 3.4 %collective-permute-done.2.rb = bf16[2,2,32,5120]{3,2,1,0:T(8,128)(2,1)S(1)} collective-permute-done((bf16[2,2,32,5120]{3,2,1,0:T(8,128)(2,1)S(1)}, bf16[2,2,32,5120]{3,2,1,0:T(8,128)(2,1)S(1)}, u32[]{:S(2)}, u32[]{:S(2)}) %collective-permute-start.2) | collective-permute-done | bytes 1310752 | tf_op jit(solution)/shard_map/ppermute | solution.py:29
  54.6 2.4 %collective-permute-done.3.ra = bf16[2,2,32,5120]{3,2,1,0:T(8,128)(2,1)S(1)} collective-permute-done((bf16[2,2,32,5120]{3,2,1,0:T(8,128)(2,1)S(1)}, bf16[2,2,32,5120]{3,2,1,0:T(8,128)(2,1)S(1)}, u32[]{:S(2)}, u32[]{:S(2)}) %collective-permute-start.3) | collective-permute-done | bytes 1310752 | tf_op jit(solution)/shard_map/ppermute | solution.py:29
  58.6 2.1 %collective-permute-start.5 = (bf16[2,2,32,5120]{3,2,1,0:T(8,128)(2,1)S(1)}, bf16[2,2,32,5120]{3,2,1,0:T(8,128)(2,1)S(1)}, u32[]{:S(2)}, u32[]{:S(2)}) collective-permute-start(bf16[2,2,32,5120]{3,2,1,0:T(8,128)(2,1)S(1)} %pad_maximum_fusion.1), channel_id=1, source_target_pairs={{1,0},{2,1},{3,2},{4,3},{5,4},{6,5},{7,6},{8,7},{9,8},{10,9},{11,1... | collective-permute-start | bytes 3932168 | tf_op jit(solution)/shard_map/ppermute | solution.py:29
  60.8 3.9 %collective-permute-start.4 = (bf16[2,2,32,5120]{3,2,1,0:T(8,128)(2,1)S(1)}, bf16[2,2,32,5120]{3,2,1,0:T(8,128)(2,1)S(1)}, u32[]{:S(2)}, u32[]{:S(2)}) collective-permute-start(bf16[2,2,32,5120]{3,2,1,0:T(8,128)(2,1)S(1)} %pad_maximum_fusion), channel_id=1, source_target_pairs={{0,1},{1,2},{2,3},{3,4},{4,5},{5,6},{6,7},{7,8},{8,9},{9,10},{10,1... | collective-permute-start | bytes 3932168 | tf_op jit(solution)/shard_map/ppermute | solution.py:29
  65.7 12.0 %collective-permute-done.5.ca = bf16[2,2,32,5120]{3,2,1,0:T(8,128)(2,1)S(1)} collective-permute-done((bf16[2,2,32,5120]{3,2,1,0:T(8,128)(2,1)S(1)}, bf16[2,2,32,5120]{3,2,1,0:T(8,128)(2,1)S(1)}, u32[]{:S(2)}, u32[]{:S(2)}) %collective-permute-start.5) | collective-permute-done | bytes 1310752 | tf_op jit(solution)/shard_map/ppermute | solution.py:29
  79.3 8.5 %attend.1 = (bf16[64,5120]{1,0:T(8,128)(2,1)S(1)}, bf16[64,5120]{1,0:T(8,128)(2,1)}) custom-call(s32[40]{0:T(128)S(1)} %add_add_fusion.combo_ref, bf16[4,32,5120]{2,1,0:T(8,128)(2,1)S(1)} %copy-done.1, bf16[2,2,32,5120]{3,2,1,0:T(8,128)(2,1)S(1)} %copy-done.3, bf16[2,2,32,5120]{3,2,1,0:T(8,128)(2,1)S(1)} %copy-done.5, ...), custom_call_target="tpu_custom_call" | custom-call | flops 1006632960 | bytes 33554432 | tf_op jit(solution)/shard_map/attend/pallas_call | solution.py:162
  89.0 11.7 %collective-permute-start.9 = (bf16[64,5120]{1,0:T(8,128)(2,1)}, bf16[64,5120]{1,0:T(8,128)(2,1)S(1)}, u32[]{:S(2)}, u32[]{:S(2)}) collective-permute-start(bf16[64,5120]{1,0:T(8,128)(2,1)} %get-tuple-element.30.refs_1_), channel_id=1, source_target_pairs={{0,96},{32,0},{64,32},{96,64},{1,97},{33,1},{65,33},{97,65},{2,98}... | collective-permute-start | bytes 1966088 | tf_op jit(solution)/shard_map/ppermute | solution.py:34
  100.6 14.9 %collective-permute-done.6.refs_2_ = bf16[64,5120]{1,0:T(8,128)(2,1)S(1)} collective-permute-done((bf16[64,5120]{1,0:T(8,128)(2,1)S(1)}, bf16[64,5120]{1,0:T(8,128)(2,1)S(1)}, u32[]{:S(2)}, u32[]{:S(2)}) %collective-permute-start.6) | collective-permute-done | bytes 655392 | tf_op jit(solution)/shard_map/ppermute | solution.py:34
  115.5 2.7 %collective-permute-start.12 = (bf16[64,5120]{1,0:T(8,128)(2,1)S(1)}, bf16[64,5120]{1,0:T(8,128)(2,1)S(1)}, u32[]{:S(2)}, u32[]{:S(2)}) collective-permute-start(bf16[64,5120]{1,0:T(8,128)(2,1)S(1)} %collective-permute-done.9.refs_5_), channel_id=1, source_target_pairs={{0,96},{32,0},{64,32},{96,64},{1,97},{33,1},{65,33},{97,65},{2,98}... | collective-permute-start | bytes 1966088 | tf_op jit(solution)/shard_map/ppermute | solution.py:34
  118.2 2.7 %collective-permute-start.8 = (bf16[64,5120]{1,0:T(8,128)(2,1)S(1)}, bf16[64,5120]{1,0:T(8,128)(2,1)}, u32[]{:S(2)}, u32[]{:S(2)}) collective-permute-start(bf16[64,5120]{1,0:T(8,128)(2,1)S(1)} %get-tuple-element.29.refs_0_), channel_id=1, source_target_pairs={{0,96},{32,0},{64,32},{96,64},{1,97},{33,1},{65,33},{97,65},{2,98}... | collective-permute-start | bytes 1966088 | tf_op jit(solution)/shard_map/ppermute | solution.py:34
  120.9 9.2 %collective-permute-done.11.refs_0_ = bf16[64,5120]{1,0:T(8,128)(2,1)S(1)} collective-permute-done((bf16[64,5120]{1,0:T(8,128)(2,1)S(1)}, bf16[64,5120]{1,0:T(8,128)(2,1)S(1)}, u32[]{:S(2)}, u32[]{:S(2)}) %collective-permute-start.11) | collective-permute-done | bytes 655392 | tf_op jit(solution)/shard_map/ppermute | solution.py:34
  130.1 18.1 %all-gather.7.cloned.1.call-done = bf16[64,160,640]{2,1,0:T(8,128)(2,1)} async-done(((bf16[8,160,640]{2,1,0:T(8,128)(2,1)}), bf16[64,160,640]{2,1,0:T(8,128)(2,1)}) %all-gather.7.cloned.1.call-update) | async-done | bytes 13107216 | tf_op jit(solution)/shard_map/all_gather | solution.py:281
  148.2 6.9 %project.3 = bf16[128,1280]{1,0:T(8,128)(2,1)S(1)} custom-call(bf16[64,5120]{1,0:T(8,128)(2,1)} %copy-done.14, bf16[64,5120]{1,0:T(8,128)(2,1)} %copy-done.15, bf16[2,2,2,8,160,640]{5,4,3,2,1,0:T(8,128)(2,1)} %bitcast.14), custom_call_target="tpu_custom_call" | custom-call | flops 1677721600 | bytes 13107200 | tf_op jit(solution)/shard_map/project/pallas_call | solution.py:212
  155.5 9.8 %project.2 = (bf16[128,1280]{1,0:T(8,128)(2,1)S(1)}, bf16[128,1280]{1,0:T(8,128)(2,1)S(1)}, bf16[128,1280]{1,0:T(8,128)(2,1)S(1)}) custom-call(bf16[64,5120]{1,0:T(8,128)(2,1)} %copy-done.13, bf16[64,5120]{1,0:T(8,128)(2,1)} %get-tuple-element.30.refs_1_, bf16[64,5120]{1,0:T(8,128)(2,1)} %copy-done.19, bf16[64,5120]{1,0:T(8,128)(2,1)} %collective-permute-done.7.refs_3_, ...), custom_call_target="tpu_custom_call" | custom-call | flops 5033164800 | bytes 13107200 | tf_op jit(solution)/shard_map/project/pallas_call | solution.py:212
  165.3 7.1 %collective-permute-start.10 = (bf16[128,1280]{1,0:T(8,128)(2,1)S(1)}, bf16[128,1280]{1,0:T(8,128)(2,1)S(1)}, u32[]{:S(2)}, u32[]{:S(2)}) collective-permute-start(bf16[128,1280]{1,0:T(8,128)(2,1)S(1)} %get-tuple-element.33), channel_id=1, source_target_pairs={{0,96},{32,0},{64,32},{96,64},{1,97},{33,1},{65,33},{97,65},{2,98}... | collective-permute-start | bytes 983048 | tf_op jit(solution)/shard_map/ppermute | solution.py:34
  173.0 7.5 %collective-permute-done.10.p1 = bf16[128,1280]{1,0:T(8,128)(2,1)S(1)} collective-permute-done((bf16[128,1280]{1,0:T(8,128)(2,1)S(1)}, bf16[128,1280]{1,0:T(8,128)(2,1)S(1)}, u32[]{:S(2)}, u32[]{:S(2)}) %collective-permute-start.10) | collective-permute-done | bytes 327712 | tf_op jit(solution)/shard_map/ppermute | solution.py:34
  180.5 1.8 collective-permute-done.14.p3
  182.3 3.6 %finish.1 = bf16[128,5120]{1,0:T(8,128)(2,1)} custom-call(s32[1]{0:T(128)} %bitcast.x_ref, bf16[128,5120]{1,0:T(8,128)(2,1)} %bitcast.17, f32[1,5120]{1,0:T(1,128)S(1)} %bitcast.11, bf16[128,1280]{1,0:T(8,128)(2,1)S(1)} %get-tuple-element.32.p0, bf16[128,1280]{1,0:T(8,128)(2,1)S(1)} %collective-permute-done.10.p1, ...), custom_call_target="tpu_custom_call" | custom-call | tf_op jit(solution)/shard_map/finish/pallas_call | solution.py:242
  (79 shorter events, 14.0 us)
Async XLA Ops:
  6.5 51.5 %all-gather.5.cloned.1.call-start = ((), (), s32[]{:S(2)}) async-start(), calls=%async_computation | async-start | bytes 1843200 | tf_op jit(solution)/shard_map/all_gather | solution.py:260
  7.3 141.0 %all-gather.7.cloned.1.call-start = ((), (), s32[]{:S(2)}) async-start(), calls=%async_computation.1 | async-start | bytes 14745600 | tf_op jit(solution)/shard_map/all_gather | solution.py:281
  8.8 49.5 %copy-start.16 = (s32[40]{0:T(128)S(1)}, s32[40]{0:T(128)}, u32[]{:S(2)}) copy-start(s32[40]{0:T(128)} %param.19) | copy-start | bytes 484
  8.8 49.5 %copy-start.17 = (s32[40]{0:T(128)S(1)}, s32[40]{0:T(128)}, u32[]{:S(2)}) copy-start(s32[40]{0:T(128)} %param.18) | copy-start | bytes 484
  8.8 49.5 %copy-start.18 = (s32[40]{0:T(128)S(1)}, s32[40]{0:T(128)}, u32[]{:S(2)}) copy-start(s32[40]{0:T(128)} %param.17) | copy-start | bytes 484
  13.7 31.4 %collective-permute-start = (bf16[2,2,32,5120]{3,2,1,0:T(8,128)(2,1)S(1)}, bf16[2,2,32,5120]{3,2,1,0:T(8,128)(2,1)S(1)}, u32[]{:S(2)}, u32[]{:S(2)}) collective-permute-start(bf16[2,2,32,5120]{3,2,1,0:T(8,128)(2,1)S(1)} %get-tuple-element.22.f1), channel_id=1, source_target_pairs={{0,32},{32,64},{64,96},{96,128},{128,160},{160,192},{192,224},{1,3... | collective-permute-start | bytes 3932168 | tf_op jit(solution)/shard_map/ppermute | solution.py:29
  18.8 31.3 %collective-permute-start.1 = (bf16[2,2,32,5120]{3,2,1,0:T(8,128)(2,1)S(1)}, bf16[2,2,32,5120]{3,2,1,0:T(8,128)(2,1)S(1)}, u32[]{:S(2)}, u32[]{:S(2)}) collective-permute-start(bf16[2,2,32,5120]{3,2,1,0:T(8,128)(2,1)S(1)} %get-tuple-element.21.f0), channel_id=1, source_target_pairs={{32,0},{64,32},{96,64},{128,96},{160,128},{192,160},{224,192},{33,... | collective-permute-start | bytes 3932168 | tf_op jit(solution)/shard_map/ppermute | solution.py:29
  21.2 32.3 %collective-permute-start.2 = (bf16[2,2,32,5120]{3,2,1,0:T(8,128)(2,1)S(1)}, bf16[2,2,32,5120]{3,2,1,0:T(8,128)(2,1)S(1)}, u32[]{:S(2)}, u32[]{:S(2)}) collective-permute-start(bf16[2,2,32,5120]{3,2,1,0:T(8,128)(2,1)S(1)} %get-tuple-element.23), channel_id=1, source_target_pairs={{0,1},{1,2},{2,3},{3,4},{4,5},{5,6},{6,7},{7,8},{8,9},{9,10},{10,1... | collective-permute-start | bytes 3932168 | tf_op jit(solution)/shard_map/ppermute | solution.py:29
  25.6 31.4 %collective-permute-start.3 = (bf16[2,2,32,5120]{3,2,1,0:T(8,128)(2,1)S(1)}, bf16[2,2,32,5120]{3,2,1,0:T(8,128)(2,1)S(1)}, u32[]{:S(2)}, u32[]{:S(2)}) collective-permute-start(bf16[2,2,32,5120]{3,2,1,0:T(8,128)(2,1)S(1)} %get-tuple-element.24), channel_id=1, source_target_pairs={{1,0},{2,1},{3,2},{4,3},{5,4},{6,5},{7,6},{8,7},{9,8},{10,9},{11,1... | collective-permute-start | bytes 3932168 | tf_op jit(solution)/shard_map/ppermute | solution.py:29
  58.6 19.1 %collective-permute-start.5 = (bf16[2,2,32,5120]{3,2,1,0:T(8,128)(2,1)S(1)}, bf16[2,2,32,5120]{3,2,1,0:T(8,128)(2,1)S(1)}, u32[]{:S(2)}, u32[]{:S(2)}) collective-permute-start(bf16[2,2,32,5120]{3,2,1,0:T(8,128)(2,1)S(1)} %pad_maximum_fusion.1), channel_id=1, source_target_pairs={{1,0},{2,1},{3,2},{4,3},{5,4},{6,5},{7,6},{8,7},{9,8},{10,9},{11,1... | collective-permute-start | bytes 3932168 | tf_op jit(solution)/shard_map/ppermute | solution.py:29
  60.8 18.4 %collective-permute-start.4 = (bf16[2,2,32,5120]{3,2,1,0:T(8,128)(2,1)S(1)}, bf16[2,2,32,5120]{3,2,1,0:T(8,128)(2,1)S(1)}, u32[]{:S(2)}, u32[]{:S(2)}) collective-permute-start(bf16[2,2,32,5120]{3,2,1,0:T(8,128)(2,1)S(1)} %pad_maximum_fusion), channel_id=1, source_target_pairs={{0,1},{1,2},{2,3},{3,4},{4,5},{5,6},{6,7},{7,8},{8,9},{9,10},{10,1... | collective-permute-start | bytes 3932168 | tf_op jit(solution)/shard_map/ppermute | solution.py:29
  87.8 67.3 %copy-start.13 = (bf16[64,5120]{1,0:T(8,128)(2,1)}, bf16[64,5120]{1,0:T(8,128)(2,1)S(1)}, u32[]{:S(2)}) copy-start(bf16[64,5120]{1,0:T(8,128)(2,1)S(1)} %get-tuple-element.29.refs_0_) | copy-start | bytes 1966084
  87.8 27.7 %collective-permute-start.6 = (bf16[64,5120]{1,0:T(8,128)(2,1)S(1)}, bf16[64,5120]{1,0:T(8,128)(2,1)S(1)}, u32[]{:S(2)}, u32[]{:S(2)}) collective-permute-start(bf16[64,5120]{1,0:T(8,128)(2,1)S(1)} %get-tuple-element.29.refs_0_), channel_id=1, source_target_pairs={{0,32},{32,64},{64,96},{96,0},{1,33},{33,65},{65,97},{97,1},{2,34}... | collective-permute-start | bytes 1966088 | tf_op jit(solution)/shard_map/ppermute | solution.py:34
  89.0 26.5 %collective-permute-start.9 = (bf16[64,5120]{1,0:T(8,128)(2,1)}, bf16[64,5120]{1,0:T(8,128)(2,1)S(1)}, u32[]{:S(2)}, u32[]{:S(2)}) collective-permute-start(bf16[64,5120]{1,0:T(8,128)(2,1)} %get-tuple-element.30.refs_1_), channel_id=1, source_target_pairs={{0,96},{32,0},{64,32},{96,64},{1,97},{33,1},{65,33},{97,65},{2,98}... | collective-permute-start | bytes 1966088 | tf_op jit(solution)/shard_map/ppermute | solution.py:34
  115.5 39.6 %copy-start.19 = (bf16[64,5120]{1,0:T(8,128)(2,1)}, bf16[64,5120]{1,0:T(8,128)(2,1)S(1)}, u32[]{:S(2)}) copy-start(bf16[64,5120]{1,0:T(8,128)(2,1)S(1)} %collective-permute-done.6.refs_2_) | copy-start | bytes 1966084
  115.5 14.6 %collective-permute-start.11 = (bf16[64,5120]{1,0:T(8,128)(2,1)S(1)}, bf16[64,5120]{1,0:T(8,128)(2,1)S(1)}, u32[]{:S(2)}, u32[]{:S(2)}) collective-permute-start(bf16[64,5120]{1,0:T(8,128)(2,1)S(1)} %collective-permute-done.6.refs_2_), channel_id=1, source_target_pairs={{0,32},{32,64},{64,96},{96,0},{1,33},{33,65},{65,97},{97,1},{2,34}... | collective-permute-start | bytes 1966088 | tf_op jit(solution)/shard_map/ppermute | solution.py:34
  115.5 39.6 %copy-start.20 = (bf16[64,5120]{1,0:T(8,128)(2,1)}, bf16[64,5120]{1,0:T(8,128)(2,1)S(1)}, u32[]{:S(2)}) copy-start(bf16[64,5120]{1,0:T(8,128)(2,1)S(1)} %collective-permute-done.9.refs_5_) | copy-start | bytes 1966084
  115.5 14.6 %collective-permute-start.12 = (bf16[64,5120]{1,0:T(8,128)(2,1)S(1)}, bf16[64,5120]{1,0:T(8,128)(2,1)S(1)}, u32[]{:S(2)}, u32[]{:S(2)}) collective-permute-start(bf16[64,5120]{1,0:T(8,128)(2,1)S(1)} %collective-permute-done.9.refs_5_), channel_id=1, source_target_pairs={{0,96},{32,0},{64,32},{96,64},{1,97},{33,1},{65,33},{97,65},{2,98}... | collective-permute-start | bytes 1966088 | tf_op jit(solution)/shard_map/ppermute | solution.py:34
  118.2 37.3 %collective-permute-start.7 = (bf16[64,5120]{1,0:T(8,128)(2,1)}, bf16[64,5120]{1,0:T(8,128)(2,1)}, u32[]{:S(2)}, u32[]{:S(2)}) collective-permute-start(bf16[64,5120]{1,0:T(8,128)(2,1)} %get-tuple-element.30.refs_1_), channel_id=1, source_target_pairs={{0,32},{32,64},{64,96},{96,0},{1,33},{33,65},{65,97},{97,1},{2,34}... | collective-permute-start | bytes 1966088 | tf_op jit(solution)/shard_map/ppermute | solution.py:34
  118.2 37.3 %collective-permute-start.8 = (bf16[64,5120]{1,0:T(8,128)(2,1)S(1)}, bf16[64,5120]{1,0:T(8,128)(2,1)}, u32[]{:S(2)}, u32[]{:S(2)}) collective-permute-start(bf16[64,5120]{1,0:T(8,128)(2,1)S(1)} %get-tuple-element.29.refs_0_), channel_id=1, source_target_pairs={{0,96},{32,0},{64,32},{96,64},{1,97},{33,1},{65,33},{97,65},{2,98}... | collective-permute-start | bytes 1966088 | tf_op jit(solution)/shard_map/ppermute | solution.py:34
  155.2 27.2 %copy-start.10 = (f32[5120]{0:T(1024)S(1)}, f32[5120]{0:T(1024)}, u32[]{:S(2)}) copy-start(f32[5120]{0:T(1024)} %param.21) | copy-start | bytes 61444
  155.2 17.8 %collective-permute-start.13 = (bf16[128,1280]{1,0:T(8,128)(2,1)S(1)}, bf16[128,1280]{1,0:T(8,128)(2,1)S(1)}, u32[]{:S(2)}, u32[]{:S(2)}) collective-permute-start(bf16[128,1280]{1,0:T(8,128)(2,1)S(1)} %project.3), channel_id=1, source_target_pairs={{0,64},{32,96},{64,0},{96,32},{1,65},{33,97},{65,1},{97,33},{2,66}... | collective-permute-start | bytes 983048 | tf_op jit(solution)/shard_map/ppermute | solution.py:34
  165.3 15.2 %collective-permute-start.10 = (bf16[128,1280]{1,0:T(8,128)(2,1)S(1)}, bf16[128,1280]{1,0:T(8,128)(2,1)S(1)}, u32[]{:S(2)}, u32[]{:S(2)}) collective-permute-start(bf16[128,1280]{1,0:T(8,128)(2,1)S(1)} %get-tuple-element.33), channel_id=1, source_target_pairs={{0,96},{32,0},{64,32},{96,64},{1,97},{33,1},{65,33},{97,65},{2,98}... | collective-permute-start | bytes 983048 | tf_op jit(solution)/shard_map/ppermute | solution.py:34
  172.4 10.0 %collective-permute-start.14 = (bf16[128,1280]{1,0:T(8,128)(2,1)S(1)}, bf16[128,1280]{1,0:T(8,128)(2,1)S(1)}, u32[]{:S(2)}, u32[]{:S(2)}) collective-permute-start(bf16[128,1280]{1,0:T(8,128)(2,1)S(1)} %get-tuple-element.34), channel_id=1, source_target_pairs={{0,32},{32,64},{64,96},{96,0},{1,33},{33,65},{65,97},{97,1},{2,34}... | collective-permute-start | bytes 983048 | tf_op jit(solution)/shard_map/ppermute | solution.py:34
  (14 other events, 140.5 us)
Sparse Core Ops, SparseCore 0:
  9.1 42.7 all-gather.4
  58.2 90.0 all-gather.6

commit v4 on v3

--- a/solution.py
+++ b/solution.py
@@ -79,10 +79,10 @@
     width = inner // CHUNKS
     token_spec = pl.BlockSpec((1, nw, inner), lambda i: (i, 0, 0))
     gain_spec = pl.BlockSpec((1, inner), lambda i: (0, 0))
-    out_shape = [jax.ShapeDtypeStruct(queries.shape, BF16)]
+    out_shape = [pltpu.HBM(queries.shape, BF16)]
     out_specs = [token_spec]
     for _ in range(CHUNKS):
-        out_shape += [jax.ShapeDtypeStruct((2, 2, nw, width), BF16)] * 4
+        out_shape += [pltpu.HBM((2, 2, nw, width), BF16)] * 4
         out_specs += [
             pl.BlockSpec((1, 2, nw, width), lambda i: (jnp.minimum(i, 1), 0, 0, 0)),
             pl.BlockSpec((1, 2, nw, width), lambda i: (jnp.maximum(i - 2, 0), 0, 0, 0)),
@@ -169,7 +169,7 @@
             + [pl.BlockSpec(masks.shape, lambda i, *_: (0, 0, 0, 0))],
             out_specs=[pl.BlockSpec((2 * nw, lanes), lambda i, *_: (0, i))] * 2,
         ),
-        out_shape=[jax.ShapeDtypeStruct((2 * nw, width), BF16)] * 2,
+        out_shape=[pltpu.HBM((2 * nw, width), BF16)] * 2,
         compiler_params=params(),
         cost_estimate=pl.CostEstimate(flops=4 * 128 * 384 * width, bytes_accessed=32 << 20, transcendentals=0),
         name="attend",
@@ -222,7 +222,7 @@
             flops=4 * devices * rows * inner * cols, bytes_accessed=2 * inner * cols, transcendentals=0
         ),
         name="project",
-    )(*[in_hbm(b) for b in blocks], in_hbm(weight))
+    )(*blocks, in_hbm(weight))
 
 
 def finish_kernel(x_ref, hidden, gate, p0, p1, p2, p3, out):
@@ -251,7 +251,7 @@
         out_shape=jax.ShapeDtypeStruct(hidden.shape, BF16),
         compiler_params=params(),
         name="finish",
-    )(x, in_hbm(hidden), gate[None], *pieces)
+    )(x, hidden, gate[None], *pieces)
 
 
 def shards(hidden_in, queries, keys, values, query_gain, key_gain, reach_time, reach_rows, reach_cols, out_weight, gate):
@@ -273,21 +273,22 @@
     for c in range(CHUNKS):
         f0, f1, r0, r1 = own[4 * c : 4 * c + 4]
         hb, ha = passed_along(f1, TM, 1), passed_along(f0, TM, -1)
-        rb, ra = passed_along(r1, SP, 1), passed_along(r0, SP, -1)
+        if c == 0:
+            hb, ha, r0, r1, weight = lax.optimization_barrier((hb, ha, r0, r1, weight))
+            weight = lax.all_gather(weight, ("y_hi", "y_lo", "core"), axis=0, tiled=False)
+            weight = weight.reshape((2, 2, 2) + weight.shape[1:])
         cb = passed_along(jnp.stack([hb[1], ha[1]]), SP, 1)
         ca = passed_along(jnp.stack([hb[0], ha[0]]), SP, -1)
-        if c == 0:
-            hb_in, ha_in, rb, ra, weight = lax.optimization_barrier((hb, ha, rb, ra, weight))
-            weight = lax.all_gather(weight, ("y_hi", "y_lo", "core"), axis=0, tiled=False)
-            weight = weight.reshape((2, 2, 2) + weight.shape[1:])
-        a = attend(combo[c * heads : (c + 1) * heads], c, qn, (f0, f1), (hb_in, ha_in, rb, ra, cb, ca), masks)
+        rb, ra = passed_along(r1, SP, 1), passed_along(r0, SP, -1)
+        a = attend(combo[c * heads : (c + 1) * heads], c, qn, (f0, f1), (hb, ha, rb, ra, cb, ca), masks)
         outs.append(a)
     a0, a1 = outs[0]
     left0, right1 = shifted(a0, "x", 1), shifted(a1, "x", -1)
     left1, right0 = shifted(a1, "x", 1), shifted(a0, "x", -1)
     far0, far1 = shifted(left0, "x", 1), shifted(right1, "x", -1)
-    mine, near_left, near_right = project([a0, a1, left0, left1, right0, right1], weight)
-    (far,) = project([far0, far1], weight)
+    far, near_left, near_right = project([far0, far1, left0, left1, right0, right1], weight)
+    a0, far = lax.optimization_barrier((a0, far))
+    (mine,) = project([a0, a1], weight)
     pieces = [mine, shifted(near_left, "x", -1), shifted(far, "x", 2), shifted(near_right, "x", 1)]
     x = lax.axis_index("x").astype(jnp.int32)[None]
     out = finish(x, hidden_in.reshape(-1, width), gate, pieces)

time: 193 us -> 189 us (0.979)
  waiting for transfers between devices: 94.3 us -> 107 us
  starting transfers between devices: 43.8 us -> 31.1 us
  local copies, waits for them, and re-layouts: 6.97 us -> 3.61 us
    ppermute x9, starting transfers between devices: 26.2 us -> 13.1 us  [shifted(): lax.ppermute(block, axis, [(i, (i + distance) % n) for i in range(n)])]
    ppermute x6, waiting for transfers between devices: 42 us -> 53.4 us  [passed_along(): return lax.ppermute(block, axes, route)]
    all_gather x1, waiting for transfers between devices: 18.1 us -> 27.5 us  [shards(): lax.all_gather(weight, ('y_hi', 'y_lo', 'core'), axis=0, tiled=False)]
    ppermute x9, waiting for transfers between devices: 33.4 us -> 24.9 us  [shifted(): lax.ppermute(block, axis, [(i, (i + distance) % n) for i in range(n)])]
    unnamed x42 -> x32, local copies, waits for them, and re-layouts: 6.79 us -> 3.44 us
    pallas_call x1, Pallas kernels: 3.91 us -> 6.24 us  [prepare(): pl.pallas_call(prepare_kernel, grid=(groups,), in_specs=[token_spec] * 3...]
  transfers between devices with their start and end apart: 17 -> 17, of which waited for: 11 -> 12; matrix products, arithmetic and copies ran while one was open for 1% -> 1% of each run, Pallas kernels for 15% -> 11%
where the time goes in v4:
time: 189 us
  waiting for transfers between devices  107 us (57%)
  Pallas kernels  32.4 us (17%)
  starting transfers between devices  31.1 us (16%)
  between operations  13.7 us (7%)
  local copies, waits for them, and re-layouts  3.61 us (2%)
    ppermute x6, waiting for transfers between devices, passed_along(): return lax.ppermute(block, axes, route)  53.4 us
    all_gather x1, waiting for transfers between devices, shards(): lax.all_gather(weight, ('y_hi', 'y_lo', 'core'), axis=0, tiled=False)  27.5 us
    ppermute x9, waiting for transfers between devices, shifted(): lax.ppermute(block, axis, [(i, (i + distance) % n) for i in range(n)])  24.9 us
    ppermute x6, starting transfers between devices, passed_along(): return lax.ppermute(block, axes, route)  18 us
    pallas_call x2, Pallas kernels, project(): pl.pallas_call(functools.partial(project_kernel, len(blocks)), grid=(grou...  15.8 us
    ppermute x9, starting transfers between devices, shifted(): lax.ppermute(block, axis, [(i, (i + distance) % n) for i in range(n)])  13.1 us
    pallas_call x1, Pallas kernels, attend(): pl.pallas_call(functools.partial(attend_kernel, heads, HEAD ** (-0.5)), g...  8.51 us
    pallas_call x1, Pallas kernels, prepare(): pl.pallas_call(prepare_kernel, grid=(groups,), in_specs=[token_spec] * 3...  6.24 us
  transfers between devices with their start and end apart: 17, of which 12 were waited for; matrix products, arithmetic and copies ran while one was open for 1% of the time, Pallas kernels for 11%

profile of v4, /device:TPU:1, one launch (start us, length us, event | category | flops | bytes accessed | tf_op | source)
XLA Modules:
  0.0 188.7 jit_solution(11564771305671031073)
XLA Ops:
  8.8 6.2 %prepare.1 = (bf16[4,32,5120]{2,1,0:T(8,128)(2,1)}, bf16[2,2,32,5120]{3,2,1,0:T(8,128)(2,1)}, bf16[2,2,32,5120]{3,2,1,0:T(8,128)(2,1)}, bf16[2,2,32,5120]{3,2,1,0:T(8,128)(2,1)}, bf16[2,2,32,5120]{3,2,1,0:T(8,128)(2,1)}) custom-call(bf16[4,32,5120]{2,1,0:T(8,128)(2,1)} %bitcast.18, bf16[4,32,5120]{2,1,0:T(8,128)(2,1)} %bitcast.19, ...), custom_call_target="tpu_custom_call" | custom-call | bytes 12582912 | tf_op jit(solution)/shard_map/prepare/pallas_call | solution.py:92
  15.0 4.0 %collective-permute-start = (bf16[2,2,32,5120]{3,2,1,0:T(8,128)(2,1)}, bf16[2,2,32,5120]{3,2,1,0:T(8,128)(2,1)S(1)}, u32[]{:S(2)}, u32[]{:S(2)}) collective-permute-start(bf16[2,2,32,5120]{3,2,1,0:T(8,128)(2,1)} %get-tuple-element.24.f1), channel_id=1, source_target_pairs={{0,32},{32,64},{64,96},{96,128},{128,160},{160,192},{192,224},{1,3... | collective-permute-start | bytes 3932168 | tf_op jit(solution)/shard_map/ppermute | solution.py:29
  20.3 26.4 %collective-permute-done.hb = bf16[2,2,32,5120]{3,2,1,0:T(8,128)(2,1)S(1)} collective-permute-done((bf16[2,2,32,5120]{3,2,1,0:T(8,128)(2,1)}, bf16[2,2,32,5120]{3,2,1,0:T(8,128)(2,1)S(1)}, u32[]{:S(2)}, u32[]{:S(2)}) %collective-permute-start) | collective-permute-done | bytes 1310752 | tf_op jit(solution)/shard_map/ppermute | solution.py:29
  46.7 3.9 %collective-permute-done.1.ha = bf16[2,2,32,5120]{3,2,1,0:T(8,128)(2,1)S(1)} collective-permute-done((bf16[2,2,32,5120]{3,2,1,0:T(8,128)(2,1)}, bf16[2,2,32,5120]{3,2,1,0:T(8,128)(2,1)S(1)}, u32[]{:S(2)}, u32[]{:S(2)}) %collective-permute-start.1) | collective-permute-done | bytes 1310752 | tf_op jit(solution)/shard_map/ppermute | solution.py:29
  51.2 5.3 %collective-permute-start.5 = (bf16[2,2,32,5120]{3,2,1,0:T(8,128)(2,1)S(1)}, bf16[2,2,32,5120]{3,2,1,0:T(8,128)(2,1)S(1)}, u32[]{:S(2)}, u32[]{:S(2)}) collective-permute-start(bf16[2,2,32,5120]{3,2,1,0:T(8,128)(2,1)S(1)} %pad_maximum_fusion.1), channel_id=1, source_target_pairs={{1,0},{2,1},{3,2},{4,3},{5,4},{6,5},{7,6},{8,7},{9,8},{10,9},{11,1... | collective-permute-start | bytes 3932168 | tf_op jit(solution)/shard_map/ppermute | solution.py:29
  56.7 3.0 %collective-permute-start.4 = (bf16[2,2,32,5120]{3,2,1,0:T(8,128)(2,1)S(1)}, bf16[2,2,32,5120]{3,2,1,0:T(8,128)(2,1)S(1)}, u32[]{:S(2)}, u32[]{:S(2)}) collective-permute-start(bf16[2,2,32,5120]{3,2,1,0:T(8,128)(2,1)S(1)} %pad_maximum_fusion), channel_id=1, source_target_pairs={{0,1},{1,2},{2,3},{3,4},{4,5},{5,6},{6,7},{7,8},{8,9},{9,10},{10,1... | collective-permute-start | bytes 3932168 | tf_op jit(solution)/shard_map/ppermute | solution.py:29
  59.6 2.4 %collective-permute-start.2 = (bf16[2,2,32,5120]{3,2,1,0:T(8,128)(2,1)S(1)}, bf16[2,2,32,5120]{3,2,1,0:T(8,128)(2,1)S(1)}, u32[]{:S(2)}, u32[]{:S(2)}) collective-permute-start(bf16[2,2,32,5120]{3,2,1,0:T(8,128)(2,1)S(1)} %copy-done.15), channel_id=1, source_target_pairs={{0,1},{1,2},{2,3},{3,4},{4,5},{5,6},{6,7},{7,8},{8,9},{9,10},{10,1... | collective-permute-start | bytes 3932168 | tf_op jit(solution)/shard_map/ppermute | solution.py:29
  62.1 2.0 %collective-permute-start.3 = (bf16[2,2,32,5120]{3,2,1,0:T(8,128)(2,1)S(1)}, bf16[2,2,32,5120]{3,2,1,0:T(8,128)(2,1)S(1)}, u32[]{:S(2)}, u32[]{:S(2)}) collective-permute-start(bf16[2,2,32,5120]{3,2,1,0:T(8,128)(2,1)S(1)} %copy-done.14), channel_id=1, source_target_pairs={{1,0},{2,1},{3,2},{4,3},{5,4},{6,5},{7,6},{8,7},{9,8},{10,9},{11,1... | collective-permute-start | bytes 3932168 | tf_op jit(solution)/shard_map/ppermute | solution.py:29
  65.0 7.6 %collective-permute-done.5.ca = bf16[2,2,32,5120]{3,2,1,0:T(8,128)(2,1)S(1)} collective-permute-done((bf16[2,2,32,5120]{3,2,1,0:T(8,128)(2,1)S(1)}, bf16[2,2,32,5120]{3,2,1,0:T(8,128)(2,1)S(1)}, u32[]{:S(2)}, u32[]{:S(2)}) %collective-permute-start.5) | collective-permute-done | bytes 1310752 | tf_op jit(solution)/shard_map/ppermute | solution.py:29
  74.2 14.0 %collective-permute-done.2.rb = bf16[2,2,32,5120]{3,2,1,0:T(8,128)(2,1)S(1)} collective-permute-done((bf16[2,2,32,5120]{3,2,1,0:T(8,128)(2,1)S(1)}, bf16[2,2,32,5120]{3,2,1,0:T(8,128)(2,1)S(1)}, u32[]{:S(2)}, u32[]{:S(2)}) %collective-permute-start.2) | collective-permute-done | bytes 1310752 | tf_op jit(solution)/shard_map/ppermute | solution.py:29
  88.2 8.5 %attend.1 = (bf16[64,5120]{1,0:T(8,128)(2,1)}, bf16[64,5120]{1,0:T(8,128)(2,1)}) custom-call(s32[40]{0:T(128)S(1)} %add_add_fusion.combo_ref, bf16[4,32,5120]{2,1,0:T(8,128)(2,1)S(1)} %copy-done.1, bf16[2,2,32,5120]{3,2,1,0:T(8,128)(2,1)S(1)} %copy-done.2, bf16[2,2,32,5120]{3,2,1,0:T(8,128)(2,1)S(1)} %copy-done.3, ...), custom_call_target="tpu_custom_call" | custom-call | flops 1006632960 | bytes 33554432 | tf_op jit(solution)/shard_map/attend/pallas_call | solution.py:162
  97.9 2.5 %collective-permute-start.8 = (bf16[64,5120]{1,0:T(8,128)(2,1)}, bf16[64,5120]{1,0:T(8,128)(2,1)S(1)}, u32[]{:S(2)}, u32[]{:S(2)}) collective-permute-start(bf16[64,5120]{1,0:T(8,128)(2,1)} %get-tuple-element.32.refs_1_), channel_id=1, source_target_pairs={{0,96},{32,0},{64,32},{96,64},{1,97},{33,1},{65,33},{97,65},{2,98}... | collective-permute-start | bytes 1966088 | tf_op jit(solution)/shard_map/ppermute | solution.py:34
  100.5 2.7 %collective-permute-start.11 = (bf16[64,5120]{1,0:T(8,128)(2,1)}, bf16[64,5120]{1,0:T(8,128)(2,1)S(1)}, u32[]{:S(2)}, u32[]{:S(2)}) collective-permute-start(bf16[64,5120]{1,0:T(8,128)(2,1)} %get-tuple-element.35.refs_0_), channel_id=1, source_target_pairs={{0,96},{32,0},{64,32},{96,64},{1,97},{33,1},{65,33},{97,65},{2,98}... | collective-permute-start | bytes 1966088 | tf_op jit(solution)/shard_map/ppermute | solution.py:34
  103.1 6.0 %collective-permute-done.6.refs_2_ = bf16[64,5120]{1,0:T(8,128)(2,1)S(1)} collective-permute-done((bf16[64,5120]{1,0:T(8,128)(2,1)}, bf16[64,5120]{1,0:T(8,128)(2,1)S(1)}, u32[]{:S(2)}, u32[]{:S(2)}) %collective-permute-start.6) | collective-permute-done | bytes 655392 | tf_op jit(solution)/shard_map/ppermute | solution.py:34
  109.2 3.0 %collective-permute-start.9 = (bf16[64,5120]{1,0:T(8,128)(2,1)S(1)}, bf16[64,5120]{1,0:T(8,128)(2,1)S(1)}, u32[]{:S(2)}, u32[]{:S(2)}) collective-permute-start(bf16[64,5120]{1,0:T(8,128)(2,1)S(1)} %collective-permute-done.8.refs_5_), channel_id=1, source_target_pairs={{0,96},{32,0},{64,32},{96,64},{1,97},{33,1},{65,33},{97,65},{2,98}... | collective-permute-start | bytes 1966088 | tf_op jit(solution)/shard_map/ppermute | solution.py:34
  112.1 4.1 %collective-permute-done.10.refs_3_ = bf16[64,5120]{1,0:T(8,128)(2,1)S(1)} collective-permute-done((bf16[64,5120]{1,0:T(8,128)(2,1)}, bf16[64,5120]{1,0:T(8,128)(2,1)S(1)}, u32[]{:S(2)}, u32[]{:S(2)}) %collective-permute-start.10) | collective-permute-done | bytes 655392 | tf_op jit(solution)/shard_map/ppermute | solution.py:34
  116.2 6.9 %collective-permute-done.7.refs_0_ = bf16[64,5120]{1,0:T(8,128)(2,1)S(1)} collective-permute-done((bf16[64,5120]{1,0:T(8,128)(2,1)S(1)}, bf16[64,5120]{1,0:T(8,128)(2,1)S(1)}, u32[]{:S(2)}, u32[]{:S(2)}) %collective-permute-start.7) | collective-permute-done | bytes 655392 | tf_op jit(solution)/shard_map/ppermute | solution.py:34
  124.0 27.5 %all-gather.7.cloned.1.call-done = bf16[64,160,640]{2,1,0:T(8,128)(2,1)} async-done(((bf16[8,160,640]{2,1,0:T(8,128)(2,1)}), bf16[64,160,640]{2,1,0:T(8,128)(2,1)}) %all-gather.7.cloned.1.call-update) | async-done | bytes 13107216 | tf_op jit(solution)/shard_map/all_gather | solution.py:278
  152.6 9.2 %project.2 = (bf16[128,1280]{1,0:T(8,128)(2,1)S(1)}, bf16[128,1280]{1,0:T(8,128)(2,1)S(1)}, bf16[128,1280]{1,0:T(8,128)(2,1)S(1)}) custom-call(bf16[64,5120]{1,0:T(8,128)(2,1)S(1)} %collective-permute-done.7.refs_0_, bf16[64,5120]{1,0:T(8,128)(2,1)S(1)} %copy-done.10, bf16[64,5120]{1,0:T(8,128)(2,1)S(1)} %collective-permute-done.6.refs_2_, ...), custom_call_target="tpu_custom_call" | custom-call | flops 5033164800 | bytes 13107200 | tf_op jit(solution)/shard_map/project/pallas_call | solution.py:212
  161.8 2.3 %collective-permute-start.13 = (bf16[128,1280]{1,0:T(8,128)(2,1)S(1)}, bf16[128,1280]{1,0:T(8,128)(2,1)S(1)}, u32[]{:S(2)}, u32[]{:S(2)}) collective-permute-start(bf16[128,1280]{1,0:T(8,128)(2,1)S(1)} %get-tuple-element.37), channel_id=1, source_target_pairs={{0,64},{32,96},{64,0},{96,32},{1,65},{33,97},{65,1},{97,33},{2,66}... | collective-permute-start | bytes 983048 | tf_op jit(solution)/shard_map/ppermute | solution.py:34
  165.5 6.6 %project.3.p0 = bf16[128,1280]{1,0:T(8,128)(2,1)S(1)} custom-call(bf16[64,5120]{1,0:T(8,128)(2,1)S(1)} %copy-done.4, bf16[64,5120]{1,0:T(8,128)(2,1)S(1)} %copy-done.5, bf16[2,2,2,8,160,640]{5,4,3,2,1,0:T(8,128)(2,1)} %bitcast.16), custom_call_target="tpu_custom_call" | custom-call | flops 1677721600 | bytes 13107200 | tf_op jit(solution)/shard_map/project/pallas_call | solution.py:212
  172.5 4.9 %collective-permute-done.12.p1 = bf16[128,1280]{1,0:T(8,128)(2,1)S(1)} collective-permute-done((bf16[128,1280]{1,0:T(8,128)(2,1)S(1)}, bf16[128,1280]{1,0:T(8,128)(2,1)S(1)}, u32[]{:S(2)}, u32[]{:S(2)}) %collective-permute-start.12) | collective-permute-done | bytes 327712 | tf_op jit(solution)/shard_map/ppermute | solution.py:34
  177.4 2.7 %collective-permute-done.14.p3 = bf16[128,1280]{1,0:T(8,128)(2,1)S(1)} collective-permute-done((bf16[128,1280]{1,0:T(8,128)(2,1)S(1)}, bf16[128,1280]{1,0:T(8,128)(2,1)S(1)}, u32[]{:S(2)}, u32[]{:S(2)}) %collective-permute-start.14) | collective-permute-done | bytes 327712 | tf_op jit(solution)/shard_map/ppermute | solution.py:34
  180.0 1.8 finish.1
  (68 shorter events, 11.6 us)
Async XLA Ops:
  6.5 44.0 %all-gather.5.cloned.1.call-start = ((), (), s32[]{:S(2)}) async-start(), calls=%async_computation | async-start | bytes 1843200 | tf_op jit(solution)/shard_map/all_gather | solution.py:260
  7.3 144.2 %all-gather.7.cloned.1.call-start = ((), (), s32[]{:S(2)}) async-start(), calls=%async_computation.1 | async-start | bytes 14745600 | tf_op jit(solution)/shard_map/all_gather | solution.py:278
  8.8 42.0 %copy-start.11 = (s32[40]{0:T(128)S(1)}, s32[40]{0:T(128)}, u32[]{:S(2)}) copy-start(s32[40]{0:T(128)} %param.19) | copy-start | bytes 484
  8.8 42.0 %copy-start.12 = (s32[40]{0:T(128)S(1)}, s32[40]{0:T(128)}, u32[]{:S(2)}) copy-start(s32[40]{0:T(128)} %param.18) | copy-start | bytes 484
  8.8 42.0 %copy-start.13 = (s32[40]{0:T(128)S(1)}, s32[40]{0:T(128)}, u32[]{:S(2)}) copy-start(s32[40]{0:T(128)} %param.17) | copy-start | bytes 484
  15.0 31.7 %collective-permute-start = (bf16[2,2,32,5120]{3,2,1,0:T(8,128)(2,1)}, bf16[2,2,32,5120]{3,2,1,0:T(8,128)(2,1)S(1)}, u32[]{:S(2)}, u32[]{:S(2)}) collective-permute-start(bf16[2,2,32,5120]{3,2,1,0:T(8,128)(2,1)} %get-tuple-element.24.f1), channel_id=1, source_target_pairs={{0,32},{32,64},{64,96},{96,128},{128,160},{160,192},{192,224},{1,3... | collective-permute-start | bytes 3932168 | tf_op jit(solution)/shard_map/ppermute | solution.py:29
  19.0 31.5 %collective-permute-start.1 = (bf16[2,2,32,5120]{3,2,1,0:T(8,128)(2,1)}, bf16[2,2,32,5120]{3,2,1,0:T(8,128)(2,1)S(1)}, u32[]{:S(2)}, u32[]{:S(2)}) collective-permute-start(bf16[2,2,32,5120]{3,2,1,0:T(8,128)(2,1)} %get-tuple-element.23.f0), channel_id=1, source_target_pairs={{32,0},{64,32},{96,64},{128,96},{160,128},{192,160},{224,192},{33,... | collective-permute-start | bytes 3932168 | tf_op jit(solution)/shard_map/ppermute | solution.py:29
  51.2 21.4 %collective-permute-start.5 = (bf16[2,2,32,5120]{3,2,1,0:T(8,128)(2,1)S(1)}, bf16[2,2,32,5120]{3,2,1,0:T(8,128)(2,1)S(1)}, u32[]{:S(2)}, u32[]{:S(2)}) collective-permute-start(bf16[2,2,32,5120]{3,2,1,0:T(8,128)(2,1)S(1)} %pad_maximum_fusion.1), channel_id=1, source_target_pairs={{1,0},{2,1},{3,2},{4,3},{5,4},{6,5},{7,6},{8,7},{9,8},{10,9},{11,1... | collective-permute-start | bytes 3932168 | tf_op jit(solution)/shard_map/ppermute | solution.py:29
  56.5 31.7 %copy-start.1 = (bf16[4,32,5120]{2,1,0:T(8,128)(2,1)S(1)}, bf16[4,32,5120]{2,1,0:T(8,128)(2,1)}, u32[]{:S(2)}) copy-start(bf16[4,32,5120]{2,1,0:T(8,128)(2,1)} %get-tuple-element.22.q_ref) | copy-start | bytes 3932164
  56.5 31.7 %copy-start.2 = (bf16[2,2,32,5120]{3,2,1,0:T(8,128)(2,1)S(1)}, bf16[2,2,32,5120]{3,2,1,0:T(8,128)(2,1)}, u32[]{:S(2)}) copy-start(bf16[2,2,32,5120]{3,2,1,0:T(8,128)(2,1)} %get-tuple-element.23.f0) | copy-start | bytes 3932164
  56.5 31.7 %copy-start.3 = (bf16[2,2,32,5120]{3,2,1,0:T(8,128)(2,1)S(1)}, bf16[2,2,32,5120]{3,2,1,0:T(8,128)(2,1)}, u32[]{:S(2)}) copy-start(bf16[2,2,32,5120]{3,2,1,0:T(8,128)(2,1)} %get-tuple-element.24.f1) | copy-start | bytes 3932164
  56.7 17.5 %collective-permute-start.4 = (bf16[2,2,32,5120]{3,2,1,0:T(8,128)(2,1)S(1)}, bf16[2,2,32,5120]{3,2,1,0:T(8,128)(2,1)S(1)}, u32[]{:S(2)}, u32[]{:S(2)}) collective-permute-start(bf16[2,2,32,5120]{3,2,1,0:T(8,128)(2,1)S(1)} %pad_maximum_fusion), channel_id=1, source_target_pairs={{0,1},{1,2},{2,3},{3,4},{4,5},{5,6},{6,7},{7,8},{8,9},{9,10},{10,1... | collective-permute-start | bytes 3932168 | tf_op jit(solution)/shard_map/ppermute | solution.py:29
  59.6 28.6 %collective-permute-start.2 = (bf16[2,2,32,5120]{3,2,1,0:T(8,128)(2,1)S(1)}, bf16[2,2,32,5120]{3,2,1,0:T(8,128)(2,1)S(1)}, u32[]{:S(2)}, u32[]{:S(2)}) collective-permute-start(bf16[2,2,32,5120]{3,2,1,0:T(8,128)(2,1)S(1)} %copy-done.15), channel_id=1, source_target_pairs={{0,1},{1,2},{2,3},{3,4},{4,5},{5,6},{6,7},{7,8},{8,9},{9,10},{10,1... | collective-permute-start | bytes 3932168 | tf_op jit(solution)/shard_map/ppermute | solution.py:29
  62.1 26.1 %collective-permute-start.3 = (bf16[2,2,32,5120]{3,2,1,0:T(8,128)(2,1)S(1)}, bf16[2,2,32,5120]{3,2,1,0:T(8,128)(2,1)S(1)}, u32[]{:S(2)}, u32[]{:S(2)}) collective-permute-start(bf16[2,2,32,5120]{3,2,1,0:T(8,128)(2,1)S(1)} %copy-done.14), channel_id=1, source_target_pairs={{1,0},{2,1},{3,2},{4,3},{5,4},{6,5},{7,6},{8,7},{9,8},{10,9},{11,1... | collective-permute-start | bytes 3932168 | tf_op jit(solution)/shard_map/ppermute | solution.py:29
  96.7 12.4 %collective-permute-start.6 = (bf16[64,5120]{1,0:T(8,128)(2,1)}, bf16[64,5120]{1,0:T(8,128)(2,1)S(1)}, u32[]{:S(2)}, u32[]{:S(2)}) collective-permute-start(bf16[64,5120]{1,0:T(8,128)(2,1)} %get-tuple-element.35.refs_0_), channel_id=1, source_target_pairs={{0,32},{32,64},{64,96},{96,0},{1,33},{33,65},{65,97},{97,1},{2,34}... | collective-permute-start | bytes 1966088 | tf_op jit(solution)/shard_map/ppermute | solution.py:34
  97.9 11.2 %collective-permute-start.8 = (bf16[64,5120]{1,0:T(8,128)(2,1)}, bf16[64,5120]{1,0:T(8,128)(2,1)S(1)}, u32[]{:S(2)}, u32[]{:S(2)}) collective-permute-start(bf16[64,5120]{1,0:T(8,128)(2,1)} %get-tuple-element.32.refs_1_), channel_id=1, source_target_pairs={{0,96},{32,0},{64,32},{96,64},{1,97},{33,1},{65,33},{97,65},{2,98}... | collective-permute-start | bytes 1966088 | tf_op jit(solution)/shard_map/ppermute | solution.py:34
  100.5 15.7 %collective-permute-start.10 = (bf16[64,5120]{1,0:T(8,128)(2,1)}, bf16[64,5120]{1,0:T(8,128)(2,1)S(1)}, u32[]{:S(2)}, u32[]{:S(2)}) collective-permute-start(bf16[64,5120]{1,0:T(8,128)(2,1)} %get-tuple-element.32.refs_1_), channel_id=1, source_target_pairs={{0,32},{32,64},{64,96},{96,0},{1,33},{33,65},{65,97},{97,1},{2,34}... | collective-permute-start | bytes 1966088 | tf_op jit(solution)/shard_map/ppermute | solution.py:34
  100.5 15.7 %collective-permute-start.11 = (bf16[64,5120]{1,0:T(8,128)(2,1)}, bf16[64,5120]{1,0:T(8,128)(2,1)S(1)}, u32[]{:S(2)}, u32[]{:S(2)}) collective-permute-start(bf16[64,5120]{1,0:T(8,128)(2,1)} %get-tuple-element.35.refs_0_), channel_id=1, source_target_pairs={{0,96},{32,0},{64,32},{96,64},{1,97},{33,1},{65,33},{97,65},{2,98}... | collective-permute-start | bytes 1966088 | tf_op jit(solution)/shard_map/ppermute | solution.py:34
  109.2 13.9 %collective-permute-start.7 = (bf16[64,5120]{1,0:T(8,128)(2,1)S(1)}, bf16[64,5120]{1,0:T(8,128)(2,1)S(1)}, u32[]{:S(2)}, u32[]{:S(2)}) collective-permute-start(bf16[64,5120]{1,0:T(8,128)(2,1)S(1)} %collective-permute-done.6.refs_2_), channel_id=1, source_target_pairs={{0,32},{32,64},{64,96},{96,0},{1,33},{33,65},{65,97},{97,1},{2,34}... | collective-permute-start | bytes 1966088 | tf_op jit(solution)/shard_map/ppermute | solution.py:34
  109.2 13.9 %collective-permute-start.9 = (bf16[64,5120]{1,0:T(8,128)(2,1)S(1)}, bf16[64,5120]{1,0:T(8,128)(2,1)S(1)}, u32[]{:S(2)}, u32[]{:S(2)}) collective-permute-start(bf16[64,5120]{1,0:T(8,128)(2,1)S(1)} %collective-permute-done.8.refs_5_), channel_id=1, source_target_pairs={{0,96},{32,0},{64,32},{96,64},{1,97},{33,1},{65,33},{97,65},{2,98}... | collective-permute-start | bytes 1966088 | tf_op jit(solution)/shard_map/ppermute | solution.py:34
  161.8 10.7 %collective-permute-start.13 = (bf16[128,1280]{1,0:T(8,128)(2,1)S(1)}, bf16[128,1280]{1,0:T(8,128)(2,1)S(1)}, u32[]{:S(2)}, u32[]{:S(2)}) collective-permute-start(bf16[128,1280]{1,0:T(8,128)(2,1)S(1)} %get-tuple-element.37), channel_id=1, source_target_pairs={{0,64},{32,96},{64,0},{96,32},{1,65},{33,97},{65,1},{97,33},{2,66}... | collective-permute-start | bytes 983048 | tf_op jit(solution)/shard_map/ppermute | solution.py:34
  164.1 13.3 %collective-permute-start.12 = (bf16[128,1280]{1,0:T(8,128)(2,1)S(1)}, bf16[128,1280]{1,0:T(8,128)(2,1)S(1)}, u32[]{:S(2)}, u32[]{:S(2)}) collective-permute-start(bf16[128,1280]{1,0:T(8,128)(2,1)S(1)} %get-tuple-element.36), channel_id=1, source_target_pairs={{0,96},{32,0},{64,32},{96,64},{1,97},{33,1},{65,33},{97,65},{2,98}... | collective-permute-start | bytes 983048 | tf_op jit(solution)/shard_map/ppermute | solution.py:34
  165.2 14.8 %copy-start.6 = (f32[5120]{0:T(1024)S(1)}, f32[5120]{0:T(1024)}, u32[]{:S(2)}) copy-start(f32[5120]{0:T(1024)} %param.21) | copy-start | bytes 61444
  165.2 14.8 %collective-permute-start.14 = (bf16[128,1280]{1,0:T(8,128)(2,1)S(1)}, bf16[128,1280]{1,0:T(8,128)(2,1)S(1)}, u32[]{:S(2)}, u32[]{:S(2)}) collective-permute-start(bf16[128,1280]{1,0:T(8,128)(2,1)S(1)} %get-tuple-element.38), channel_id=1, source_target_pairs={{0,32},{32,64},{64,96},{96,0},{1,33},{33,65},{65,97},{97,1},{2,34}... | collective-permute-start | bytes 983048 | tf_op jit(solution)/shard_map/ppermute | solution.py:34
  (9 other events, 63.8 us)
Sparse Core Ops, SparseCore 0:
  9.1 39.8 all-gather.4
  50.9 100.5 all-gather.6

commit v5 on v4

--- a/solution.py
+++ b/solution.py
@@ -11,7 +11,7 @@
 HEAD = 128
 TM = ("y_lo", "x")
 SP = ("y_hi", "z", "core")
-CHUNKS = 1
+CHUNKS = 2
 COMBOS = 12
 F32, BF16 = jnp.float32, jnp.bfloat16
 
@@ -34,6 +34,11 @@
     return lax.ppermute(block, axis, [(i, (i + distance) % n) for i in range(n)])
 
 
+def along_y(block, distance):
+    at = lambda y: (y % 2) * 2 + y // 2
+    return lax.ppermute(block, ("y_lo", "y_hi"), [(at(y), at((y + distance) % 4)) for y in range(4)])
+
+
 def in_hbm(array):
     return pltpu.with_memory_space_constraint(array, pltpu.HBM)
 
@@ -55,20 +60,19 @@
     qn_ref[0] = normed(q_ref, qg_ref)
     kn = normed(k_ref, kg_ref)
     v = v_ref[0]
-    width = inner // (len(outs) // 4)
-    for c in range(len(outs) // 4):
-        f0, f1, r0, r1 = outs[4 * c : 4 * c + 4]
+    for which, ref in ((0, outs[0]), (1, outs[1])):
+
+        @pl.when(r == which)
+        def _(ref=ref):
+            ref[0, 0] = kn
+            ref[0, 1] = v
+
+    width = inner // CHUNKS
+    for c in range(CHUNKS):
         lanes = slice(c * width, (c + 1) * width)
-        for which, ref in ((0, f0), (1, f1)):
+        for which, ref in ((0, outs[2 + 2 * c]), (1, outs[3 + 2 * c])):
 
             @pl.when(f == which)
-            def _(ref=ref):
-                ref[0, 0] = kn[:, lanes]
-                ref[0, 1] = v[:, lanes]
-
-        for which, ref in ((0, r0), (1, r1)):
-
-            @pl.when(r == which)
             def _(ref=ref):
                 ref[0, 0] = kn[:, lanes]
                 ref[0, 1] = v[:, lanes]
@@ -79,15 +83,13 @@
     width = inner // CHUNKS
     token_spec = pl.BlockSpec((1, nw, inner), lambda i: (i, 0, 0))
     gain_spec = pl.BlockSpec((1, inner), lambda i: (0, 0))
-    out_shape = [pltpu.HBM(queries.shape, BF16)]
-    out_specs = [token_spec]
+    out_shape = [pltpu.HBM(queries.shape, BF16)] + [pltpu.HBM((2, 2, nw, inner), BF16)] * 2
+    out_specs = [token_spec] + [pl.BlockSpec((1, 2, nw, inner), lambda i: (i // 2, 0, 0, 0))] * 2
     for _ in range(CHUNKS):
-        out_shape += [pltpu.HBM((2, 2, nw, width), BF16)] * 4
+        out_shape += [pltpu.HBM((2, 2, nw, width), BF16)] * 2
         out_specs += [
             pl.BlockSpec((1, 2, nw, width), lambda i: (jnp.minimum(i, 1), 0, 0, 0)),
             pl.BlockSpec((1, 2, nw, width), lambda i: (jnp.maximum(i - 2, 0), 0, 0, 0)),
-            pl.BlockSpec((1, 2, nw, width), lambda i: (i // 2, 0, 0, 0)),
-            pl.BlockSpec((1, 2, nw, width), lambda i: (i // 2, 0, 0, 0)),
         ]
     return pl.pallas_call(
         prepare_kernel,
@@ -117,7 +119,7 @@
     return jnp.where(allowed, 0.0, -jnp.inf).astype(F32)
 
 
-def attend_kernel(heads, scale, combo_ref, q_ref, f0, f1, hb, ha, rb, ra, cb, ca, mask_ref, *out_refs):
+def attend_kernel(heads, scale, combo_ref, q_ref, f0, f1, hb, ha, rb, ra, cb, ca, mask_ref, out_ref):
     step = pl.program_id(0)
     frames = ((cb.at[0], hb, ca.at[0]), (rb.at[0], f0, ra.at[0]), (rb.at[1], f1, ra.at[1]), (cb.at[1], ha, ca.at[1]))
 
@@ -150,45 +152,51 @@
         for f in range(2):
             w, total = weights[h, f]
             o = jnp.dot(w, values[f * group : (f + 3) * group], preferred_element_type=F32)
-            out_refs[f][:, lanes] = (o / total).astype(BF16)
-
-
-def attend(combo, chunk, qn, own, halos, masks, heads=8):
+            out_ref[f, :, lanes] = (o / total).astype(BF16)
+
+
+def attend(combo, chunk, qn, own, frames, rows, corners, masks, heads=10):
     groups, nw, inner = qn.shape
     width = own[0].shape[-1]
     lanes = heads * HEAD
     steps = width // lanes
     kv_spec = pl.BlockSpec((2, 2, nw, lanes), lambda i, *_: (0, 0, 0, i))
+    row_spec = pl.BlockSpec((2, 2, nw, lanes), lambda i, *_: (0, 0, 0, chunk * steps + i))
     return pl.pallas_call(
         functools.partial(attend_kernel, heads, HEAD**-0.5),
         grid_spec=pltpu.PrefetchScalarGridSpec(
             num_scalar_prefetch=1,
             grid=(steps,),
             in_specs=[pl.BlockSpec((groups, nw, lanes), lambda i, *_: (0, 0, chunk * steps + i))]
-            + [kv_spec] * 8
+            + [kv_spec] * 4
+            + [row_spec] * 2
+            + [kv_spec] * 2
             + [pl.BlockSpec(masks.shape, lambda i, *_: (0, 0, 0, 0))],
-            out_specs=[pl.BlockSpec((2 * nw, lanes), lambda i, *_: (0, i))] * 2,
+            out_specs=pl.BlockSpec((2, 2 * nw, lanes), lambda i, *_: (0, 0, i)),
         ),
-        out_shape=[pltpu.HBM((2 * nw, width), BF16)] * 2,
+        out_shape=pltpu.HBM((2, 2 * nw, width), BF16),
         compiler_params=params(),
         cost_estimate=pl.CostEstimate(flops=4 * 128 * 384 * width, bytes_accessed=32 << 20, transcendentals=0),
         name="attend",
-    )(combo, qn, *own, *halos, masks)
-
-
-def project_kernel(blocks, *refs):
-    ins, w_ref, outs, acc = refs[:blocks], refs[blocks], refs[blocks + 1 : -1], refs[-1]
+    )(combo, qn, *own, *frames, *rows, *corners, masks)
+
+
+def project_kernel(inside, blocks, _, *refs):
+    ins, (w0, w1), outs, (acc, a_buf) = refs[:blocks], refs[blocks : blocks + 2], refs[blocks + 2 : -2], refs[-2:]
     k = pl.program_id(0)
-    a = jnp.concatenate([i[...] for i in ins], axis=0)
-    _, halves, cores, zs, _, _ = w_ref.shape
+    for c in range(CHUNKS):
+
+        @pl.when(k // inside == c)
+        def _(c=c):
+            of_chunk = ins[c * (blocks // CHUNKS) : (c + 1) * (blocks // CHUNKS)]
+            a_buf[...] = jnp.concatenate([i[...].reshape(-1, i.shape[-1]) for i in of_chunk], axis=0)
+
+    zs, cores = w0.shape[:2]
     w = jnp.concatenate(
-        [
-            jnp.concatenate([w_ref[0, n, c, z] for z in range(zs) for c in range(cores)], axis=0)
-            for n in range(halves)
-        ],
+        [jnp.concatenate([w_ref[z, c, 0] for z in range(zs) for c in range(cores)], axis=0) for w_ref in (w0, w1)],
         axis=1,
     )
-    term = jnp.dot(a, w, preferred_element_type=F32)
+    term = jnp.dot(a_buf[...], w, preferred_element_type=F32)
 
     @pl.when(k == 0)
     def _():
@@ -205,24 +213,44 @@
             o[...] = acc[d * rows : (d + 1) * rows, :].astype(BF16)
 
 
-def project(blocks, weight, zs=4):
-    rows, inner = blocks[0].shape
-    groups, halves, cores, depth, part, half = weight.shape
-    cols, devices, inside, step = halves * half, len(blocks) // 2, depth // zs, cores * zs * part
+def project(y, chunks, weight, rows=128, zs=4):
+    depth, cores, ys, part, half = weight.shape
+    step, inside = cores * zs * part, depth // zs
+    steps = 2 * inside
+    inside_chunk = steps // CHUNKS
+    blocks = [b for blocks in chunks for b in blocks]
+    tokens = sum(b.shape[0] * b.shape[1] for b in chunks[0])
+    devices, cols = tokens // rows, 2 * half
+
+    def block_spec(c, b):
+        return pl.BlockSpec(
+            b.shape[:2] + (step,), lambda k, _: (0, 0, jnp.clip(k - c * inside_chunk, 0, inside_chunk - 1))
+        )
+
+    def weight_spec(y_lo):
+        return pl.BlockSpec(
+            (zs, cores, 1, part, half),
+            lambda k, y_ref: (k % inside, 0, lax.rem(y_ref[0] + ys - (2 * (k // inside) + y_lo), ys), 0, 0),
+        )
+
+    weight = in_hbm(weight)
     return pl.pallas_call(
-        functools.partial(project_kernel, len(blocks)),
-        grid=(groups * inside,),
-        in_specs=[pl.BlockSpec((rows, step), lambda k: (0, k))] * len(blocks)
-        + [pl.BlockSpec((1, halves, cores, zs, part, half), lambda k: (k // inside, 0, 0, k % inside, 0, 0))],
-        out_specs=[pl.BlockSpec((2 * rows, cols), lambda k: (0, 0))] * devices,
-        out_shape=[jax.ShapeDtypeStruct((2 * rows, cols), BF16)] * devices,
-        scratch_shapes=[pltpu.VMEM((2 * devices * rows, cols), F32)],
-        compiler_params=params(40),
+        functools.partial(project_kernel, inside_chunk, len(blocks)),
+        grid_spec=pltpu.PrefetchScalarGridSpec(
+            num_scalar_prefetch=1,
+            grid=(steps,),
+            in_specs=[block_spec(c, b) for c, blocks in enumerate(chunks) for b in blocks]
+            + [weight_spec(0), weight_spec(1)],
+            out_specs=[pl.BlockSpec((rows, cols), lambda k, _: (0, 0))] * devices,
+            scratch_shapes=[pltpu.VMEM((tokens, cols), F32), pltpu.VMEM((tokens, step), BF16)],
+        ),
+        out_shape=[jax.ShapeDtypeStruct((rows, cols), BF16)] * devices,
+        compiler_params=params(28),
         cost_estimate=pl.CostEstimate(
-            flops=4 * devices * rows * inner * cols, bytes_accessed=2 * inner * cols, transcendentals=0
+            flops=2 * tokens * step * steps * cols, bytes_accessed=2 * step * steps * cols, transcendentals=0
         ),
         name="project",
-    )(*blocks, in_hbm(weight))
+    )(y, *blocks, weight, weight)
 
 
 def finish_kernel(x_ref, hidden, gate, p0, p1, p2, p3, out):
@@ -257,9 +285,13 @@
 def shards(hidden_in, queries, keys, values, query_gain, key_gain, reach_time, reach_rows, reach_cols, out_weight, gate):
     frames, rows, nw, inner = queries.shape
     width = hidden_in.shape[3]
-    weight = lax.all_gather(out_weight, "z", axis=0, tiled=False)
+    near_weights = [out_weight] + [along_y(out_weight, d) for d in (1, 2, 3)]
+
     tokens = [a.reshape(frames * rows, nw, inner) for a in (queries, keys, values)]
-    qn, *own = prepare(*tokens, query_gain, key_gain)
+    qn, r0, r1, *own = prepare(*tokens, query_gain, key_gain)
+    *near_weights, qn = lax.optimization_barrier((*near_weights, qn))
+    weight = lax.all_gather(jnp.stack(near_weights), ("z", "core"), axis=0, tiled=False)
+    weight = weight.reshape((lax.axis_size("z"), lax.axis_size("core")) + weight.shape[1:])
     masks = mask_tables(
         lax.axis_index(TM) * frames,
         lax.axis_index(SP) * rows,
@@ -269,26 +301,32 @@
     )
     combo = reach_time * 6 + reach_rows * 3 + reach_cols
     heads = reach_time.shape[0] // CHUNKS
-    outs = []
+    rb, ra = passed_along(r1, SP, 1), passed_along(r0, SP, -1)
+    mine, near, hb, a = [], [], None, None
     for c in range(CHUNKS):
-        f0, f1, r0, r1 = own[4 * c : 4 * c + 4]
+        f0, f1 = own[2 * c : 2 * c + 2]
         hb, ha = passed_along(f1, TM, 1), passed_along(f0, TM, -1)
+        corner_b, corner_a = hb, ha
+        if c:
+            corner_b, corner_a, a = lax.optimization_barrier((hb, ha, a))
+            mine[-1] = a
+        to_above = jnp.stack([corner_b[1], corner_a[1]])
         if c == 0:
-            hb, ha, r0, r1, weight = lax.optimization_barrier((hb, ha, r0, r1, weight))
-            weight = lax.all_gather(weight, ("y_hi", "y_lo", "core"), axis=0, tiled=False)
-            weight = weight.reshape((2, 2, 2) + weight.shape[1:])
-        cb = passed_along(jnp.stack([hb[1], ha[1]]), SP, 1)
-        ca = passed_along(jnp.stack([hb[0], ha[0]]), SP, -1)
-        rb, ra = passed_along(r1, SP, 1), passed_along(r0, SP, -1)
-        a = attend(combo[c * heads : (c + 1) * heads], c, qn, (f0, f1), (hb, ha, rb, ra, cb, ca), masks)
-        outs.append(a)
-    a0, a1 = outs[0]
-    left0, right1 = shifted(a0, "x", 1), shifted(a1, "x", -1)
-    left1, right0 = shifted(a1, "x", 1), shifted(a0, "x", -1)
-    far0, far1 = shifted(left0, "x", 1), shifted(right1, "x", -1)
-    far, near_left, near_right = project([far0, far1, left0, left1, right0, right1], weight)
-    a0, far = lax.optimization_barrier((a0, far))
-    (mine,) = project([a0, a1], weight)
+            to_above, rb = lax.optimization_barrier((to_above, rb))
+        cb = passed_along(to_above, SP, 1)
+        ca = passed_along(jnp.stack([corner_b[0], corner_a[0]]), SP, -1)
+        a = attend(
+            combo[c * heads : (c + 1) * heads], c, qn, (f0, f1), (hb, ha), (rb, ra), (cb, ca), masks
+        )
+        mine.append(a)
+    for a in mine:
+        left, right = shifted(a, "x", 1), shifted(a, "x", -1)
+        far0, far1 = shifted(left[:1], "x", 1), shifted(right[1:], "x", -1)
+        near.append([far0, far1, left, right])
+    y = (2 * lax.axis_index("y_hi") + lax.axis_index("y_lo")).astype(jnp.int32)[None]
+    far, near_left, near_right = project(y, near, weight)
+    mine[0], far = lax.optimization_barrier((mine[0], far))
+    (mine,) = project(y, [[a] for a in mine], weight)
     pieces = [mine, shifted(near_left, "x", -1), shifted(far, "x", 2), shifted(near_right, "x", 1)]
     x = lax.axis_index("x").astype(jnp.int32)[None]
     out = finish(x, hidden_in.reshape(-1, width), gate, pieces)

time: 189 us -> 210 us (1.11)
  the two profiles are of different devices: /device:TPU:1 before, /device:TPU:41 now
where the time goes in v5:
time: 210 us; the launch traced here: 209 us
  waiting for transfers between devices  85.1 us (41%)
  starting transfers between devices  52.6 us (25%)
  Pallas kernels  34.9 us (17%)
  local copies, waits for them, and re-layouts  19.8 us (9%)
  between operations  13.8 us (7%)
  other arithmetic  2.29 us (1%)
    ppermute x10, waiting for transfers between devices, passed_along(): return lax.ppermute(block, axes, route)  59.2 us
    ppermute x10, starting transfers between devices, passed_along(): return lax.ppermute(block, axes, route)  34.5 us
    ppermute x11, waiting for transfers between devices, shifted(): lax.ppermute(block, axis, [(i, (i + distance) % n) for i in range(n)])  25 us
    pallas_call x2, Pallas kernels, project(): pl.pallas_call(functools.partial(project_kernel, inside_chunk, len(blocks...  16.2 us
    unnamed x58, local copies, waits for them, and re-layouts  15.7 us
    ppermute x11, starting transfers between devices, shifted(): lax.ppermute(block, axis, [(i, (i + distance) % n) for i in range(n)])  14 us
    pallas_call x2, Pallas kernels, attend(): pl.pallas_call(functools.partial(attend_kernel, heads, HEAD ** (-0.5)), g...  10.6 us
    pallas_call x1, Pallas kernels, prepare(): pl.pallas_call(prepare_kernel, grid=(groups,), in_specs=[token_spec] * 3...  6.29 us
  transfers between devices with their start and end apart: 25, of which 11 were waited for; matrix products, arithmetic and copies ran while one was open for 3% of the time, Pallas kernels for 11%

profile of v5, /device:TPU:41, one launch (start us, length us, event | category | flops | bytes accessed | tf_op | source)
XLA Modules:
  0.0 208.6 jit_solution(12068142533056879519)
XLA Ops:
  8.6 2.1 collective-permute-start.4
  12.1 6.3 %prepare.1 = (bf16[4,32,5120]{2,1,0:T(8,128)(2,1)}, bf16[2,2,32,5120]{3,2,1,0:T(8,128)(2,1)}, bf16[2,2,32,5120]{3,2,1,0:T(8,128)(2,1)}, bf16[2,2,32,2560]{3,2,1,...) custom-call(bf16[4,32,5120]{2,1,0:T(8,128)(2,1)} %bitcast.23, ...), custom_call_target="tpu_custom_call" | custom-call | bytes 12582912 | tf_op jit(solution)/shard_map/prepare/pallas_call | solution.py:94
  20.4 3.1 %collective-permute-start.5 = (bf16[2,2,32,2560]{3,2,1,0:T(8,128)(2,1)}, bf16[2,2,32,2560]{3,2,1,0:T(8,128)(2,1)S(1)}, u32[]{:S(2)}, u32[]{:S(2)}) collective-permute-start(bf16[2,2,32,2560]{3,2,1,0:T(8,128)(2,1)} %get-tuple-element.32.f1), channel_id=1, source_target_pairs={{0,32},{32,64},{64,96},{96,128},{128,160},{160,192},{192,224},{1,3... | collective-permute-start | bytes 1966088 | tf_op jit(solution)/shard_map/ppermute | solution.py:29
  23.5 4.3 %collective-permute-start.6 = (bf16[2,2,32,2560]{3,2,1,0:T(8,128)(2,1)}, bf16[2,2,32,2560]{3,2,1,0:T(8,128)(2,1)}, u32[]{:S(2)}, u32[]{:S(2)}) collective-permute-start(bf16[2,2,32,2560]{3,2,1,0:T(8,128)(2,1)} %get-tuple-element.31.f0), channel_id=1, source_target_pairs={{32,0},{64,32},{96,64},{128,96},{160,128},{192,160},{224,192},{33,... | collective-permute-start | bytes 1966088 | tf_op jit(solution)/shard_map/ppermute | solution.py:29
  27.8 5.3 %collective-permute-start.7 = (bf16[2,2,32,5120]{3,2,1,0:T(8,128)(2,1)}, bf16[2,2,32,5120]{3,2,1,0:T(8,128)(2,1)S(1)}, u32[]{:S(2)}, u32[]{:S(2)}) collective-permute-start(bf16[2,2,32,5120]{3,2,1,0:T(8,128)(2,1)} %get-tuple-element.33), channel_id=1, source_target_pairs={{0,1},{1,2},{2,3},{3,4},{4,5},{5,6},{6,7},{7,8},{8,9},{9,10},{10,1... | collective-permute-start | bytes 3932168 | tf_op jit(solution)/shard_map/ppermute | solution.py:29
  37.2 2.3 %collective-permute-done.5.hb = bf16[2,2,32,2560]{3,2,1,0:T(8,128)(2,1)S(1)} collective-permute-done((bf16[2,2,32,2560]{3,2,1,0:T(8,128)(2,1)}, bf16[2,2,32,2560]{3,2,1,0:T(8,128)(2,1)S(1)}, u32[]{:S(2)}, u32[]{:S(2)}) %collective-permute-start.5) | collective-permute-done | bytes 655392 | tf_op jit(solution)/shard_map/ppermute | solution.py:29
  39.5 3.2 %collective-permute-start.1 = (bf16[2,2,32,2560]{3,2,1,0:T(8,128)(2,1)}, bf16[2,2,32,2560]{3,2,1,0:T(8,128)(2,1)S(1)}, u32[]{:S(2)}, u32[]{:S(2)}) collective-permute-start(bf16[2,2,32,2560]{3,2,1,0:T(8,128)(2,1)} %get-tuple-element.28.f0), channel_id=1, source_target_pairs={{32,0},{64,32},{96,64},{128,96},{160,128},{192,160},{224,192},{33,... | collective-permute-start | bytes 1966088 | tf_op jit(solution)/shard_map/ppermute | solution.py:29
  44.0 4.9 %collective-permute-start.10 = (bf16[2,2,32,2560]{3,2,1,0:T(8,128)(2,1)S(1)}, bf16[2,2,32,2560]{3,2,1,0:T(8,128)(2,1)S(1)}, u32[]{:S(2)}, u32[]{:S(2)}) collective-permute-start(bf16[2,2,32,2560]{3,2,1,0:T(8,128)(2,1)S(1)} %pad_maximum_fusion.2), channel_id=1, source_target_pairs={{1,0},{2,1},{3,2},{4,3},{5,4},{6,5},{7,6},{8,7},{9,8},{10,9},{11,1... | collective-permute-start | bytes 1966088 | tf_op jit(solution)/shard_map/ppermute | solution.py:29
  49.0 24.8 %collective-permute-done.7.rb = bf16[2,2,32,5120]{3,2,1,0:T(8,128)(2,1)S(1)} collective-permute-done((bf16[2,2,32,5120]{3,2,1,0:T(8,128)(2,1)}, bf16[2,2,32,5120]{3,2,1,0:T(8,128)(2,1)S(1)}, u32[]{:S(2)}, u32[]{:S(2)}) %collective-permute-start.7) | collective-permute-done | bytes 1310752 | tf_op jit(solution)/shard_map/ppermute | solution.py:29
  73.8 4.3 %collective-permute-start.9 = (bf16[2,2,32,2560]{3,2,1,0:T(8,128)(2,1)S(1)}, bf16[2,2,32,2560]{3,2,1,0:T(8,128)(2,1)S(1)}, u32[]{:S(2)}, u32[]{:S(2)}) collective-permute-start(bf16[2,2,32,2560]{3,2,1,0:T(8,128)(2,1)S(1)} %pad_maximum_fusion.1), channel_id=1, source_target_pairs={{0,1},{1,2},{2,3},{3,4},{4,5},{5,6},{6,7},{7,8},{8,9},{9,10},{10,1... | collective-permute-start | bytes 1966088 | tf_op jit(solution)/shard_map/ppermute | solution.py:29
  79.1 22.5 %collective-permute-done.10.ca = bf16[2,2,32,2560]{3,2,1,0:T(8,128)(2,1)S(1)} collective-permute-done((bf16[2,2,32,2560]{3,2,1,0:T(8,128)(2,1)S(1)}, bf16[2,2,32,2560]{3,2,1,0:T(8,128)(2,1)S(1)}, u32[]{:S(2)}, u32[]{:S(2)}) %collective-permute-start.10) | collective-permute-done | bytes 655392 | tf_op jit(solution)/shard_map/ppermute | solution.py:29
  101.7 5.4 %attend.2.refs_0_ = bf16[2,64,2560]{2,1,0:T(8,128)(2,1)} custom-call(s32[20]{0:T(128)S(1)} %get-tuple-element.58.combo_ref, bf16[4,32,5120]{2,1,0:T(8,128)(2,1)S(1)} %copy-done, bf16[2,2,32,2560]{3,2,1,0:T(8,128)(2,1)} %get-tuple-element.31.f0, bf16[2,2,32,2560]{3,2,1,0:T(8,128)(2,1)} %get-tuple-element.32.f1, ...), custom_call_target="tpu_custom_call" | custom-call | flops 503316480 | bytes 33554432 | tf_op jit(solution)/shard_map/attend/pallas_call | solution.py:165
  110.5 3.6 %collective-permute-start.15 = (bf16[2,2,32,2560]{3,2,1,0:T(8,128)(2,1)S(1)}, bf16[2,2,32,2560]{3,2,1,0:T(8,128)(2,1)S(1)}, u32[]{:S(2)}, u32[]{:S(2)}) collective-permute-start(bf16[2,2,32,2560]{3,2,1,0:T(8,128)(2,1)S(1)} %pad_maximum_fusion.3), channel_id=1, source_target_pairs={{0,1},{1,2},{2,3},{3,4},{4,5},{5,6},{6,7},{7,8},{8,9},{9,10},{10,1... | collective-permute-start | bytes 1966088 | tf_op jit(solution)/shard_map/ppermute | solution.py:29
  114.2 2.7 %collective-permute-start.13 = (bf16[2,64,2560]{2,1,0:T(8,128)(2,1)S(1)}, bf16[2,64,2560]{2,1,0:T(8,128)(2,1)S(1)}, u32[]{:S(2)}, u32[]{:S(2)}) collective-permute-start(bf16[2,64,2560]{2,1,0:T(8,128)(2,1)S(1)} %copy-done.1), channel_id=1, source_target_pairs={{0,96},{32,0},{64,32},{96,64},{1,97},{33,1},{65,33},{97,65},{2,98}... | collective-permute-start | bytes 1966088 | tf_op jit(solution)/shard_map/ppermute | solution.py:34
  116.9 9.6 %collective-permute-done.16.ca = bf16[2,2,32,2560]{3,2,1,0:T(8,128)(2,1)S(1)} collective-permute-done((bf16[2,2,32,2560]{3,2,1,0:T(8,128)(2,1)S(1)}, bf16[2,2,32,2560]{3,2,1,0:T(8,128)(2,1)S(1)}, u32[]{:S(2)}, u32[]{:S(2)}) %collective-permute-start.16) | collective-permute-done | bytes 655392 | tf_op jit(solution)/shard_map/ppermute | solution.py:29
  126.5 5.2 %attend.3.refs_1_ = bf16[2,64,2560]{2,1,0:T(8,128)(2,1)} custom-call(s32[20]{0:T(128)S(1)} %get-tuple-element.57.combo_ref, bf16[4,32,5120]{2,1,0:T(8,128)(2,1)S(1)} %copy-done, bf16[2,2,32,2560]{3,2,1,0:T(8,128)(2,1)S(1)} %copy-done.12, bf16[2,2,32,2560]{3,2,1,0:T(8,128)(2,1)S(1)} %copy-done.13, bf16[2,2,32,2560]{3,2,1,0:T(8,128)(2,1)} %collective-permute-done.hb, ...), custom_call_target="tpu_custom_call" | custom-call | flops 503316480 | bytes 33554432 | tf_op jit(solution)/shard_map/attend/pallas_call | solution.py:165
  136.0 2.1 %collective-permute-start.14 = (bf16[1,64,2560]{2,1,0:T(8,128)(2,1)S(1)}, bf16[1,64,2560]{2,1,0:T(8,128)(2,1)S(1)}, u32[]{:S(2)}, u32[]{:S(2)}) collective-permute-start(bf16[1,64,2560]{2,1,0:T(8,128)(2,1)S(1)} %slice.61), channel_id=1, source_target_pairs={{0,96},{32,0},{64,32},{96,64},{1,97},{33,1},{65,33},{97,65},{2,98}... | collective-permute-start | bytes 983048 | tf_op jit(solution)/shard_map/ppermute | solution.py:34
  138.2 11.7 %collective-permute-done.17.refs_6_ = bf16[2,64,2560]{2,1,0:T(8,128)(2,1)S(1)} collective-permute-done((bf16[2,64,2560]{2,1,0:T(8,128)(2,1)}, bf16[2,64,2560]{2,1,0:T(8,128)(2,1)S(1)}, u32[]{:S(2)}, u32[]{:S(2)}) %collective-permute-start.17) | collective-permute-done | bytes 655392 | tf_op jit(solution)/shard_map/ppermute | solution.py:34
  153.0 2.7 %collective-permute-start.20 = (bf16[1,64,2560]{2,1,0:T(8,128)(2,1)}, bf16[1,64,2560]{2,1,0:T(8,128)(2,1)S(1)}, u32[]{:S(2)}, u32[]{:S(2)}) collective-permute-start(bf16[1,64,2560]{2,1,0:T(8,128)(2,1)} %slice.63), channel_id=1, source_target_pairs={{0,96},{32,0},{64,32},{96,64},{1,97},{33,1},{65,33},{97,65},{2,98}... | collective-permute-start | bytes 983048 | tf_op jit(solution)/shard_map/ppermute | solution.py:34
  158.4 4.1 %collective-permute-done.18.refs_4_ = bf16[1,64,2560]{2,1,0:T(8,128)(2,1)S(1)} collective-permute-done((bf16[1,64,2560]{2,1,0:T(8,128)(2,1)}, bf16[1,64,2560]{2,1,0:T(8,128)(2,1)S(1)}, u32[]{:S(2)}, u32[]{:S(2)}) %collective-permute-start.18) | collective-permute-done | bytes 327712 | tf_op jit(solution)/shard_map/ppermute | solution.py:34
  172.1 9.5 %project.2 = (bf16[128,1280]{1,0:T(8,128)(2,1)S(1)}, bf16[128,1280]{1,0:T(8,128)(2,1)S(1)}, bf16[128,1280]{1,0:T(8,128)(2,1)S(1)}) custom-call(s32[1]{0:T(128)} %bitcast.3._, bf16[1,64,2560]{2,1,0:T(8,128)(2,1)S(1)} %copy-done.15, bf16[1,64,2560]{2,1,0:T(8,128)(2,1)S(1)} %copy-done.17, bf16[2,64,2560]{2,1,0:T(8,128)(2,1)S(1)} %copy-done.4, ...), custom_call_target="tpu_custom_call" | custom-call | flops 5033164800 | bytes 13107200 | tf_op jit(solution)/shard_map/project/pallas_call | solution.py:237
  181.6 2.0 collective-permute-start.22
  185.1 6.7 %project.3.p0 = bf16[128,1280]{1,0:T(8,128)(2,1)S(1)} custom-call(s32[1]{0:T(128)} %bitcast.3._, bf16[2,64,2560]{2,1,0:T(8,128)(2,1)S(1)} %copy-done.1, bf16[2,64,2560]{2,1,0:T(8,128)(2,1)S(1)} %copy-done.2, bf16[8,2,4,160,640]{4,3,2,1,0:T(8,128)(2,1)} %bitcast.21, bf16[8,2,4,160,640]{4,3,2,1,0:T(8,128)(2,1)} %bitcast.22), custom_call_target="tpu_custom_call" | custom-call | flops 1677721600 | bytes 13107200 | tf_op jit(solution)/shard_map/project/pallas_call | solution.py:237
  192.9 6.9 %collective-permute-done.21.p1 = bf16[128,1280]{1,0:T(8,128)(2,1)S(1)} collective-permute-done((bf16[128,1280]{1,0:T(8,128)(2,1)S(1)}, bf16[128,1280]{1,0:T(8,128)(2,1)S(1)}, u32[]{:S(2)}, u32[]{:S(2)}) %collective-permute-start.21) | collective-permute-done | bytes 327712 | tf_op jit(solution)/shard_map/ppermute | solution.py:34
  (121 shorter events, 39.5 us)
Async XLA Ops:
  6.5 157.3 %all-gather.3.cloned.1.call-start = ((), (), s32[]{:S(2)}) async-start(), calls=%async_computation | async-start | bytes 13926400 | tf_op jit(solution)/shard_map/all_gather | solution.py:293
  6.5 11.8 %collective-permute-start.2 = (bf16[160,640]{1,0:T(8,128)(2,1)}, bf16[160,640]{1,0:T(8,128)(2,1)S(1)}, u32[]{:S(2)}, u32[]{:S(2)}) collective-permute-start(bf16[160,640]{1,0:T(8,128)(2,1)} %param.20), channel_id=1, source_target_pairs={{0,128},{128,16},{16,144},{144,0},{1,129},{129,17},{17,145},{145,1... | collective-permute-start | bytes 614408 | tf_op jit(solution)/shard_map/ppermute | solution.py:39
  7.8 10.5 %collective-permute-start.3 = (bf16[160,640]{1,0:T(8,128)(2,1)}, bf16[160,640]{1,0:T(8,128)(2,1)S(1)}, u32[]{:S(2)}, u32[]{:S(2)}) collective-permute-start(bf16[160,640]{1,0:T(8,128)(2,1)} %param.20), channel_id=1, source_target_pairs={{0,16},{128,144},{16,0},{144,128},{1,17},{129,145},{17,1},{145,129... | collective-permute-start | bytes 614408 | tf_op jit(solution)/shard_map/ppermute | solution.py:39
  8.6 10.7 %collective-permute-start.4 = (bf16[160,640]{1,0:T(8,128)(2,1)}, bf16[160,640]{1,0:T(8,128)(2,1)S(1)}, u32[]{:S(2)}, u32[]{:S(2)}) collective-permute-start(bf16[160,640]{1,0:T(8,128)(2,1)} %param.20), channel_id=1, source_target_pairs={{0,144},{128,0},{16,128},{144,16},{1,145},{129,1},{17,129},{145,17... | collective-permute-start | bytes 614408 | tf_op jit(solution)/shard_map/ppermute | solution.py:39
  20.4 19.1 %collective-permute-start.5 = (bf16[2,2,32,2560]{3,2,1,0:T(8,128)(2,1)}, bf16[2,2,32,2560]{3,2,1,0:T(8,128)(2,1)S(1)}, u32[]{:S(2)}, u32[]{:S(2)}) collective-permute-start(bf16[2,2,32,2560]{3,2,1,0:T(8,128)(2,1)} %get-tuple-element.32.f1), channel_id=1, source_target_pairs={{0,32},{32,64},{64,96},{96,128},{128,160},{160,192},{192,224},{1,3... | collective-permute-start | bytes 1966088 | tf_op jit(solution)/shard_map/ppermute | solution.py:29
  23.5 19.2 %collective-permute-start.6 = (bf16[2,2,32,2560]{3,2,1,0:T(8,128)(2,1)}, bf16[2,2,32,2560]{3,2,1,0:T(8,128)(2,1)}, u32[]{:S(2)}, u32[]{:S(2)}) collective-permute-start(bf16[2,2,32,2560]{3,2,1,0:T(8,128)(2,1)} %get-tuple-element.31.f0), channel_id=1, source_target_pairs={{32,0},{64,32},{96,64},{128,96},{160,128},{192,160},{224,192},{33,... | collective-permute-start | bytes 1966088 | tf_op jit(solution)/shard_map/ppermute | solution.py:29
  27.8 46.1 %collective-permute-start.7 = (bf16[2,2,32,5120]{3,2,1,0:T(8,128)(2,1)}, bf16[2,2,32,5120]{3,2,1,0:T(8,128)(2,1)S(1)}, u32[]{:S(2)}, u32[]{:S(2)}) collective-permute-start(bf16[2,2,32,5120]{3,2,1,0:T(8,128)(2,1)} %get-tuple-element.33), channel_id=1, source_target_pairs={{0,1},{1,2},{2,3},{3,4},{4,5},{5,6},{6,7},{7,8},{8,9},{9,10},{10,1... | collective-permute-start | bytes 3932168 | tf_op jit(solution)/shard_map/ppermute | solution.py:29
  33.1 68.5 %collective-permute-start.8 = (bf16[2,2,32,5120]{3,2,1,0:T(8,128)(2,1)}, bf16[2,2,32,5120]{3,2,1,0:T(8,128)(2,1)S(1)}, u32[]{:S(2)}, u32[]{:S(2)}) collective-permute-start(bf16[2,2,32,5120]{3,2,1,0:T(8,128)(2,1)} %get-tuple-element.35), channel_id=1, source_target_pairs={{1,0},{2,1},{3,2},{4,3},{5,4},{6,5},{7,6},{8,7},{9,8},{10,9},{11,1... | collective-permute-start | bytes 3932168 | tf_op jit(solution)/shard_map/ppermute | solution.py:29
  35.0 72.0 %collective-permute-start = (bf16[2,2,32,2560]{3,2,1,0:T(8,128)(2,1)}, bf16[2,2,32,2560]{3,2,1,0:T(8,128)(2,1)}, u32[]{:S(2)}, u32[]{:S(2)}) collective-permute-start(bf16[2,2,32,2560]{3,2,1,0:T(8,128)(2,1)} %get-tuple-element.27.f1), channel_id=1, source_target_pairs={{0,32},{32,64},{64,96},{96,128},{128,160},{160,192},{192,224},{1,3... | collective-permute-start | bytes 1966088 | tf_op jit(solution)/shard_map/ppermute | solution.py:29
  39.5 67.6 %collective-permute-start.1 = (bf16[2,2,32,2560]{3,2,1,0:T(8,128)(2,1)}, bf16[2,2,32,2560]{3,2,1,0:T(8,128)(2,1)S(1)}, u32[]{:S(2)}, u32[]{:S(2)}) collective-permute-start(bf16[2,2,32,2560]{3,2,1,0:T(8,128)(2,1)} %get-tuple-element.28.f0), channel_id=1, source_target_pairs={{32,0},{64,32},{96,64},{128,96},{160,128},{192,160},{224,192},{33,... | collective-permute-start | bytes 1966088 | tf_op jit(solution)/shard_map/ppermute | solution.py:29
  44.0 57.6 %collective-permute-start.10 = (bf16[2,2,32,2560]{3,2,1,0:T(8,128)(2,1)S(1)}, bf16[2,2,32,2560]{3,2,1,0:T(8,128)(2,1)S(1)}, u32[]{:S(2)}, u32[]{:S(2)}) collective-permute-start(bf16[2,2,32,2560]{3,2,1,0:T(8,128)(2,1)S(1)} %pad_maximum_fusion.2), channel_id=1, source_target_pairs={{1,0},{2,1},{3,2},{4,3},{5,4},{6,5},{7,6},{8,7},{9,8},{10,9},{11,1... | collective-permute-start | bytes 1966088 | tf_op jit(solution)/shard_map/ppermute | solution.py:29
  73.8 27.8 %collective-permute-start.9 = (bf16[2,2,32,2560]{3,2,1,0:T(8,128)(2,1)S(1)}, bf16[2,2,32,2560]{3,2,1,0:T(8,128)(2,1)S(1)}, u32[]{:S(2)}, u32[]{:S(2)}) collective-permute-start(bf16[2,2,32,2560]{3,2,1,0:T(8,128)(2,1)S(1)} %pad_maximum_fusion.1), channel_id=1, source_target_pairs={{0,1},{1,2},{2,3},{3,4},{4,5},{5,6},{6,7},{7,8},{8,9},{9,10},{10,1... | collective-permute-start | bytes 1966088 | tf_op jit(solution)/shard_map/ppermute | solution.py:29
  108.5 18.0 %collective-permute-start.16 = (bf16[2,2,32,2560]{3,2,1,0:T(8,128)(2,1)S(1)}, bf16[2,2,32,2560]{3,2,1,0:T(8,128)(2,1)S(1)}, u32[]{:S(2)}, u32[]{:S(2)}) collective-permute-start(bf16[2,2,32,2560]{3,2,1,0:T(8,128)(2,1)S(1)} %pad_maximum_fusion.4), channel_id=1, source_target_pairs={{1,0},{2,1},{3,2},{4,3},{5,4},{6,5},{7,6},{8,7},{9,8},{10,9},{11,1... | collective-permute-start | bytes 1966088 | tf_op jit(solution)/shard_map/ppermute | solution.py:29
  110.5 16.0 %collective-permute-start.15 = (bf16[2,2,32,2560]{3,2,1,0:T(8,128)(2,1)S(1)}, bf16[2,2,32,2560]{3,2,1,0:T(8,128)(2,1)S(1)}, u32[]{:S(2)}, u32[]{:S(2)}) collective-permute-start(bf16[2,2,32,2560]{3,2,1,0:T(8,128)(2,1)S(1)} %pad_maximum_fusion.3), channel_id=1, source_target_pairs={{0,1},{1,2},{2,3},{3,4},{4,5},{5,6},{6,7},{7,8},{8,9},{9,10},{10,1... | collective-permute-start | bytes 1966088 | tf_op jit(solution)/shard_map/ppermute | solution.py:29
  114.1 20.2 %collective-permute-start.11 = (bf16[2,64,2560]{2,1,0:T(8,128)(2,1)S(1)}, bf16[2,64,2560]{2,1,0:T(8,128)(2,1)S(1)}, u32[]{:S(2)}, u32[]{:S(2)}) collective-permute-start(bf16[2,64,2560]{2,1,0:T(8,128)(2,1)S(1)} %copy-done.1), channel_id=1, source_target_pairs={{0,32},{32,64},{64,96},{96,0},{1,33},{33,65},{65,97},{97,1},{2,34}... | collective-permute-start | bytes 1966088 | tf_op jit(solution)/shard_map/ppermute | solution.py:34
  114.2 20.4 %collective-permute-start.13 = (bf16[2,64,2560]{2,1,0:T(8,128)(2,1)S(1)}, bf16[2,64,2560]{2,1,0:T(8,128)(2,1)S(1)}, u32[]{:S(2)}, u32[]{:S(2)}) collective-permute-start(bf16[2,64,2560]{2,1,0:T(8,128)(2,1)S(1)} %copy-done.1), channel_id=1, source_target_pairs={{0,96},{32,0},{64,32},{96,64},{1,97},{33,1},{65,33},{97,65},{2,98}... | collective-permute-start | bytes 1966088 | tf_op jit(solution)/shard_map/ppermute | solution.py:34
  131.7 18.2 %collective-permute-start.17 = (bf16[2,64,2560]{2,1,0:T(8,128)(2,1)}, bf16[2,64,2560]{2,1,0:T(8,128)(2,1)S(1)}, u32[]{:S(2)}, u32[]{:S(2)}) collective-permute-start(bf16[2,64,2560]{2,1,0:T(8,128)(2,1)} %attend.3.refs_1_), channel_id=1, source_target_pairs={{0,32},{32,64},{64,96},{96,0},{1,33},{33,65},{65,97},{97,1},{2,34}... | collective-permute-start | bytes 1966088 | tf_op jit(solution)/shard_map/ppermute | solution.py:34
  132.4 19.1 %collective-permute-start.19 = (bf16[2,64,2560]{2,1,0:T(8,128)(2,1)}, bf16[2,64,2560]{2,1,0:T(8,128)(2,1)S(1)}, u32[]{:S(2)}, u32[]{:S(2)}) collective-permute-start(bf16[2,64,2560]{2,1,0:T(8,128)(2,1)} %attend.3.refs_1_), channel_id=1, source_target_pairs={{0,96},{32,0},{64,32},{96,64},{1,97},{33,1},{65,33},{97,65},{2,98}... | collective-permute-start | bytes 1966088 | tf_op jit(solution)/shard_map/ppermute | solution.py:34
  134.4 22.5 %collective-permute-start.12 = (bf16[1,64,2560]{2,1,0:T(8,128)(2,1)S(1)}, bf16[1,64,2560]{2,1,0:T(8,128)(2,1)S(1)}, u32[]{:S(2)}, u32[]{:S(2)}) collective-permute-start(bf16[1,64,2560]{2,1,0:T(8,128)(2,1)S(1)} %slice.60), channel_id=1, source_target_pairs={{0,32},{32,64},{64,96},{96,0},{1,33},{33,65},{65,97},{97,1},{2,34}... | collective-permute-start | bytes 983048 | tf_op jit(solution)/shard_map/ppermute | solution.py:34
  136.0 21.6 %collective-permute-start.14 = (bf16[1,64,2560]{2,1,0:T(8,128)(2,1)S(1)}, bf16[1,64,2560]{2,1,0:T(8,128)(2,1)S(1)}, u32[]{:S(2)}, u32[]{:S(2)}) collective-permute-start(bf16[1,64,2560]{2,1,0:T(8,128)(2,1)S(1)} %slice.61), channel_id=1, source_target_pairs={{0,96},{32,0},{64,32},{96,64},{1,97},{33,1},{65,33},{97,65},{2,98}... | collective-permute-start | bytes 983048 | tf_op jit(solution)/shard_map/ppermute | solution.py:34
  151.4 11.0 %collective-permute-start.18 = (bf16[1,64,2560]{2,1,0:T(8,128)(2,1)}, bf16[1,64,2560]{2,1,0:T(8,128)(2,1)S(1)}, u32[]{:S(2)}, u32[]{:S(2)}) collective-permute-start(bf16[1,64,2560]{2,1,0:T(8,128)(2,1)} %slice.62), channel_id=1, source_target_pairs={{0,32},{32,64},{64,96},{96,0},{1,33},{33,65},{65,97},{97,1},{2,34}... | collective-permute-start | bytes 983048 | tf_op jit(solution)/shard_map/ppermute | solution.py:34
  181.6 11.3 %collective-permute-start.22 = (bf16[128,1280]{1,0:T(8,128)(2,1)S(1)}, bf16[128,1280]{1,0:T(8,128)(2,1)S(1)}, u32[]{:S(2)}, u32[]{:S(2)}) collective-permute-start(bf16[128,1280]{1,0:T(8,128)(2,1)S(1)} %get-tuple-element.47), channel_id=1, source_target_pairs={{0,64},{32,96},{64,0},{96,32},{1,65},{33,97},{65,1},{97,33},{2,66}... | collective-permute-start | bytes 983048 | tf_op jit(solution)/shard_map/ppermute | solution.py:34
  183.6 16.1 %collective-permute-start.21 = (bf16[128,1280]{1,0:T(8,128)(2,1)S(1)}, bf16[128,1280]{1,0:T(8,128)(2,1)S(1)}, u32[]{:S(2)}, u32[]{:S(2)}) collective-permute-start(bf16[128,1280]{1,0:T(8,128)(2,1)S(1)} %get-tuple-element.46), channel_id=1, source_target_pairs={{0,96},{32,0},{64,32},{96,64},{1,97},{33,1},{65,33},{97,65},{2,98}... | collective-permute-start | bytes 983048 | tf_op jit(solution)/shard_map/ppermute | solution.py:34
  184.0 15.8 %collective-permute-start.23 = (bf16[128,1280]{1,0:T(8,128)(2,1)S(1)}, bf16[128,1280]{1,0:T(8,128)(2,1)S(1)}, u32[]{:S(2)}, u32[]{:S(2)}) collective-permute-start(bf16[128,1280]{1,0:T(8,128)(2,1)S(1)} %get-tuple-element.48), channel_id=1, source_target_pairs={{0,32},{32,64},{64,96},{96,0},{1,33},{33,65},{65,97},{97,1},{2,34}... | collective-permute-start | bytes 983048 | tf_op jit(solution)/shard_map/ppermute | solution.py:34
  (30 other events, 287.1 us)
Sparse Core Ops, SparseCore 0:
  20.5 103.7 all-gather.2

commit v6 on v5

--- a/solution.py
+++ b/solution.py
@@ -34,16 +34,11 @@
     return lax.ppermute(block, axis, [(i, (i + distance) % n) for i in range(n)])
 
 
-def along_y(block, distance):
-    at = lambda y: (y % 2) * 2 + y // 2
-    return lax.ppermute(block, ("y_lo", "y_hi"), [(at(y), at((y + distance) % 4)) for y in range(4)])
-
-
 def in_hbm(array):
     return pltpu.with_memory_space_constraint(array, pltpu.HBM)
 
 
-def params(megabytes=24):
+def params(megabytes=60):
     return pltpu.CompilerParams(vmem_limit_bytes=megabytes << 20)
 
 
@@ -181,8 +176,8 @@
     )(combo, qn, *own, *frames, *rows, *corners, masks)
 
 
-def project_kernel(inside, blocks, _, *refs):
-    ins, (w0, w1), outs, (acc, a_buf) = refs[:blocks], refs[blocks : blocks + 2], refs[blocks + 2 : -2], refs[-2:]
+def project_kernel(inside, blocks, *refs):
+    ins, w_ref, outs, (acc, a_buf) = refs[:blocks], refs[blocks], refs[blocks + 1 : -2], refs[-2:]
     k = pl.program_id(0)
     for c in range(CHUNKS):
 
@@ -191,9 +186,12 @@
             of_chunk = ins[c * (blocks // CHUNKS) : (c + 1) * (blocks // CHUNKS)]
             a_buf[...] = jnp.concatenate([i[...].reshape(-1, i.shape[-1]) for i in of_chunk], axis=0)
 
-    zs, cores = w0.shape[:2]
+    _, halves, cores, zs, _, _ = w_ref.shape
     w = jnp.concatenate(
-        [jnp.concatenate([w_ref[z, c, 0] for z in range(zs) for c in range(cores)], axis=0) for w_ref in (w0, w1)],
+        [
+            jnp.concatenate([w_ref[0, n, c, z] for z in range(zs) for c in range(cores)], axis=0)
+            for n in range(halves)
+        ],
         axis=1,
     )
     term = jnp.dot(a_buf[...], w, preferred_element_type=F32)
@@ -213,44 +211,34 @@
             o[...] = acc[d * rows : (d + 1) * rows, :].astype(BF16)
 
 
-def project(y, chunks, weight, rows=128, zs=4):
-    depth, cores, ys, part, half = weight.shape
+def project(chunks, weight, rows=128, zs=4):
+    groups, halves, cores, depth, part, half = weight.shape
     step, inside = cores * zs * part, depth // zs
-    steps = 2 * inside
+    steps = groups * inside
     inside_chunk = steps // CHUNKS
     blocks = [b for blocks in chunks for b in blocks]
     tokens = sum(b.shape[0] * b.shape[1] for b in chunks[0])
-    devices, cols = tokens // rows, 2 * half
+    devices, cols = tokens // rows, halves * half
 
     def block_spec(c, b):
         return pl.BlockSpec(
-            b.shape[:2] + (step,), lambda k, _: (0, 0, jnp.clip(k - c * inside_chunk, 0, inside_chunk - 1))
+            b.shape[:2] + (step,), lambda k: (0, 0, jnp.clip(k - c * inside_chunk, 0, inside_chunk - 1))
         )
 
-    def weight_spec(y_lo):
-        return pl.BlockSpec(
-            (zs, cores, 1, part, half),
-            lambda k, y_ref: (k % inside, 0, lax.rem(y_ref[0] + ys - (2 * (k // inside) + y_lo), ys), 0, 0),
-        )
-
-    weight = in_hbm(weight)
     return pl.pallas_call(
         functools.partial(project_kernel, inside_chunk, len(blocks)),
-        grid_spec=pltpu.PrefetchScalarGridSpec(
-            num_scalar_prefetch=1,
-            grid=(steps,),
-            in_specs=[block_spec(c, b) for c, blocks in enumerate(chunks) for b in blocks]
-            + [weight_spec(0), weight_spec(1)],
-            out_specs=[pl.BlockSpec((rows, cols), lambda k, _: (0, 0))] * devices,
-            scratch_shapes=[pltpu.VMEM((tokens, cols), F32), pltpu.VMEM((tokens, step), BF16)],
-        ),
+        grid=(steps,),
+        in_specs=[block_spec(c, b) for c, blocks in enumerate(chunks) for b in blocks]
+        + [pl.BlockSpec((1, halves, cores, zs, part, half), lambda k: (k // inside, 0, 0, k % inside, 0, 0))],
+        out_specs=[pl.BlockSpec((rows, cols), lambda k: (0, 0))] * devices,
         out_shape=[jax.ShapeDtypeStruct((rows, cols), BF16)] * devices,
-        compiler_params=params(28),
+        scratch_shapes=[pltpu.VMEM((tokens, cols), F32), pltpu.VMEM((tokens, step), BF16)],
+        compiler_params=params(),
         cost_estimate=pl.CostEstimate(
             flops=2 * tokens * step * steps * cols, bytes_accessed=2 * step * steps * cols, transcendentals=0
         ),
         name="project",
-    )(y, *blocks, weight, weight)
+    )(*blocks, in_hbm(weight))
 
 
 def finish_kernel(x_ref, hidden, gate, p0, p1, p2, p3, out):
@@ -285,13 +273,9 @@
 def shards(hidden_in, queries, keys, values, query_gain, key_gain, reach_time, reach_rows, reach_cols, out_weight, gate):
     frames, rows, nw, inner = queries.shape
     width = hidden_in.shape[3]
-    near_weights = [out_weight] + [along_y(out_weight, d) for d in (1, 2, 3)]
-
+    weight = lax.all_gather(out_weight, "z", axis=0, tiled=False)
     tokens = [a.reshape(frames * rows, nw, inner) for a in (queries, keys, values)]
     qn, r0, r1, *own = prepare(*tokens, query_gain, key_gain)
-    *near_weights, qn = lax.optimization_barrier((*near_weights, qn))
-    weight = lax.all_gather(jnp.stack(near_weights), ("z", "core"), axis=0, tiled=False)
-    weight = weight.reshape((lax.axis_size("z"), lax.axis_size("core")) + weight.shape[1:])
     masks = mask_tables(
         lax.axis_index(TM) * frames,
         lax.axis_index(SP) * rows,
@@ -302,17 +286,20 @@
     combo = reach_time * 6 + reach_rows * 3 + reach_cols
     heads = reach_time.shape[0] // CHUNKS
     rb, ra = passed_along(r1, SP, 1), passed_along(r0, SP, -1)
-    mine, near, hb, a = [], [], None, None
+    mine, near, a = [], [], None
+    halos = [(passed_along(f1, TM, 1), passed_along(f0, TM, -1)) for f0, f1 in zip(own[::2], own[1::2])]
     for c in range(CHUNKS):
         f0, f1 = own[2 * c : 2 * c + 2]
-        hb, ha = passed_along(f1, TM, 1), passed_along(f0, TM, -1)
+        hb, ha = halos[c]
         corner_b, corner_a = hb, ha
         if c:
             corner_b, corner_a, a = lax.optimization_barrier((hb, ha, a))
             mine[-1] = a
         to_above = jnp.stack([corner_b[1], corner_a[1]])
         if c == 0:
-            to_above, rb = lax.optimization_barrier((to_above, rb))
+            to_above, rb, ra, weight, halos[1] = lax.optimization_barrier((to_above, rb, ra, weight, halos[1]))
+            weight = lax.all_gather(weight, ("y_hi", "y_lo", "core"), axis=0, tiled=False)
+            weight = weight.reshape((2, 2, 2) + weight.shape[1:])
         cb = passed_along(to_above, SP, 1)
         ca = passed_along(jnp.stack([corner_b[0], corner_a[0]]), SP, -1)
         a = attend(
@@ -323,10 +310,9 @@
         left, right = shifted(a, "x", 1), shifted(a, "x", -1)
         far0, far1 = shifted(left[:1], "x", 1), shifted(right[1:], "x", -1)
         near.append([far0, far1, left, right])
-    y = (2 * lax.axis_index("y_hi") + lax.axis_index("y_lo")).astype(jnp.int32)[None]
-    far, near_left, near_right = project(y, near, weight)
+    far, near_left, near_right = project(near, weight)
     mine[0], far = lax.optimization_barrier((mine[0], far))
-    (mine,) = project(y, [[a] for a in mine], weight)
+    (mine,) = project([[a] for a in mine], weight)
     pieces = [mine, shifted(near_left, "x", -1), shifted(far, "x", 2), shifted(near_right, "x", 1)]
     x = lax.axis_index("x").astype(jnp.int32)[None]
     out = finish(x, hidden_in.reshape(-1, width), gate, pieces)

time: 210 us -> 194 us (0.924)
  the two profiles are of different devices: /device:TPU:41 before, /device:TPU:1 now
where the time goes in v6:
time: 194 us; the launch traced here: 193 us
  waiting for transfers between devices  66.3 us (34%)
  starting transfers between devices  57.2 us (29%)
  Pallas kernels  44.9 us (23%)
  between operations  13.8 us (7%)
  local copies, waits for them, and re-layouts  5.77 us (3%)
  other arithmetic  5.17 us (3%)
    ppermute x10, starting transfers between devices, passed_along(): return lax.ppermute(block, axes, route)  31.9 us
    ppermute x11, waiting for transfers between devices, shifted(): lax.ppermute(block, axis, [(i, (i + distance) % n) for i in range(n)])  30.9 us
    ppermute x10, waiting for transfers between devices, passed_along(): return lax.ppermute(block, axes, route)  30.4 us
    ppermute x11, starting transfers between devices, shifted(): lax.ppermute(block, axis, [(i, (i + distance) % n) for i in range(n)])  25.3 us
    pallas_call x2, Pallas kernels, project(): pl.pallas_call(functools.partial(project_kernel, inside_chunk, len(blocks...  18.8 us
    pallas_call x2, Pallas kernels, attend(): pl.pallas_call(functools.partial(attend_kernel, heads, HEAD ** (-0.5)), g...  15.9 us
    pallas_call x1, Pallas kernels, prepare(): pl.pallas_call(prepare_kernel, grid=(groups,), in_specs=[token_spec] * 3...  6.32 us
    all_gather x1, waiting for transfers between devices, shards(): lax.all_gather(weight, ('y_hi', 'y_lo', 'core'), axis=0, tiled=False)  4.19 us
  transfers between devices with their start and end apart: 23, of which 14 were waited for; matrix products, arithmetic and copies ran while one was open for 4% of the time, Pallas kernels for 15%

profile of v6, /device:TPU:1, one launch (start us, length us, event | category | flops | bytes accessed | tf_op | source)
XLA Modules:
  0.0 193.1 jit_solution(11491098052252165346)
XLA Ops:
  7.3 6.3 %prepare.1 = (bf16[4,32,5120]{2,1,0:T(8,128)(2,1)}, bf16[2,2,32,5120]{3,2,1,0:T(8,128)(2,1)}, bf16[2,2,32,5120]{3,2,1,0:T(8,128)(2,1)}, bf16[2,2,32,2560]{3,2,1,...) custom-call(bf16[4,32,5120]{2,1,0:T(8,128)(2,1)} %bitcast.15, ...), custom_call_target="tpu_custom_call" | custom-call | bytes 12582912 | tf_op jit(solution)/shard_map/prepare/pallas_call | solution.py:89
  13.6 4.0 %collective-permute-start = (bf16[2,2,32,2560]{3,2,1,0:T(8,128)(2,1)}, bf16[2,2,32,2560]{3,2,1,0:T(8,128)(2,1)S(1)}, u32[]{:S(2)}, u32[]{:S(2)}) collective-permute-start(bf16[2,2,32,2560]{3,2,1,0:T(8,128)(2,1)} %get-tuple-element.26.f1), channel_id=1, source_target_pairs={{0,32},{32,64},{64,96},{96,128},{128,160},{160,192},{192,224},{1,3... | collective-permute-start | bytes 1966088 | tf_op jit(solution)/shard_map/ppermute | solution.py:29
  18.9 4.0 %collective-permute-start.4 = (bf16[2,2,32,2560]{3,2,1,0:T(8,128)(2,1)}, bf16[2,2,32,2560]{3,2,1,0:T(8,128)(2,1)S(1)}, u32[]{:S(2)}, u32[]{:S(2)}) collective-permute-start(bf16[2,2,32,2560]{3,2,1,0:T(8,128)(2,1)} %get-tuple-element.30.f1), channel_id=1, source_target_pairs={{0,32},{32,64},{64,96},{96,128},{128,160},{160,192},{192,224},{1,3... | collective-permute-start | bytes 1966088 | tf_op jit(solution)/shard_map/ppermute | solution.py:29
  24.2 4.9 %collective-permute-start.2 = (bf16[2,2,32,5120]{3,2,1,0:T(8,128)(2,1)}, bf16[2,2,32,5120]{3,2,1,0:T(8,128)(2,1)S(1)}, u32[]{:S(2)}, u32[]{:S(2)}) collective-permute-start(bf16[2,2,32,5120]{3,2,1,0:T(8,128)(2,1)} %get-tuple-element.28), channel_id=1, source_target_pairs={{0,1},{1,2},{2,3},{3,4},{4,5},{5,6},{6,7},{7,8},{8,9},{9,10},{10,1... | collective-permute-start | bytes 3932168 | tf_op jit(solution)/shard_map/ppermute | solution.py:29
  31.3 4.6 %collective-permute-start.3 = (bf16[2,2,32,5120]{3,2,1,0:T(8,128)(2,1)}, bf16[2,2,32,5120]{3,2,1,0:T(8,128)(2,1)S(1)}, u32[]{:S(2)}, u32[]{:S(2)}) collective-permute-start(bf16[2,2,32,5120]{3,2,1,0:T(8,128)(2,1)} %get-tuple-element.29), channel_id=1, source_target_pairs={{1,0},{2,1},{3,2},{4,3},{5,4},{6,5},{7,6},{8,7},{9,8},{10,9},{11,1... | collective-permute-start | bytes 3932168 | tf_op jit(solution)/shard_map/ppermute | solution.py:29
  38.3 7.0 %collective-permute-done.4.hb = bf16[2,2,32,2560]{3,2,1,0:T(8,128)(2,1)S(1)} collective-permute-done((bf16[2,2,32,2560]{3,2,1,0:T(8,128)(2,1)}, bf16[2,2,32,2560]{3,2,1,0:T(8,128)(2,1)S(1)}, u32[]{:S(2)}, u32[]{:S(2)}) %collective-permute-start.4) | collective-permute-done | bytes 655392 | tf_op jit(solution)/shard_map/ppermute | solution.py:29
  45.3 3.8 %collective-permute-done.5.ha = bf16[2,2,32,2560]{3,2,1,0:T(8,128)(2,1)S(1)} collective-permute-done((bf16[2,2,32,2560]{3,2,1,0:T(8,128)(2,1)}, bf16[2,2,32,2560]{3,2,1,0:T(8,128)(2,1)S(1)}, u32[]{:S(2)}, u32[]{:S(2)}) %collective-permute-start.5) | collective-permute-done | bytes 655392 | tf_op jit(solution)/shard_map/ppermute | solution.py:29
  49.1 7.8 %collective-permute-done.2.rb = bf16[2,2,32,5120]{3,2,1,0:T(8,128)(2,1)S(1)} collective-permute-done((bf16[2,2,32,5120]{3,2,1,0:T(8,128)(2,1)}, bf16[2,2,32,5120]{3,2,1,0:T(8,128)(2,1)S(1)}, u32[]{:S(2)}, u32[]{:S(2)}) %collective-permute-start.2) | collective-permute-done | bytes 1310752 | tf_op jit(solution)/shard_map/ppermute | solution.py:29
  56.9 3.9 %collective-permute-done.3.ra = bf16[2,2,32,5120]{3,2,1,0:T(8,128)(2,1)S(1)} collective-permute-done((bf16[2,2,32,5120]{3,2,1,0:T(8,128)(2,1)}, bf16[2,2,32,5120]{3,2,1,0:T(8,128)(2,1)S(1)}, u32[]{:S(2)}, u32[]{:S(2)}) %collective-permute-start.3) | collective-permute-done | bytes 1310752 | tf_op jit(solution)/shard_map/ppermute | solution.py:29
  64.4 3.6 %collective-permute-start.6 = (bf16[2,2,32,2560]{3,2,1,0:T(8,128)(2,1)}, bf16[2,2,32,2560]{3,2,1,0:T(8,128)(2,1)S(1)}, u32[]{:S(2)}, u32[]{:S(2)}) collective-permute-start(bf16[2,2,32,2560]{3,2,1,0:T(8,128)(2,1)} %pad_maximum_fusion), channel_id=1, source_target_pairs={{0,1},{1,2},{2,3},{3,4},{4,5},{5,6},{6,7},{7,8},{8,9},{9,10},{10,1... | collective-permute-start | bytes 1966088 | tf_op jit(solution)/shard_map/ppermute | solution.py:29
  76.7 8.4 %attend.2.refs_0_ = bf16[2,64,2560]{2,1,0:T(8,128)(2,1)} custom-call(s32[20]{0:T(128)} %get-tuple-element.56.combo_ref, bf16[4,32,5120]{2,1,0:T(8,128)(2,1)} %get-tuple-element.34.q_ref, bf16[2,2,32,2560]{3,2,1,0:T(8,128)(2,1)} %get-tuple-element.27.f0, bf16[2,2,32,2560]{3,2,1,0:T(8,128)(2,1)} %get-tuple-element.26.f1, bf16[2,2,32,2560]{3,2,1,0:T(8,128)(2,1)} %copy-done.6, ...), custom_call_target="tpu_custom_call" | custom-call | flops 503316480 | bytes 33554432 | tf_op jit(solution)/shard_map/attend/pallas_call | solution.py:160
  87.3 4.3 %collective-permute-start.12 = (bf16[2,2,32,2560]{3,2,1,0:T(8,128)(2,1)S(1)}, bf16[2,2,32,2560]{3,2,1,0:T(8,128)(2,1)S(1)}, u32[]{:S(2)}, u32[]{:S(2)}) collective-permute-start(bf16[2,2,32,2560]{3,2,1,0:T(8,128)(2,1)S(1)} %pad_maximum_fusion.2), channel_id=1, source_target_pairs={{0,1},{1,2},{2,3},{3,4},{4,5},{5,6},{6,7},{7,8},{8,9},{9,10},{10,1... | collective-permute-start | bytes 1966088 | tf_op jit(solution)/shard_map/ppermute | solution.py:29
  91.6 6.2 %collective-permute-start.10 = (bf16[2,64,2560]{2,1,0:T(8,128)(2,1)S(1)}, bf16[2,64,2560]{2,1,0:T(8,128)(2,1)S(1)}, u32[]{:S(2)}, u32[]{:S(2)}) collective-permute-start(bf16[2,64,2560]{2,1,0:T(8,128)(2,1)S(1)} %copy-done.2), channel_id=1, source_target_pairs={{0,96},{32,0},{64,32},{96,64},{1,97},{33,1},{65,33},{97,65},{2,98}... | collective-permute-start | bytes 1966088 | tf_op jit(solution)/shard_map/ppermute | solution.py:34
  100.0 7.5 %attend.3.refs_1_ = bf16[2,64,2560]{2,1,0:T(8,128)(2,1)} custom-call(s32[20]{0:T(128)} %get-tuple-element.55.combo_ref, bf16[4,32,5120]{2,1,0:T(8,128)(2,1)} %get-tuple-element.34.q_ref, bf16[2,2,32,2560]{3,2,1,0:T(8,128)(2,1)} %get-tuple-element.31.f0, bf16[2,2,32,2560]{3,2,1,0:T(8,128)(2,1)} %get-tuple-element.30.f1, bf16[2,2,32,2560]{3,2,1,0:T(8,128)(2,1)} %copy-done.3, ...), custom_call_target="tpu_custom_call" | custom-call | flops 503316480 | bytes 33554432 | tf_op jit(solution)/shard_map/attend/pallas_call | solution.py:160
  109.0 4.7 %collective-permute-start.16 = (bf16[2,64,2560]{2,1,0:T(8,128)(2,1)}, bf16[2,64,2560]{2,1,0:T(8,128)(2,1)S(1)}, u32[]{:S(2)}, u32[]{:S(2)}) collective-permute-start(bf16[2,64,2560]{2,1,0:T(8,128)(2,1)} %attend.3.refs_1_), channel_id=1, source_target_pairs={{0,96},{32,0},{64,32},{96,64},{1,97},{33,1},{65,33},{97,65},{2,98}... | collective-permute-start | bytes 1966088 | tf_op jit(solution)/shard_map/ppermute | solution.py:34
  116.1 13.8 %collective-permute-done.14.refs_6_ = bf16[2,64,2560]{2,1,0:T(8,128)(2,1)S(1)} collective-permute-done((bf16[2,64,2560]{2,1,0:T(8,128)(2,1)}, bf16[2,64,2560]{2,1,0:T(8,128)(2,1)S(1)}, u32[]{:S(2)}, u32[]{:S(2)}) %collective-permute-start.14) | collective-permute-done | bytes 655392 | tf_op jit(solution)/shard_map/ppermute | solution.py:34
  132.9 3.9 %collective-permute-done.9.refs_0_ = bf16[1,64,2560]{2,1,0:T(8,128)(2,1)S(1)} collective-permute-done((bf16[1,64,2560]{2,1,0:T(8,128)(2,1)S(1)}, bf16[1,64,2560]{2,1,0:T(8,128)(2,1)S(1)}, u32[]{:S(2)}, u32[]{:S(2)}) %collective-permute-start.9) | collective-permute-done | bytes 327712 | tf_op jit(solution)/shard_map/ppermute | solution.py:34
  136.9 6.0 %collective-permute-done.15.refs_4_ = bf16[1,64,2560]{2,1,0:T(8,128)(2,1)S(1)} collective-permute-done((bf16[1,64,2560]{2,1,0:T(8,128)(2,1)S(1)}, bf16[1,64,2560]{2,1,0:T(8,128)(2,1)S(1)}, u32[]{:S(2)}, u32[]{:S(2)}) %collective-permute-start.15) | collective-permute-done | bytes 327712 | tf_op jit(solution)/shard_map/ppermute | solution.py:34
  143.6 4.2 %all-gather.7.cloned.1.call-done = bf16[64,160,640]{2,1,0:T(8,128)(2,1)} async-done(((bf16[8,160,640]{2,1,0:T(8,128)(2,1)}), bf16[64,160,640]{2,1,0:T(8,128)(2,1)}) %all-gather.7.cloned.1.call-update) | async-done | bytes 13107216 | tf_op jit(solution)/shard_map/all_gather | solution.py:301
  147.8 11.1 %project.2 = (bf16[128,1280]{1,0:T(8,128)(2,1)}, bf16[128,1280]{1,0:T(8,128)(2,1)}, bf16[128,1280]{1,0:T(8,128)(2,1)}) custom-call(bf16[1,64,2560]{2,1,0:T(8,128)(2,1)} %copy-done.23, bf16[1,64,2560]{2,1,0:T(8,128)(2,1)} %copy-done.22, bf16[2,64,2560]{2,1,0:T(8,128)(2,1)} %copy-done.16, bf16[2,64,2560]{2,1,0:T(8,128)(2,1)} %copy-done.15, ...), custom_call_target="tpu_custom_call" | custom-call | flops 5033164800 | bytes 13107200 | tf_op jit(solution)/shard_map/project/pallas_call | solution.py:228
  161.3 4.8 %collective-permute-start.18 = (bf16[128,1280]{1,0:T(8,128)(2,1)}, bf16[128,1280]{1,0:T(8,128)(2,1)S(1)}, u32[]{:S(2)}, u32[]{:S(2)}) collective-permute-start(bf16[128,1280]{1,0:T(8,128)(2,1)} %get-tuple-element.44), channel_id=1, source_target_pairs={{0,96},{32,0},{64,32},{96,64},{1,97},{33,1},{65,33},{97,65},{2,98}... | collective-permute-start | bytes 983048 | tf_op jit(solution)/shard_map/ppermute | solution.py:34
  166.6 7.7 %project.3.p0 = bf16[128,1280]{1,0:T(8,128)(2,1)} custom-call(bf16[2,64,2560]{2,1,0:T(8,128)(2,1)} %attend.2.refs_0_, bf16[2,64,2560]{2,1,0:T(8,128)(2,1)} %attend.3.refs_1_, bf16[2,2,2,8,160,640]{5,4,3,2,1,0:T(8,128)(2,1)} %bitcast.12), custom_call_target="tpu_custom_call" | custom-call | flops 1677721600 | bytes 13107200 | tf_op jit(solution)/shard_map/project/pallas_call | solution.py:228
  174.3 7.2 %collective-permute-done.18.p1 = bf16[128,1280]{1,0:T(8,128)(2,1)S(1)} collective-permute-done((bf16[128,1280]{1,0:T(8,128)(2,1)}, bf16[128,1280]{1,0:T(8,128)(2,1)S(1)}, u32[]{:S(2)}, u32[]{:S(2)}) %collective-permute-start.18) | collective-permute-done | bytes 327712 | tf_op jit(solution)/shard_map/ppermute | solution.py:34
  182.4 3.9 %finish.1 = bf16[128,5120]{1,0:T(8,128)(2,1)} custom-call(s32[1]{0:T(128)} %bitcast.x_ref, bf16[128,5120]{1,0:T(8,128)(2,1)} %bitcast.14, f32[1,5120]{1,0:T(1,128)} %bitcast.18, bf16[128,1280]{1,0:T(8,128)(2,1)} %project.3.p0, bf16[128,1280]{1,0:T(8,128)(2,1)} %copy-done.13, bf16[128,1280]{1,0:T(8,128)(2,1)} %copy-done.12, bf16[128,1280]{1,0:T(8,128)(2,1)} %copy-done.14), custom_call_target="tpu_custom_call" | custom-call | tf_op jit(solution)/shard_map/finish/pallas_call | solution.py:258
  (109 shorter events, 35.8 us)
Async XLA Ops:
  6.5 54.3 %all-gather.5.cloned.1.call-start = ((), (), s32[]{:S(2)}) async-start(), calls=%async_computation | async-start | bytes 1843200 | tf_op jit(solution)/shard_map/all_gather | solution.py:276
  7.3 140.5 %all-gather.7.cloned.1.call-start = ((), (), s32[]{:S(2)}) async-start(), calls=%async_computation.1 | async-start | bytes 14745600 | tf_op jit(solution)/shard_map/all_gather | solution.py:301
  13.6 17.6 %collective-permute-start = (bf16[2,2,32,2560]{3,2,1,0:T(8,128)(2,1)}, bf16[2,2,32,2560]{3,2,1,0:T(8,128)(2,1)S(1)}, u32[]{:S(2)}, u32[]{:S(2)}) collective-permute-start(bf16[2,2,32,2560]{3,2,1,0:T(8,128)(2,1)} %get-tuple-element.26.f1), channel_id=1, source_target_pairs={{0,32},{32,64},{64,96},{96,128},{128,160},{160,192},{192,224},{1,3... | collective-permute-start | bytes 1966088 | tf_op jit(solution)/shard_map/ppermute | solution.py:29
  17.6 19.0 %collective-permute-start.1 = (bf16[2,2,32,2560]{3,2,1,0:T(8,128)(2,1)}, bf16[2,2,32,2560]{3,2,1,0:T(8,128)(2,1)S(1)}, u32[]{:S(2)}, u32[]{:S(2)}) collective-permute-start(bf16[2,2,32,2560]{3,2,1,0:T(8,128)(2,1)} %get-tuple-element.27.f0), channel_id=1, source_target_pairs={{32,0},{64,32},{96,64},{128,96},{160,128},{192,160},{224,192},{33,... | collective-permute-start | bytes 1966088 | tf_op jit(solution)/shard_map/ppermute | solution.py:29
  18.9 26.4 %collective-permute-start.4 = (bf16[2,2,32,2560]{3,2,1,0:T(8,128)(2,1)}, bf16[2,2,32,2560]{3,2,1,0:T(8,128)(2,1)S(1)}, u32[]{:S(2)}, u32[]{:S(2)}) collective-permute-start(bf16[2,2,32,2560]{3,2,1,0:T(8,128)(2,1)} %get-tuple-element.30.f1), channel_id=1, source_target_pairs={{0,32},{32,64},{64,96},{96,128},{128,160},{160,192},{192,224},{1,3... | collective-permute-start | bytes 1966088 | tf_op jit(solution)/shard_map/ppermute | solution.py:29
  22.9 26.2 %collective-permute-start.5 = (bf16[2,2,32,2560]{3,2,1,0:T(8,128)(2,1)}, bf16[2,2,32,2560]{3,2,1,0:T(8,128)(2,1)S(1)}, u32[]{:S(2)}, u32[]{:S(2)}) collective-permute-start(bf16[2,2,32,2560]{3,2,1,0:T(8,128)(2,1)} %get-tuple-element.31.f0), channel_id=1, source_target_pairs={{32,0},{64,32},{96,64},{128,96},{160,128},{192,160},{224,192},{33,... | collective-permute-start | bytes 1966088 | tf_op jit(solution)/shard_map/ppermute | solution.py:29
  24.2 32.7 %collective-permute-start.2 = (bf16[2,2,32,5120]{3,2,1,0:T(8,128)(2,1)}, bf16[2,2,32,5120]{3,2,1,0:T(8,128)(2,1)S(1)}, u32[]{:S(2)}, u32[]{:S(2)}) collective-permute-start(bf16[2,2,32,5120]{3,2,1,0:T(8,128)(2,1)} %get-tuple-element.28), channel_id=1, source_target_pairs={{0,1},{1,2},{2,3},{3,4},{4,5},{5,6},{6,7},{7,8},{8,9},{9,10},{10,1... | collective-permute-start | bytes 3932168 | tf_op jit(solution)/shard_map/ppermute | solution.py:29
  31.3 29.6 %collective-permute-start.3 = (bf16[2,2,32,5120]{3,2,1,0:T(8,128)(2,1)}, bf16[2,2,32,5120]{3,2,1,0:T(8,128)(2,1)S(1)}, u32[]{:S(2)}, u32[]{:S(2)}) collective-permute-start(bf16[2,2,32,5120]{3,2,1,0:T(8,128)(2,1)} %get-tuple-element.29), channel_id=1, source_target_pairs={{1,0},{2,1},{3,2},{4,3},{5,4},{6,5},{7,6},{8,7},{9,8},{10,9},{11,1... | collective-permute-start | bytes 3932168 | tf_op jit(solution)/shard_map/ppermute | solution.py:29
  45.3 39.8 %copy-start.3 = (bf16[2,2,32,2560]{3,2,1,0:T(8,128)(2,1)}, bf16[2,2,32,2560]{3,2,1,0:T(8,128)(2,1)S(1)}, u32[]{:S(2)}) copy-start(bf16[2,2,32,2560]{3,2,1,0:T(8,128)(2,1)S(1)} %collective-permute-done.4.hb) | copy-start | bytes 1966084
  62.5 11.9 %collective-permute-start.7 = (bf16[2,2,32,2560]{3,2,1,0:T(8,128)(2,1)S(1)}, bf16[2,2,32,2560]{3,2,1,0:T(8,128)(2,1)S(1)}, u32[]{:S(2)}, u32[]{:S(2)}) collective-permute-start(bf16[2,2,32,2560]{3,2,1,0:T(8,128)(2,1)S(1)} %pad_maximum_fusion.1), channel_id=1, source_target_pairs={{1,0},{2,1},{3,2},{4,3},{5,4},{6,5},{7,6},{8,7},{9,8},{10,9},{11,1... | collective-permute-start | bytes 1966088 | tf_op jit(solution)/shard_map/ppermute | solution.py:29
  64.4 11.5 %collective-permute-start.6 = (bf16[2,2,32,2560]{3,2,1,0:T(8,128)(2,1)}, bf16[2,2,32,2560]{3,2,1,0:T(8,128)(2,1)S(1)}, u32[]{:S(2)}, u32[]{:S(2)}) collective-permute-start(bf16[2,2,32,2560]{3,2,1,0:T(8,128)(2,1)} %pad_maximum_fusion), channel_id=1, source_target_pairs={{0,1},{1,2},{2,3},{3,4},{4,5},{5,6},{6,7},{7,8},{8,9},{9,10},{10,1... | collective-permute-start | bytes 1966088 | tf_op jit(solution)/shard_map/ppermute | solution.py:29
  85.3 12.9 %collective-permute-start.13 = (bf16[2,2,32,2560]{3,2,1,0:T(8,128)(2,1)S(1)}, bf16[2,2,32,2560]{3,2,1,0:T(8,128)(2,1)S(1)}, u32[]{:S(2)}, u32[]{:S(2)}) collective-permute-start(bf16[2,2,32,2560]{3,2,1,0:T(8,128)(2,1)S(1)} %pad_maximum_fusion.3), channel_id=1, source_target_pairs={{1,0},{2,1},{3,2},{4,3},{5,4},{6,5},{7,6},{8,7},{9,8},{10,9},{11,1... | collective-permute-start | bytes 1966088 | tf_op jit(solution)/shard_map/ppermute | solution.py:29
  87.3 11.8 %collective-permute-start.12 = (bf16[2,2,32,2560]{3,2,1,0:T(8,128)(2,1)S(1)}, bf16[2,2,32,2560]{3,2,1,0:T(8,128)(2,1)S(1)}, u32[]{:S(2)}, u32[]{:S(2)}) collective-permute-start(bf16[2,2,32,2560]{3,2,1,0:T(8,128)(2,1)S(1)} %pad_maximum_fusion.2), channel_id=1, source_target_pairs={{0,1},{1,2},{2,3},{3,4},{4,5},{5,6},{6,7},{7,8},{8,9},{9,10},{10,1... | collective-permute-start | bytes 1966088 | tf_op jit(solution)/shard_map/ppermute | solution.py:29
  91.6 22.1 %collective-permute-start.10 = (bf16[2,64,2560]{2,1,0:T(8,128)(2,1)S(1)}, bf16[2,64,2560]{2,1,0:T(8,128)(2,1)S(1)}, u32[]{:S(2)}, u32[]{:S(2)}) collective-permute-start(bf16[2,64,2560]{2,1,0:T(8,128)(2,1)S(1)} %copy-done.2), channel_id=1, source_target_pairs={{0,96},{32,0},{64,32},{96,64},{1,97},{33,1},{65,33},{97,65},{2,98}... | collective-permute-start | bytes 1966088 | tf_op jit(solution)/shard_map/ppermute | solution.py:34
  97.8 18.2 %collective-permute-start.8 = (bf16[2,64,2560]{2,1,0:T(8,128)(2,1)S(1)}, bf16[2,64,2560]{2,1,0:T(8,128)(2,1)S(1)}, u32[]{:S(2)}, u32[]{:S(2)}) collective-permute-start(bf16[2,64,2560]{2,1,0:T(8,128)(2,1)S(1)} %copy-done.2), channel_id=1, source_target_pairs={{0,32},{32,64},{64,96},{96,0},{1,33},{33,65},{65,97},{97,1},{2,34}... | collective-permute-start | bytes 1966088 | tf_op jit(solution)/shard_map/ppermute | solution.py:34
  107.5 22.3 %collective-permute-start.14 = (bf16[2,64,2560]{2,1,0:T(8,128)(2,1)}, bf16[2,64,2560]{2,1,0:T(8,128)(2,1)S(1)}, u32[]{:S(2)}, u32[]{:S(2)}) collective-permute-start(bf16[2,64,2560]{2,1,0:T(8,128)(2,1)} %attend.3.refs_1_), channel_id=1, source_target_pairs={{0,32},{32,64},{64,96},{96,0},{1,33},{33,65},{65,97},{97,1},{2,34}... | collective-permute-start | bytes 1966088 | tf_op jit(solution)/shard_map/ppermute | solution.py:34
  109.0 21.1 %collective-permute-start.16 = (bf16[2,64,2560]{2,1,0:T(8,128)(2,1)}, bf16[2,64,2560]{2,1,0:T(8,128)(2,1)S(1)}, u32[]{:S(2)}, u32[]{:S(2)}) collective-permute-start(bf16[2,64,2560]{2,1,0:T(8,128)(2,1)} %attend.3.refs_1_), channel_id=1, source_target_pairs={{0,96},{32,0},{64,32},{96,64},{1,97},{33,1},{65,33},{97,65},{2,98}... | collective-permute-start | bytes 1966088 | tf_op jit(solution)/shard_map/ppermute | solution.py:34
  113.8 19.2 %collective-permute-start.11 = (bf16[1,64,2560]{2,1,0:T(8,128)(2,1)S(1)}, bf16[1,64,2560]{2,1,0:T(8,128)(2,1)S(1)}, u32[]{:S(2)}, u32[]{:S(2)}) collective-permute-start(bf16[1,64,2560]{2,1,0:T(8,128)(2,1)S(1)} %slice.61), channel_id=1, source_target_pairs={{0,96},{32,0},{64,32},{96,64},{1,97},{33,1},{65,33},{97,65},{2,98}... | collective-permute-start | bytes 983048 | tf_op jit(solution)/shard_map/ppermute | solution.py:34
  116.0 20.9 %collective-permute-start.9 = (bf16[1,64,2560]{2,1,0:T(8,128)(2,1)S(1)}, bf16[1,64,2560]{2,1,0:T(8,128)(2,1)S(1)}, u32[]{:S(2)}, u32[]{:S(2)}) collective-permute-start(bf16[1,64,2560]{2,1,0:T(8,128)(2,1)S(1)} %slice.60), channel_id=1, source_target_pairs={{0,32},{32,64},{64,96},{96,0},{1,33},{33,65},{65,97},{97,1},{2,34}... | collective-permute-start | bytes 983048 | tf_op jit(solution)/shard_map/ppermute | solution.py:34
  129.9 13.0 %collective-permute-start.15 = (bf16[1,64,2560]{2,1,0:T(8,128)(2,1)S(1)}, bf16[1,64,2560]{2,1,0:T(8,128)(2,1)S(1)}, u32[]{:S(2)}, u32[]{:S(2)}) collective-permute-start(bf16[1,64,2560]{2,1,0:T(8,128)(2,1)S(1)} %slice.62), channel_id=1, source_target_pairs={{0,32},{32,64},{64,96},{96,0},{1,33},{33,65},{65,97},{97,1},{2,34}... | collective-permute-start | bytes 983048 | tf_op jit(solution)/shard_map/ppermute | solution.py:34
  130.2 13.4 %collective-permute-start.17 = (bf16[1,64,2560]{2,1,0:T(8,128)(2,1)S(1)}, bf16[1,64,2560]{2,1,0:T(8,128)(2,1)}, u32[]{:S(2)}, u32[]{:S(2)}) collective-permute-start(bf16[1,64,2560]{2,1,0:T(8,128)(2,1)S(1)} %slice.63), channel_id=1, source_target_pairs={{0,96},{32,0},{64,32},{96,64},{1,97},{33,1},{65,33},{97,65},{2,98}... | collective-permute-start | bytes 983048 | tf_op jit(solution)/shard_map/ppermute | solution.py:34
  158.9 15.4 %collective-permute-start.19 = (bf16[128,1280]{1,0:T(8,128)(2,1)}, bf16[128,1280]{1,0:T(8,128)(2,1)S(1)}, u32[]{:S(2)}, u32[]{:S(2)}) collective-permute-start(bf16[128,1280]{1,0:T(8,128)(2,1)} %get-tuple-element.45), channel_id=1, source_target_pairs={{0,64},{32,96},{64,0},{96,32},{1,65},{33,97},{65,1},{97,33},{2,66}... | collective-permute-start | bytes 983048 | tf_op jit(solution)/shard_map/ppermute | solution.py:34
  161.3 20.2 %collective-permute-start.18 = (bf16[128,1280]{1,0:T(8,128)(2,1)}, bf16[128,1280]{1,0:T(8,128)(2,1)S(1)}, u32[]{:S(2)}, u32[]{:S(2)}) collective-permute-start(bf16[128,1280]{1,0:T(8,128)(2,1)} %get-tuple-element.44), channel_id=1, source_target_pairs={{0,96},{32,0},{64,32},{96,64},{1,97},{33,1},{65,33},{97,65},{2,98}... | collective-permute-start | bytes 983048 | tf_op jit(solution)/shard_map/ppermute | solution.py:34
  166.1 15.4 %collective-permute-start.20 = (bf16[128,1280]{1,0:T(8,128)(2,1)}, bf16[128,1280]{1,0:T(8,128)(2,1)S(1)}, u32[]{:S(2)}, u32[]{:S(2)}) collective-permute-start(bf16[128,1280]{1,0:T(8,128)(2,1)} %get-tuple-element.46), channel_id=1, source_target_pairs={{0,32},{32,64},{64,96},{96,0},{1,33},{33,65},{65,97},{97,1},{2,34}... | collective-permute-start | bytes 983048 | tf_op jit(solution)/shard_map/ppermute | solution.py:34
  (24 other events, 253.1 us)
Sparse Core Ops, SparseCore 0:
  9.1 42.1 all-gather.4
  61.0 86.7 all-gather.6

commit v7 on v4

v7 whole, which is shorter than its diff:
```python
import functools

import jax
import jax.numpy as jnp
from jax import lax
from jax.experimental import pallas as pl
from jax.experimental.pallas import tpu as pltpu
from jax.sharding import Mesh, PartitionSpec as P

TW = 8
HEAD = 128
TM = ("y_lo", "x")
SP = ("y_hi", "z", "core")
COMBOS = 12
F32, BF16 = jnp.float32, jnp.bfloat16


def axis_size(axes):
    n = 1
    for a in axes:
        n *= lax.axis_size(a)
    return n


def passed_along(block, axes, distance):
    n = axis_size(axes)
    route = [(i - distance, i) for i in range(n) if 0 <= i - distance < n]
    return lax.ppermute(block, axes, route)


def along_y(block, target):
    at = lambda y: (y % 2) * 2 + y // 2
    return lax.ppermute(block, ("y_lo", "y_hi"), [(at(y), at(target(y))) for y in range(4)])


def in_hbm(array):
    return pltpu.with_memory_space_constraint(array, pltpu.HBM)


def params(megabytes=24):
    return pltpu.CompilerParams(vmem_limit_bytes=megabytes << 20)


def prepare_kernel(q_ref, k_ref, v_ref, qg_ref, kg_ref, qn_ref, *outs):
    i = pl.program_id(0)
    f, r = i // 2, i % 2
    inner = q_ref.shape[-1]

    def normed(ref, gain):
        a = ref[0].astype(F32)
        ms = jnp.sum(a * a, axis=-1, keepdims=True) * (1.0 / inner)
        return (a * lax.rsqrt(ms + 1e-06) * gain[...]).astype(BF16)

    qn_ref[0] = normed(q_ref, qg_ref)
    kn = normed(k_ref, kg_ref)
    v = v_ref[0]
    f0, f1, r0, r1 = outs
    for chosen, ref in ((f == 0, f0), (f == 1, f1), (r == 0, r0), (r == 1, r1)):

        @pl.when(chosen)
        def _(ref=ref):
            ref[0, 0] = kn
            ref[0, 1] = v


def prepare(queries, keys, values, query_gain, key_gain):
    groups, nw, inner = queries.shape
    token_spec = pl.BlockSpec((1, nw, inner), lambda i: (i, 0, 0))
    gain_spec = pl.BlockSpec((1, inner), lambda i: (0, 0))
    out_shape = [pltpu.HBM(queries.shape, BF16)]
    out_specs = [token_spec]
    out_shape += [pltpu.HBM((2, 2, nw, inner), BF16)] * 4
    out_specs += [
        pl.BlockSpec((1, 2, nw, inner), lambda i: (jnp.minimum(i, 1), 0, 0, 0)),
            pl.BlockSpec((1, 2, nw, inner), lambda i: (jnp.maximum(i - 2, 0), 0, 0, 0)),
            pl.BlockSpec((1, 2, nw, inner), lambda i: (i // 2, 0, 0, 0)),
            pl.BlockSpec((1, 2, nw, inner), lambda i: (i // 2, 0, 0, 0)),
        ]
    return pl.pallas_call(
        prepare_kernel,
        grid=(groups,),
        in_specs=[token_spec] * 3 + [gain_spec] * 2,
        out_specs=out_specs,
        out_shape=out_shape,
        compiler_params=params(),
        cost_estimate=pl.CostEstimate(flops=0, bytes_accessed=12 << 20, transcendentals=0),
        name="prepare",
    )(*[in_hbm(a) for a in (queries, keys, values)], query_gain[None], key_gain[None])


def mask_tables(first_frame, first_row, frame_count, row_count, nw):
    i32 = jnp.int32
    shape = (COMBOS, 2, 2 * nw, 3 * 4 * nw)
    t = lax.broadcasted_iota(i32, shape, 0)
    f = lax.broadcasted_iota(i32, shape, 1)
    q = lax.broadcasted_iota(i32, shape, 2)
    k = lax.broadcasted_iota(i32, shape, 3)
    kf, kr, kc = k // (4 * nw), k // nw % 4, k % nw
    frame, row = first_frame - 1 + f + kf, first_row - 1 + kr
    allowed = jnp.abs(kf - 1) <= t // 6
    allowed &= jnp.abs(q // nw + 1 - kr) <= t // 3 % 2
    allowed &= jnp.abs(q % nw // TW - kc // TW) <= t % 3
    allowed &= (frame >= 0) & (frame < frame_count) & (row >= 0) & (row < row_count)
    return jnp.where(allowed, 0.0, -jnp.inf).astype(F32)


def attend_kernel(heads, scale, combo_ref, half_ref, q_ref, f0, f1, hb, ha, rb, ra, cb, ca, mask_ref, same_ref, other_ref):
    step = pl.program_id(0)
    frames = ((cb.at[0], hb, ca.at[0]), (rb.at[0], f0, ra.at[0]), (rb.at[1], f1, ra.at[1]), (cb.at[1], ha, ca.at[1]))

    def region(kv, lanes):
        parts = []
        for below, own, above in frames:
            parts += [below[kv, :, lanes], own[0, kv, :, lanes], own[1, kv, :, lanes], above[kv, :, lanes]]
        return jnp.concatenate(parts, axis=0)

    scores = {}
    for h in range(heads):
        lanes = slice(h * HEAD, (h + 1) * HEAD)
        keys = region(0, lanes)
        group = keys.shape[0] // 4
        combo = combo_ref[step * heads + h]
        for f in range(2):
            q = q_ref[2 * f : 2 * f + 2, :, lanes].reshape(-1, HEAD)
            k = keys[f * group : (f + 3) * group]
            s = lax.dot_general(q, k, (((1,), (1,)), ((), ())), preferred_element_type=F32)
            scores[h, f] = s + mask_ref[combo, f]
    weights = {}
    for at, s in scores.items():
        peak = jnp.max(s, axis=1, keepdims=True)
        w = jnp.exp((s - peak) * scale)
        weights[at] = w.astype(BF16), jnp.sum(w, axis=1, keepdims=True)
    mixed = {}
    for h in range(heads):
        lanes = slice(h * HEAD, (h + 1) * HEAD)
        values = region(1, lanes)
        group = values.shape[0] // 4
        for f in range(2):
            w, total = weights[h, f]
            o = jnp.dot(w, values[f * group : (f + 3) * group], preferred_element_type=F32)
            mixed[h, f] = (o / total).astype(BF16)
    in_half = step // (pl.num_programs(0) // 2) == half_ref[0]
    for chosen, ref in ((in_half, same_ref), (jnp.logical_not(in_half), other_ref)):

        @pl.when(chosen)
        def _(ref=ref):
            for (h, f), o in mixed.items():
                ref[f * o.shape[0] : (f + 1) * o.shape[0], h * HEAD : (h + 1) * HEAD] = o


def attend(combo, half, qn, own, halos, masks, heads=10):
    groups, nw, inner = qn.shape
    lanes = heads * HEAD
    steps = inner // lanes
    inside = steps // 2
    kv_spec = pl.BlockSpec((2, 2, nw, lanes), lambda i, *_: (0, 0, 0, i))
    same = lambda i, _, half_ref: (0, jnp.clip(i - inside * half_ref[0], 0, inside - 1))
    other = lambda i, _, half_ref: (0, jnp.clip(i - inside * (1 - half_ref[0]), 0, inside - 1))
    return pl.pallas_call(
        functools.partial(attend_kernel, heads, HEAD**-0.5),
        grid_spec=pltpu.PrefetchScalarGridSpec(
            num_scalar_prefetch=2,
            grid=(steps,),
            in_specs=[pl.BlockSpec((groups, nw, lanes), lambda i, *_: (0, 0, i))]
            + [kv_spec] * 8
            + [pl.BlockSpec(masks.shape, lambda i, *_: (0, 0, 0, 0))],
            out_specs=[pl.BlockSpec((groups * nw, lanes), same), pl.BlockSpec((groups * nw, lanes), other)],
        ),
        out_shape=[pltpu.HBM((groups * nw, inner // 2), BF16)] * 2,
        compiler_params=params(),
        cost_estimate=pl.CostEstimate(flops=4 * 128 * 384 * inner, bytes_accessed=32 << 20, transcendentals=0),
        name="attend",
    )(combo, half, qn, *own, *halos, masks)


def project_kernel(blocks, *refs):
    ins, w_ref, outs, a_buf = refs[:blocks], refs[blocks], refs[blocks + 1 : -1], refs[-1]

    @pl.when(pl.program_id(0) == 0)
    def _():
        a_buf[...] = jnp.concatenate([i[...] for i in ins], axis=0)

    _, cores, zs, _, _ = w_ref.shape
    w = jnp.concatenate([w_ref[0, c, z] for z in range(zs) for c in range(cores)], axis=0)
    term = jnp.dot(a_buf[...], w, preferred_element_type=F32)
    rows = outs[0].shape[0]
    for d, o in enumerate(outs):
        o[...] = term[d * rows : (d + 1) * rows, :].astype(BF16)


def project(blocks, weight):
    rows, depth = blocks[0].shape
    xs, cores, zs, part, cols = weight.shape
    return pl.pallas_call(
        functools.partial(project_kernel, len(blocks)),
        grid=(xs,),
        in_specs=[pl.BlockSpec((rows, depth), lambda j: (0, 0))] * len(blocks)
        + [pl.BlockSpec((1, cores, zs, part, cols), lambda j: (j, 0, 0, 0, 0))],
        out_specs=[pl.BlockSpec((rows, cols), lambda j: (0, j))] * len(blocks),
        out_shape=[jax.ShapeDtypeStruct((rows, xs * cols), BF16)] * len(blocks),
        scratch_shapes=[pltpu.VMEM((len(blocks) * rows, depth), BF16)],
        compiler_params=params(32),
        cost_estimate=pl.CostEstimate(
            flops=2 * len(blocks) * rows * depth * xs * cols, bytes_accessed=2 * depth * xs * cols, transcendentals=0
        ),
        name="project",
    )(*blocks, in_hbm(weight))


def finish_kernel(y_ref, hidden, gate, same0, same1, other0, other1, out):
    half = same0.shape[-1]
    for side, (p, q) in ((y_ref[0], (same0, same1)), (1 - y_ref[0], (other0, other1))):
        where = pl.ds(pl.multiple_of(side * half, HEAD), half)
        branch = p[...].astype(F32) + q[...].astype(F32)
        out[:, where] = (hidden[:, where].astype(F32) + gate[:, where] * branch).astype(BF16)


def finish(y_lo, hidden, gate, pieces, blocks=4):
    rows, width = hidden.shape
    step = rows // blocks
    row_spec = pl.BlockSpec((step, width), lambda i, *_: (i, 0))
    return pl.pallas_call(
        finish_kernel,
        grid_spec=pltpu.PrefetchScalarGridSpec(
            num_scalar_prefetch=1,
            grid=(blocks,),
            in_specs=[row_spec, pl.BlockSpec((1, width), lambda i, *_: (0, 0))]
            + [pl.BlockSpec((step, pieces[0].shape[1]), lambda i, *_: (i, 0))] * 4,
            out_specs=row_spec,
        ),
        out_shape=jax.ShapeDtypeStruct(hidden.shape, BF16),
        compiler_params=params(),
        name="finish",
    )(y_lo, hidden, gate[None], *pieces)


def shards(hidden_in, queries, keys, values, query_gain, key_gain, reach_time, reach_rows, reach_cols, out_weight, gate):
    frames, rows, nw, inner = queries.shape
    width = hidden_in.shape[3]
    weight = lax.all_gather(out_weight, "z", axis=0, tiled=False)
    tokens = [a.reshape(frames * rows, nw, inner) for a in (queries, keys, values)]
    qn, *own = prepare(*tokens, query_gain, key_gain)
    masks = mask_tables(
        lax.axis_index(TM) * frames,
        lax.axis_index(SP) * rows,
        frames * axis_size(TM),
        rows * axis_size(SP),
        nw,
    )
    combo = reach_time * 6 + reach_rows * 3 + reach_cols
    f0, f1, r0, r1 = own
    hb, ha = passed_along(f1, TM, 1), passed_along(f0, TM, -1)
    rb, ra = passed_along(r1, SP, 1), passed_along(r0, SP, -1)
    cb = passed_along(jnp.stack([hb[1], ha[1]]), SP, 1)
    ca = passed_along(jnp.stack([hb[0], ha[0]]), SP, -1)
    hb_in, ha_in, rb, ra, weight = lax.optimization_barrier((hb, ha, rb, ra, weight))
    weight = lax.all_gather(weight, ("x", "core"), axis=0, tiled=False)
    weight = weight.reshape((lax.axis_size("x"), lax.axis_size("core")) + weight.shape[1:])
    y_hi, y_lo = (lax.axis_index(a).astype(jnp.int32)[None] for a in ("y_hi", "y_lo"))
    same, other = attend(combo, y_hi, qn, (f0, f1), (hb_in, ha_in, rb, ra, cb, ca), masks)
    pair = [along_y(same, lambda y: y ^ 1), along_y(other, lambda y: 3 - y), along_y(other, lambda y: y ^ 2)]
    to_pair, to_across, to_far = project(pair, weight)
    same, to_far = lax.optimization_barrier((same, to_far))
    (mine,) = project([same], weight)
    far = along_y(to_far, lambda y: y ^ 2)
    pieces = [mine, far, along_y(to_pair, lambda y: y ^ 1), along_y(to_across, lambda y: 3 - y)]
    out = finish(y_lo, hidden_in.reshape(-1, width), gate, pieces)
    return out.reshape(hidden_in.shape)


def solution(mesh):
    inner_mesh = Mesh(mesh.devices.reshape(2, 4, 2, 8, 2), TM + SP)
    tokens = P(TM, SP, None, None)
    in_specs = (tokens,) * 4 + (P(),) * 5 + (P(SP, TM), P())
    return jax.shard_map(shards, mesh=inner_mesh, in_specs=in_specs, out_specs=tokens, check_vma=False)
```

time: 189 us -> 195 us (1.032)
  starting transfers between devices: 31.1 us -> 33.5 us
  waiting for transfers between devices: 107 us -> 109 us
    ppermute x9 -> x6, waiting for transfers between devices: 24.9 us -> 49.5 us  [along_y(): lax.ppermute(block, ('y_lo', 'y_hi'), [(at(y), at(target(y))) for y in ra...]
    all_gather x1, waiting for transfers between devices: 27.5 us -> 16.3 us  [shards(): weight = lax.all_gather(weight, ('x', 'core'), axis=0, tiled=False)]
    ppermute x6, waiting for transfers between devices: 53.4 us -> 42.6 us  [passed_along(): return lax.ppermute(block, axes, route)]
    ppermute x9 -> x6, starting transfers between devices: 13.1 us -> 15.9 us  [along_y(): lax.ppermute(block, ('y_lo', 'y_hi'), [(at(y), at(target(y))) for y in ra...]
  transfers between devices with their start and end apart: 17 -> 14, of which waited for: 12 -> 12; matrix products, arithmetic and copies ran while one was open for 1% -> 1% of each run, Pallas kernels for 11% -> 11%
where the time goes in v7:
time: 195 us; the launch traced here: 194 us
  waiting for transfers between devices  109 us (56%)
  starting transfers between devices  33.5 us (17%)
  Pallas kernels  32.7 us (17%)
  between operations  13.7 us (7%)
  local copies, waits for them, and re-layouts  3.8 us (2%)
    ppermute x6, waiting for transfers between devices, along_y(): lax.ppermute(block, ('y_lo', 'y_hi'), [(at(y), at(target(y))) for y in ra...  49.5 us
    ppermute x6, waiting for transfers between devices, passed_along(): return lax.ppermute(block, axes, route)  42.6 us
    ppermute x6, starting transfers between devices, passed_along(): return lax.ppermute(block, axes, route)  17.6 us
    all_gather x1, waiting for transfers between devices, shards(): weight = lax.all_gather(weight, ('x', 'core'), axis=0, tiled=False)  16.3 us
    ppermute x6, starting transfers between devices, along_y(): lax.ppermute(block, ('y_lo', 'y_hi'), [(at(y), at(target(y))) for y in ra...  15.9 us
    pallas_call x2, Pallas kernels, project(): pl.pallas_call(functools.partial(project_kernel, len(blocks)), grid=(xs,)...  15.8 us
    pallas_call x1, Pallas kernels, attend(): pl.pallas_call(functools.partial(attend_kernel, heads, HEAD ** (-0.5)), g...  8.66 us
    pallas_call x1, Pallas kernels, prepare(): pl.pallas_call(prepare_kernel, grid=(groups,), in_specs=[token_spec] * 3...  6.25 us
  transfers between devices with their start and end apart: 14, of which 12 were waited for; matrix products, arithmetic and copies ran while one was open for 1% of the time, Pallas kernels for 11%

profile of v7, /device:TPU:1, one launch (start us, length us, event | category | flops | bytes accessed | tf_op | source)
XLA Modules:
  0.0 194.1 jit_solution(5368628437747553952)
XLA Ops:
  8.8 6.2 %prepare.1 = (bf16[4,32,5120]{2,1,0:T(8,128)(2,1)}, bf16[2,2,32,5120]{3,2,1,0:T(8,128)(2,1)}, bf16[2,2,32,5120]{3,2,1,0:T(8,128)(2,1)}, bf16[2,2,32,5120]{3,2,1,0:T(8,128)(2,1)}, bf16[2,2,32,5120]{3,2,1,0:T(8,128)(2,1)}) custom-call(bf16[4,32,5120]{2,1,0:T(8,128)(2,1)} %bitcast.19, bf16[4,32,5120]{2,1,0:T(8,128)(2,1)} %bitcast.20, ...), custom_call_target="tpu_custom_call" | custom-call | bytes 12582912 | tf_op jit(solution)/shard_map/prepare/pallas_call | solution.py:79
  15.0 4.0 %collective-permute-start = (bf16[2,2,32,5120]{3,2,1,0:T(8,128)(2,1)}, bf16[2,2,32,5120]{3,2,1,0:T(8,128)(2,1)S(1)}, u32[]{:S(2)}, u32[]{:S(2)}) collective-permute-start(bf16[2,2,32,5120]{3,2,1,0:T(8,128)(2,1)} %get-tuple-element.24.f1), channel_id=1, source_target_pairs={{0,32},{32,64},{64,96},{96,128},{128,160},{160,192},{192,224},{1,3... | collective-permute-start | bytes 3932168 | tf_op jit(solution)/shard_map/ppermute | solution.py:28
  20.3 4.4 %collective-permute-start.2 = (bf16[2,2,32,5120]{3,2,1,0:T(8,128)(2,1)}, bf16[2,2,32,5120]{3,2,1,0:T(8,128)(2,1)S(1)}, u32[]{:S(2)}, u32[]{:S(2)}) collective-permute-start(bf16[2,2,32,5120]{3,2,1,0:T(8,128)(2,1)} %get-tuple-element.25), channel_id=1, source_target_pairs={{0,1},{1,2},{2,3},{3,4},{4,5},{5,6},{6,7},{7,8},{8,9},{9,10},{10,1... | collective-permute-start | bytes 3932168 | tf_op jit(solution)/shard_map/ppermute | solution.py:28
  24.7 1.9 collective-permute-start.3
  26.7 20.0 %collective-permute-done.hb = bf16[2,2,32,5120]{3,2,1,0:T(8,128)(2,1)S(1)} collective-permute-done((bf16[2,2,32,5120]{3,2,1,0:T(8,128)(2,1)}, bf16[2,2,32,5120]{3,2,1,0:T(8,128)(2,1)S(1)}, u32[]{:S(2)}, u32[]{:S(2)}) %collective-permute-start) | collective-permute-done | bytes 1310752 | tf_op jit(solution)/shard_map/ppermute | solution.py:28
  46.7 3.9 %collective-permute-done.1.ha = bf16[2,2,32,5120]{3,2,1,0:T(8,128)(2,1)S(1)} collective-permute-done((bf16[2,2,32,5120]{3,2,1,0:T(8,128)(2,1)}, bf16[2,2,32,5120]{3,2,1,0:T(8,128)(2,1)S(1)}, u32[]{:S(2)}, u32[]{:S(2)}) %collective-permute-start.1) | collective-permute-done | bytes 1310752 | tf_op jit(solution)/shard_map/ppermute | solution.py:28
  50.6 3.1 %collective-permute-done.2.rb = bf16[2,2,32,5120]{3,2,1,0:T(8,128)(2,1)S(1)} collective-permute-done((bf16[2,2,32,5120]{3,2,1,0:T(8,128)(2,1)}, bf16[2,2,32,5120]{3,2,1,0:T(8,128)(2,1)S(1)}, u32[]{:S(2)}, u32[]{:S(2)}) %collective-permute-start.2) | collective-permute-done | bytes 1310752 | tf_op jit(solution)/shard_map/ppermute | solution.py:28
  54.7 2.1 %collective-permute-done.3.ra = bf16[2,2,32,5120]{3,2,1,0:T(8,128)(2,1)S(1)} collective-permute-done((bf16[2,2,32,5120]{3,2,1,0:T(8,128)(2,1)}, bf16[2,2,32,5120]{3,2,1,0:T(8,128)(2,1)S(1)}, u32[]{:S(2)}, u32[]{:S(2)}) %collective-permute-start.3) | collective-permute-done | bytes 1310752 | tf_op jit(solution)/shard_map/ppermute | solution.py:28
  58.4 2.1 %collective-permute-start.5 = (bf16[2,2,32,5120]{3,2,1,0:T(8,128)(2,1)S(1)}, bf16[2,2,32,5120]{3,2,1,0:T(8,128)(2,1)S(1)}, u32[]{:S(2)}, u32[]{:S(2)}) collective-permute-start(bf16[2,2,32,5120]{3,2,1,0:T(8,128)(2,1)S(1)} %pad_maximum_fusion.1), channel_id=1, source_target_pairs={{1,0},{2,1},{3,2},{4,3},{5,4},{6,5},{7,6},{8,7},{9,8},{10,9},{11,1... | collective-permute-start | bytes 3932168 | tf_op jit(solution)/shard_map/ppermute | solution.py:28
  60.7 3.9 %collective-permute-start.4 = (bf16[2,2,32,5120]{3,2,1,0:T(8,128)(2,1)S(1)}, bf16[2,2,32,5120]{3,2,1,0:T(8,128)(2,1)S(1)}, u32[]{:S(2)}, u32[]{:S(2)}) collective-permute-start(bf16[2,2,32,5120]{3,2,1,0:T(8,128)(2,1)S(1)} %pad_maximum_fusion), channel_id=1, source_target_pairs={{0,1},{1,2},{2,3},{3,4},{4,5},{5,6},{6,7},{7,8},{8,9},{9,10},{10,1... | collective-permute-start | bytes 3932168 | tf_op jit(solution)/shard_map/ppermute | solution.py:28
  65.5 12.0 %collective-permute-done.5.ca = bf16[2,2,32,5120]{3,2,1,0:T(8,128)(2,1)S(1)} collective-permute-done((bf16[2,2,32,5120]{3,2,1,0:T(8,128)(2,1)S(1)}, bf16[2,2,32,5120]{3,2,1,0:T(8,128)(2,1)S(1)}, u32[]{:S(2)}, u32[]{:S(2)}) %collective-permute-start.5) | collective-permute-done | bytes 1310752 | tf_op jit(solution)/shard_map/ppermute | solution.py:28
  77.5 1.6 collective-permute-done.4.cb
  79.1 8.7 %attend.1 = (bf16[128,2560]{1,0:T(8,128)(2,1)}, bf16[128,2560]{1,0:T(8,128)(2,1)}) custom-call(s32[40]{0:T(128)S(1)} %add_add_fusion.combo_ref, s32[1]{0:T(128)} %bitcast.3.half_ref, bf16[4,32,5120]{2,1,0:T(8,128)(2,1)S(1)} %copy-done, bf16[2,2,32,5120]{3,2,1,0:T(8,128)(2,1)S(1)} %copy-done.1, bf16[2,2,32,5120]{3,2,1,0:T(8,128)(2,1)S(1)} %copy-done.2, ...), custom_call_target="tpu_custom_call" | custom-call | flops 1006632960 | bytes 33554432 | tf_op jit(solution)/shard_map/attend/pallas_call | solution.py:159
  87.8 10.4 %collective-permute-start.6 = (bf16[128,2560]{1,0:T(8,128)(2,1)}, bf16[128,2560]{1,0:T(8,128)(2,1)S(1)}, u32[]{:S(2)}, u32[]{:S(2)}) collective-permute-start(bf16[128,2560]{1,0:T(8,128)(2,1)} %get-tuple-element.35.refs_0_), channel_id=1, source_target_pairs={{0,128},{128,0},{16,144},{144,16},{1,129},{129,1},{17,145},{145,17... | collective-permute-start | bytes 1966088 | tf_op jit(solution)/shard_map/ppermute | solution.py:33
  98.2 1.8 collective-permute-start.8
  100.0 9.5 %collective-permute-done.6.refs_0_ = bf16[128,2560]{1,0:T(8,128)(2,1)S(1)} collective-permute-done((bf16[128,2560]{1,0:T(8,128)(2,1)}, bf16[128,2560]{1,0:T(8,128)(2,1)S(1)}, u32[]{:S(2)}, u32[]{:S(2)}) %collective-permute-start.6) | collective-permute-done | bytes 655392 | tf_op jit(solution)/shard_map/ppermute | solution.py:33
  109.4 17.9 %collective-permute-done.7.refs_1_ = bf16[128,2560]{1,0:T(8,128)(2,1)S(1)} collective-permute-done((bf16[128,2560]{1,0:T(8,128)(2,1)}, bf16[128,2560]{1,0:T(8,128)(2,1)S(1)}, u32[]{:S(2)}, u32[]{:S(2)}) %collective-permute-start.7) | collective-permute-done | bytes 655392 | tf_op jit(solution)/shard_map/ppermute | solution.py:33
  127.3 16.3 %all-gather.7.cloned.1.call-done = bf16[64,160,640]{2,1,0:T(8,128)(2,1)} async-done(((bf16[8,160,640]{2,1,0:T(8,128)(2,1)}), bf16[64,160,640]{2,1,0:T(8,128)(2,1)}) %all-gather.7.cloned.1.call-update) | async-done | bytes 13107216 | tf_op jit(solution)/shard_map/all_gather | solution.py:257
  143.6 9.3 %project.2 = (bf16[128,2560]{1,0:T(8,128)(2,1)S(1)}, bf16[128,2560]{1,0:T(8,128)(2,1)S(1)}, bf16[128,2560]{1,0:T(8,128)(2,1)S(1)}) custom-call(bf16[128,2560]{1,0:T(8,128)(2,1)S(1)} %collective-permute-done.6.refs_0_, bf16[128,2560]{1,0:T(8,128)(2,1)S(1)} %collective-permute-done.7.refs_1_, bf16[128,2560]{1,0:T(8,128)(2,1)S(1)} %collective-permute-done.8.refs_2_, ...), custom_call_target="tpu_custom_call" | custom-call | flops 5033164800 | bytes 13107200 | tf_op jit(solution)/shard_map/project/pallas_call | solution.py:194
  152.9 2.8 %collective-permute-start.9 = (bf16[128,2560]{1,0:T(8,128)(2,1)S(1)}, bf16[128,2560]{1,0:T(8,128)(2,1)S(1)}, u32[]{:S(2)}, u32[]{:S(2)}) collective-permute-start(bf16[128,2560]{1,0:T(8,128)(2,1)S(1)} %get-tuple-element.36), channel_id=1, source_target_pairs={{0,16},{128,144},{16,0},{144,128},{1,17},{129,145},{17,1},{145,129... | collective-permute-start | bytes 1966088 | tf_op jit(solution)/shard_map/ppermute | solution.py:33
  156.6 6.5 %project.3.same0 = bf16[128,2560]{1,0:T(8,128)(2,1)S(1)} custom-call(bf16[128,2560]{1,0:T(8,128)(2,1)S(1)} %copy-done.8, bf16[4,2,8,160,640]{4,3,2,1,0:T(8,128)(2,1)} %bitcast.17), custom_call_target="tpu_custom_call" | custom-call | flops 1677721600 | bytes 13107200 | tf_op jit(solution)/shard_map/project/pallas_call | solution.py:194
  163.1 7.5 %collective-permute-done.9.same1 = bf16[128,2560]{1,0:T(8,128)(2,1)S(1)} collective-permute-done((bf16[128,2560]{1,0:T(8,128)(2,1)S(1)}, bf16[128,2560]{1,0:T(8,128)(2,1)S(1)}, u32[]{:S(2)}, u32[]{:S(2)}) %collective-permute-start.9) | collective-permute-done | bytes 655392 | tf_op jit(solution)/shard_map/ppermute | solution.py:33
  170.6 14.1 %collective-permute-done.10.other0 = bf16[128,2560]{1,0:T(8,128)(2,1)S(1)} collective-permute-done((bf16[128,2560]{1,0:T(8,128)(2,1)S(1)}, bf16[128,2560]{1,0:T(8,128)(2,1)S(1)}, u32[]{:S(2)}, u32[]{:S(2)}) %collective-permute-start.10) | collective-permute-done | bytes 655392 | tf_op jit(solution)/shard_map/ppermute | solution.py:33
  185.2 2.0 %finish.1 = bf16[128,5120]{1,0:T(8,128)(2,1)} custom-call(s32[1]{0:T(128)} %bitcast.y_ref, bf16[128,5120]{1,0:T(8,128)(2,1)S(1)} %bitcast.12, f32[1,5120]{1,0:T(1,128)S(1)} %bitcast.13, bf16[128,2560]{1,0:T(8,128)(2,1)S(1)} %project.3.same0, bf16[128,2560]{1,0:T(8,128)(2,1)S(1)} %collective-permute-done.9.same1, ...), custom_call_target="tpu_custom_call" | custom-call | tf_op jit(solution)/shard_map/finish/pallas_call | solution.py:222
  (61 shorter events, 8.5 us)
Async XLA Ops:
  6.5 51.3 %all-gather.5.cloned.1.call-start = ((), (), s32[]{:S(2)}) async-start(), calls=%async_computation | async-start | bytes 1843200 | tf_op jit(solution)/shard_map/all_gather | solution.py:240
  7.3 136.4 %all-gather.7.cloned.1.call-start = ((), (), s32[]{:S(2)}) async-start(), calls=%async_computation.1 | async-start | bytes 14745600 | tf_op jit(solution)/shard_map/all_gather | solution.py:257
  8.8 49.3 %copy-start.12 = (s32[40]{0:T(128)S(1)}, s32[40]{0:T(128)}, u32[]{:S(2)}) copy-start(s32[40]{0:T(128)} %param.19) | copy-start | bytes 484
  8.8 49.3 %copy-start.13 = (s32[40]{0:T(128)S(1)}, s32[40]{0:T(128)}, u32[]{:S(2)}) copy-start(s32[40]{0:T(128)} %param.18) | copy-start | bytes 484
  8.8 49.3 %copy-start.14 = (s32[40]{0:T(128)S(1)}, s32[40]{0:T(128)}, u32[]{:S(2)}) copy-start(s32[40]{0:T(128)} %param.17) | copy-start | bytes 484
  15.0 31.7 %collective-permute-start = (bf16[2,2,32,5120]{3,2,1,0:T(8,128)(2,1)}, bf16[2,2,32,5120]{3,2,1,0:T(8,128)(2,1)S(1)}, u32[]{:S(2)}, u32[]{:S(2)}) collective-permute-start(bf16[2,2,32,5120]{3,2,1,0:T(8,128)(2,1)} %get-tuple-element.24.f1), channel_id=1, source_target_pairs={{0,32},{32,64},{64,96},{96,128},{128,160},{160,192},{192,224},{1,3... | collective-permute-start | bytes 3932168 | tf_op jit(solution)/shard_map/ppermute | solution.py:28
  19.0 31.5 %collective-permute-start.1 = (bf16[2,2,32,5120]{3,2,1,0:T(8,128)(2,1)}, bf16[2,2,32,5120]{3,2,1,0:T(8,128)(2,1)S(1)}, u32[]{:S(2)}, u32[]{:S(2)}) collective-permute-start(bf16[2,2,32,5120]{3,2,1,0:T(8,128)(2,1)} %get-tuple-element.23.f0), channel_id=1, source_target_pairs={{32,0},{64,32},{96,64},{128,96},{160,128},{192,160},{224,192},{33,... | collective-permute-start | bytes 3932168 | tf_op jit(solution)/shard_map/ppermute | solution.py:28
  20.3 33.3 %collective-permute-start.2 = (bf16[2,2,32,5120]{3,2,1,0:T(8,128)(2,1)}, bf16[2,2,32,5120]{3,2,1,0:T(8,128)(2,1)S(1)}, u32[]{:S(2)}, u32[]{:S(2)}) collective-permute-start(bf16[2,2,32,5120]{3,2,1,0:T(8,128)(2,1)} %get-tuple-element.25), channel_id=1, source_target_pairs={{0,1},{1,2},{2,3},{3,4},{4,5},{5,6},{6,7},{7,8},{8,9},{9,10},{10,1... | collective-permute-start | bytes 3932168 | tf_op jit(solution)/shard_map/ppermute | solution.py:28
  24.7 32.0 %collective-permute-start.3 = (bf16[2,2,32,5120]{3,2,1,0:T(8,128)(2,1)}, bf16[2,2,32,5120]{3,2,1,0:T(8,128)(2,1)S(1)}, u32[]{:S(2)}, u32[]{:S(2)}) collective-permute-start(bf16[2,2,32,5120]{3,2,1,0:T(8,128)(2,1)} %get-tuple-element.26), channel_id=1, source_target_pairs={{1,0},{2,1},{3,2},{4,3},{5,4},{6,5},{7,6},{8,7},{9,8},{10,9},{11,1... | collective-permute-start | bytes 3932168 | tf_op jit(solution)/shard_map/ppermute | solution.py:28
  58.3 20.8 %copy-start.4 = (bf16[2,2,32,5120]{3,2,1,0:T(8,128)(2,1)S(1)}, bf16[2,2,32,5120]{3,2,1,0:T(8,128)(2,1)}, u32[]{:S(2)}) copy-start(bf16[2,2,32,5120]{3,2,1,0:T(8,128)(2,1)} %copy-done.3) | copy-start | bytes 3932164
  58.3 20.8 %copy-start.6 = (bf16[2,2,32,5120]{3,2,1,0:T(8,128)(2,1)S(1)}, bf16[2,2,32,5120]{3,2,1,0:T(8,128)(2,1)}, u32[]{:S(2)}) copy-start(bf16[2,2,32,5120]{3,2,1,0:T(8,128)(2,1)} %copy-done.5) | copy-start | bytes 3932164
  58.4 19.1 %collective-permute-start.5 = (bf16[2,2,32,5120]{3,2,1,0:T(8,128)(2,1)S(1)}, bf16[2,2,32,5120]{3,2,1,0:T(8,128)(2,1)S(1)}, u32[]{:S(2)}, u32[]{:S(2)}) collective-permute-start(bf16[2,2,32,5120]{3,2,1,0:T(8,128)(2,1)S(1)} %pad_maximum_fusion.1), channel_id=1, source_target_pairs={{1,0},{2,1},{3,2},{4,3},{5,4},{6,5},{7,6},{8,7},{9,8},{10,9},{11,1... | collective-permute-start | bytes 3932168 | tf_op jit(solution)/shard_map/ppermute | solution.py:28
  60.5 18.6 %copy-start = (bf16[4,32,5120]{2,1,0:T(8,128)(2,1)S(1)}, bf16[4,32,5120]{2,1,0:T(8,128)(2,1)}, u32[]{:S(2)}) copy-start(bf16[4,32,5120]{2,1,0:T(8,128)(2,1)} %get-tuple-element.22.q_ref) | copy-start | bytes 3932164
  60.5 18.6 %copy-start.1 = (bf16[2,2,32,5120]{3,2,1,0:T(8,128)(2,1)S(1)}, bf16[2,2,32,5120]{3,2,1,0:T(8,128)(2,1)}, u32[]{:S(2)}) copy-start(bf16[2,2,32,5120]{3,2,1,0:T(8,128)(2,1)} %get-tuple-element.23.f0) | copy-start | bytes 3932164
  60.5 18.6 %copy-start.2 = (bf16[2,2,32,5120]{3,2,1,0:T(8,128)(2,1)S(1)}, bf16[2,2,32,5120]{3,2,1,0:T(8,128)(2,1)}, u32[]{:S(2)}) copy-start(bf16[2,2,32,5120]{3,2,1,0:T(8,128)(2,1)} %get-tuple-element.24.f1) | copy-start | bytes 3932164
  60.7 18.4 %collective-permute-start.4 = (bf16[2,2,32,5120]{3,2,1,0:T(8,128)(2,1)S(1)}, bf16[2,2,32,5120]{3,2,1,0:T(8,128)(2,1)S(1)}, u32[]{:S(2)}, u32[]{:S(2)}) collective-permute-start(bf16[2,2,32,5120]{3,2,1,0:T(8,128)(2,1)S(1)} %pad_maximum_fusion), channel_id=1, source_target_pairs={{0,1},{1,2},{2,3},{3,4},{4,5},{5,6},{6,7},{7,8},{8,9},{9,10},{10,1... | collective-permute-start | bytes 3932168 | tf_op jit(solution)/shard_map/ppermute | solution.py:28
  87.8 21.7 %collective-permute-start.6 = (bf16[128,2560]{1,0:T(8,128)(2,1)}, bf16[128,2560]{1,0:T(8,128)(2,1)S(1)}, u32[]{:S(2)}, u32[]{:S(2)}) collective-permute-start(bf16[128,2560]{1,0:T(8,128)(2,1)} %get-tuple-element.35.refs_0_), channel_id=1, source_target_pairs={{0,128},{128,0},{16,144},{144,16},{1,129},{129,1},{17,145},{145,17... | collective-permute-start | bytes 1966088 | tf_op jit(solution)/shard_map/ppermute | solution.py:33
  98.2 29.2 %collective-permute-start.7 = (bf16[128,2560]{1,0:T(8,128)(2,1)}, bf16[128,2560]{1,0:T(8,128)(2,1)S(1)}, u32[]{:S(2)}, u32[]{:S(2)}) collective-permute-start(bf16[128,2560]{1,0:T(8,128)(2,1)} %get-tuple-element.32), channel_id=1, source_target_pairs={{0,144},{128,16},{16,128},{144,0},{1,145},{129,17},{17,129},{145,1... | collective-permute-start | bytes 1966088 | tf_op jit(solution)/shard_map/ppermute | solution.py:33
  98.2 29.2 %collective-permute-start.8 = (bf16[128,2560]{1,0:T(8,128)(2,1)}, bf16[128,2560]{1,0:T(8,128)(2,1)S(1)}, u32[]{:S(2)}, u32[]{:S(2)}) collective-permute-start(bf16[128,2560]{1,0:T(8,128)(2,1)} %get-tuple-element.32), channel_id=1, source_target_pairs={{0,16},{128,144},{16,0},{144,128},{1,17},{129,145},{17,1},{145,129... | collective-permute-start | bytes 1966088 | tf_op jit(solution)/shard_map/ppermute | solution.py:33
  152.9 17.7 %collective-permute-start.9 = (bf16[128,2560]{1,0:T(8,128)(2,1)S(1)}, bf16[128,2560]{1,0:T(8,128)(2,1)S(1)}, u32[]{:S(2)}, u32[]{:S(2)}) collective-permute-start(bf16[128,2560]{1,0:T(8,128)(2,1)S(1)} %get-tuple-element.36), channel_id=1, source_target_pairs={{0,16},{128,144},{16,0},{144,128},{1,17},{129,145},{17,1},{145,129... | collective-permute-start | bytes 1966088 | tf_op jit(solution)/shard_map/ppermute | solution.py:33
  155.7 29.0 %collective-permute-start.10 = (bf16[128,2560]{1,0:T(8,128)(2,1)S(1)}, bf16[128,2560]{1,0:T(8,128)(2,1)S(1)}, u32[]{:S(2)}, u32[]{:S(2)}) collective-permute-start(bf16[128,2560]{1,0:T(8,128)(2,1)S(1)} %get-tuple-element.37), channel_id=1, source_target_pairs={{0,128},{128,0},{16,144},{144,16},{1,129},{129,1},{17,145},{145,17... | collective-permute-start | bytes 1966088 | tf_op jit(solution)/shard_map/ppermute | solution.py:33
  156.0 29.2 %copy-start.7 = (bf16[2,2,32,5120]{3,2,1,0:T(8,128)(2,1)S(1)}, bf16[2,2,32,5120]{3,2,1,0:T(8,128)(2,1)}, u32[]{:S(2)}) copy-start(bf16[2,2,32,5120]{3,2,1,0:T(8,128)(2,1)} %param.11) | copy-start | bytes 3932164
  156.1 29.2 %copy-start.9 = (f32[5120]{0:T(1024)S(1)}, f32[5120]{0:T(1024)}, u32[]{:S(2)}) copy-start(f32[5120]{0:T(1024)} %param.21) | copy-start | bytes 61444
  156.1 29.2 %collective-permute-start.11 = (bf16[128,2560]{1,0:T(8,128)(2,1)S(1)}, bf16[128,2560]{1,0:T(8,128)(2,1)S(1)}, u32[]{:S(2)}, u32[]{:S(2)}) collective-permute-start(bf16[128,2560]{1,0:T(8,128)(2,1)S(1)} %get-tuple-element.38), channel_id=1, source_target_pairs={{0,144},{128,16},{16,128},{144,0},{1,145},{129,17},{17,129},{145,1... | collective-permute-start | bytes 1966088 | tf_op jit(solution)/shard_map/ppermute | solution.py:33
  (5 other events, 16.6 us)
Sparse Core Ops, SparseCore 0:
  9.1 42.2 all-gather.4
  58.0 85.5 all-gather.6

commit v8 on v4

--- a/solution.py
+++ b/solution.py
@@ -11,7 +11,6 @@
 HEAD = 128
 TM = ("y_lo", "x")
 SP = ("y_hi", "z", "core")
-CHUNKS = 1
 COMBOS = 12
 F32, BF16 = jnp.float32, jnp.bfloat16
 
@@ -42,7 +41,7 @@
     return pltpu.CompilerParams(vmem_limit_bytes=megabytes << 20)
 
 
-def prepare_kernel(q_ref, k_ref, v_ref, qg_ref, kg_ref, qn_ref, *outs):
+def prepare_kernel(q_ref, k_ref, qg_ref, kg_ref, qn_ref, *outs):
     i = pl.program_id(0)
     f, r = i // 2, i % 2
     inner = q_ref.shape[-1]
@@ -54,51 +53,37 @@
 
     qn_ref[0] = normed(q_ref, qg_ref)
     kn = normed(k_ref, kg_ref)
-    v = v_ref[0]
-    width = inner // (len(outs) // 4)
-    for c in range(len(outs) // 4):
-        f0, f1, r0, r1 = outs[4 * c : 4 * c + 4]
-        lanes = slice(c * width, (c + 1) * width)
-        for which, ref in ((0, f0), (1, f1)):
-
-            @pl.when(f == which)
-            def _(ref=ref):
-                ref[0, 0] = kn[:, lanes]
-                ref[0, 1] = v[:, lanes]
-
-        for which, ref in ((0, r0), (1, r1)):
-
-            @pl.when(r == which)
-            def _(ref=ref):
-                ref[0, 0] = kn[:, lanes]
-                ref[0, 1] = v[:, lanes]
-
-
-def prepare(queries, keys, values, query_gain, key_gain):
+    f0, f1, r0, r1 = outs
+    for chosen, ref in ((f == 0, f0), (f == 1, f1), (r == 0, r0), (r == 1, r1)):
+
+        @pl.when(chosen)
+        def _(ref=ref):
+            ref[0] = kn
+
+
+def prepare(queries, keys, query_gain, key_gain):
     groups, nw, inner = queries.shape
-    width = inner // CHUNKS
     token_spec = pl.BlockSpec((1, nw, inner), lambda i: (i, 0, 0))
     gain_spec = pl.BlockSpec((1, inner), lambda i: (0, 0))
     out_shape = [pltpu.HBM(queries.shape, BF16)]
-    out_specs = [token_spec]
-    for _ in range(CHUNKS):
-        out_shape += [pltpu.HBM((2, 2, nw, width), BF16)] * 4
-        out_specs += [
-            pl.BlockSpec((1, 2, nw, width), lambda i: (jnp.minimum(i, 1), 0, 0, 0)),
-            pl.BlockSpec((1, 2, nw, width), lambda i: (jnp.maximum(i - 2, 0), 0, 0, 0)),
-            pl.BlockSpec((1, 2, nw, width), lambda i: (i // 2, 0, 0, 0)),
-            pl.BlockSpec((1, 2, nw, width), lambda i: (i // 2, 0, 0, 0)),
-        ]
+    out_shape += [pltpu.HBM((2, nw, inner), BF16)] * 4
+    out_specs = [
+        token_spec,
+        pl.BlockSpec((1, nw, inner), lambda i: (jnp.minimum(i, 1), 0, 0)),
+        pl.BlockSpec((1, nw, inner), lambda i: (jnp.maximum(i - 2, 0), 0, 0)),
+        pl.BlockSpec((1, nw, inner), lambda i: (i // 2, 0, 0)),
+        pl.BlockSpec((1, nw, inner), lambda i: (i // 2, 0, 0)),
+    ]
     return pl.pallas_call(
         prepare_kernel,
         grid=(groups,),
-        in_specs=[token_spec] * 3 + [gain_spec] * 2,
+        in_specs=[token_spec] * 2 + [gain_spec] * 2,
         out_specs=out_specs,
         out_shape=out_shape,
         compiler_params=params(),
         cost_estimate=pl.CostEstimate(flops=0, bytes_accessed=12 << 20, transcendentals=0),
         name="prepare",
-    )(*[in_hbm(a) for a in (queries, keys, values)], query_gain[None], key_gain[None])
+    )(in_hbm(queries), in_hbm(keys), query_gain[None], key_gain[None])
 
 
 def mask_tables(first_frame, first_row, frame_count, row_count, nw):
@@ -117,14 +102,21 @@
     return jnp.where(allowed, 0.0, -jnp.inf).astype(F32)
 
 
-def attend_kernel(heads, scale, combo_ref, q_ref, f0, f1, hb, ha, rb, ra, cb, ca, mask_ref, *out_refs):
+def attend_kernel(
+    heads, scale, combo_ref, q_ref, k0, k1, v_ref, kb, ka, vb, va, rkb, rka, rvb, rva, cb, ca, mask_ref, *out_refs
+):
     step = pl.program_id(0)
-    frames = ((cb.at[0], hb, ca.at[0]), (rb.at[0], f0, ra.at[0]), (rb.at[1], f1, ra.at[1]), (cb.at[1], ha, ca.at[1]))
+    keys_by_frame, values_by_frame = (kb, k0, k1, ka), (vb, v_ref.at[:2], v_ref.at[2:], va)
+    rows = ((rkb, rka), (rvb, rva))
 
     def region(kv, lanes):
         parts = []
-        for below, own, above in frames:
-            parts += [below[kv, :, lanes], own[0, kv, :, lanes], own[1, kv, :, lanes], above[kv, :, lanes]]
+        for frame, own in enumerate((keys_by_frame, values_by_frame)[kv]):
+            if frame in (0, 3):
+                below, above = (ref[frame // 3, kv, :, lanes] for ref in (cb, ca))
+            else:
+                below, above = (ref[frame - 1, :, lanes] for ref in rows[kv])
+            parts += [below, own[0, :, lanes], own[1, :, lanes], above]
         return jnp.concatenate(parts, axis=0)
 
     scores = {}
@@ -153,27 +145,30 @@
             out_refs[f][:, lanes] = (o / total).astype(BF16)
 
 
-def attend(combo, chunk, qn, own, halos, masks, heads=8):
+def attend(combo, qn, keys, values, halos, corners, masks, heads=8):
     groups, nw, inner = qn.shape
-    width = own[0].shape[-1]
     lanes = heads * HEAD
-    steps = width // lanes
-    kv_spec = pl.BlockSpec((2, 2, nw, lanes), lambda i, *_: (0, 0, 0, i))
+    token_spec = pl.BlockSpec((groups, nw, lanes), lambda i, *_: (0, 0, i))
+    frame_spec = pl.BlockSpec((2, nw, lanes), lambda i, *_: (0, 0, i))
+    corner_spec = pl.BlockSpec((2, 2, nw, lanes), lambda i, *_: (0, 0, 0, i))
     return pl.pallas_call(
         functools.partial(attend_kernel, heads, HEAD**-0.5),
         grid_spec=pltpu.PrefetchScalarGridSpec(
             num_scalar_prefetch=1,
-            grid=(steps,),
-            in_specs=[pl.BlockSpec((groups, nw, lanes), lambda i, *_: (0, 0, chunk * steps + i))]
-            + [kv_spec] * 8
+            grid=(inner // lanes,),
+            in_specs=[token_spec]
+            + [frame_spec] * 2
+            + [token_spec]
+            + [frame_spec] * 8
+            + [corner_spec] * 2
             + [pl.BlockSpec(masks.shape, lambda i, *_: (0, 0, 0, 0))],
             out_specs=[pl.BlockSpec((2 * nw, lanes), lambda i, *_: (0, i))] * 2,
         ),
-        out_shape=[pltpu.HBM((2 * nw, width), BF16)] * 2,
+        out_shape=[pltpu.HBM((2 * nw, inner), BF16)] * 2,
         compiler_params=params(),
-        cost_estimate=pl.CostEstimate(flops=4 * 128 * 384 * width, bytes_accessed=32 << 20, transcendentals=0),
+        cost_estimate=pl.CostEstimate(flops=4 * 128 * 384 * inner, bytes_accessed=32 << 20, transcendentals=0),
         name="attend",
-    )(combo, qn, *own, *halos, masks)
+    )(combo, qn, *keys, values, *halos, *corners, masks)
 
 
 def project_kernel(blocks, *refs):
@@ -258,8 +253,11 @@
     frames, rows, nw, inner = queries.shape
     width = hidden_in.shape[3]
     weight = lax.all_gather(out_weight, "z", axis=0, tiled=False)
-    tokens = [a.reshape(frames * rows, nw, inner) for a in (queries, keys, values)]
-    qn, *own = prepare(*tokens, query_gain, key_gain)
+    vb, va = passed_along(values[1], TM, 1), passed_along(values[0], TM, -1)
+    rvb, rva = passed_along(values[:, 1], SP, 1), passed_along(values[:, 0], SP, -1)
+
+    q_tokens, k_tokens, v_tokens = [a.reshape(frames * rows, nw, inner) for a in (queries, keys, values)]
+    qn, k0, k1, kr0, kr1 = prepare(q_tokens, k_tokens, query_gain, key_gain)
     masks = mask_tables(
         lax.axis_index(TM) * frames,
         lax.axis_index(SP) * rows,
@@ -268,21 +266,18 @@
         nw,
     )
     combo = reach_time * 6 + reach_rows * 3 + reach_cols
-    heads = reach_time.shape[0] // CHUNKS
-    outs = []
-    for c in range(CHUNKS):
-        f0, f1, r0, r1 = own[4 * c : 4 * c + 4]
-        hb, ha = passed_along(f1, TM, 1), passed_along(f0, TM, -1)
-        if c == 0:
-            hb, ha, r0, r1, weight = lax.optimization_barrier((hb, ha, r0, r1, weight))
-            weight = lax.all_gather(weight, ("y_hi", "y_lo", "core"), axis=0, tiled=False)
-            weight = weight.reshape((2, 2, 2) + weight.shape[1:])
-        cb = passed_along(jnp.stack([hb[1], ha[1]]), SP, 1)
-        ca = passed_along(jnp.stack([hb[0], ha[0]]), SP, -1)
-        rb, ra = passed_along(r1, SP, 1), passed_along(r0, SP, -1)
-        a = attend(combo[c * heads : (c + 1) * heads], c, qn, (f0, f1), (hb, ha, rb, ra, cb, ca), masks)
-        outs.append(a)
-    a0, a1 = outs[0]
+    sent = lax.optimization_barrier((k0, k1, kr0, kr1, vb, va, rvb, rva))
+    k0, k1, kr0, kr1, vb, va, rvb, rva = sent
+    kb, ka = passed_along(k1, TM, 1), passed_along(k0, TM, -1)
+    rkb, rka = passed_along(kr1, SP, 1), passed_along(kr0, SP, -1)
+    halos = kb, ka, vb, va, rkb, rka, rvb, rva
+    *halos, weight = lax.optimization_barrier((*halos, weight))
+    kb, ka, vb, va = halos[:4]
+    weight = lax.all_gather(weight, ("y_hi", "y_lo", "core"), axis=0, tiled=False)
+    weight = weight.reshape((2, 2, 2) + weight.shape[1:])
+    cb = passed_along(jnp.stack([jnp.stack([kb[1], vb[1]]), jnp.stack([ka[1], va[1]])]), SP, 1)
+    ca = passed_along(jnp.stack([jnp.stack([kb[0], vb[0]]), jnp.stack([ka[0], va[0]])]), SP, -1)
+    a0, a1 = attend(combo, qn, (k0, k1), v_tokens, halos, (cb, ca), masks)
     left0, right1 = shifted(a0, "x", 1), shifted(a1, "x", -1)
     left1, right0 = shifted(a1, "x", 1), shifted(a0, "x", -1)
     far0, far1 = shifted(left0, "x", 1), shifted(right1, "x", -1)

time: 189 us -> 196 us (1.037)
  starting transfers between devices: 31.1 us -> 53.6 us
  waiting for transfers between devices: 107 us -> 86.8 us
  local copies, waits for them, and re-layouts: 3.61 us -> 8.09 us
    ppermute x6 -> x10, waiting for transfers between devices: 53.4 us -> 33.9 us  [passed_along(): return lax.ppermute(block, axes, route)]
    ppermute x9, starting transfers between devices: 13.1 us -> 24.9 us  [shifted(): lax.ppermute(block, axis, [(i, (i + distance) % n) for i in range(n)])]
    ppermute x6 -> x10, starting transfers between devices: 18 us -> 28.6 us  [passed_along(): return lax.ppermute(block, axes, route)]
    all_gather x1, waiting for transfers between devices: 27.5 us -> 18.1 us  [shards(): lax.all_gather(weight, ('y_hi', 'y_lo', 'core'), axis=0, tiled=False)]
    ppermute x9, waiting for transfers between devices: 24.9 us -> 34 us  [shifted(): lax.ppermute(block, axis, [(i, (i + distance) % n) for i in range(n)])]
    unnamed x32 -> x46, local copies, waits for them, and re-layouts: 3.44 us -> 5.38 us
  transfers between devices with their start and end apart: 17 -> 21, of which waited for: 12 -> 16; matrix products, arithmetic and copies ran while one was open for 1% -> 2% of each run, Pallas kernels for 11% -> 11%
where the time goes in v8:
time: 196 us
  waiting for transfers between devices  86.8 us (44%)
  starting transfers between devices  53.6 us (27%)
  Pallas kernels  31.9 us (16%)
  between operations  13.9 us (7%)
  local copies, waits for them, and re-layouts  8.09 us (4%)
    ppermute x9, waiting for transfers between devices, shifted(): lax.ppermute(block, axis, [(i, (i + distance) % n) for i in range(n)])  34 us
    ppermute x10, waiting for transfers between devices, passed_along(): return lax.ppermute(block, axes, route)  33.9 us
    ppermute x10, starting transfers between devices, passed_along(): return lax.ppermute(block, axes, route)  28.6 us
    ppermute x9, starting transfers between devices, shifted(): lax.ppermute(block, axis, [(i, (i + distance) % n) for i in range(n)])  24.9 us
    all_gather x1, waiting for transfers between devices, shards(): lax.all_gather(weight, ('y_hi', 'y_lo', 'core'), axis=0, tiled=False)  18.1 us
    pallas_call x2, Pallas kernels, project(): pl.pallas_call(functools.partial(project_kernel, len(blocks)), grid=(grou...  15.8 us
    pallas_call x1, Pallas kernels, attend(): pl.pallas_call(functools.partial(attend_kernel, heads, HEAD ** (-0.5)), g...  9.2 us
    unnamed x46, local copies, waits for them, and re-layouts  5.38 us
  transfers between devices with their start and end apart: 21, of which 16 were waited for; matrix products, arithmetic and copies ran while one was open for 2% of the time, Pallas kernels for 11%

profile of v8, /device:TPU:1, one launch (start us, length us, event | category | flops | bytes accessed | tf_op | source)
XLA Modules:
  0.0 195.7 jit_solution(17335086797169977168)
XLA Ops:
  8.7 4.0 %collective-permute-start = (bf16[2,32,5120]{2,1,0:T(8,128)(2,1)S(1)}, bf16[2,32,5120]{2,1,0:T(8,128)(2,1)S(1)}, u32[]{:S(2)}, u32[]{:S(2)}) collective-permute-start(bf16[2,32,5120]{2,1,0:T(8,128)(2,1)S(1)} %get-tuple-element.66), channel_id=1, source_target_pairs={{0,32},{32,64},{64,96},{96,128},{128,160},{160,192},{192,224},{1,3... | collective-permute-start | bytes 1966088 | tf_op jit(solution)/shard_map/ppermute | solution.py:28
  14.1 4.5 %collective-permute-start.2 = (bf16[2,32,5120]{2,1,0:T(8,128)(2,1)S(1)}, bf16[2,32,5120]{2,1,0:T(8,128)(2,1)S(1)}, u32[]{:S(2)}, u32[]{:S(2)}) collective-permute-start(bf16[2,32,5120]{2,1,0:T(8,128)(2,1)S(1)} %get-tuple-element.64), channel_id=1, source_target_pairs={{0,1},{1,2},{2,3},{3,4},{4,5},{5,6},{6,7},{7,8},{8,9},{9,10},{10,1... | collective-permute-start | bytes 1966088 | tf_op jit(solution)/shard_map/ppermute | solution.py:28
  20.6 5.1 %prepare.1 = (bf16[4,32,5120]{2,1,0:T(8,128)(2,1)}, bf16[2,32,5120]{2,1,0:T(8,128)(2,1)}, bf16[2,32,5120]{2,1,0:T(8,128)(2,1)}, bf16[2,32,5120]{2,1,0:T(8,128)(2,1)}, bf16[2,32,5120]{2,1,0:T(8,128)(2,1)}) custom-call(bf16[4,32,5120]{2,1,0:T(8,128)(2,1)} %bitcast.39, bf16[4,32,5120]{2,1,0:T(8,128)(2,1)} %bitcast.40, f32[1,5120]{1,0:T(1,128)S(1)} %bitcast.34, ...), custom_call_target="tpu_custom_call" | custom-call | bytes 12582912 | tf_op jit(solution)/shard_map/prepare/pallas_call | solution.py:77
  26.0 3.9 %collective-permute-done.1.va = bf16[2,32,5120]{2,1,0:T(8,128)(2,1)S(1)} collective-permute-done((bf16[2,32,5120]{2,1,0:T(8,128)(2,1)S(1)}, bf16[2,32,5120]{2,1,0:T(8,128)(2,1)S(1)}, u32[]{:S(2)}, u32[]{:S(2)}) %collective-permute-start.1) | collective-permute-done | bytes 655392 | tf_op jit(solution)/shard_map/ppermute | solution.py:28
  30.8 5.9 %collective-permute-done.3.rva = bf16[2,32,5120]{2,1,0:T(8,128)(2,1)S(1)} collective-permute-done((bf16[2,32,5120]{2,1,0:T(8,128)(2,1)S(1)}, bf16[2,32,5120]{2,1,0:T(8,128)(2,1)S(1)}, u32[]{:S(2)}, u32[]{:S(2)}) %collective-permute-start.3) | collective-permute-done | bytes 655392 | tf_op jit(solution)/shard_map/ppermute | solution.py:28
  37.5 5.4 %collective-permute-start.4 = (bf16[2,32,5120]{2,1,0:T(8,128)(2,1)}, bf16[2,32,5120]{2,1,0:T(8,128)(2,1)S(1)}, u32[]{:S(2)}, u32[]{:S(2)}) collective-permute-start(bf16[2,32,5120]{2,1,0:T(8,128)(2,1)} %get-tuple-element.40.k1), channel_id=1, source_target_pairs={{0,32},{32,64},{64,96},{96,128},{128,160},{160,192},{192,224},{1,3... | collective-permute-start | bytes 1966088 | tf_op jit(solution)/shard_map/ppermute | solution.py:28
  48.6 3.2 %collective-permute-done.4.kb = bf16[2,32,5120]{2,1,0:T(8,128)(2,1)S(1)} collective-permute-done((bf16[2,32,5120]{2,1,0:T(8,128)(2,1)}, bf16[2,32,5120]{2,1,0:T(8,128)(2,1)S(1)}, u32[]{:S(2)}, u32[]{:S(2)}) %collective-permute-start.4) | collective-permute-done | bytes 655392 | tf_op jit(solution)/shard_map/ppermute | solution.py:28
  51.8 4.1 %collective-permute-done.5.ka = bf16[2,32,5120]{2,1,0:T(8,128)(2,1)} collective-permute-done((bf16[2,32,5120]{2,1,0:T(8,128)(2,1)}, bf16[2,32,5120]{2,1,0:T(8,128)(2,1)}, u32[]{:S(2)}, u32[]{:S(2)}) %collective-permute-start.5) | collective-permute-done | bytes 655392 | tf_op jit(solution)/shard_map/ppermute | solution.py:28
  57.1 2.5 %collective-permute-done.7.rka = bf16[2,32,5120]{2,1,0:T(8,128)(2,1)S(1)} collective-permute-done((bf16[2,32,5120]{2,1,0:T(8,128)(2,1)}, bf16[2,32,5120]{2,1,0:T(8,128)(2,1)S(1)}, u32[]{:S(2)}, u32[]{:S(2)}) %collective-permute-start.7) | collective-permute-done | bytes 655392 | tf_op jit(solution)/shard_map/ppermute | solution.py:28
  64.5 3.9 %collective-permute-start.8 = (bf16[2,2,32,5120]{3,2,1,0:T(8,128)(2,1)S(1)}, bf16[2,2,32,5120]{3,2,1,0:T(8,128)(2,1)S(1)}, u32[]{:S(2)}, u32[]{:S(2)}) collective-permute-start(bf16[2,2,32,5120]{3,2,1,0:T(8,128)(2,1)S(1)} %pad_maximum_fusion), channel_id=1, source_target_pairs={{0,1},{1,2},{2,3},{3,4},{4,5},{5,6},{6,7},{7,8},{8,9},{9,10},{10,1... | collective-permute-start | bytes 3932168 | tf_op jit(solution)/shard_map/ppermute | solution.py:28
  69.4 11.8 %collective-permute-done.9.ca = bf16[2,2,32,5120]{3,2,1,0:T(8,128)(2,1)S(1)} collective-permute-done((bf16[2,2,32,5120]{3,2,1,0:T(8,128)(2,1)S(1)}, bf16[2,2,32,5120]{3,2,1,0:T(8,128)(2,1)S(1)}, u32[]{:S(2)}, u32[]{:S(2)}) %collective-permute-start.9) | collective-permute-done | bytes 1310752 | tf_op jit(solution)/shard_map/ppermute | solution.py:28
  83.0 9.2 %attend.1 = (bf16[64,5120]{1,0:T(8,128)(2,1)}, bf16[64,5120]{1,0:T(8,128)(2,1)}) custom-call(s32[40]{0:T(128)S(1)} %add_add_fusion.combo_ref, bf16[4,32,5120]{2,1,0:T(8,128)(2,1)S(1)} %copy-done.2, bf16[2,32,5120]{2,1,0:T(8,128)(2,1)S(1)} %copy-done.7, bf16[2,32,5120]{2,1,0:T(8,128)(2,1)S(1)} %copy-done.8, bf16[4,32,5120]{2,1,0:T(8,128)(2,1)S(1)} %bitcast.31, ...), custom_call_target="tpu_custom_call" | custom-call | flops 1006632960 | bytes 33554432 | tf_op jit(solution)/shard_map/attend/pallas_call | solution.py:154
  92.2 3.0 %collective-permute-start.10 = (bf16[64,5120]{1,0:T(8,128)(2,1)}, bf16[64,5120]{1,0:T(8,128)(2,1)S(1)}, u32[]{:S(2)}, u32[]{:S(2)}) collective-permute-start(bf16[64,5120]{1,0:T(8,128)(2,1)} %get-tuple-element.59.refs_0_), channel_id=1, source_target_pairs={{0,32},{32,64},{64,96},{96,0},{1,33},{33,65},{65,97},{97,1},{2,34}... | collective-permute-start | bytes 1966088 | tf_op jit(solution)/shard_map/ppermute | solution.py:33
  95.2 13.3 %collective-permute-start.12 = (bf16[64,5120]{1,0:T(8,128)(2,1)}, bf16[64,5120]{1,0:T(8,128)(2,1)S(1)}, u32[]{:S(2)}, u32[]{:S(2)}) collective-permute-start(bf16[64,5120]{1,0:T(8,128)(2,1)} %get-tuple-element.56.refs_1_), channel_id=1, source_target_pairs={{0,96},{32,0},{64,32},{96,64},{1,97},{33,1},{65,33},{97,65},{2,98}... | collective-permute-start | bytes 1966088 | tf_op jit(solution)/shard_map/ppermute | solution.py:33
  108.5 2.7 %collective-permute-start.15 = (bf16[64,5120]{1,0:T(8,128)(2,1)}, bf16[64,5120]{1,0:T(8,128)(2,1)S(1)}, u32[]{:S(2)}, u32[]{:S(2)}) collective-permute-start(bf16[64,5120]{1,0:T(8,128)(2,1)} %get-tuple-element.59.refs_0_), channel_id=1, source_target_pairs={{0,96},{32,0},{64,32},{96,64},{1,97},{33,1},{65,33},{97,65},{2,98}... | collective-permute-start | bytes 1966088 | tf_op jit(solution)/shard_map/ppermute | solution.py:33
  111.2 13.0 %collective-permute-done.10.refs_2_ = bf16[64,5120]{1,0:T(8,128)(2,1)S(1)} collective-permute-done((bf16[64,5120]{1,0:T(8,128)(2,1)}, bf16[64,5120]{1,0:T(8,128)(2,1)S(1)}, u32[]{:S(2)}, u32[]{:S(2)}) %collective-permute-start.10) | collective-permute-done | bytes 655392 | tf_op jit(solution)/shard_map/ppermute | solution.py:33
  124.2 2.7 %collective-permute-start.13 = (bf16[64,5120]{1,0:T(8,128)(2,1)S(1)}, bf16[64,5120]{1,0:T(8,128)(2,1)S(1)}, u32[]{:S(2)}, u32[]{:S(2)}) collective-permute-start(bf16[64,5120]{1,0:T(8,128)(2,1)S(1)} %collective-permute-done.12.refs_5_), channel_id=1, source_target_pairs={{0,96},{32,0},{64,32},{96,64},{1,97},{33,1},{65,33},{97,65},{2,98}... | collective-permute-start | bytes 1966088 | tf_op jit(solution)/shard_map/ppermute | solution.py:33
  126.9 5.4 %collective-permute-done.14.refs_3_ = bf16[64,5120]{1,0:T(8,128)(2,1)S(1)} collective-permute-done((bf16[64,5120]{1,0:T(8,128)(2,1)}, bf16[64,5120]{1,0:T(8,128)(2,1)S(1)}, u32[]{:S(2)}, u32[]{:S(2)}) %collective-permute-start.14) | collective-permute-done | bytes 655392 | tf_op jit(solution)/shard_map/ppermute | solution.py:33
  132.3 7.0 %collective-permute-done.11.refs_0_ = bf16[64,5120]{1,0:T(8,128)(2,1)S(1)} collective-permute-done((bf16[64,5120]{1,0:T(8,128)(2,1)S(1)}, bf16[64,5120]{1,0:T(8,128)(2,1)S(1)}, u32[]{:S(2)}, u32[]{:S(2)}) %collective-permute-start.11) | collective-permute-done | bytes 655392 | tf_op jit(solution)/shard_map/ppermute | solution.py:33
  140.1 18.1 %all-gather.7.cloned.1.call-done = bf16[64,160,640]{2,1,0:T(8,128)(2,1)} async-done(((bf16[8,160,640]{2,1,0:T(8,128)(2,1)}), bf16[64,160,640]{2,1,0:T(8,128)(2,1)}) %all-gather.7.cloned.1.call-update) | async-done | bytes 13107216 | tf_op jit(solution)/shard_map/all_gather | solution.py:276
  159.4 9.2 %project.2 = (bf16[128,1280]{1,0:T(8,128)(2,1)S(1)}, bf16[128,1280]{1,0:T(8,128)(2,1)S(1)}, bf16[128,1280]{1,0:T(8,128)(2,1)S(1)}) custom-call(bf16[64,5120]{1,0:T(8,128)(2,1)S(1)} %collective-permute-done.11.refs_0_, bf16[64,5120]{1,0:T(8,128)(2,1)S(1)} %copy-done.19, bf16[64,5120]{1,0:T(8,128)(2,1)S(1)} %collective-permute-done.10.refs_2_, ...), custom_call_target="tpu_custom_call" | custom-call | flops 5033164800 | bytes 13107200 | tf_op jit(solution)/shard_map/project/pallas_call | solution.py:207
  168.9 2.5 %collective-permute-start.16 = (bf16[128,1280]{1,0:T(8,128)(2,1)S(1)}, bf16[128,1280]{1,0:T(8,128)(2,1)S(1)}, u32[]{:S(2)}, u32[]{:S(2)}) collective-permute-start(bf16[128,1280]{1,0:T(8,128)(2,1)S(1)} %get-tuple-element.60), channel_id=1, source_target_pairs={{0,96},{32,0},{64,32},{96,64},{1,97},{33,1},{65,33},{97,65},{2,98}... | collective-permute-start | bytes 983048 | tf_op jit(solution)/shard_map/ppermute | solution.py:33
  171.9 6.6 %project.3.p0 = bf16[128,1280]{1,0:T(8,128)(2,1)S(1)} custom-call(bf16[64,5120]{1,0:T(8,128)(2,1)S(1)} %copy-done.13, bf16[64,5120]{1,0:T(8,128)(2,1)S(1)} %copy-done.14, bf16[2,2,2,8,160,640]{5,4,3,2,1,0:T(8,128)(2,1)} %bitcast.37), custom_call_target="tpu_custom_call" | custom-call | flops 1677721600 | bytes 13107200 | tf_op jit(solution)/shard_map/project/pallas_call | solution.py:207
  179.5 7.0 %collective-permute-done.16.p1 = bf16[128,1280]{1,0:T(8,128)(2,1)S(1)} collective-permute-done((bf16[128,1280]{1,0:T(8,128)(2,1)S(1)}, bf16[128,1280]{1,0:T(8,128)(2,1)S(1)}, u32[]{:S(2)}, u32[]{:S(2)}) %collective-permute-start.16) | collective-permute-done | bytes 327712 | tf_op jit(solution)/shard_map/ppermute | solution.py:33
  (97 shorter events, 27.7 us)
Async XLA Ops:
  6.5 53.9 %all-gather.5.cloned.1.call-start = ((), (), s32[]{:S(2)}) async-start(), calls=%async_computation | async-start | bytes 1843200 | tf_op jit(solution)/shard_map/all_gather | solution.py:255
  7.3 151.0 %all-gather.7.cloned.1.call-start = ((), (), s32[]{:S(2)}) async-start(), calls=%async_computation.1 | async-start | bytes 14745600 | tf_op jit(solution)/shard_map/all_gather | solution.py:276
  8.7 17.3 %collective-permute-start = (bf16[2,32,5120]{2,1,0:T(8,128)(2,1)S(1)}, bf16[2,32,5120]{2,1,0:T(8,128)(2,1)S(1)}, u32[]{:S(2)}, u32[]{:S(2)}) collective-permute-start(bf16[2,32,5120]{2,1,0:T(8,128)(2,1)S(1)} %get-tuple-element.66), channel_id=1, source_target_pairs={{0,32},{32,64},{64,96},{96,128},{128,160},{160,192},{192,224},{1,3... | collective-permute-start | bytes 1966088 | tf_op jit(solution)/shard_map/ppermute | solution.py:28
  12.7 17.3 %collective-permute-start.1 = (bf16[2,32,5120]{2,1,0:T(8,128)(2,1)S(1)}, bf16[2,32,5120]{2,1,0:T(8,128)(2,1)S(1)}, u32[]{:S(2)}, u32[]{:S(2)}) collective-permute-start(bf16[2,32,5120]{2,1,0:T(8,128)(2,1)S(1)} %get-tuple-element.65), channel_id=1, source_target_pairs={{32,0},{64,32},{96,64},{128,96},{160,128},{192,160},{224,192},{33,... | collective-permute-start | bytes 1966088 | tf_op jit(solution)/shard_map/ppermute | solution.py:28
  14.1 46.6 %copy-start.20 = (s32[40]{0:T(128)S(1)}, s32[40]{0:T(128)}, u32[]{:S(2)}) copy-start(s32[40]{0:T(128)} %param.19) | copy-start | bytes 484
  14.1 46.6 %copy-start.21 = (s32[40]{0:T(128)S(1)}, s32[40]{0:T(128)}, u32[]{:S(2)}) copy-start(s32[40]{0:T(128)} %param.18) | copy-start | bytes 484
  14.1 46.6 %copy-start.22 = (s32[40]{0:T(128)S(1)}, s32[40]{0:T(128)}, u32[]{:S(2)}) copy-start(s32[40]{0:T(128)} %param.17) | copy-start | bytes 484
  14.1 15.8 %collective-permute-start.2 = (bf16[2,32,5120]{2,1,0:T(8,128)(2,1)S(1)}, bf16[2,32,5120]{2,1,0:T(8,128)(2,1)S(1)}, u32[]{:S(2)}, u32[]{:S(2)}) collective-permute-start(bf16[2,32,5120]{2,1,0:T(8,128)(2,1)S(1)} %get-tuple-element.64), channel_id=1, source_target_pairs={{0,1},{1,2},{2,3},{3,4},{4,5},{5,6},{6,7},{7,8},{8,9},{9,10},{10,1... | collective-permute-start | bytes 1966088 | tf_op jit(solution)/shard_map/ppermute | solution.py:28
  18.7 18.0 %collective-permute-start.3 = (bf16[2,32,5120]{2,1,0:T(8,128)(2,1)S(1)}, bf16[2,32,5120]{2,1,0:T(8,128)(2,1)S(1)}, u32[]{:S(2)}, u32[]{:S(2)}) collective-permute-start(bf16[2,32,5120]{2,1,0:T(8,128)(2,1)S(1)} %get-tuple-element.63), channel_id=1, source_target_pairs={{1,0},{2,1},{3,2},{4,3},{5,4},{6,5},{7,6},{8,7},{9,8},{10,9},{11,1... | collective-permute-start | bytes 1966088 | tf_op jit(solution)/shard_map/ppermute | solution.py:28
  37.5 14.3 %collective-permute-start.4 = (bf16[2,32,5120]{2,1,0:T(8,128)(2,1)}, bf16[2,32,5120]{2,1,0:T(8,128)(2,1)S(1)}, u32[]{:S(2)}, u32[]{:S(2)}) collective-permute-start(bf16[2,32,5120]{2,1,0:T(8,128)(2,1)} %get-tuple-element.40.k1), channel_id=1, source_target_pairs={{0,32},{32,64},{64,96},{96,128},{128,160},{160,192},{192,224},{1,3... | collective-permute-start | bytes 1966088 | tf_op jit(solution)/shard_map/ppermute | solution.py:28
  43.0 13.0 %collective-permute-start.5 = (bf16[2,32,5120]{2,1,0:T(8,128)(2,1)}, bf16[2,32,5120]{2,1,0:T(8,128)(2,1)}, u32[]{:S(2)}, u32[]{:S(2)}) collective-permute-start(bf16[2,32,5120]{2,1,0:T(8,128)(2,1)} %get-tuple-element.39.k0), channel_id=1, source_target_pairs={{32,0},{64,32},{96,64},{128,96},{160,128},{192,160},{224,192},{33,... | collective-permute-start | bytes 1966088 | tf_op jit(solution)/shard_map/ppermute | solution.py:28
  44.3 11.9 %collective-permute-start.6 = (bf16[2,32,5120]{2,1,0:T(8,128)(2,1)}, bf16[2,32,5120]{2,1,0:T(8,128)(2,1)S(1)}, u32[]{:S(2)}, u32[]{:S(2)}) collective-permute-start(bf16[2,32,5120]{2,1,0:T(8,128)(2,1)} %get-tuple-element.43), channel_id=1, source_target_pairs={{0,1},{1,2},{2,3},{3,4},{4,5},{5,6},{6,7},{7,8},{8,9},{9,10},{10,1... | collective-permute-start | bytes 1966088 | tf_op jit(solution)/shard_map/ppermute | solution.py:28
  46.2 13.4 %collective-permute-start.7 = (bf16[2,32,5120]{2,1,0:T(8,128)(2,1)}, bf16[2,32,5120]{2,1,0:T(8,128)(2,1)S(1)}, u32[]{:S(2)}, u32[]{:S(2)}) collective-permute-start(bf16[2,32,5120]{2,1,0:T(8,128)(2,1)} %get-tuple-element.44), channel_id=1, source_target_pairs={{1,0},{2,1},{3,2},{4,3},{5,4},{6,5},{7,6},{8,7},{9,8},{10,9},{11,1... | collective-permute-start | bytes 1966088 | tf_op jit(solution)/shard_map/ppermute | solution.py:28
  62.2 18.9 %collective-permute-start.9 = (bf16[2,2,32,5120]{3,2,1,0:T(8,128)(2,1)S(1)}, bf16[2,2,32,5120]{3,2,1,0:T(8,128)(2,1)S(1)}, u32[]{:S(2)}, u32[]{:S(2)}) collective-permute-start(bf16[2,2,32,5120]{3,2,1,0:T(8,128)(2,1)S(1)} %pad_maximum_fusion.1), channel_id=1, source_target_pairs={{1,0},{2,1},{3,2},{4,3},{5,4},{6,5},{7,6},{8,7},{9,8},{10,9},{11,1... | collective-permute-start | bytes 3932168 | tf_op jit(solution)/shard_map/ppermute | solution.py:28
  64.5 18.4 %collective-permute-start.8 = (bf16[2,2,32,5120]{3,2,1,0:T(8,128)(2,1)S(1)}, bf16[2,2,32,5120]{3,2,1,0:T(8,128)(2,1)S(1)}, u32[]{:S(2)}, u32[]{:S(2)}) collective-permute-start(bf16[2,2,32,5120]{3,2,1,0:T(8,128)(2,1)S(1)} %pad_maximum_fusion), channel_id=1, source_target_pairs={{0,1},{1,2},{2,3},{3,4},{4,5},{5,6},{6,7},{7,8},{8,9},{9,10},{10,1... | collective-permute-start | bytes 3932168 | tf_op jit(solution)/shard_map/ppermute | solution.py:28
  92.2 32.0 %collective-permute-start.10 = (bf16[64,5120]{1,0:T(8,128)(2,1)}, bf16[64,5120]{1,0:T(8,128)(2,1)S(1)}, u32[]{:S(2)}, u32[]{:S(2)}) collective-permute-start(bf16[64,5120]{1,0:T(8,128)(2,1)} %get-tuple-element.59.refs_0_), channel_id=1, source_target_pairs={{0,32},{32,64},{64,96},{96,0},{1,33},{33,65},{65,97},{97,1},{2,34}... | collective-permute-start | bytes 1966088 | tf_op jit(solution)/shard_map/ppermute | solution.py:33
  95.2 29.0 %collective-permute-start.12 = (bf16[64,5120]{1,0:T(8,128)(2,1)}, bf16[64,5120]{1,0:T(8,128)(2,1)S(1)}, u32[]{:S(2)}, u32[]{:S(2)}) collective-permute-start(bf16[64,5120]{1,0:T(8,128)(2,1)} %get-tuple-element.56.refs_1_), channel_id=1, source_target_pairs={{0,96},{32,0},{64,32},{96,64},{1,97},{33,1},{65,33},{97,65},{2,98}... | collective-permute-start | bytes 1966088 | tf_op jit(solution)/shard_map/ppermute | solution.py:33
  108.5 23.8 %collective-permute-start.14 = (bf16[64,5120]{1,0:T(8,128)(2,1)}, bf16[64,5120]{1,0:T(8,128)(2,1)S(1)}, u32[]{:S(2)}, u32[]{:S(2)}) collective-permute-start(bf16[64,5120]{1,0:T(8,128)(2,1)} %get-tuple-element.56.refs_1_), channel_id=1, source_target_pairs={{0,32},{32,64},{64,96},{96,0},{1,33},{33,65},{65,97},{97,1},{2,34}... | collective-permute-start | bytes 1966088 | tf_op jit(solution)/shard_map/ppermute | solution.py:33
  108.5 23.8 %collective-permute-start.15 = (bf16[64,5120]{1,0:T(8,128)(2,1)}, bf16[64,5120]{1,0:T(8,128)(2,1)S(1)}, u32[]{:S(2)}, u32[]{:S(2)}) collective-permute-start(bf16[64,5120]{1,0:T(8,128)(2,1)} %get-tuple-element.59.refs_0_), channel_id=1, source_target_pairs={{0,96},{32,0},{64,32},{96,64},{1,97},{33,1},{65,33},{97,65},{2,98}... | collective-permute-start | bytes 1966088 | tf_op jit(solution)/shard_map/ppermute | solution.py:33
  124.2 15.1 %collective-permute-start.11 = (bf16[64,5120]{1,0:T(8,128)(2,1)S(1)}, bf16[64,5120]{1,0:T(8,128)(2,1)S(1)}, u32[]{:S(2)}, u32[]{:S(2)}) collective-permute-start(bf16[64,5120]{1,0:T(8,128)(2,1)S(1)} %collective-permute-done.10.refs_2_), channel_id=1, source_target_pairs={{0,32},{32,64},{64,96},{96,0},{1,33},{33,65},{65,97},{97,1},{2,34}... | collective-permute-start | bytes 1966088 | tf_op jit(solution)/shard_map/ppermute | solution.py:33
  124.2 15.1 %collective-permute-start.13 = (bf16[64,5120]{1,0:T(8,128)(2,1)S(1)}, bf16[64,5120]{1,0:T(8,128)(2,1)S(1)}, u32[]{:S(2)}, u32[]{:S(2)}) collective-permute-start(bf16[64,5120]{1,0:T(8,128)(2,1)S(1)} %collective-permute-done.12.refs_5_), channel_id=1, source_target_pairs={{0,96},{32,0},{64,32},{96,64},{1,97},{33,1},{65,33},{97,65},{2,98}... | collective-permute-start | bytes 1966088 | tf_op jit(solution)/shard_map/ppermute | solution.py:33
  168.6 10.9 %collective-permute-start.17 = (bf16[128,1280]{1,0:T(8,128)(2,1)S(1)}, bf16[128,1280]{1,0:T(8,128)(2,1)S(1)}, u32[]{:S(2)}, u32[]{:S(2)}) collective-permute-start(bf16[128,1280]{1,0:T(8,128)(2,1)S(1)} %get-tuple-element.61), channel_id=1, source_target_pairs={{0,64},{32,96},{64,0},{96,32},{1,65},{33,97},{65,1},{97,33},{2,66}... | collective-permute-start | bytes 983048 | tf_op jit(solution)/shard_map/ppermute | solution.py:33
  168.9 17.6 %collective-permute-start.16 = (bf16[128,1280]{1,0:T(8,128)(2,1)S(1)}, bf16[128,1280]{1,0:T(8,128)(2,1)S(1)}, u32[]{:S(2)}, u32[]{:S(2)}) collective-permute-start(bf16[128,1280]{1,0:T(8,128)(2,1)S(1)} %get-tuple-element.60), channel_id=1, source_target_pairs={{0,96},{32,0},{64,32},{96,64},{1,97},{33,1},{65,33},{97,65},{2,98}... | collective-permute-start | bytes 983048 | tf_op jit(solution)/shard_map/ppermute | solution.py:33
  171.4 15.7 %collective-permute-start.18 = (bf16[128,1280]{1,0:T(8,128)(2,1)S(1)}, bf16[128,1280]{1,0:T(8,128)(2,1)S(1)}, u32[]{:S(2)}, u32[]{:S(2)}) collective-permute-start(bf16[128,1280]{1,0:T(8,128)(2,1)S(1)} %get-tuple-element.62), channel_id=1, source_target_pairs={{0,32},{32,64},{64,96},{96,0},{1,33},{33,65},{65,97},{97,1},{2,34}... | collective-permute-start | bytes 983048 | tf_op jit(solution)/shard_map/ppermute | solution.py:33
  (20 other events, 226.2 us)
Sparse Core Ops, SparseCore 0:
  9.1 42.0 all-gather.4
  60.6 97.6 all-gather.6

commit v9 on v7

--- a/solution.py
+++ b/solution.py
@@ -188,31 +188,35 @@
         o[...] = term[d * rows : (d + 1) * rows, :].astype(BF16)
 
 
-def project(blocks, weight):
+def project(blocks, weight, first, count):
     rows, depth = blocks[0].shape
-    xs, cores, zs, part, cols = weight.shape
+    _, cores, zs, part, cols = weight.shape
     return pl.pallas_call(
         functools.partial(project_kernel, len(blocks)),
-        grid=(xs,),
+        grid=(count,),
         in_specs=[pl.BlockSpec((rows, depth), lambda j: (0, 0))] * len(blocks)
-        + [pl.BlockSpec((1, cores, zs, part, cols), lambda j: (j, 0, 0, 0, 0))],
+        + [pl.BlockSpec((1, cores, zs, part, cols), lambda j: (first + j, 0, 0, 0, 0))],
         out_specs=[pl.BlockSpec((rows, cols), lambda j: (0, j))] * len(blocks),
-        out_shape=[jax.ShapeDtypeStruct((rows, xs * cols), BF16)] * len(blocks),
+        out_shape=[jax.ShapeDtypeStruct((rows, count * cols), BF16)] * len(blocks),
         scratch_shapes=[pltpu.VMEM((len(blocks) * rows, depth), BF16)],
         compiler_params=params(32),
         cost_estimate=pl.CostEstimate(
-            flops=2 * len(blocks) * rows * depth * xs * cols, bytes_accessed=2 * depth * xs * cols, transcendentals=0
+            flops=2 * len(blocks) * rows * depth * count * cols,
+            bytes_accessed=2 * depth * count * cols,
+            transcendentals=0,
         ),
         name="project",
     )(*blocks, in_hbm(weight))
 
 
-def finish_kernel(y_ref, hidden, gate, same0, same1, other0, other1, out):
-    half = same0.shape[-1]
-    for side, (p, q) in ((y_ref[0], (same0, same1)), (1 - y_ref[0], (other0, other1))):
-        where = pl.ds(pl.multiple_of(side * half, HEAD), half)
-        branch = p[...].astype(F32) + q[...].astype(F32)
-        out[:, where] = (hidden[:, where].astype(F32) + gate[:, where] * branch).astype(BF16)
+def finish_kernel(y_ref, hidden, gate, mine, far0, pair0, across0, far1, pair1, across1, out):
+    half, split = mine.shape[-1], far0.shape[-1]
+    for first, last, far, pair, across in ((0, split, far0, pair0, across0), (split, half, far1, pair1, across1)):
+        same = mine[:, first:last].astype(F32) + far[...].astype(F32)
+        other = pair[...].astype(F32) + across[...].astype(F32)
+        for side, branch in ((y_ref[0], same), (1 - y_ref[0], other)):
+            where = pl.ds(pl.multiple_of(side * half + first, HEAD), last - first)
+            out[:, where] = (hidden[:, where].astype(F32) + gate[:, where] * branch).astype(BF16)
 
 
 def finish(y_lo, hidden, gate, pieces, blocks=4):
@@ -225,7 +229,7 @@
             num_scalar_prefetch=1,
             grid=(blocks,),
             in_specs=[row_spec, pl.BlockSpec((1, width), lambda i, *_: (0, 0))]
-            + [pl.BlockSpec((step, pieces[0].shape[1]), lambda i, *_: (i, 0))] * 4,
+            + [pl.BlockSpec((step, p.shape[1]), lambda i, *_: (i, 0)) for p in pieces],
             out_specs=row_spec,
         ),
         out_shape=jax.ShapeDtypeStruct(hidden.shape, BF16),
@@ -250,20 +254,25 @@
     combo = reach_time * 6 + reach_rows * 3 + reach_cols
     f0, f1, r0, r1 = own
     hb, ha = passed_along(f1, TM, 1), passed_along(f0, TM, -1)
-    rb, ra = passed_along(r1, SP, 1), passed_along(r0, SP, -1)
+    hb, ha, r0, r1, weight = lax.optimization_barrier((hb, ha, r0, r1, weight))
+    weight = lax.all_gather(weight, ("x", "core"), axis=0, tiled=False)
+    weight = weight.reshape((lax.axis_size("x"), lax.axis_size("core")) + weight.shape[1:])
     cb = passed_along(jnp.stack([hb[1], ha[1]]), SP, 1)
     ca = passed_along(jnp.stack([hb[0], ha[0]]), SP, -1)
-    hb_in, ha_in, rb, ra, weight = lax.optimization_barrier((hb, ha, rb, ra, weight))
-    weight = lax.all_gather(weight, ("x", "core"), axis=0, tiled=False)
-    weight = weight.reshape((lax.axis_size("x"), lax.axis_size("core")) + weight.shape[1:])
+    rb, ra = passed_along(r1, SP, 1), passed_along(r0, SP, -1)
     y_hi, y_lo = (lax.axis_index(a).astype(jnp.int32)[None] for a in ("y_hi", "y_lo"))
-    same, other = attend(combo, y_hi, qn, (f0, f1), (hb_in, ha_in, rb, ra, cb, ca), masks)
+    same, other = attend(combo, y_hi, qn, (f0, f1), (hb, ha, rb, ra, cb, ca), masks)
     pair = [along_y(same, lambda y: y ^ 1), along_y(other, lambda y: 3 - y), along_y(other, lambda y: y ^ 2)]
-    to_pair, to_across, to_far = project(pair, weight)
-    same, to_far = lax.optimization_barrier((same, to_far))
-    (mine,) = project([same], weight)
-    far = along_y(to_far, lambda y: y ^ 2)
-    pieces = [mine, far, along_y(to_pair, lambda y: y ^ 1), along_y(to_across, lambda y: 3 - y)]
+    (mine,) = project([same], weight, 0, 4)
+    pair[0], mine = lax.optimization_barrier((pair[0], mine))
+    parts = []
+    for first, count in ((0, 3), (3, 1)):
+        to_pair, to_across, to_far = project(pair, weight, first, count)
+        parts.append(
+            [along_y(to_far, lambda y: y ^ 2), along_y(to_pair, lambda y: y ^ 1), along_y(to_across, lambda y: 3 - y)]
+        )
+        pair[0], to_far = lax.optimization_barrier((pair[0], to_far))
+    pieces = [mine] + parts[0] + parts[1]
     out = finish(y_lo, hidden_in.reshape(-1, width), gate, pieces)
     return out.reshape(hidden_in.shape)
 

time: 195 us -> 189 us (0.969)
  starting transfers between devices: 33.5 us -> 28.3 us
  waiting for transfers between devices: 109 us -> 107 us
    ppermute x6 -> x9, waiting for transfers between devices: 49.5 us -> 24 us  [along_y(): lax.ppermute(block, ('y_lo', 'y_hi'), [(at(y), at(target(y))) for y in ra...]
    all_gather x1, waiting for transfers between devices: 16.3 us -> 28.3 us  [shards(): weight = lax.all_gather(weight, ('x', 'core'), axis=0, tiled=False)]
    ppermute x6, waiting for transfers between devices: 42.6 us -> 53.4 us  [passed_along(): return lax.ppermute(block, axes, route)]
    ppermute x6 -> x9, starting transfers between devices: 15.9 us -> 10.2 us  [along_y(): lax.ppermute(block, ('y_lo', 'y_hi'), [(at(y), at(target(y))) for y in ra...]
    pallas_call x2 -> x3, Pallas kernels: 15.8 us -> 17.5 us  [project(): pl.pallas_call(functools.partial(project_kernel, len(blocks)), grid=(coun...]
  transfers between devices with their start and end apart: 14 -> 17, of which waited for: 12 -> 9; matrix products, arithmetic and copies ran while one was open for 1% -> 1% of each run, Pallas kernels for 11% -> 13%
where the time goes in v9:
time: 189 us; the launch traced here: 187 us
  waiting for transfers between devices  107 us (57%)
  Pallas kernels  34.5 us (18%)
  starting transfers between devices  28.3 us (15%)
  between operations  13.8 us (7%)
  local copies, waits for them, and re-layouts  2.75 us (1%)
    ppermute x6, waiting for transfers between devices, passed_along(): return lax.ppermute(block, axes, route)  53.4 us
    all_gather x1, waiting for transfers between devices, shards(): weight = lax.all_gather(weight, ('x', 'core'), axis=0, tiled=False)  28.3 us
    ppermute x9, waiting for transfers between devices, along_y(): lax.ppermute(block, ('y_lo', 'y_hi'), [(at(y), at(target(y))) for y in ra...  24 us
    ppermute x6, starting transfers between devices, passed_along(): return lax.ppermute(block, axes, route)  18 us
    pallas_call x3, Pallas kernels, project(): pl.pallas_call(functools.partial(project_kernel, len(blocks)), grid=(coun...  17.5 us
    ppermute x9, starting transfers between devices, along_y(): lax.ppermute(block, ('y_lo', 'y_hi'), [(at(y), at(target(y))) for y in ra...  10.2 us
    pallas_call x1, Pallas kernels, attend(): pl.pallas_call(functools.partial(attend_kernel, heads, HEAD ** (-0.5)), g...  8.67 us
    pallas_call x1, Pallas kernels, prepare(): pl.pallas_call(prepare_kernel, grid=(groups,), in_specs=[token_spec] * 3...  6.23 us
  transfers between devices with their start and end apart: 17, of which 9 were waited for; matrix products, arithmetic and copies ran while one was open for 1% of the time, Pallas kernels for 13%

profile of v9, /device:TPU:1, one launch (start us, length us, event | category | flops | bytes accessed | tf_op | source)
XLA Modules:
  0.0 187.0 jit_solution(7033022027969366398)
XLA Ops:
  8.8 6.2 %prepare.1 = (bf16[4,32,5120]{2,1,0:T(8,128)(2,1)}, bf16[2,2,32,5120]{3,2,1,0:T(8,128)(2,1)}, bf16[2,2,32,5120]{3,2,1,0:T(8,128)(2,1)}, bf16[2,2,32,5120]{3,2,1,0:T(8,128)(2,1)}, bf16[2,2,32,5120]{3,2,1,0:T(8,128)(2,1)}) custom-call(bf16[4,32,5120]{2,1,0:T(8,128)(2,1)} %bitcast.20, bf16[4,32,5120]{2,1,0:T(8,128)(2,1)} %bitcast.21, ...), custom_call_target="tpu_custom_call" | custom-call | bytes 12582912 | tf_op jit(solution)/shard_map/prepare/pallas_call | solution.py:79
  15.0 4.0 %collective-permute-start = (bf16[2,2,32,5120]{3,2,1,0:T(8,128)(2,1)}, bf16[2,2,32,5120]{3,2,1,0:T(8,128)(2,1)S(1)}, u32[]{:S(2)}, u32[]{:S(2)}) collective-permute-start(bf16[2,2,32,5120]{3,2,1,0:T(8,128)(2,1)} %get-tuple-element.28.f1), channel_id=1, source_target_pairs={{0,32},{32,64},{64,96},{96,128},{128,160},{160,192},{192,224},{1,3... | collective-permute-start | bytes 3932168 | tf_op jit(solution)/shard_map/ppermute | solution.py:28
  19.0 1.3 collective-permute-start.1
  20.3 26.4 %collective-permute-done.hb = bf16[2,2,32,5120]{3,2,1,0:T(8,128)(2,1)S(1)} collective-permute-done((bf16[2,2,32,5120]{3,2,1,0:T(8,128)(2,1)}, bf16[2,2,32,5120]{3,2,1,0:T(8,128)(2,1)S(1)}, u32[]{:S(2)}, u32[]{:S(2)}) %collective-permute-start) | collective-permute-done | bytes 1310752 | tf_op jit(solution)/shard_map/ppermute | solution.py:28
  46.7 3.9 %collective-permute-done.1.ha = bf16[2,2,32,5120]{3,2,1,0:T(8,128)(2,1)S(1)} collective-permute-done((bf16[2,2,32,5120]{3,2,1,0:T(8,128)(2,1)}, bf16[2,2,32,5120]{3,2,1,0:T(8,128)(2,1)S(1)}, u32[]{:S(2)}, u32[]{:S(2)}) %collective-permute-start.1) | collective-permute-done | bytes 1310752 | tf_op jit(solution)/shard_map/ppermute | solution.py:28
  51.1 5.3 %collective-permute-start.5 = (bf16[2,2,32,5120]{3,2,1,0:T(8,128)(2,1)S(1)}, bf16[2,2,32,5120]{3,2,1,0:T(8,128)(2,1)S(1)}, u32[]{:S(2)}, u32[]{:S(2)}) collective-permute-start(bf16[2,2,32,5120]{3,2,1,0:T(8,128)(2,1)S(1)} %pad_maximum_fusion.1), channel_id=1, source_target_pairs={{1,0},{2,1},{3,2},{4,3},{5,4},{6,5},{7,6},{8,7},{9,8},{10,9},{11,1... | collective-permute-start | bytes 3932168 | tf_op jit(solution)/shard_map/ppermute | solution.py:28
  56.7 3.0 %collective-permute-start.4 = (bf16[2,2,32,5120]{3,2,1,0:T(8,128)(2,1)S(1)}, bf16[2,2,32,5120]{3,2,1,0:T(8,128)(2,1)S(1)}, u32[]{:S(2)}, u32[]{:S(2)}) collective-permute-start(bf16[2,2,32,5120]{3,2,1,0:T(8,128)(2,1)S(1)} %pad_maximum_fusion), channel_id=1, source_target_pairs={{0,1},{1,2},{2,3},{3,4},{4,5},{5,6},{6,7},{7,8},{8,9},{9,10},{10,1... | collective-permute-start | bytes 3932168 | tf_op jit(solution)/shard_map/ppermute | solution.py:28
  59.6 2.4 %collective-permute-start.2 = (bf16[2,2,32,5120]{3,2,1,0:T(8,128)(2,1)S(1)}, bf16[2,2,32,5120]{3,2,1,0:T(8,128)(2,1)S(1)}, u32[]{:S(2)}, u32[]{:S(2)}) collective-permute-start(bf16[2,2,32,5120]{3,2,1,0:T(8,128)(2,1)S(1)} %copy-done.12), channel_id=1, source_target_pairs={{0,1},{1,2},{2,3},{3,4},{4,5},{5,6},{6,7},{7,8},{8,9},{9,10},{10,1... | collective-permute-start | bytes 3932168 | tf_op jit(solution)/shard_map/ppermute | solution.py:28
  62.1 2.0 %collective-permute-start.3 = (bf16[2,2,32,5120]{3,2,1,0:T(8,128)(2,1)S(1)}, bf16[2,2,32,5120]{3,2,1,0:T(8,128)(2,1)S(1)}, u32[]{:S(2)}, u32[]{:S(2)}) collective-permute-start(bf16[2,2,32,5120]{3,2,1,0:T(8,128)(2,1)S(1)} %copy-done.11), channel_id=1, source_target_pairs={{1,0},{2,1},{3,2},{4,3},{5,4},{6,5},{7,6},{8,7},{9,8},{10,9},{11,1... | collective-permute-start | bytes 3932168 | tf_op jit(solution)/shard_map/ppermute | solution.py:28
  65.0 7.6 %collective-permute-done.5.ca = bf16[2,2,32,5120]{3,2,1,0:T(8,128)(2,1)S(1)} collective-permute-done((bf16[2,2,32,5120]{3,2,1,0:T(8,128)(2,1)S(1)}, bf16[2,2,32,5120]{3,2,1,0:T(8,128)(2,1)S(1)}, u32[]{:S(2)}, u32[]{:S(2)}) %collective-permute-start.5) | collective-permute-done | bytes 1310752 | tf_op jit(solution)/shard_map/ppermute | solution.py:28
  72.5 1.6 collective-permute-done.4.cb
  74.2 14.0 %collective-permute-done.2.rb = bf16[2,2,32,5120]{3,2,1,0:T(8,128)(2,1)S(1)} collective-permute-done((bf16[2,2,32,5120]{3,2,1,0:T(8,128)(2,1)S(1)}, bf16[2,2,32,5120]{3,2,1,0:T(8,128)(2,1)S(1)}, u32[]{:S(2)}, u32[]{:S(2)}) %collective-permute-start.2) | collective-permute-done | bytes 1310752 | tf_op jit(solution)/shard_map/ppermute | solution.py:28
  88.2 8.7 %attend.1 = (bf16[128,2560]{1,0:T(8,128)(2,1)}, bf16[128,2560]{1,0:T(8,128)(2,1)}) custom-call(s32[40]{0:T(128)S(1)} %add_add_fusion.combo_ref, s32[1]{0:T(128)} %bitcast.3.half_ref, bf16[4,32,5120]{2,1,0:T(8,128)(2,1)S(1)} %copy-done, bf16[2,2,32,5120]{3,2,1,0:T(8,128)(2,1)S(1)} %copy-done.1, bf16[2,2,32,5120]{3,2,1,0:T(8,128)(2,1)S(1)} %copy-done.2, ...), custom_call_target="tpu_custom_call" | custom-call | flops 1006632960 | bytes 33554432 | tf_op jit(solution)/shard_map/attend/pallas_call | solution.py:159
  98.0 1.9 %collective-permute-start.7 = (bf16[128,2560]{1,0:T(8,128)(2,1)}, bf16[128,2560]{1,0:T(8,128)(2,1)S(1)}, u32[]{:S(2)}, u32[]{:S(2)}) collective-permute-start(bf16[128,2560]{1,0:T(8,128)(2,1)} %get-tuple-element.39), channel_id=1, source_target_pairs={{0,144},{128,16},{16,128},{144,0},{1,145},{129,17},{17,129},{145,1... | collective-permute-start | bytes 1966088 | tf_op jit(solution)/shard_map/ppermute | solution.py:33
  100.4 28.3 %all-gather.7.cloned.1.call-done = bf16[64,160,640]{2,1,0:T(8,128)(2,1)} async-done(((bf16[8,160,640]{2,1,0:T(8,128)(2,1)}), bf16[64,160,640]{2,1,0:T(8,128)(2,1)}) %all-gather.7.cloned.1.call-update) | async-done | bytes 13107216 | tf_op jit(solution)/shard_map/all_gather | solution.py:258
  129.8 6.5 %project.3.mine = bf16[128,2560]{1,0:T(8,128)(2,1)S(1)} custom-call(bf16[128,2560]{1,0:T(8,128)(2,1)S(1)} %copy-done.4, bf16[4,2,8,160,640]{4,3,2,1,0:T(8,128)(2,1)} %bitcast.16), custom_call_target="tpu_custom_call" | custom-call | flops 1677721600 | bytes 13107200 | tf_op jit(solution)/shard_map/project/pallas_call | solution.py:194
  136.4 7.4 %project.4 = (bf16[128,1920]{1,0:T(8,128)(2,1)S(1)}, bf16[128,1920]{1,0:T(8,128)(2,1)S(1)}, bf16[128,1920]{1,0:T(8,128)(2,1)S(1)}) custom-call(bf16[128,2560]{1,0:T(8,128)(2,1)S(1)} %collective-permute-done.6.refs_0_, bf16[128,2560]{1,0:T(8,128)(2,1)S(1)} %collective-permute-done.7.refs_1_, bf16[128,2560]{1,0:T(8,128)(2,1)S(1)} %collective-permute-done.8.refs_2_, ...), custom_call_target="tpu_custom_call" | custom-call | flops 3774873600 | bytes 9830400 | tf_op jit(solution)/shard_map/project/pallas_call | solution.py:194
  143.8 1.3 collective-permute-start.10
  145.1 1.8 collective-permute-start.11
  147.6 3.6 %project.5 = (bf16[128,640]{1,0:T(8,128)(2,1)S(1)}, bf16[128,640]{1,0:T(8,128)(2,1)S(1)}, bf16[128,640]{1,0:T(8,128)(2,1)S(1)}) custom-call(bf16[128,2560]{1,0:T(8,128)(2,1)S(1)} %collective-permute-done.6.refs_0_, bf16[128,2560]{1,0:T(8,128)(2,1)S(1)} %collective-permute-done.7.refs_1_, bf16[128,2560]{1,0:T(8,128)(2,1)S(1)} %collective-permute-done.8.refs_2_, ...), custom_call_target="tpu_custom_call" | custom-call | flops 1258291200 | bytes 3276800 | tf_op jit(solution)/shard_map/project/pallas_call | solution.py:194
  151.2 2.4 %collective-permute-start.12 = (bf16[128,640]{1,0:T(8,128)(2,1)S(1)}, bf16[128,640]{1,0:T(8,128)(2,1)S(1)}, u32[]{:S(2)}, u32[]{:S(2)}) collective-permute-start(bf16[128,640]{1,0:T(8,128)(2,1)S(1)} %get-tuple-element.44), channel_id=1, source_target_pairs={{0,16},{128,144},{16,0},{144,128},{1,17},{129,145},{17,1},{145,129... | collective-permute-start | bytes 491528 | tf_op jit(solution)/shard_map/ppermute | solution.py:33
  153.9 18.8 %collective-permute-done.12.far1 = bf16[128,640]{1,0:T(8,128)(2,1)S(1)} collective-permute-done((bf16[128,640]{1,0:T(8,128)(2,1)S(1)}, bf16[128,640]{1,0:T(8,128)(2,1)S(1)}, u32[]{:S(2)}, u32[]{:S(2)}) %collective-permute-start.12) | collective-permute-done | bytes 163872 | tf_op jit(solution)/shard_map/ppermute | solution.py:33
  174.1 4.1 %collective-permute-done.14.across1 = bf16[128,640]{1,0:T(8,128)(2,1)S(1)} collective-permute-done((bf16[128,640]{1,0:T(8,128)(2,1)S(1)}, bf16[128,640]{1,0:T(8,128)(2,1)S(1)}, u32[]{:S(2)}, u32[]{:S(2)}) %collective-permute-start.14) | collective-permute-done | bytes 163872 | tf_op jit(solution)/shard_map/ppermute | solution.py:33
  178.2 2.0 %finish.1 = bf16[128,5120]{1,0:T(8,128)(2,1)} custom-call(s32[1]{0:T(128)} %bitcast.y_ref, bf16[128,5120]{1,0:T(8,128)(2,1)S(1)} %bitcast.12, f32[1,5120]{1,0:T(1,128)S(1)} %bitcast.13, bf16[128,2560]{1,0:T(8,128)(2,1)S(1)} %project.3.mine, bf16[128,1920]{1,0:T(8,128)(2,1)S(1)} %collective-permute-done.9.far0, ...), custom_call_target="tpu_custom_call" | custom-call | tf_op jit(solution)/shard_map/finish/pallas_call | solution.py:226
  (63 shorter events, 8.7 us)
Async XLA Ops:
  6.5 44.0 %all-gather.5.cloned.1.call-start = ((), (), s32[]{:S(2)}) async-start(), calls=%async_computation | async-start | bytes 1843200 | tf_op jit(solution)/shard_map/all_gather | solution.py:244
  7.3 121.5 %all-gather.7.cloned.1.call-start = ((), (), s32[]{:S(2)}) async-start(), calls=%async_computation.1 | async-start | bytes 14745600 | tf_op jit(solution)/shard_map/all_gather | solution.py:258
  8.8 42.0 %copy-start.8 = (s32[40]{0:T(128)S(1)}, s32[40]{0:T(128)}, u32[]{:S(2)}) copy-start(s32[40]{0:T(128)} %param.19) | copy-start | bytes 484
  8.8 42.0 %copy-start.9 = (s32[40]{0:T(128)S(1)}, s32[40]{0:T(128)}, u32[]{:S(2)}) copy-start(s32[40]{0:T(128)} %param.18) | copy-start | bytes 484
  8.8 42.0 %copy-start.10 = (s32[40]{0:T(128)S(1)}, s32[40]{0:T(128)}, u32[]{:S(2)}) copy-start(s32[40]{0:T(128)} %param.17) | copy-start | bytes 484
  15.0 31.7 %collective-permute-start = (bf16[2,2,32,5120]{3,2,1,0:T(8,128)(2,1)}, bf16[2,2,32,5120]{3,2,1,0:T(8,128)(2,1)S(1)}, u32[]{:S(2)}, u32[]{:S(2)}) collective-permute-start(bf16[2,2,32,5120]{3,2,1,0:T(8,128)(2,1)} %get-tuple-element.28.f1), channel_id=1, source_target_pairs={{0,32},{32,64},{64,96},{96,128},{128,160},{160,192},{192,224},{1,3... | collective-permute-start | bytes 3932168 | tf_op jit(solution)/shard_map/ppermute | solution.py:28
  19.0 31.5 %collective-permute-start.1 = (bf16[2,2,32,5120]{3,2,1,0:T(8,128)(2,1)}, bf16[2,2,32,5120]{3,2,1,0:T(8,128)(2,1)S(1)}, u32[]{:S(2)}, u32[]{:S(2)}) collective-permute-start(bf16[2,2,32,5120]{3,2,1,0:T(8,128)(2,1)} %get-tuple-element.27.f0), channel_id=1, source_target_pairs={{32,0},{64,32},{96,64},{128,96},{160,128},{192,160},{224,192},{33,... | collective-permute-start | bytes 3932168 | tf_op jit(solution)/shard_map/ppermute | solution.py:28
  51.1 21.4 %collective-permute-start.5 = (bf16[2,2,32,5120]{3,2,1,0:T(8,128)(2,1)S(1)}, bf16[2,2,32,5120]{3,2,1,0:T(8,128)(2,1)S(1)}, u32[]{:S(2)}, u32[]{:S(2)}) collective-permute-start(bf16[2,2,32,5120]{3,2,1,0:T(8,128)(2,1)S(1)} %pad_maximum_fusion.1), channel_id=1, source_target_pairs={{1,0},{2,1},{3,2},{4,3},{5,4},{6,5},{7,6},{8,7},{9,8},{10,9},{11,1... | collective-permute-start | bytes 3932168 | tf_op jit(solution)/shard_map/ppermute | solution.py:28
  56.5 31.7 %copy-start = (bf16[4,32,5120]{2,1,0:T(8,128)(2,1)S(1)}, bf16[4,32,5120]{2,1,0:T(8,128)(2,1)}, u32[]{:S(2)}) copy-start(bf16[4,32,5120]{2,1,0:T(8,128)(2,1)} %get-tuple-element.26.q_ref) | copy-start | bytes 3932164
  56.5 31.7 %copy-start.1 = (bf16[2,2,32,5120]{3,2,1,0:T(8,128)(2,1)S(1)}, bf16[2,2,32,5120]{3,2,1,0:T(8,128)(2,1)}, u32[]{:S(2)}) copy-start(bf16[2,2,32,5120]{3,2,1,0:T(8,128)(2,1)} %get-tuple-element.27.f0) | copy-start | bytes 3932164
  56.5 31.7 %copy-start.2 = (bf16[2,2,32,5120]{3,2,1,0:T(8,128)(2,1)S(1)}, bf16[2,2,32,5120]{3,2,1,0:T(8,128)(2,1)}, u32[]{:S(2)}) copy-start(bf16[2,2,32,5120]{3,2,1,0:T(8,128)(2,1)} %get-tuple-element.28.f1) | copy-start | bytes 3932164
  56.7 17.5 %collective-permute-start.4 = (bf16[2,2,32,5120]{3,2,1,0:T(8,128)(2,1)S(1)}, bf16[2,2,32,5120]{3,2,1,0:T(8,128)(2,1)S(1)}, u32[]{:S(2)}, u32[]{:S(2)}) collective-permute-start(bf16[2,2,32,5120]{3,2,1,0:T(8,128)(2,1)S(1)} %pad_maximum_fusion), channel_id=1, source_target_pairs={{0,1},{1,2},{2,3},{3,4},{4,5},{5,6},{6,7},{7,8},{8,9},{9,10},{10,1... | collective-permute-start | bytes 3932168 | tf_op jit(solution)/shard_map/ppermute | solution.py:28
  59.6 28.6 %collective-permute-start.2 = (bf16[2,2,32,5120]{3,2,1,0:T(8,128)(2,1)S(1)}, bf16[2,2,32,5120]{3,2,1,0:T(8,128)(2,1)S(1)}, u32[]{:S(2)}, u32[]{:S(2)}) collective-permute-start(bf16[2,2,32,5120]{3,2,1,0:T(8,128)(2,1)S(1)} %copy-done.12), channel_id=1, source_target_pairs={{0,1},{1,2},{2,3},{3,4},{4,5},{5,6},{6,7},{7,8},{8,9},{9,10},{10,1... | collective-permute-start | bytes 3932168 | tf_op jit(solution)/shard_map/ppermute | solution.py:28
  62.1 26.1 %collective-permute-start.3 = (bf16[2,2,32,5120]{3,2,1,0:T(8,128)(2,1)S(1)}, bf16[2,2,32,5120]{3,2,1,0:T(8,128)(2,1)S(1)}, u32[]{:S(2)}, u32[]{:S(2)}) collective-permute-start(bf16[2,2,32,5120]{3,2,1,0:T(8,128)(2,1)S(1)} %copy-done.11), channel_id=1, source_target_pairs={{1,0},{2,1},{3,2},{4,3},{5,4},{6,5},{7,6},{8,7},{9,8},{10,9},{11,1... | collective-permute-start | bytes 3932168 | tf_op jit(solution)/shard_map/ppermute | solution.py:28
  96.9 39.4 %collective-permute-start.6 = (bf16[128,2560]{1,0:T(8,128)(2,1)}, bf16[128,2560]{1,0:T(8,128)(2,1)S(1)}, u32[]{:S(2)}, u32[]{:S(2)}) collective-permute-start(bf16[128,2560]{1,0:T(8,128)(2,1)} %get-tuple-element.35.refs_0_), channel_id=1, source_target_pairs={{0,128},{128,0},{16,144},{144,16},{1,129},{129,1},{17,145},{145,17... | collective-permute-start | bytes 1966088 | tf_op jit(solution)/shard_map/ppermute | solution.py:33
  98.0 38.4 %collective-permute-start.7 = (bf16[128,2560]{1,0:T(8,128)(2,1)}, bf16[128,2560]{1,0:T(8,128)(2,1)S(1)}, u32[]{:S(2)}, u32[]{:S(2)}) collective-permute-start(bf16[128,2560]{1,0:T(8,128)(2,1)} %get-tuple-element.39), channel_id=1, source_target_pairs={{0,144},{128,16},{16,128},{144,0},{1,145},{129,17},{17,129},{145,1... | collective-permute-start | bytes 1966088 | tf_op jit(solution)/shard_map/ppermute | solution.py:33
  99.9 36.5 %collective-permute-start.8 = (bf16[128,2560]{1,0:T(8,128)(2,1)}, bf16[128,2560]{1,0:T(8,128)(2,1)S(1)}, u32[]{:S(2)}, u32[]{:S(2)}) collective-permute-start(bf16[128,2560]{1,0:T(8,128)(2,1)} %get-tuple-element.39), channel_id=1, source_target_pairs={{0,16},{128,144},{16,0},{144,128},{1,17},{129,145},{17,1},{145,129... | collective-permute-start | bytes 1966088 | tf_op jit(solution)/shard_map/ppermute | solution.py:33
  143.8 34.3 %collective-permute-start.10 = (bf16[128,1920]{1,0:T(8,128)(2,1)S(1)}, bf16[128,1920]{1,0:T(8,128)(2,1)S(1)}, u32[]{:S(2)}, u32[]{:S(2)}) collective-permute-start(bf16[128,1920]{1,0:T(8,128)(2,1)S(1)} %get-tuple-element.41), channel_id=1, source_target_pairs={{0,128},{128,0},{16,144},{144,16},{1,129},{129,1},{17,145},{145,17... | collective-permute-start | bytes 1474568 | tf_op jit(solution)/shard_map/ppermute | solution.py:33
  145.1 33.0 %collective-permute-start.11 = (bf16[128,1920]{1,0:T(8,128)(2,1)S(1)}, bf16[128,1920]{1,0:T(8,128)(2,1)S(1)}, u32[]{:S(2)}, u32[]{:S(2)}) collective-permute-start(bf16[128,1920]{1,0:T(8,128)(2,1)S(1)} %get-tuple-element.42), channel_id=1, source_target_pairs={{0,144},{128,16},{16,128},{144,0},{1,145},{129,17},{17,129},{145,1... | collective-permute-start | bytes 1474568 | tf_op jit(solution)/shard_map/ppermute | solution.py:33
  146.9 31.2 %copy-start.5 = (f32[5120]{0:T(1024)S(1)}, f32[5120]{0:T(1024)}, u32[]{:S(2)}) copy-start(f32[5120]{0:T(1024)} %param.21) | copy-start | bytes 61444
  146.9 31.2 %collective-permute-start.9 = (bf16[128,1920]{1,0:T(8,128)(2,1)S(1)}, bf16[128,1920]{1,0:T(8,128)(2,1)S(1)}, u32[]{:S(2)}, u32[]{:S(2)}) collective-permute-start(bf16[128,1920]{1,0:T(8,128)(2,1)S(1)} %get-tuple-element.40), channel_id=1, source_target_pairs={{0,16},{128,144},{16,0},{144,128},{1,17},{129,145},{17,1},{145,129... | collective-permute-start | bytes 1474568 | tf_op jit(solution)/shard_map/ppermute | solution.py:33
  151.2 21.6 %collective-permute-start.12 = (bf16[128,640]{1,0:T(8,128)(2,1)S(1)}, bf16[128,640]{1,0:T(8,128)(2,1)S(1)}, u32[]{:S(2)}, u32[]{:S(2)}) collective-permute-start(bf16[128,640]{1,0:T(8,128)(2,1)S(1)} %get-tuple-element.44), channel_id=1, source_target_pairs={{0,16},{128,144},{16,0},{144,128},{1,17},{129,145},{17,1},{145,129... | collective-permute-start | bytes 491528 | tf_op jit(solution)/shard_map/ppermute | solution.py:33
  153.6 20.5 %collective-permute-start.13 = (bf16[128,640]{1,0:T(8,128)(2,1)S(1)}, bf16[128,640]{1,0:T(8,128)(2,1)S(1)}, u32[]{:S(2)}, u32[]{:S(2)}) collective-permute-start(bf16[128,640]{1,0:T(8,128)(2,1)S(1)} %get-tuple-element.45), channel_id=1, source_target_pairs={{0,128},{128,0},{16,144},{144,16},{1,129},{129,1},{17,145},{145,17... | collective-permute-start | bytes 491528 | tf_op jit(solution)/shard_map/ppermute | solution.py:33
  172.7 5.4 %collective-permute-start.14 = (bf16[128,640]{1,0:T(8,128)(2,1)S(1)}, bf16[128,640]{1,0:T(8,128)(2,1)S(1)}, u32[]{:S(2)}, u32[]{:S(2)}) collective-permute-start(bf16[128,640]{1,0:T(8,128)(2,1)S(1)} %get-tuple-element.46), channel_id=1, source_target_pairs={{0,144},{128,16},{16,128},{144,0},{1,145},{129,17},{17,129},{145,1... | collective-permute-start | bytes 491528 | tf_op jit(solution)/shard_map/ppermute | solution.py:33
  (6 other events, 53.4 us)
Sparse Core Ops, SparseCore 0:
  9.1 39.8 all-gather.4
  50.9 77.8 all-gather.6

commit v10 on v9

--- a/solution.py
+++ b/solution.py
@@ -85,7 +85,7 @@
         compiler_params=params(),
         cost_estimate=pl.CostEstimate(flops=0, bytes_accessed=12 << 20, transcendentals=0),
         name="prepare",
-    )(*[in_hbm(a) for a in (queries, keys, values)], query_gain[None], key_gain[None])
+    )(*[in_hbm(a) for a in (queries, keys, values, query_gain[None], key_gain[None])])
 
 
 def mask_tables(first_frame, first_row, frame_count, row_count, nw):
@@ -263,15 +263,17 @@
     y_hi, y_lo = (lax.axis_index(a).astype(jnp.int32)[None] for a in ("y_hi", "y_lo"))
     same, other = attend(combo, y_hi, qn, (f0, f1), (hb, ha, rb, ra, cb, ca), masks)
     pair = [along_y(same, lambda y: y ^ 1), along_y(other, lambda y: 3 - y), along_y(other, lambda y: y ^ 2)]
+    to_pair, to_across, to_far = project(pair, weight, 0, 3)
+    large = [along_y(to_far, lambda y: y ^ 2), along_y(to_pair, lambda y: y ^ 1), along_y(to_across, lambda y: 3 - y)]
+    pair[0], to_far = lax.optimization_barrier((pair[0], to_far))
+    to_pair, to_across, to_far = project(pair, weight, 3, 1)
+    same, to_far = lax.optimization_barrier((same, to_far))
     (mine,) = project([same], weight, 0, 4)
-    pair[0], mine = lax.optimization_barrier((pair[0], mine))
-    parts = []
-    for first, count in ((0, 3), (3, 1)):
-        to_pair, to_across, to_far = project(pair, weight, first, count)
-        parts.append(
-            [along_y(to_far, lambda y: y ^ 2), along_y(to_pair, lambda y: y ^ 1), along_y(to_across, lambda y: 3 - y)]
-        )
-        pair[0], to_far = lax.optimization_barrier((pair[0], to_far))
+    to_across, large[1], mine = lax.optimization_barrier((to_across, large[1], mine))
+    parts = [
+        large,
+        [along_y(to_far, lambda y: y ^ 2), along_y(to_pair, lambda y: y ^ 1), along_y(to_across, lambda y: 3 - y)],
+    ]
     pieces = [mine] + parts[0] + parts[1]
     out = finish(y_lo, hidden_in.reshape(-1, width), gate, pieces)
     return out.reshape(hidden_in.shape)

time: 189 us -> 181 us (0.958)
  the two profiles are of different devices: /device:TPU:1 before, /device:TPU:102 now
where the time goes in v10:
time: 181 us
  waiting for transfers between devices  101 us (56%)
  Pallas kernels  34.4 us (19%)
  starting transfers between devices  30.3 us (17%)
  between operations  13.7 us (8%)
    ppermute x6, waiting for transfers between devices, passed_along(): return lax.ppermute(block, axes, route)  55 us
    ppermute x9, waiting for transfers between devices, along_y(): lax.ppermute(block, ('y_lo', 'y_hi'), [(at(y), at(target(y))) for y in ra...  45.4 us
    pallas_call x3, Pallas kernels, project(): pl.pallas_call(functools.partial(project_kernel, len(blocks)), grid=(coun...  17.5 us
    ppermute x6, starting transfers between devices, passed_along(): return lax.ppermute(block, axes, route)  17.1 us
    ppermute x9, starting transfers between devices, along_y(): lax.ppermute(block, ('y_lo', 'y_hi'), [(at(y), at(target(y))) for y in ra...  13.1 us
    pallas_call x1, Pallas kernels, attend(): pl.pallas_call(functools.partial(attend_kernel, heads, HEAD ** (-0.5)), g...  8.63 us
    pallas_call x1, Pallas kernels, prepare(): pl.pallas_call(prepare_kernel, grid=(groups,), in_specs=[token_spec] * 3...  6.23 us
  transfers between devices with their start and end apart: 17, of which 10 were waited for; matrix products, arithmetic and copies ran while one was open for 1% of the time, Pallas kernels for 14%

profile of v10, /device:TPU:102, one launch (start us, length us, event | category | flops | bytes accessed | tf_op | source)
XLA Modules:
  0.0 181.1 jit_solution(1355183455799341200)
XLA Ops:
  7.3 6.2 %prepare.1 = (bf16[4,32,5120]{2,1,0:T(8,128)(2,1)}, bf16[2,2,32,5120]{3,2,1,0:T(8,128)(2,1)}, bf16[2,2,32,5120]{3,2,1,0:T(8,128)(2,1)}, bf16[2,2,32,5120]{3,2,1,0:T(8,128)(2,1)}, bf16[2,2,32,5120]{3,2,1,0:T(8,128)(2,1)}) custom-call(bf16[4,32,5120]{2,1,0:T(8,128)(2,1)} %bitcast.18, bf16[4,32,5120]{2,1,0:T(8,128)(2,1)} %bitcast.19, ...), custom_call_target="tpu_custom_call" | custom-call | bytes 12582912 | tf_op jit(solution)/shard_map/prepare/pallas_call | solution.py:79
  13.6 3.4 %collective-permute-start = (bf16[2,2,32,5120]{3,2,1,0:T(8,128)(2,1)}, bf16[2,2,32,5120]{3,2,1,0:T(8,128)(2,1)S(1)}, u32[]{:S(2)}, u32[]{:S(2)}) collective-permute-start(bf16[2,2,32,5120]{3,2,1,0:T(8,128)(2,1)} %get-tuple-element.31.f1), channel_id=1, source_target_pairs={{0,32},{32,64},{64,96},{96,128},{128,160},{160,192},{192,224},{1,3... | collective-permute-start | bytes 3932168 | tf_op jit(solution)/shard_map/ppermute | solution.py:28
  17.0 2.4 %collective-permute-start.1 = (bf16[2,2,32,5120]{3,2,1,0:T(8,128)(2,1)}, bf16[2,2,32,5120]{3,2,1,0:T(8,128)(2,1)S(1)}, u32[]{:S(2)}, u32[]{:S(2)}) collective-permute-start(bf16[2,2,32,5120]{3,2,1,0:T(8,128)(2,1)} %get-tuple-element.30.f0), channel_id=1, source_target_pairs={{32,0},{64,32},{96,64},{128,96},{160,128},{192,160},{224,192},{33,... | collective-permute-start | bytes 3932168 | tf_op jit(solution)/shard_map/ppermute | solution.py:28
  19.4 26.8 %collective-permute-done.hb = bf16[2,2,32,5120]{3,2,1,0:T(8,128)(2,1)S(1)} collective-permute-done((bf16[2,2,32,5120]{3,2,1,0:T(8,128)(2,1)}, bf16[2,2,32,5120]{3,2,1,0:T(8,128)(2,1)S(1)}, u32[]{:S(2)}, u32[]{:S(2)}) %collective-permute-start) | collective-permute-done | bytes 1310752 | tf_op jit(solution)/shard_map/ppermute | solution.py:28
  46.2 5.2 %collective-permute-done.1.ha = bf16[2,2,32,5120]{3,2,1,0:T(8,128)(2,1)S(1)} collective-permute-done((bf16[2,2,32,5120]{3,2,1,0:T(8,128)(2,1)}, bf16[2,2,32,5120]{3,2,1,0:T(8,128)(2,1)S(1)}, u32[]{:S(2)}, u32[]{:S(2)}) %collective-permute-start.1) | collective-permute-done | bytes 1310752 | tf_op jit(solution)/shard_map/ppermute | solution.py:28
  52.0 2.1 %collective-permute-start.5 = (bf16[2,2,32,5120]{3,2,1,0:T(8,128)(2,1)S(1)}, bf16[2,2,32,5120]{3,2,1,0:T(8,128)(2,1)S(1)}, u32[]{:S(2)}, u32[]{:S(2)}) collective-permute-start(bf16[2,2,32,5120]{3,2,1,0:T(8,128)(2,1)S(1)} %pad_maximum_fusion.1), channel_id=1, source_target_pairs={{1,0},{2,1},{3,2},{4,3},{5,4},{6,5},{7,6},{8,7},{9,8},{10,9},{11,1... | collective-permute-start | bytes 3932168 | tf_op jit(solution)/shard_map/ppermute | solution.py:28
  54.2 2.7 %collective-permute-start.4 = (bf16[2,2,32,5120]{3,2,1,0:T(8,128)(2,1)S(1)}, bf16[2,2,32,5120]{3,2,1,0:T(8,128)(2,1)S(1)}, u32[]{:S(2)}, u32[]{:S(2)}) collective-permute-start(bf16[2,2,32,5120]{3,2,1,0:T(8,128)(2,1)S(1)} %pad_maximum_fusion), channel_id=1, source_target_pairs={{0,1},{1,2},{2,3},{3,4},{4,5},{5,6},{6,7},{7,8},{8,9},{9,10},{10,1... | collective-permute-start | bytes 3932168 | tf_op jit(solution)/shard_map/ppermute | solution.py:28
  56.9 4.7 %collective-permute-start.2 = (bf16[2,2,32,5120]{3,2,1,0:T(8,128)(2,1)S(1)}, bf16[2,2,32,5120]{3,2,1,0:T(8,128)(2,1)S(1)}, u32[]{:S(2)}, u32[]{:S(2)}) collective-permute-start(bf16[2,2,32,5120]{3,2,1,0:T(8,128)(2,1)S(1)} %copy-done.10), channel_id=1, source_target_pairs={{0,1},{1,2},{2,3},{3,4},{4,5},{5,6},{6,7},{7,8},{8,9},{9,10},{10,1... | collective-permute-start | bytes 3932168 | tf_op jit(solution)/shard_map/ppermute | solution.py:28
  61.6 1.9 %collective-permute-start.3 = (bf16[2,2,32,5120]{3,2,1,0:T(8,128)(2,1)S(1)}, bf16[2,2,32,5120]{3,2,1,0:T(8,128)(2,1)S(1)}, u32[]{:S(2)}, u32[]{:S(2)}) collective-permute-start(bf16[2,2,32,5120]{3,2,1,0:T(8,128)(2,1)S(1)} %copy-done.9), channel_id=1, source_target_pairs={{1,0},{2,1},{3,2},{4,3},{5,4},{6,5},{7,6},{8,7},{9,8},{10,9},{11,1... | collective-permute-start | bytes 3932168 | tf_op jit(solution)/shard_map/ppermute | solution.py:28
  64.4 4.7 %collective-permute-done.5.ca = bf16[2,2,32,5120]{3,2,1,0:T(8,128)(2,1)S(1)} collective-permute-done((bf16[2,2,32,5120]{3,2,1,0:T(8,128)(2,1)S(1)}, bf16[2,2,32,5120]{3,2,1,0:T(8,128)(2,1)S(1)}, u32[]{:S(2)}, u32[]{:S(2)}) %collective-permute-start.5) | collective-permute-done | bytes 1310752 | tf_op jit(solution)/shard_map/ppermute | solution.py:28
  69.2 4.2 %collective-permute-done.4.cb = bf16[2,2,32,5120]{3,2,1,0:T(8,128)(2,1)S(1)} collective-permute-done((bf16[2,2,32,5120]{3,2,1,0:T(8,128)(2,1)S(1)}, bf16[2,2,32,5120]{3,2,1,0:T(8,128)(2,1)S(1)}, u32[]{:S(2)}, u32[]{:S(2)}) %collective-permute-start.4) | collective-permute-done | bytes 1310752 | tf_op jit(solution)/shard_map/ppermute | solution.py:28
  73.4 14.0 %collective-permute-done.2.rb = bf16[2,2,32,5120]{3,2,1,0:T(8,128)(2,1)S(1)} collective-permute-done((bf16[2,2,32,5120]{3,2,1,0:T(8,128)(2,1)S(1)}, bf16[2,2,32,5120]{3,2,1,0:T(8,128)(2,1)S(1)}, u32[]{:S(2)}, u32[]{:S(2)}) %collective-permute-start.2) | collective-permute-done | bytes 1310752 | tf_op jit(solution)/shard_map/ppermute | solution.py:28
  87.5 8.6 %attend.1 = (bf16[128,2560]{1,0:T(8,128)(2,1)}, bf16[128,2560]{1,0:T(8,128)(2,1)}) custom-call(s32[40]{0:T(128)S(1)} %add_add_fusion.combo_ref, s32[1]{0:T(128)} %bitcast.3.half_ref, bf16[4,32,5120]{2,1,0:T(8,128)(2,1)S(1)} %copy-done, bf16[2,2,32,5120]{3,2,1,0:T(8,128)(2,1)S(1)} %copy-done.1, bf16[2,2,32,5120]{3,2,1,0:T(8,128)(2,1)S(1)} %copy-done.2, ...), custom_call_target="tpu_custom_call" | custom-call | flops 1006632960 | bytes 33554432 | tf_op jit(solution)/shard_map/attend/pallas_call | solution.py:159
  96.8 2.8 %collective-permute-start.7 = (bf16[128,2560]{1,0:T(8,128)(2,1)}, bf16[128,2560]{1,0:T(8,128)(2,1)S(1)}, u32[]{:S(2)}, u32[]{:S(2)}) collective-permute-start(bf16[128,2560]{1,0:T(8,128)(2,1)} %get-tuple-element.39), channel_id=1, source_target_pairs={{0,144},{128,16},{16,128},{144,0},{1,145},{129,17},{17,129},{145,1... | collective-permute-start | bytes 1966088 | tf_op jit(solution)/shard_map/ppermute | solution.py:33
  100.2 13.7 %collective-permute-done.6.refs_0_ = bf16[128,2560]{1,0:T(8,128)(2,1)S(1)} collective-permute-done((bf16[128,2560]{1,0:T(8,128)(2,1)}, bf16[128,2560]{1,0:T(8,128)(2,1)S(1)}, u32[]{:S(2)}, u32[]{:S(2)}) %collective-permute-start.6) | collective-permute-done | bytes 655392 | tf_op jit(solution)/shard_map/ppermute | solution.py:33
  113.9 15.3 %collective-permute-done.7.refs_1_ = bf16[128,2560]{1,0:T(8,128)(2,1)S(1)} collective-permute-done((bf16[128,2560]{1,0:T(8,128)(2,1)}, bf16[128,2560]{1,0:T(8,128)(2,1)S(1)}, u32[]{:S(2)}, u32[]{:S(2)}) %collective-permute-start.7) | collective-permute-done | bytes 655392 | tf_op jit(solution)/shard_map/ppermute | solution.py:33
  129.2 7.4 %project.3 = (bf16[128,1920]{1,0:T(8,128)(2,1)S(1)}, bf16[128,1920]{1,0:T(8,128)(2,1)S(1)}, bf16[128,1920]{1,0:T(8,128)(2,1)S(1)}) custom-call(bf16[128,2560]{1,0:T(8,128)(2,1)S(1)} %collective-permute-done.6.refs_0_, bf16[128,2560]{1,0:T(8,128)(2,1)S(1)} %collective-permute-done.7.refs_1_, bf16[128,2560]{1,0:T(8,128)(2,1)S(1)} %collective-permute-done.8.refs_2_, ...), custom_call_target="tpu_custom_call" | custom-call | flops 3774873600 | bytes 9830400 | tf_op jit(solution)/shard_map/project/pallas_call | solution.py:194
  137.6 3.6 %collective-permute-start.10 = (bf16[128,1920]{1,0:T(8,128)(2,1)S(1)}, bf16[128,1920]{1,0:T(8,128)(2,1)S(1)}, u32[]{:S(2)}, u32[]{:S(2)}) collective-permute-start(bf16[128,1920]{1,0:T(8,128)(2,1)S(1)} %get-tuple-element.41), channel_id=1, source_target_pairs={{0,16},{128,144},{16,0},{144,128},{1,17},{129,145},{17,1},{145,129... | collective-permute-start | bytes 1474568 | tf_op jit(solution)/shard_map/ppermute | solution.py:33
  141.5 3.6 %project.4 = (bf16[128,640]{1,0:T(8,128)(2,1)S(1)}, bf16[128,640]{1,0:T(8,128)(2,1)S(1)}, bf16[128,640]{1,0:T(8,128)(2,1)S(1)}) custom-call(bf16[128,2560]{1,0:T(8,128)(2,1)S(1)} %collective-permute-done.6.refs_0_, bf16[128,2560]{1,0:T(8,128)(2,1)S(1)} %collective-permute-done.7.refs_1_, bf16[128,2560]{1,0:T(8,128)(2,1)S(1)} %collective-permute-done.8.refs_2_, ...), custom_call_target="tpu_custom_call" | custom-call | flops 1258291200 | bytes 3276800 | tf_op jit(solution)/shard_map/project/pallas_call | solution.py:194
  146.4 2.5 %collective-permute-start.13 = (bf16[128,640]{1,0:T(8,128)(2,1)S(1)}, bf16[128,640]{1,0:T(8,128)(2,1)S(1)}, u32[]{:S(2)}, u32[]{:S(2)}) collective-permute-start(bf16[128,640]{1,0:T(8,128)(2,1)S(1)} %get-tuple-element.51), channel_id=1, source_target_pairs={{0,128},{128,0},{16,144},{144,16},{1,129},{129,1},{17,145},{145,17... | collective-permute-start | bytes 491528 | tf_op jit(solution)/shard_map/ppermute | solution.py:33
  149.0 6.5 %project.5.mine = bf16[128,2560]{1,0:T(8,128)(2,1)S(1)} custom-call(bf16[128,2560]{1,0:T(8,128)(2,1)S(1)} %copy-done.4, bf16[4,2,8,160,640]{4,3,2,1,0:T(8,128)(2,1)} %bitcast.16), custom_call_target="tpu_custom_call" | custom-call | flops 1677721600 | bytes 13107200 | tf_op jit(solution)/shard_map/project/pallas_call | solution.py:194
  155.8 11.5 %collective-permute-done.12.far1 = bf16[128,640]{1,0:T(8,128)(2,1)S(1)} collective-permute-done((bf16[128,640]{1,0:T(8,128)(2,1)S(1)}, bf16[128,640]{1,0:T(8,128)(2,1)S(1)}, u32[]{:S(2)}, u32[]{:S(2)}) %collective-permute-start.12) | collective-permute-done | bytes 163872 | tf_op jit(solution)/shard_map/ppermute | solution.py:33
  167.4 3.1 %collective-permute-done.11.across0 = bf16[128,1920]{1,0:T(8,128)(2,1)S(1)} collective-permute-done((bf16[128,1920]{1,0:T(8,128)(2,1)S(1)}, bf16[128,1920]{1,0:T(8,128)(2,1)S(1)}, u32[]{:S(2)}, u32[]{:S(2)}) %collective-permute-start.11) | collective-permute-done | bytes 491552 | tf_op jit(solution)/shard_map/ppermute | solution.py:33
  172.2 2.0 %finish.1 = bf16[128,5120]{1,0:T(8,128)(2,1)} custom-call(s32[1]{0:T(128)} %bitcast.y_ref, bf16[128,5120]{1,0:T(8,128)(2,1)S(1)} %bitcast.12, f32[1,5120]{1,0:T(1,128)S(1)} %bitcast.13, bf16[128,2560]{1,0:T(8,128)(2,1)S(1)} %project.5.mine, bf16[128,1920]{1,0:T(8,128)(2,1)S(1)} %collective-permute-done.10.far0, ...), custom_call_target="tpu_custom_call" | custom-call | tf_op jit(solution)/shard_map/finish/pallas_call | solution.py:226
  (59 shorter events, 8.3 us)
Async XLA Ops:
  6.5 44.9 %all-gather.5.cloned.1.call-start = ((), (), s32[]{:S(2)}) async-start(), calls=%async_computation | async-start | bytes 1843200 | tf_op jit(solution)/shard_map/all_gather | solution.py:244
  7.3 122.0 %all-gather.7.cloned.1.call-start = ((), (), s32[]{:S(2)}) async-start(), calls=%async_computation.1 | async-start | bytes 14745600 | tf_op jit(solution)/shard_map/all_gather | solution.py:258
  7.3 44.3 %copy-start.6 = (s32[40]{0:T(128)S(1)}, s32[40]{0:T(128)}, u32[]{:S(2)}) copy-start(s32[40]{0:T(128)} %param.19) | copy-start | bytes 484
  7.3 44.3 %copy-start.7 = (s32[40]{0:T(128)S(1)}, s32[40]{0:T(128)}, u32[]{:S(2)}) copy-start(s32[40]{0:T(128)} %param.18) | copy-start | bytes 484
  7.3 44.3 %copy-start.8 = (s32[40]{0:T(128)S(1)}, s32[40]{0:T(128)}, u32[]{:S(2)}) copy-start(s32[40]{0:T(128)} %param.17) | copy-start | bytes 484
  13.6 32.6 %collective-permute-start = (bf16[2,2,32,5120]{3,2,1,0:T(8,128)(2,1)}, bf16[2,2,32,5120]{3,2,1,0:T(8,128)(2,1)S(1)}, u32[]{:S(2)}, u32[]{:S(2)}) collective-permute-start(bf16[2,2,32,5120]{3,2,1,0:T(8,128)(2,1)} %get-tuple-element.31.f1), channel_id=1, source_target_pairs={{0,32},{32,64},{64,96},{96,128},{128,160},{160,192},{192,224},{1,3... | collective-permute-start | bytes 3932168 | tf_op jit(solution)/shard_map/ppermute | solution.py:28
  17.0 34.5 %collective-permute-start.1 = (bf16[2,2,32,5120]{3,2,1,0:T(8,128)(2,1)}, bf16[2,2,32,5120]{3,2,1,0:T(8,128)(2,1)S(1)}, u32[]{:S(2)}, u32[]{:S(2)}) collective-permute-start(bf16[2,2,32,5120]{3,2,1,0:T(8,128)(2,1)} %get-tuple-element.30.f0), channel_id=1, source_target_pairs={{32,0},{64,32},{96,64},{128,96},{160,128},{192,160},{224,192},{33,... | collective-permute-start | bytes 3932168 | tf_op jit(solution)/shard_map/ppermute | solution.py:28
  52.0 17.2 %collective-permute-start.5 = (bf16[2,2,32,5120]{3,2,1,0:T(8,128)(2,1)S(1)}, bf16[2,2,32,5120]{3,2,1,0:T(8,128)(2,1)S(1)}, u32[]{:S(2)}, u32[]{:S(2)}) collective-permute-start(bf16[2,2,32,5120]{3,2,1,0:T(8,128)(2,1)S(1)} %pad_maximum_fusion.1), channel_id=1, source_target_pairs={{1,0},{2,1},{3,2},{4,3},{5,4},{6,5},{7,6},{8,7},{9,8},{10,9},{11,1... | collective-permute-start | bytes 3932168 | tf_op jit(solution)/shard_map/ppermute | solution.py:28
  54.1 33.4 %copy-start = (bf16[4,32,5120]{2,1,0:T(8,128)(2,1)S(1)}, bf16[4,32,5120]{2,1,0:T(8,128)(2,1)}, u32[]{:S(2)}) copy-start(bf16[4,32,5120]{2,1,0:T(8,128)(2,1)} %get-tuple-element.29.q_ref) | copy-start | bytes 3932164
  54.1 33.4 %copy-start.1 = (bf16[2,2,32,5120]{3,2,1,0:T(8,128)(2,1)S(1)}, bf16[2,2,32,5120]{3,2,1,0:T(8,128)(2,1)}, u32[]{:S(2)}) copy-start(bf16[2,2,32,5120]{3,2,1,0:T(8,128)(2,1)} %get-tuple-element.30.f0) | copy-start | bytes 3932164
  54.1 33.4 %copy-start.2 = (bf16[2,2,32,5120]{3,2,1,0:T(8,128)(2,1)S(1)}, bf16[2,2,32,5120]{3,2,1,0:T(8,128)(2,1)}, u32[]{:S(2)}) copy-start(bf16[2,2,32,5120]{3,2,1,0:T(8,128)(2,1)} %get-tuple-element.31.f1) | copy-start | bytes 3932164
  54.2 19.2 %collective-permute-start.4 = (bf16[2,2,32,5120]{3,2,1,0:T(8,128)(2,1)S(1)}, bf16[2,2,32,5120]{3,2,1,0:T(8,128)(2,1)S(1)}, u32[]{:S(2)}, u32[]{:S(2)}) collective-permute-start(bf16[2,2,32,5120]{3,2,1,0:T(8,128)(2,1)S(1)} %pad_maximum_fusion), channel_id=1, source_target_pairs={{0,1},{1,2},{2,3},{3,4},{4,5},{5,6},{6,7},{7,8},{8,9},{9,10},{10,1... | collective-permute-start | bytes 3932168 | tf_op jit(solution)/shard_map/ppermute | solution.py:28
  56.9 30.5 %collective-permute-start.2 = (bf16[2,2,32,5120]{3,2,1,0:T(8,128)(2,1)S(1)}, bf16[2,2,32,5120]{3,2,1,0:T(8,128)(2,1)S(1)}, u32[]{:S(2)}, u32[]{:S(2)}) collective-permute-start(bf16[2,2,32,5120]{3,2,1,0:T(8,128)(2,1)S(1)} %copy-done.10), channel_id=1, source_target_pairs={{0,1},{1,2},{2,3},{3,4},{4,5},{5,6},{6,7},{7,8},{8,9},{9,10},{10,1... | collective-permute-start | bytes 3932168 | tf_op jit(solution)/shard_map/ppermute | solution.py:28
  61.6 25.9 %collective-permute-start.3 = (bf16[2,2,32,5120]{3,2,1,0:T(8,128)(2,1)S(1)}, bf16[2,2,32,5120]{3,2,1,0:T(8,128)(2,1)S(1)}, u32[]{:S(2)}, u32[]{:S(2)}) collective-permute-start(bf16[2,2,32,5120]{3,2,1,0:T(8,128)(2,1)S(1)} %copy-done.9), channel_id=1, source_target_pairs={{1,0},{2,1},{3,2},{4,3},{5,4},{6,5},{7,6},{8,7},{9,8},{10,9},{11,1... | collective-permute-start | bytes 3932168 | tf_op jit(solution)/shard_map/ppermute | solution.py:28
  96.1 17.8 %collective-permute-start.6 = (bf16[128,2560]{1,0:T(8,128)(2,1)}, bf16[128,2560]{1,0:T(8,128)(2,1)S(1)}, u32[]{:S(2)}, u32[]{:S(2)}) collective-permute-start(bf16[128,2560]{1,0:T(8,128)(2,1)} %get-tuple-element.46.refs_0_), channel_id=1, source_target_pairs={{0,128},{128,0},{16,144},{144,16},{1,129},{129,1},{17,145},{145,17... | collective-permute-start | bytes 1966088 | tf_op jit(solution)/shard_map/ppermute | solution.py:33
  96.8 32.4 %collective-permute-start.7 = (bf16[128,2560]{1,0:T(8,128)(2,1)}, bf16[128,2560]{1,0:T(8,128)(2,1)S(1)}, u32[]{:S(2)}, u32[]{:S(2)}) collective-permute-start(bf16[128,2560]{1,0:T(8,128)(2,1)} %get-tuple-element.39), channel_id=1, source_target_pairs={{0,144},{128,16},{16,128},{144,0},{1,145},{129,17},{17,129},{145,1... | collective-permute-start | bytes 1966088 | tf_op jit(solution)/shard_map/ppermute | solution.py:33
  99.6 29.6 %collective-permute-start.8 = (bf16[128,2560]{1,0:T(8,128)(2,1)}, bf16[128,2560]{1,0:T(8,128)(2,1)S(1)}, u32[]{:S(2)}, u32[]{:S(2)}) collective-permute-start(bf16[128,2560]{1,0:T(8,128)(2,1)} %get-tuple-element.39), channel_id=1, source_target_pairs={{0,16},{128,144},{16,0},{144,128},{1,17},{129,145},{17,1},{145,129... | collective-permute-start | bytes 1966088 | tf_op jit(solution)/shard_map/ppermute | solution.py:33
  136.7 18.8 %collective-permute-start.9 = (bf16[128,1920]{1,0:T(8,128)(2,1)S(1)}, bf16[128,1920]{1,0:T(8,128)(2,1)S(1)}, u32[]{:S(2)}, u32[]{:S(2)}) collective-permute-start(bf16[128,1920]{1,0:T(8,128)(2,1)S(1)} %get-tuple-element.44), channel_id=1, source_target_pairs={{0,128},{128,0},{16,144},{144,16},{1,129},{129,1},{17,145},{145,17... | collective-permute-start | bytes 1474568 | tf_op jit(solution)/shard_map/ppermute | solution.py:33
  137.6 29.8 %collective-permute-start.10 = (bf16[128,1920]{1,0:T(8,128)(2,1)S(1)}, bf16[128,1920]{1,0:T(8,128)(2,1)S(1)}, u32[]{:S(2)}, u32[]{:S(2)}) collective-permute-start(bf16[128,1920]{1,0:T(8,128)(2,1)S(1)} %get-tuple-element.41), channel_id=1, source_target_pairs={{0,16},{128,144},{16,0},{144,128},{1,17},{129,145},{17,1},{145,129... | collective-permute-start | bytes 1474568 | tf_op jit(solution)/shard_map/ppermute | solution.py:33
  141.2 29.3 %collective-permute-start.11 = (bf16[128,1920]{1,0:T(8,128)(2,1)S(1)}, bf16[128,1920]{1,0:T(8,128)(2,1)S(1)}, u32[]{:S(2)}, u32[]{:S(2)}) collective-permute-start(bf16[128,1920]{1,0:T(8,128)(2,1)S(1)} %get-tuple-element.49), channel_id=1, source_target_pairs={{0,144},{128,16},{16,128},{144,0},{1,145},{129,17},{17,129},{145,1... | collective-permute-start | bytes 1474568 | tf_op jit(solution)/shard_map/ppermute | solution.py:33
  145.1 22.3 %collective-permute-start.12 = (bf16[128,640]{1,0:T(8,128)(2,1)S(1)}, bf16[128,640]{1,0:T(8,128)(2,1)S(1)}, u32[]{:S(2)}, u32[]{:S(2)}) collective-permute-start(bf16[128,640]{1,0:T(8,128)(2,1)S(1)} %get-tuple-element.50), channel_id=1, source_target_pairs={{0,16},{128,144},{16,0},{144,128},{1,17},{129,145},{17,1},{145,129... | collective-permute-start | bytes 491528 | tf_op jit(solution)/shard_map/ppermute | solution.py:33
  146.4 25.8 %copy-start.5 = (f32[5120]{0:T(1024)S(1)}, f32[5120]{0:T(1024)}, u32[]{:S(2)}) copy-start(f32[5120]{0:T(1024)} %param.21) | copy-start | bytes 61444
  146.4 20.9 %collective-permute-start.13 = (bf16[128,640]{1,0:T(8,128)(2,1)S(1)}, bf16[128,640]{1,0:T(8,128)(2,1)S(1)}, u32[]{:S(2)}, u32[]{:S(2)}) collective-permute-start(bf16[128,640]{1,0:T(8,128)(2,1)S(1)} %get-tuple-element.51), channel_id=1, source_target_pairs={{0,128},{128,0},{16,144},{144,16},{1,129},{129,1},{17,145},{145,17... | collective-permute-start | bytes 491528 | tf_op jit(solution)/shard_map/ppermute | solution.py:33
  155.5 16.7 %collective-permute-start.14 = (bf16[128,640]{1,0:T(8,128)(2,1)S(1)}, bf16[128,640]{1,0:T(8,128)(2,1)S(1)}, u32[]{:S(2)}, u32[]{:S(2)}) collective-permute-start(bf16[128,640]{1,0:T(8,128)(2,1)S(1)} %get-tuple-element.52), channel_id=1, source_target_pairs={{0,144},{128,16},{16,128},{144,0},{1,145},{129,17},{17,129},{145,1... | collective-permute-start | bytes 491528 | tf_op jit(solution)/shard_map/ppermute | solution.py:33
  (4 other events, 48.4 us)
Sparse Core Ops, SparseCore 0:
  9.1 41.1 all-gather.4
  52.2 71.2 all-gather.6

commit v11 on v10

--- a/solution.py
+++ b/solution.py
@@ -263,13 +263,13 @@
     y_hi, y_lo = (lax.axis_index(a).astype(jnp.int32)[None] for a in ("y_hi", "y_lo"))
     same, other = attend(combo, y_hi, qn, (f0, f1), (hb, ha, rb, ra, cb, ca), masks)
     pair = [along_y(same, lambda y: y ^ 1), along_y(other, lambda y: 3 - y), along_y(other, lambda y: y ^ 2)]
-    to_pair, to_across, to_far = project(pair, weight, 0, 3)
+    to_pair, to_across, to_far = project(pair, weight, 0, 2)
     large = [along_y(to_far, lambda y: y ^ 2), along_y(to_pair, lambda y: y ^ 1), along_y(to_across, lambda y: 3 - y)]
     pair[0], to_far = lax.optimization_barrier((pair[0], to_far))
-    to_pair, to_across, to_far = project(pair, weight, 3, 1)
+    to_pair, to_across, to_far = project(pair, weight, 2, 2)
     same, to_far = lax.optimization_barrier((same, to_far))
     (mine,) = project([same], weight, 0, 4)
-    to_across, large[1], mine = lax.optimization_barrier((to_across, large[1], mine))
+    to_across, large[1], large[2], mine = lax.optimization_barrier((to_across, large[1], large[2], mine))
     parts = [
         large,
         [along_y(to_far, lambda y: y ^ 2), along_y(to_pair, lambda y: y ^ 1), along_y(to_across, lambda y: 3 - y)],

time: 181 us -> 176 us (0.972)
  the two profiles are of different devices: /device:TPU:102 before, /device:TPU:1 now
where the time goes in v11:
time: 176 us; the launch traced here: 175 us
  waiting for transfers between devices  91.6 us (52%)
  Pallas kernels  34.6 us (20%)
  starting transfers between devices  33.6 us (19%)
  between operations  13.7 us (8%)
    ppermute x6, waiting for transfers between devices, passed_along(): return lax.ppermute(block, axes, route)  53.4 us
    ppermute x9, waiting for transfers between devices, along_y(): lax.ppermute(block, ('y_lo', 'y_hi'), [(at(y), at(target(y))) for y in ra...  31.6 us
    ppermute x6, starting transfers between devices, passed_along(): return lax.ppermute(block, axes, route)  19.4 us
    pallas_call x3, Pallas kernels, project(): pl.pallas_call(functools.partial(project_kernel, len(blocks)), grid=(coun...  17.7 us
    ppermute x9, starting transfers between devices, along_y(): lax.ppermute(block, ('y_lo', 'y_hi'), [(at(y), at(target(y))) for y in ra...  14.1 us
    pallas_call x1, Pallas kernels, attend(): pl.pallas_call(functools.partial(attend_kernel, heads, HEAD ** (-0.5)), g...  8.64 us
    pallas_call x1, Pallas kernels, prepare(): pl.pallas_call(prepare_kernel, grid=(groups,), in_specs=[token_spec] * 3...  6.23 us
    all_gather x1, waiting for transfers between devices, shards(): weight = lax.all_gather(weight, ('x', 'core'), axis=0, tiled=False)  5.86 us
  transfers between devices with their start and end apart: 17, of which 12 were waited for; matrix products, arithmetic and copies ran while one was open for 1% of the time, Pallas kernels for 15%

profile of v11, /device:TPU:1, one launch (start us, length us, event | category | flops | bytes accessed | tf_op | source)
XLA Modules:
  0.0 175.0 jit_solution(16256758899439326208)
XLA Ops:
  7.3 6.2 %prepare.1 = (bf16[4,32,5120]{2,1,0:T(8,128)(2,1)}, bf16[2,2,32,5120]{3,2,1,0:T(8,128)(2,1)}, bf16[2,2,32,5120]{3,2,1,0:T(8,128)(2,1)}, bf16[2,2,32,5120]{3,2,1,0:T(8,128)(2,1)}, bf16[2,2,32,5120]{3,2,1,0:T(8,128)(2,1)}) custom-call(bf16[4,32,5120]{2,1,0:T(8,128)(2,1)} %bitcast.18, bf16[4,32,5120]{2,1,0:T(8,128)(2,1)} %bitcast.19, ...), custom_call_target="tpu_custom_call" | custom-call | bytes 12582912 | tf_op jit(solution)/shard_map/prepare/pallas_call | solution.py:79
  13.6 4.0 %collective-permute-start = (bf16[2,2,32,5120]{3,2,1,0:T(8,128)(2,1)}, bf16[2,2,32,5120]{3,2,1,0:T(8,128)(2,1)S(1)}, u32[]{:S(2)}, u32[]{:S(2)}) collective-permute-start(bf16[2,2,32,5120]{3,2,1,0:T(8,128)(2,1)} %get-tuple-element.32.f1), channel_id=1, source_target_pairs={{0,32},{32,64},{64,96},{96,128},{128,160},{160,192},{192,224},{1,3... | collective-permute-start | bytes 3932168 | tf_op jit(solution)/shard_map/ppermute | solution.py:28
  18.9 26.4 %collective-permute-done.hb = bf16[2,2,32,5120]{3,2,1,0:T(8,128)(2,1)S(1)} collective-permute-done((bf16[2,2,32,5120]{3,2,1,0:T(8,128)(2,1)}, bf16[2,2,32,5120]{3,2,1,0:T(8,128)(2,1)S(1)}, u32[]{:S(2)}, u32[]{:S(2)}) %collective-permute-start) | collective-permute-done | bytes 1310752 | tf_op jit(solution)/shard_map/ppermute | solution.py:28
  45.2 3.9 %collective-permute-done.1.ha = bf16[2,2,32,5120]{3,2,1,0:T(8,128)(2,1)S(1)} collective-permute-done((bf16[2,2,32,5120]{3,2,1,0:T(8,128)(2,1)}, bf16[2,2,32,5120]{3,2,1,0:T(8,128)(2,1)S(1)}, u32[]{:S(2)}, u32[]{:S(2)}) %collective-permute-start.1) | collective-permute-done | bytes 1310752 | tf_op jit(solution)/shard_map/ppermute | solution.py:28
  49.7 6.8 %collective-permute-start.5 = (bf16[2,2,32,5120]{3,2,1,0:T(8,128)(2,1)S(1)}, bf16[2,2,32,5120]{3,2,1,0:T(8,128)(2,1)S(1)}, u32[]{:S(2)}, u32[]{:S(2)}) collective-permute-start(bf16[2,2,32,5120]{3,2,1,0:T(8,128)(2,1)S(1)} %pad_maximum_fusion.1), channel_id=1, source_target_pairs={{1,0},{2,1},{3,2},{4,3},{5,4},{6,5},{7,6},{8,7},{9,8},{10,9},{11,1... | collective-permute-start | bytes 3932168 | tf_op jit(solution)/shard_map/ppermute | solution.py:28
  56.7 3.0 %collective-permute-start.4 = (bf16[2,2,32,5120]{3,2,1,0:T(8,128)(2,1)S(1)}, bf16[2,2,32,5120]{3,2,1,0:T(8,128)(2,1)S(1)}, u32[]{:S(2)}, u32[]{:S(2)}) collective-permute-start(bf16[2,2,32,5120]{3,2,1,0:T(8,128)(2,1)S(1)} %pad_maximum_fusion), channel_id=1, source_target_pairs={{0,1},{1,2},{2,3},{3,4},{4,5},{5,6},{6,7},{7,8},{8,9},{9,10},{10,1... | collective-permute-start | bytes 3932168 | tf_op jit(solution)/shard_map/ppermute | solution.py:28
  59.6 2.4 %collective-permute-start.2 = (bf16[2,2,32,5120]{3,2,1,0:T(8,128)(2,1)S(1)}, bf16[2,2,32,5120]{3,2,1,0:T(8,128)(2,1)S(1)}, u32[]{:S(2)}, u32[]{:S(2)}) collective-permute-start(bf16[2,2,32,5120]{3,2,1,0:T(8,128)(2,1)S(1)} %copy-done.10), channel_id=1, source_target_pairs={{0,1},{1,2},{2,3},{3,4},{4,5},{5,6},{6,7},{7,8},{8,9},{9,10},{10,1... | collective-permute-start | bytes 3932168 | tf_op jit(solution)/shard_map/ppermute | solution.py:28
  62.1 2.0 %collective-permute-start.3 = (bf16[2,2,32,5120]{3,2,1,0:T(8,128)(2,1)S(1)}, bf16[2,2,32,5120]{3,2,1,0:T(8,128)(2,1)S(1)}, u32[]{:S(2)}, u32[]{:S(2)}) collective-permute-start(bf16[2,2,32,5120]{3,2,1,0:T(8,128)(2,1)S(1)} %copy-done.9), channel_id=1, source_target_pairs={{1,0},{2,1},{3,2},{4,3},{5,4},{6,5},{7,6},{8,7},{9,8},{10,9},{11,1... | collective-permute-start | bytes 3932168 | tf_op jit(solution)/shard_map/ppermute | solution.py:28
  65.0 8.0 %collective-permute-done.5.ca = bf16[2,2,32,5120]{3,2,1,0:T(8,128)(2,1)S(1)} collective-permute-done((bf16[2,2,32,5120]{3,2,1,0:T(8,128)(2,1)S(1)}, bf16[2,2,32,5120]{3,2,1,0:T(8,128)(2,1)S(1)}, u32[]{:S(2)}, u32[]{:S(2)}) %collective-permute-start.5) | collective-permute-done | bytes 1310752 | tf_op jit(solution)/shard_map/ppermute | solution.py:28
  74.2 14.0 %collective-permute-done.2.rb = bf16[2,2,32,5120]{3,2,1,0:T(8,128)(2,1)S(1)} collective-permute-done((bf16[2,2,32,5120]{3,2,1,0:T(8,128)(2,1)S(1)}, bf16[2,2,32,5120]{3,2,1,0:T(8,128)(2,1)S(1)}, u32[]{:S(2)}, u32[]{:S(2)}) %collective-permute-start.2) | collective-permute-done | bytes 1310752 | tf_op jit(solution)/shard_map/ppermute | solution.py:28
  88.2 8.6 %attend.1 = (bf16[128,2560]{1,0:T(8,128)(2,1)}, bf16[128,2560]{1,0:T(8,128)(2,1)}) custom-call(s32[40]{0:T(128)S(1)} %add_add_fusion.combo_ref, s32[1]{0:T(128)} %bitcast.3.half_ref, bf16[4,32,5120]{2,1,0:T(8,128)(2,1)S(1)} %copy-done, bf16[2,2,32,5120]{3,2,1,0:T(8,128)(2,1)S(1)} %copy-done.1, bf16[2,2,32,5120]{3,2,1,0:T(8,128)(2,1)S(1)} %copy-done.2, ...), custom_call_target="tpu_custom_call" | custom-call | flops 1006632960 | bytes 33554432 | tf_op jit(solution)/shard_map/attend/pallas_call | solution.py:159
  98.0 1.9 %collective-permute-start.7 = (bf16[128,2560]{1,0:T(8,128)(2,1)}, bf16[128,2560]{1,0:T(8,128)(2,1)S(1)}, u32[]{:S(2)}, u32[]{:S(2)}) collective-permute-start(bf16[128,2560]{1,0:T(8,128)(2,1)} %get-tuple-element.40), channel_id=1, source_target_pairs={{0,144},{128,16},{16,128},{144,0},{1,145},{129,17},{17,129},{145,1... | collective-permute-start | bytes 1966088 | tf_op jit(solution)/shard_map/ppermute | solution.py:33
  100.4 9.2 %collective-permute-done.6.refs_0_ = bf16[128,2560]{1,0:T(8,128)(2,1)S(1)} collective-permute-done((bf16[128,2560]{1,0:T(8,128)(2,1)}, bf16[128,2560]{1,0:T(8,128)(2,1)S(1)}, u32[]{:S(2)}, u32[]{:S(2)}) %collective-permute-start.6) | collective-permute-done | bytes 655392 | tf_op jit(solution)/shard_map/ppermute | solution.py:33
  111.5 10.0 %collective-permute-done.8.refs_2_ = bf16[128,2560]{1,0:T(8,128)(2,1)S(1)} collective-permute-done((bf16[128,2560]{1,0:T(8,128)(2,1)}, bf16[128,2560]{1,0:T(8,128)(2,1)S(1)}, u32[]{:S(2)}, u32[]{:S(2)}) %collective-permute-start.8) | collective-permute-done | bytes 655392 | tf_op jit(solution)/shard_map/ppermute | solution.py:33
  121.5 5.9 %all-gather.7.cloned.1.call-done = bf16[64,160,640]{2,1,0:T(8,128)(2,1)} async-done(((bf16[8,160,640]{2,1,0:T(8,128)(2,1)}), bf16[64,160,640]{2,1,0:T(8,128)(2,1)}) %all-gather.7.cloned.1.call-update) | async-done | bytes 13107216 | tf_op jit(solution)/shard_map/all_gather | solution.py:258
  127.3 5.5 %project.3 = (bf16[128,1280]{1,0:T(8,128)(2,1)S(1)}, bf16[128,1280]{1,0:T(8,128)(2,1)S(1)}, bf16[128,1280]{1,0:T(8,128)(2,1)S(1)}) custom-call(bf16[128,2560]{1,0:T(8,128)(2,1)S(1)} %collective-permute-done.6.refs_0_, bf16[128,2560]{1,0:T(8,128)(2,1)S(1)} %collective-permute-done.7.refs_1_, bf16[128,2560]{1,0:T(8,128)(2,1)S(1)} %collective-permute-done.8.refs_2_, ...), custom_call_target="tpu_custom_call" | custom-call | flops 2516582400 | bytes 6553600 | tf_op jit(solution)/shard_map/project/pallas_call | solution.py:194
  132.9 2.8 %collective-permute-start.11 = (bf16[128,1280]{1,0:T(8,128)(2,1)S(1)}, bf16[128,1280]{1,0:T(8,128)(2,1)S(1)}, u32[]{:S(2)}, u32[]{:S(2)}) collective-permute-start(bf16[128,1280]{1,0:T(8,128)(2,1)S(1)} %get-tuple-element.42), channel_id=1, source_target_pairs={{0,16},{128,144},{16,0},{144,128},{1,17},{129,145},{17,1},{145,129... | collective-permute-start | bytes 983048 | tf_op jit(solution)/shard_map/ppermute | solution.py:33
  136.5 5.6 %project.4 = (bf16[128,1280]{1,0:T(8,128)(2,1)S(1)}, bf16[128,1280]{1,0:T(8,128)(2,1)S(1)}, bf16[128,1280]{1,0:T(8,128)(2,1)S(1)}) custom-call(bf16[128,2560]{1,0:T(8,128)(2,1)S(1)} %collective-permute-done.6.refs_0_, bf16[128,2560]{1,0:T(8,128)(2,1)S(1)} %collective-permute-done.7.refs_1_, bf16[128,2560]{1,0:T(8,128)(2,1)S(1)} %collective-permute-done.8.refs_2_, ...), custom_call_target="tpu_custom_call" | custom-call | flops 2516582400 | bytes 6553600 | tf_op jit(solution)/shard_map/project/pallas_call | solution.py:194
  142.2 3.0 %collective-permute-start.12 = (bf16[128,1280]{1,0:T(8,128)(2,1)S(1)}, bf16[128,1280]{1,0:T(8,128)(2,1)S(1)}, u32[]{:S(2)}, u32[]{:S(2)}) collective-permute-start(bf16[128,1280]{1,0:T(8,128)(2,1)S(1)} %get-tuple-element.52), channel_id=1, source_target_pairs={{0,16},{128,144},{16,0},{144,128},{1,17},{129,145},{17,1},{145,129... | collective-permute-start | bytes 983048 | tf_op jit(solution)/shard_map/ppermute | solution.py:33
  145.2 6.6 %project.5.mine = bf16[128,2560]{1,0:T(8,128)(2,1)S(1)} custom-call(bf16[128,2560]{1,0:T(8,128)(2,1)S(1)} %copy-done.4, bf16[4,2,8,160,640]{4,3,2,1,0:T(8,128)(2,1)} %bitcast.16), custom_call_target="tpu_custom_call" | custom-call | flops 1677721600 | bytes 13107200 | tf_op jit(solution)/shard_map/project/pallas_call | solution.py:194
  153.1 3.9 %collective-permute-start.14 = (bf16[128,1280]{1,0:T(8,128)(2,1)S(1)}, bf16[128,1280]{1,0:T(8,128)(2,1)S(1)}, u32[]{:S(2)}, u32[]{:S(2)}) collective-permute-start(bf16[128,1280]{1,0:T(8,128)(2,1)S(1)} %get-tuple-element.54), channel_id=1, source_target_pairs={{0,144},{128,16},{16,128},{144,0},{1,145},{129,17},{17,129},{145,1... | collective-permute-start | bytes 983048 | tf_op jit(solution)/shard_map/ppermute | solution.py:33
  157.0 4.6 %collective-permute-done.13.pair1 = bf16[128,1280]{1,0:T(8,128)(2,1)S(1)} collective-permute-done((bf16[128,1280]{1,0:T(8,128)(2,1)S(1)}, bf16[128,1280]{1,0:T(8,128)(2,1)S(1)}, u32[]{:S(2)}, u32[]{:S(2)}) %collective-permute-start.13) | collective-permute-done | bytes 327712 | tf_op jit(solution)/shard_map/ppermute | solution.py:33
  161.6 4.6 %collective-permute-done.14.across1 = bf16[128,1280]{1,0:T(8,128)(2,1)S(1)} collective-permute-done((bf16[128,1280]{1,0:T(8,128)(2,1)S(1)}, bf16[128,1280]{1,0:T(8,128)(2,1)S(1)}, u32[]{:S(2)}, u32[]{:S(2)}) %collective-permute-start.14) | collective-permute-done | bytes 327712 | tf_op jit(solution)/shard_map/ppermute | solution.py:33
  166.2 2.0 %finish.1 = bf16[128,5120]{1,0:T(8,128)(2,1)} custom-call(s32[1]{0:T(128)} %bitcast.y_ref, bf16[128,5120]{1,0:T(8,128)(2,1)S(1)} %bitcast.12, f32[1,5120]{1,0:T(1,128)S(1)} %bitcast.13, bf16[128,2560]{1,0:T(8,128)(2,1)S(1)} %project.5.mine, bf16[128,1280]{1,0:T(8,128)(2,1)S(1)} %collective-permute-done.11.far0, ...), custom_call_target="tpu_custom_call" | custom-call | tf_op jit(solution)/shard_map/finish/pallas_call | solution.py:226
  (59 shorter events, 10.5 us)
Async XLA Ops:
  6.5 42.6 %all-gather.5.cloned.1.call-start = ((), (), s32[]{:S(2)}) async-start(), calls=%async_computation | async-start | bytes 1843200 | tf_op jit(solution)/shard_map/all_gather | solution.py:244
  7.3 120.1 %all-gather.7.cloned.1.call-start = ((), (), s32[]{:S(2)}) async-start(), calls=%async_computation.1 | async-start | bytes 14745600 | tf_op jit(solution)/shard_map/all_gather | solution.py:258
  7.3 42.0 %copy-start.6 = (s32[40]{0:T(128)S(1)}, s32[40]{0:T(128)}, u32[]{:S(2)}) copy-start(s32[40]{0:T(128)} %param.19) | copy-start | bytes 484
  7.3 42.0 %copy-start.7 = (s32[40]{0:T(128)S(1)}, s32[40]{0:T(128)}, u32[]{:S(2)}) copy-start(s32[40]{0:T(128)} %param.18) | copy-start | bytes 484
  7.3 42.0 %copy-start.8 = (s32[40]{0:T(128)S(1)}, s32[40]{0:T(128)}, u32[]{:S(2)}) copy-start(s32[40]{0:T(128)} %param.17) | copy-start | bytes 484
  13.6 31.7 %collective-permute-start = (bf16[2,2,32,5120]{3,2,1,0:T(8,128)(2,1)}, bf16[2,2,32,5120]{3,2,1,0:T(8,128)(2,1)S(1)}, u32[]{:S(2)}, u32[]{:S(2)}) collective-permute-start(bf16[2,2,32,5120]{3,2,1,0:T(8,128)(2,1)} %get-tuple-element.32.f1), channel_id=1, source_target_pairs={{0,32},{32,64},{64,96},{96,128},{128,160},{160,192},{192,224},{1,3... | collective-permute-start | bytes 3932168 | tf_op jit(solution)/shard_map/ppermute | solution.py:28
  17.6 31.5 %collective-permute-start.1 = (bf16[2,2,32,5120]{3,2,1,0:T(8,128)(2,1)}, bf16[2,2,32,5120]{3,2,1,0:T(8,128)(2,1)S(1)}, u32[]{:S(2)}, u32[]{:S(2)}) collective-permute-start(bf16[2,2,32,5120]{3,2,1,0:T(8,128)(2,1)} %get-tuple-element.31.f0), channel_id=1, source_target_pairs={{32,0},{64,32},{96,64},{128,96},{160,128},{192,160},{224,192},{33,... | collective-permute-start | bytes 3932168 | tf_op jit(solution)/shard_map/ppermute | solution.py:28
  49.7 23.2 %collective-permute-start.5 = (bf16[2,2,32,5120]{3,2,1,0:T(8,128)(2,1)S(1)}, bf16[2,2,32,5120]{3,2,1,0:T(8,128)(2,1)S(1)}, u32[]{:S(2)}, u32[]{:S(2)}) collective-permute-start(bf16[2,2,32,5120]{3,2,1,0:T(8,128)(2,1)S(1)} %pad_maximum_fusion.1), channel_id=1, source_target_pairs={{1,0},{2,1},{3,2},{4,3},{5,4},{6,5},{7,6},{8,7},{9,8},{10,9},{11,1... | collective-permute-start | bytes 3932168 | tf_op jit(solution)/shard_map/ppermute | solution.py:28
  56.5 31.7 %copy-start = (bf16[4,32,5120]{2,1,0:T(8,128)(2,1)S(1)}, bf16[4,32,5120]{2,1,0:T(8,128)(2,1)}, u32[]{:S(2)}) copy-start(bf16[4,32,5120]{2,1,0:T(8,128)(2,1)} %get-tuple-element.30.q_ref) | copy-start | bytes 3932164
  56.5 31.7 %copy-start.1 = (bf16[2,2,32,5120]{3,2,1,0:T(8,128)(2,1)S(1)}, bf16[2,2,32,5120]{3,2,1,0:T(8,128)(2,1)}, u32[]{:S(2)}) copy-start(bf16[2,2,32,5120]{3,2,1,0:T(8,128)(2,1)} %get-tuple-element.31.f0) | copy-start | bytes 3932164
  56.5 31.7 %copy-start.2 = (bf16[2,2,32,5120]{3,2,1,0:T(8,128)(2,1)S(1)}, bf16[2,2,32,5120]{3,2,1,0:T(8,128)(2,1)}, u32[]{:S(2)}) copy-start(bf16[2,2,32,5120]{3,2,1,0:T(8,128)(2,1)} %get-tuple-element.32.f1) | copy-start | bytes 3932164
  56.7 17.5 %collective-permute-start.4 = (bf16[2,2,32,5120]{3,2,1,0:T(8,128)(2,1)S(1)}, bf16[2,2,32,5120]{3,2,1,0:T(8,128)(2,1)S(1)}, u32[]{:S(2)}, u32[]{:S(2)}) collective-permute-start(bf16[2,2,32,5120]{3,2,1,0:T(8,128)(2,1)S(1)} %pad_maximum_fusion), channel_id=1, source_target_pairs={{0,1},{1,2},{2,3},{3,4},{4,5},{5,6},{6,7},{7,8},{8,9},{9,10},{10,1... | collective-permute-start | bytes 3932168 | tf_op jit(solution)/shard_map/ppermute | solution.py:28
  59.6 28.6 %collective-permute-start.2 = (bf16[2,2,32,5120]{3,2,1,0:T(8,128)(2,1)S(1)}, bf16[2,2,32,5120]{3,2,1,0:T(8,128)(2,1)S(1)}, u32[]{:S(2)}, u32[]{:S(2)}) collective-permute-start(bf16[2,2,32,5120]{3,2,1,0:T(8,128)(2,1)S(1)} %copy-done.10), channel_id=1, source_target_pairs={{0,1},{1,2},{2,3},{3,4},{4,5},{5,6},{6,7},{7,8},{8,9},{9,10},{10,1... | collective-permute-start | bytes 3932168 | tf_op jit(solution)/shard_map/ppermute | solution.py:28
  62.1 26.1 %collective-permute-start.3 = (bf16[2,2,32,5120]{3,2,1,0:T(8,128)(2,1)S(1)}, bf16[2,2,32,5120]{3,2,1,0:T(8,128)(2,1)S(1)}, u32[]{:S(2)}, u32[]{:S(2)}) collective-permute-start(bf16[2,2,32,5120]{3,2,1,0:T(8,128)(2,1)S(1)} %copy-done.9), channel_id=1, source_target_pairs={{1,0},{2,1},{3,2},{4,3},{5,4},{6,5},{7,6},{8,7},{9,8},{10,9},{11,1... | collective-permute-start | bytes 3932168 | tf_op jit(solution)/shard_map/ppermute | solution.py:28
  96.9 12.7 %collective-permute-start.6 = (bf16[128,2560]{1,0:T(8,128)(2,1)}, bf16[128,2560]{1,0:T(8,128)(2,1)S(1)}, u32[]{:S(2)}, u32[]{:S(2)}) collective-permute-start(bf16[128,2560]{1,0:T(8,128)(2,1)} %get-tuple-element.48.refs_0_), channel_id=1, source_target_pairs={{0,128},{128,0},{16,144},{144,16},{1,129},{129,1},{17,145},{145,17... | collective-permute-start | bytes 1966088 | tf_op jit(solution)/shard_map/ppermute | solution.py:33
  98.0 13.5 %collective-permute-start.7 = (bf16[128,2560]{1,0:T(8,128)(2,1)}, bf16[128,2560]{1,0:T(8,128)(2,1)S(1)}, u32[]{:S(2)}, u32[]{:S(2)}) collective-permute-start(bf16[128,2560]{1,0:T(8,128)(2,1)} %get-tuple-element.40), channel_id=1, source_target_pairs={{0,144},{128,16},{16,128},{144,0},{1,145},{129,17},{17,129},{145,1... | collective-permute-start | bytes 1966088 | tf_op jit(solution)/shard_map/ppermute | solution.py:33
  99.9 21.6 %collective-permute-start.8 = (bf16[128,2560]{1,0:T(8,128)(2,1)}, bf16[128,2560]{1,0:T(8,128)(2,1)S(1)}, u32[]{:S(2)}, u32[]{:S(2)}) collective-permute-start(bf16[128,2560]{1,0:T(8,128)(2,1)} %get-tuple-element.40), channel_id=1, source_target_pairs={{0,16},{128,144},{16,0},{144,128},{1,17},{129,145},{17,1},{145,129... | collective-permute-start | bytes 1966088 | tf_op jit(solution)/shard_map/ppermute | solution.py:33
  132.9 28.7 %collective-permute-start.11 = (bf16[128,1280]{1,0:T(8,128)(2,1)S(1)}, bf16[128,1280]{1,0:T(8,128)(2,1)S(1)}, u32[]{:S(2)}, u32[]{:S(2)}) collective-permute-start(bf16[128,1280]{1,0:T(8,128)(2,1)S(1)} %get-tuple-element.42), channel_id=1, source_target_pairs={{0,16},{128,144},{16,0},{144,128},{1,17},{129,145},{17,1},{145,129... | collective-permute-start | bytes 983048 | tf_op jit(solution)/shard_map/ppermute | solution.py:33
  135.7 17.4 %collective-permute-start.10 = (bf16[128,1280]{1,0:T(8,128)(2,1)S(1)}, bf16[128,1280]{1,0:T(8,128)(2,1)S(1)}, u32[]{:S(2)}, u32[]{:S(2)}) collective-permute-start(bf16[128,1280]{1,0:T(8,128)(2,1)S(1)} %get-tuple-element.46), channel_id=1, source_target_pairs={{0,144},{128,16},{16,128},{144,0},{1,145},{129,17},{17,129},{145,1... | collective-permute-start | bytes 983048 | tf_op jit(solution)/shard_map/ppermute | solution.py:33
  136.5 16.6 %collective-permute-start.9 = (bf16[128,1280]{1,0:T(8,128)(2,1)S(1)}, bf16[128,1280]{1,0:T(8,128)(2,1)S(1)}, u32[]{:S(2)}, u32[]{:S(2)}) collective-permute-start(bf16[128,1280]{1,0:T(8,128)(2,1)S(1)} %get-tuple-element.45), channel_id=1, source_target_pairs={{0,128},{128,0},{16,144},{144,16},{1,129},{129,1},{17,145},{145,17... | collective-permute-start | bytes 983048 | tf_op jit(solution)/shard_map/ppermute | solution.py:33
  142.2 14.8 %collective-permute-start.12 = (bf16[128,1280]{1,0:T(8,128)(2,1)S(1)}, bf16[128,1280]{1,0:T(8,128)(2,1)S(1)}, u32[]{:S(2)}, u32[]{:S(2)}) collective-permute-start(bf16[128,1280]{1,0:T(8,128)(2,1)S(1)} %get-tuple-element.52), channel_id=1, source_target_pairs={{0,16},{128,144},{16,0},{144,128},{1,17},{129,145},{17,1},{145,129... | collective-permute-start | bytes 983048 | tf_op jit(solution)/shard_map/ppermute | solution.py:33
  145.2 21.0 %copy-start.5 = (f32[5120]{0:T(1024)S(1)}, f32[5120]{0:T(1024)}, u32[]{:S(2)}) copy-start(f32[5120]{0:T(1024)} %param.21) | copy-start | bytes 61444
  145.2 16.4 %collective-permute-start.13 = (bf16[128,1280]{1,0:T(8,128)(2,1)S(1)}, bf16[128,1280]{1,0:T(8,128)(2,1)S(1)}, u32[]{:S(2)}, u32[]{:S(2)}) collective-permute-start(bf16[128,1280]{1,0:T(8,128)(2,1)S(1)} %get-tuple-element.53), channel_id=1, source_target_pairs={{0,128},{128,0},{16,144},{144,16},{1,129},{129,1},{17,145},{145,17... | collective-permute-start | bytes 983048 | tf_op jit(solution)/shard_map/ppermute | solution.py:33
  153.1 13.1 %collective-permute-start.14 = (bf16[128,1280]{1,0:T(8,128)(2,1)S(1)}, bf16[128,1280]{1,0:T(8,128)(2,1)S(1)}, u32[]{:S(2)}, u32[]{:S(2)}) collective-permute-start(bf16[128,1280]{1,0:T(8,128)(2,1)S(1)} %get-tuple-element.54), channel_id=1, source_target_pairs={{0,144},{128,16},{16,128},{144,0},{1,145},{129,17},{17,129},{145,1... | collective-permute-start | bytes 983048 | tf_op jit(solution)/shard_map/ppermute | solution.py:33
  (4 other events, 52.2 us)
Sparse Core Ops, SparseCore 0:
  9.1 39.8 all-gather.4
  50.9 76.4 all-gather.6

commit v12 on v11

--- a/solution.py
+++ b/solution.py
@@ -269,7 +269,7 @@
     to_pair, to_across, to_far = project(pair, weight, 2, 2)
     same, to_far = lax.optimization_barrier((same, to_far))
     (mine,) = project([same], weight, 0, 4)
-    to_across, large[1], large[2], mine = lax.optimization_barrier((to_across, large[1], large[2], mine))
+    to_across, large[1], large[2] = lax.optimization_barrier((to_across, large[1], large[2]))
     parts = [
         large,
         [along_y(to_far, lambda y: y ^ 2), along_y(to_pair, lambda y: y ^ 1), along_y(to_across, lambda y: 3 - y)],

time: 176 us -> 178 us (1.011)
  the two profiles are of different devices: /device:TPU:1 before, /device:TPU:102 now
where the time goes in v12:
time: 178 us
  waiting for transfers between devices  95.2 us (53%)
  Pallas kernels  34.4 us (19%)
  starting transfers between devices  33 us (19%)
  between operations  13.8 us (8%)
    ppermute x6, waiting for transfers between devices, passed_along(): return lax.ppermute(block, axes, route)  55 us
    ppermute x9, waiting for transfers between devices, along_y(): lax.ppermute(block, ('y_lo', 'y_hi'), [(at(y), at(target(y))) for y in ra...  39.5 us
    pallas_call x3, Pallas kernels, project(): pl.pallas_call(functools.partial(project_kernel, len(blocks)), grid=(coun...  17.5 us
    ppermute x6, starting transfers between devices, passed_along(): return lax.ppermute(block, axes, route)  17.1 us
    ppermute x9, starting transfers between devices, along_y(): lax.ppermute(block, ('y_lo', 'y_hi'), [(at(y), at(target(y))) for y in ra...  15.8 us
    pallas_call x1, Pallas kernels, attend(): pl.pallas_call(functools.partial(attend_kernel, heads, HEAD ** (-0.5)), g...  8.63 us
    pallas_call x1, Pallas kernels, prepare(): pl.pallas_call(prepare_kernel, grid=(groups,), in_specs=[token_spec] * 3...  6.23 us
  transfers between devices with their start and end apart: 17, of which 8 were waited for; matrix products, arithmetic and copies ran while one was open for 1% of the time, Pallas kernels for 15%

profile of v12, /device:TPU:102, one launch (start us, length us, event | category | flops | bytes accessed | tf_op | source)
XLA Modules:
  0.0 177.9 jit_solution(15605890167740286722)
XLA Ops:
  7.3 6.2 %prepare.1 = (bf16[4,32,5120]{2,1,0:T(8,128)(2,1)}, bf16[2,2,32,5120]{3,2,1,0:T(8,128)(2,1)}, bf16[2,2,32,5120]{3,2,1,0:T(8,128)(2,1)}, bf16[2,2,32,5120]{3,2,1,0:T(8,128)(2,1)}, bf16[2,2,32,5120]{3,2,1,0:T(8,128)(2,1)}) custom-call(bf16[4,32,5120]{2,1,0:T(8,128)(2,1)} %bitcast.18, bf16[4,32,5120]{2,1,0:T(8,128)(2,1)} %bitcast.19, ...), custom_call_target="tpu_custom_call" | custom-call | bytes 12582912 | tf_op jit(solution)/shard_map/prepare/pallas_call | solution.py:79
  13.6 3.4 %collective-permute-start = (bf16[2,2,32,5120]{3,2,1,0:T(8,128)(2,1)}, bf16[2,2,32,5120]{3,2,1,0:T(8,128)(2,1)S(1)}, u32[]{:S(2)}, u32[]{:S(2)}) collective-permute-start(bf16[2,2,32,5120]{3,2,1,0:T(8,128)(2,1)} %get-tuple-element.31.f1), channel_id=1, source_target_pairs={{0,32},{32,64},{64,96},{96,128},{128,160},{160,192},{192,224},{1,3... | collective-permute-start | bytes 3932168 | tf_op jit(solution)/shard_map/ppermute | solution.py:28
  17.0 2.4 %collective-permute-start.1 = (bf16[2,2,32,5120]{3,2,1,0:T(8,128)(2,1)}, bf16[2,2,32,5120]{3,2,1,0:T(8,128)(2,1)S(1)}, u32[]{:S(2)}, u32[]{:S(2)}) collective-permute-start(bf16[2,2,32,5120]{3,2,1,0:T(8,128)(2,1)} %get-tuple-element.30.f0), channel_id=1, source_target_pairs={{32,0},{64,32},{96,64},{128,96},{160,128},{192,160},{224,192},{33,... | collective-permute-start | bytes 3932168 | tf_op jit(solution)/shard_map/ppermute | solution.py:28
  19.4 26.8 %collective-permute-done.hb = bf16[2,2,32,5120]{3,2,1,0:T(8,128)(2,1)S(1)} collective-permute-done((bf16[2,2,32,5120]{3,2,1,0:T(8,128)(2,1)}, bf16[2,2,32,5120]{3,2,1,0:T(8,128)(2,1)S(1)}, u32[]{:S(2)}, u32[]{:S(2)}) %collective-permute-start) | collective-permute-done | bytes 1310752 | tf_op jit(solution)/shard_map/ppermute | solution.py:28
  46.2 5.2 %collective-permute-done.1.ha = bf16[2,2,32,5120]{3,2,1,0:T(8,128)(2,1)S(1)} collective-permute-done((bf16[2,2,32,5120]{3,2,1,0:T(8,128)(2,1)}, bf16[2,2,32,5120]{3,2,1,0:T(8,128)(2,1)S(1)}, u32[]{:S(2)}, u32[]{:S(2)}) %collective-permute-start.1) | collective-permute-done | bytes 1310752 | tf_op jit(solution)/shard_map/ppermute | solution.py:28
  52.0 2.1 %collective-permute-start.5 = (bf16[2,2,32,5120]{3,2,1,0:T(8,128)(2,1)S(1)}, bf16[2,2,32,5120]{3,2,1,0:T(8,128)(2,1)S(1)}, u32[]{:S(2)}, u32[]{:S(2)}) collective-permute-start(bf16[2,2,32,5120]{3,2,1,0:T(8,128)(2,1)S(1)} %pad_maximum_fusion.1), channel_id=1, source_target_pairs={{1,0},{2,1},{3,2},{4,3},{5,4},{6,5},{7,6},{8,7},{9,8},{10,9},{11,1... | collective-permute-start | bytes 3932168 | tf_op jit(solution)/shard_map/ppermute | solution.py:28
  54.2 2.7 %collective-permute-start.4 = (bf16[2,2,32,5120]{3,2,1,0:T(8,128)(2,1)S(1)}, bf16[2,2,32,5120]{3,2,1,0:T(8,128)(2,1)S(1)}, u32[]{:S(2)}, u32[]{:S(2)}) collective-permute-start(bf16[2,2,32,5120]{3,2,1,0:T(8,128)(2,1)S(1)} %pad_maximum_fusion), channel_id=1, source_target_pairs={{0,1},{1,2},{2,3},{3,4},{4,5},{5,6},{6,7},{7,8},{8,9},{9,10},{10,1... | collective-permute-start | bytes 3932168 | tf_op jit(solution)/shard_map/ppermute | solution.py:28
  56.9 4.7 %collective-permute-start.2 = (bf16[2,2,32,5120]{3,2,1,0:T(8,128)(2,1)S(1)}, bf16[2,2,32,5120]{3,2,1,0:T(8,128)(2,1)S(1)}, u32[]{:S(2)}, u32[]{:S(2)}) collective-permute-start(bf16[2,2,32,5120]{3,2,1,0:T(8,128)(2,1)S(1)} %copy-done.10), channel_id=1, source_target_pairs={{0,1},{1,2},{2,3},{3,4},{4,5},{5,6},{6,7},{7,8},{8,9},{9,10},{10,1... | collective-permute-start | bytes 3932168 | tf_op jit(solution)/shard_map/ppermute | solution.py:28
  61.6 1.9 %collective-permute-start.3 = (bf16[2,2,32,5120]{3,2,1,0:T(8,128)(2,1)S(1)}, bf16[2,2,32,5120]{3,2,1,0:T(8,128)(2,1)S(1)}, u32[]{:S(2)}, u32[]{:S(2)}) collective-permute-start(bf16[2,2,32,5120]{3,2,1,0:T(8,128)(2,1)S(1)} %copy-done.9), channel_id=1, source_target_pairs={{1,0},{2,1},{3,2},{4,3},{5,4},{6,5},{7,6},{8,7},{9,8},{10,9},{11,1... | collective-permute-start | bytes 3932168 | tf_op jit(solution)/shard_map/ppermute | solution.py:28
  64.4 4.7 %collective-permute-done.5.ca = bf16[2,2,32,5120]{3,2,1,0:T(8,128)(2,1)S(1)} collective-permute-done((bf16[2,2,32,5120]{3,2,1,0:T(8,128)(2,1)S(1)}, bf16[2,2,32,5120]{3,2,1,0:T(8,128)(2,1)S(1)}, u32[]{:S(2)}, u32[]{:S(2)}) %collective-permute-start.5) | collective-permute-done | bytes 1310752 | tf_op jit(solution)/shard_map/ppermute | solution.py:28
  69.2 4.2 %collective-permute-done.4.cb = bf16[2,2,32,5120]{3,2,1,0:T(8,128)(2,1)S(1)} collective-permute-done((bf16[2,2,32,5120]{3,2,1,0:T(8,128)(2,1)S(1)}, bf16[2,2,32,5120]{3,2,1,0:T(8,128)(2,1)S(1)}, u32[]{:S(2)}, u32[]{:S(2)}) %collective-permute-start.4) | collective-permute-done | bytes 1310752 | tf_op jit(solution)/shard_map/ppermute | solution.py:28
  73.4 14.0 %collective-permute-done.2.rb = bf16[2,2,32,5120]{3,2,1,0:T(8,128)(2,1)S(1)} collective-permute-done((bf16[2,2,32,5120]{3,2,1,0:T(8,128)(2,1)S(1)}, bf16[2,2,32,5120]{3,2,1,0:T(8,128)(2,1)S(1)}, u32[]{:S(2)}, u32[]{:S(2)}) %collective-permute-start.2) | collective-permute-done | bytes 1310752 | tf_op jit(solution)/shard_map/ppermute | solution.py:28
  87.5 8.6 %attend.1 = (bf16[128,2560]{1,0:T(8,128)(2,1)}, bf16[128,2560]{1,0:T(8,128)(2,1)}) custom-call(s32[40]{0:T(128)S(1)} %add_add_fusion.combo_ref, s32[1]{0:T(128)} %bitcast.3.half_ref, bf16[4,32,5120]{2,1,0:T(8,128)(2,1)S(1)} %copy-done, bf16[2,2,32,5120]{3,2,1,0:T(8,128)(2,1)S(1)} %copy-done.1, bf16[2,2,32,5120]{3,2,1,0:T(8,128)(2,1)S(1)} %copy-done.2, ...), custom_call_target="tpu_custom_call" | custom-call | flops 1006632960 | bytes 33554432 | tf_op jit(solution)/shard_map/attend/pallas_call | solution.py:159
  96.8 2.8 %collective-permute-start.7 = (bf16[128,2560]{1,0:T(8,128)(2,1)}, bf16[128,2560]{1,0:T(8,128)(2,1)S(1)}, u32[]{:S(2)}, u32[]{:S(2)}) collective-permute-start(bf16[128,2560]{1,0:T(8,128)(2,1)} %get-tuple-element.39), channel_id=1, source_target_pairs={{0,144},{128,16},{16,128},{144,0},{1,145},{129,17},{17,129},{145,1... | collective-permute-start | bytes 1966088 | tf_op jit(solution)/shard_map/ppermute | solution.py:33
  100.2 13.7 %collective-permute-done.6.refs_0_ = bf16[128,2560]{1,0:T(8,128)(2,1)S(1)} collective-permute-done((bf16[128,2560]{1,0:T(8,128)(2,1)}, bf16[128,2560]{1,0:T(8,128)(2,1)S(1)}, u32[]{:S(2)}, u32[]{:S(2)}) %collective-permute-start.6) | collective-permute-done | bytes 655392 | tf_op jit(solution)/shard_map/ppermute | solution.py:33
  113.9 15.3 %collective-permute-done.7.refs_1_ = bf16[128,2560]{1,0:T(8,128)(2,1)S(1)} collective-permute-done((bf16[128,2560]{1,0:T(8,128)(2,1)}, bf16[128,2560]{1,0:T(8,128)(2,1)S(1)}, u32[]{:S(2)}, u32[]{:S(2)}) %collective-permute-start.7) | collective-permute-done | bytes 655392 | tf_op jit(solution)/shard_map/ppermute | solution.py:33
  129.2 5.5 %project.3 = (bf16[128,1280]{1,0:T(8,128)(2,1)S(1)}, bf16[128,1280]{1,0:T(8,128)(2,1)S(1)}, bf16[128,1280]{1,0:T(8,128)(2,1)S(1)}) custom-call(bf16[128,2560]{1,0:T(8,128)(2,1)S(1)} %collective-permute-done.6.refs_0_, bf16[128,2560]{1,0:T(8,128)(2,1)S(1)} %collective-permute-done.7.refs_1_, bf16[128,2560]{1,0:T(8,128)(2,1)S(1)} %collective-permute-done.8.refs_2_, ...), custom_call_target="tpu_custom_call" | custom-call | flops 2516582400 | bytes 6553600 | tf_op jit(solution)/shard_map/project/pallas_call | solution.py:194
  135.7 2.2 %collective-permute-start.11 = (bf16[128,1280]{1,0:T(8,128)(2,1)S(1)}, bf16[128,1280]{1,0:T(8,128)(2,1)S(1)}, u32[]{:S(2)}, u32[]{:S(2)}) collective-permute-start(bf16[128,1280]{1,0:T(8,128)(2,1)S(1)} %get-tuple-element.47), channel_id=1, source_target_pairs={{0,144},{128,16},{16,128},{144,0},{1,145},{129,17},{17,129},{145,1... | collective-permute-start | bytes 983048 | tf_op jit(solution)/shard_map/ppermute | solution.py:33
  139.3 5.5 %project.4 = (bf16[128,1280]{1,0:T(8,128)(2,1)S(1)}, bf16[128,1280]{1,0:T(8,128)(2,1)S(1)}, bf16[128,1280]{1,0:T(8,128)(2,1)S(1)}) custom-call(bf16[128,2560]{1,0:T(8,128)(2,1)S(1)} %collective-permute-done.6.refs_0_, bf16[128,2560]{1,0:T(8,128)(2,1)S(1)} %collective-permute-done.7.refs_1_, bf16[128,2560]{1,0:T(8,128)(2,1)S(1)} %collective-permute-done.8.refs_2_, ...), custom_call_target="tpu_custom_call" | custom-call | flops 2516582400 | bytes 6553600 | tf_op jit(solution)/shard_map/project/pallas_call | solution.py:194
  144.8 2.3 %collective-permute-start.12 = (bf16[128,1280]{1,0:T(8,128)(2,1)S(1)}, bf16[128,1280]{1,0:T(8,128)(2,1)S(1)}, u32[]{:S(2)}, u32[]{:S(2)}) collective-permute-start(bf16[128,1280]{1,0:T(8,128)(2,1)S(1)} %get-tuple-element.50), channel_id=1, source_target_pairs={{0,16},{128,144},{16,0},{144,128},{1,17},{129,145},{17,1},{145,129... | collective-permute-start | bytes 983048 | tf_op jit(solution)/shard_map/ppermute | solution.py:33
  148.4 10.4 %collective-permute-done.11.across0 = bf16[128,1280]{1,0:T(8,128)(2,1)S(1)} collective-permute-done((bf16[128,1280]{1,0:T(8,128)(2,1)S(1)}, bf16[128,1280]{1,0:T(8,128)(2,1)S(1)}, u32[]{:S(2)}, u32[]{:S(2)}) %collective-permute-start.11) | collective-permute-done | bytes 327712 | tf_op jit(solution)/shard_map/ppermute | solution.py:33
  158.8 3.7 %collective-permute-start.14 = (bf16[128,1280]{1,0:T(8,128)(2,1)S(1)}, bf16[128,1280]{1,0:T(8,128)(2,1)S(1)}, u32[]{:S(2)}, u32[]{:S(2)}) collective-permute-start(bf16[128,1280]{1,0:T(8,128)(2,1)S(1)} %get-tuple-element.52), channel_id=1, source_target_pairs={{0,144},{128,16},{16,128},{144,0},{1,145},{129,17},{17,129},{145,1... | collective-permute-start | bytes 983048 | tf_op jit(solution)/shard_map/ppermute | solution.py:33
  162.5 6.5 %project.5.mine = bf16[128,2560]{1,0:T(8,128)(2,1)S(1)} custom-call(bf16[128,2560]{1,0:T(8,128)(2,1)S(1)} %copy-done.4, bf16[4,2,8,160,640]{4,3,2,1,0:T(8,128)(2,1)} %bitcast.16), custom_call_target="tpu_custom_call" | custom-call | flops 1677721600 | bytes 13107200 | tf_op jit(solution)/shard_map/project/pallas_call | solution.py:194
  169.0 2.0 %finish.1 = bf16[128,5120]{1,0:T(8,128)(2,1)} custom-call(s32[1]{0:T(128)} %bitcast.y_ref, bf16[128,5120]{1,0:T(8,128)(2,1)S(1)} %bitcast.12, f32[1,5120]{1,0:T(1,128)S(1)} %bitcast.13, bf16[128,2560]{1,0:T(8,128)(2,1)S(1)} %project.5.mine, bf16[128,1280]{1,0:T(8,128)(2,1)S(1)} %collective-permute-done.9.far0, ...), custom_call_target="tpu_custom_call" | custom-call | tf_op jit(solution)/shard_map/finish/pallas_call | solution.py:226
  (59 shorter events, 7.2 us)
Async XLA Ops:
  6.5 44.9 %all-gather.5.cloned.1.call-start = ((), (), s32[]{:S(2)}) async-start(), calls=%async_computation | async-start | bytes 1843200 | tf_op jit(solution)/shard_map/all_gather | solution.py:244
  7.3 122.0 %all-gather.7.cloned.1.call-start = ((), (), s32[]{:S(2)}) async-start(), calls=%async_computation.1 | async-start | bytes 14745600 | tf_op jit(solution)/shard_map/all_gather | solution.py:258
  7.3 44.3 %copy-start.6 = (s32[40]{0:T(128)S(1)}, s32[40]{0:T(128)}, u32[]{:S(2)}) copy-start(s32[40]{0:T(128)} %param.19) | copy-start | bytes 484
  7.3 44.3 %copy-start.7 = (s32[40]{0:T(128)S(1)}, s32[40]{0:T(128)}, u32[]{:S(2)}) copy-start(s32[40]{0:T(128)} %param.18) | copy-start | bytes 484
  7.3 44.3 %copy-start.8 = (s32[40]{0:T(128)S(1)}, s32[40]{0:T(128)}, u32[]{:S(2)}) copy-start(s32[40]{0:T(128)} %param.17) | copy-start | bytes 484
  13.6 32.6 %collective-permute-start = (bf16[2,2,32,5120]{3,2,1,0:T(8,128)(2,1)}, bf16[2,2,32,5120]{3,2,1,0:T(8,128)(2,1)S(1)}, u32[]{:S(2)}, u32[]{:S(2)}) collective-permute-start(bf16[2,2,32,5120]{3,2,1,0:T(8,128)(2,1)} %get-tuple-element.31.f1), channel_id=1, source_target_pairs={{0,32},{32,64},{64,96},{96,128},{128,160},{160,192},{192,224},{1,3... | collective-permute-start | bytes 3932168 | tf_op jit(solution)/shard_map/ppermute | solution.py:28
  17.0 34.5 %collective-permute-start.1 = (bf16[2,2,32,5120]{3,2,1,0:T(8,128)(2,1)}, bf16[2,2,32,5120]{3,2,1,0:T(8,128)(2,1)S(1)}, u32[]{:S(2)}, u32[]{:S(2)}) collective-permute-start(bf16[2,2,32,5120]{3,2,1,0:T(8,128)(2,1)} %get-tuple-element.30.f0), channel_id=1, source_target_pairs={{32,0},{64,32},{96,64},{128,96},{160,128},{192,160},{224,192},{33,... | collective-permute-start | bytes 3932168 | tf_op jit(solution)/shard_map/ppermute | solution.py:28
  52.0 17.2 %collective-permute-start.5 = (bf16[2,2,32,5120]{3,2,1,0:T(8,128)(2,1)S(1)}, bf16[2,2,32,5120]{3,2,1,0:T(8,128)(2,1)S(1)}, u32[]{:S(2)}, u32[]{:S(2)}) collective-permute-start(bf16[2,2,32,5120]{3,2,1,0:T(8,128)(2,1)S(1)} %pad_maximum_fusion.1), channel_id=1, source_target_pairs={{1,0},{2,1},{3,2},{4,3},{5,4},{6,5},{7,6},{8,7},{9,8},{10,9},{11,1... | collective-permute-start | bytes 3932168 | tf_op jit(solution)/shard_map/ppermute | solution.py:28
  54.1 33.4 %copy-start = (bf16[4,32,5120]{2,1,0:T(8,128)(2,1)S(1)}, bf16[4,32,5120]{2,1,0:T(8,128)(2,1)}, u32[]{:S(2)}) copy-start(bf16[4,32,5120]{2,1,0:T(8,128)(2,1)} %get-tuple-element.29.q_ref) | copy-start | bytes 3932164
  54.1 33.4 %copy-start.1 = (bf16[2,2,32,5120]{3,2,1,0:T(8,128)(2,1)S(1)}, bf16[2,2,32,5120]{3,2,1,0:T(8,128)(2,1)}, u32[]{:S(2)}) copy-start(bf16[2,2,32,5120]{3,2,1,0:T(8,128)(2,1)} %get-tuple-element.30.f0) | copy-start | bytes 3932164
  54.1 33.4 %copy-start.2 = (bf16[2,2,32,5120]{3,2,1,0:T(8,128)(2,1)S(1)}, bf16[2,2,32,5120]{3,2,1,0:T(8,128)(2,1)}, u32[]{:S(2)}) copy-start(bf16[2,2,32,5120]{3,2,1,0:T(8,128)(2,1)} %get-tuple-element.31.f1) | copy-start | bytes 3932164
  54.2 19.2 %collective-permute-start.4 = (bf16[2,2,32,5120]{3,2,1,0:T(8,128)(2,1)S(1)}, bf16[2,2,32,5120]{3,2,1,0:T(8,128)(2,1)S(1)}, u32[]{:S(2)}, u32[]{:S(2)}) collective-permute-start(bf16[2,2,32,5120]{3,2,1,0:T(8,128)(2,1)S(1)} %pad_maximum_fusion), channel_id=1, source_target_pairs={{0,1},{1,2},{2,3},{3,4},{4,5},{5,6},{6,7},{7,8},{8,9},{9,10},{10,1... | collective-permute-start | bytes 3932168 | tf_op jit(solution)/shard_map/ppermute | solution.py:28
  56.9 30.5 %collective-permute-start.2 = (bf16[2,2,32,5120]{3,2,1,0:T(8,128)(2,1)S(1)}, bf16[2,2,32,5120]{3,2,1,0:T(8,128)(2,1)S(1)}, u32[]{:S(2)}, u32[]{:S(2)}) collective-permute-start(bf16[2,2,32,5120]{3,2,1,0:T(8,128)(2,1)S(1)} %copy-done.10), channel_id=1, source_target_pairs={{0,1},{1,2},{2,3},{3,4},{4,5},{5,6},{6,7},{7,8},{8,9},{9,10},{10,1... | collective-permute-start | bytes 3932168 | tf_op jit(solution)/shard_map/ppermute | solution.py:28
  61.6 25.9 %collective-permute-start.3 = (bf16[2,2,32,5120]{3,2,1,0:T(8,128)(2,1)S(1)}, bf16[2,2,32,5120]{3,2,1,0:T(8,128)(2,1)S(1)}, u32[]{:S(2)}, u32[]{:S(2)}) collective-permute-start(bf16[2,2,32,5120]{3,2,1,0:T(8,128)(2,1)S(1)} %copy-done.9), channel_id=1, source_target_pairs={{1,0},{2,1},{3,2},{4,3},{5,4},{6,5},{7,6},{8,7},{9,8},{10,9},{11,1... | collective-permute-start | bytes 3932168 | tf_op jit(solution)/shard_map/ppermute | solution.py:28
  96.1 17.8 %collective-permute-start.6 = (bf16[128,2560]{1,0:T(8,128)(2,1)}, bf16[128,2560]{1,0:T(8,128)(2,1)S(1)}, u32[]{:S(2)}, u32[]{:S(2)}) collective-permute-start(bf16[128,2560]{1,0:T(8,128)(2,1)} %get-tuple-element.44.refs_0_), channel_id=1, source_target_pairs={{0,128},{128,0},{16,144},{144,16},{1,129},{129,1},{17,145},{145,17... | collective-permute-start | bytes 1966088 | tf_op jit(solution)/shard_map/ppermute | solution.py:33
  96.8 32.4 %collective-permute-start.7 = (bf16[128,2560]{1,0:T(8,128)(2,1)}, bf16[128,2560]{1,0:T(8,128)(2,1)S(1)}, u32[]{:S(2)}, u32[]{:S(2)}) collective-permute-start(bf16[128,2560]{1,0:T(8,128)(2,1)} %get-tuple-element.39), channel_id=1, source_target_pairs={{0,144},{128,16},{16,128},{144,0},{1,145},{129,17},{17,129},{145,1... | collective-permute-start | bytes 1966088 | tf_op jit(solution)/shard_map/ppermute | solution.py:33
  99.6 29.6 %collective-permute-start.8 = (bf16[128,2560]{1,0:T(8,128)(2,1)}, bf16[128,2560]{1,0:T(8,128)(2,1)S(1)}, u32[]{:S(2)}, u32[]{:S(2)}) collective-permute-start(bf16[128,2560]{1,0:T(8,128)(2,1)} %get-tuple-element.39), channel_id=1, source_target_pairs={{0,16},{128,144},{16,0},{144,128},{1,17},{129,145},{17,1},{145,129... | collective-permute-start | bytes 1966088 | tf_op jit(solution)/shard_map/ppermute | solution.py:33
  134.8 13.6 %collective-permute-start.10 = (bf16[128,1280]{1,0:T(8,128)(2,1)S(1)}, bf16[128,1280]{1,0:T(8,128)(2,1)S(1)}, u32[]{:S(2)}, u32[]{:S(2)}) collective-permute-start(bf16[128,1280]{1,0:T(8,128)(2,1)S(1)} %get-tuple-element.46), channel_id=1, source_target_pairs={{0,128},{128,0},{16,144},{144,16},{1,129},{129,1},{17,145},{145,17... | collective-permute-start | bytes 983048 | tf_op jit(solution)/shard_map/ppermute | solution.py:33
  135.7 23.1 %collective-permute-start.11 = (bf16[128,1280]{1,0:T(8,128)(2,1)S(1)}, bf16[128,1280]{1,0:T(8,128)(2,1)S(1)}, u32[]{:S(2)}, u32[]{:S(2)}) collective-permute-start(bf16[128,1280]{1,0:T(8,128)(2,1)S(1)} %get-tuple-element.47), channel_id=1, source_target_pairs={{0,144},{128,16},{16,128},{144,0},{1,145},{129,17},{17,129},{145,1... | collective-permute-start | bytes 983048 | tf_op jit(solution)/shard_map/ppermute | solution.py:33
  137.9 24.6 %copy-start.4 = (bf16[128,2560]{1,0:T(8,128)(2,1)S(1)}, bf16[128,2560]{1,0:T(8,128)(2,1)}, u32[]{:S(2)}) copy-start(bf16[128,2560]{1,0:T(8,128)(2,1)} %get-tuple-element.44.refs_0_) | copy-start | bytes 1966084
  137.9 31.1 %collective-permute-start.9 = (bf16[128,1280]{1,0:T(8,128)(2,1)S(1)}, bf16[128,1280]{1,0:T(8,128)(2,1)S(1)}, u32[]{:S(2)}, u32[]{:S(2)}) collective-permute-start(bf16[128,1280]{1,0:T(8,128)(2,1)S(1)} %get-tuple-element.41), channel_id=1, source_target_pairs={{0,16},{128,144},{16,0},{144,128},{1,17},{129,145},{17,1},{145,129... | collective-permute-start | bytes 983048 | tf_op jit(solution)/shard_map/ppermute | solution.py:33
  144.8 24.2 %collective-permute-start.12 = (bf16[128,1280]{1,0:T(8,128)(2,1)S(1)}, bf16[128,1280]{1,0:T(8,128)(2,1)S(1)}, u32[]{:S(2)}, u32[]{:S(2)}) collective-permute-start(bf16[128,1280]{1,0:T(8,128)(2,1)S(1)} %get-tuple-element.50), channel_id=1, source_target_pairs={{0,16},{128,144},{16,0},{144,128},{1,17},{129,145},{17,1},{145,129... | collective-permute-start | bytes 983048 | tf_op jit(solution)/shard_map/ppermute | solution.py:33
  147.1 21.9 %collective-permute-start.13 = (bf16[128,1280]{1,0:T(8,128)(2,1)S(1)}, bf16[128,1280]{1,0:T(8,128)(2,1)S(1)}, u32[]{:S(2)}, u32[]{:S(2)}) collective-permute-start(bf16[128,1280]{1,0:T(8,128)(2,1)S(1)} %get-tuple-element.51), channel_id=1, source_target_pairs={{0,128},{128,0},{16,144},{144,16},{1,129},{129,1},{17,145},{145,17... | collective-permute-start | bytes 983048 | tf_op jit(solution)/shard_map/ppermute | solution.py:33
  158.8 10.2 %collective-permute-start.14 = (bf16[128,1280]{1,0:T(8,128)(2,1)S(1)}, bf16[128,1280]{1,0:T(8,128)(2,1)S(1)}, u32[]{:S(2)}, u32[]{:S(2)}) collective-permute-start(bf16[128,1280]{1,0:T(8,128)(2,1)S(1)} %get-tuple-element.52), channel_id=1, source_target_pairs={{0,144},{128,16},{16,128},{144,0},{1,145},{129,17},{17,129},{145,1... | collective-permute-start | bytes 983048 | tf_op jit(solution)/shard_map/ppermute | solution.py:33
  (4 other events, 35.2 us)
Sparse Core Ops, SparseCore 0:
  9.1 41.1 all-gather.4
  52.2 71.2 all-gather.6

commit v13 on v11

--- a/solution.py
+++ b/solution.py
@@ -174,15 +174,12 @@
 
 
 def project_kernel(blocks, *refs):
-    ins, w_ref, outs, a_buf = refs[:blocks], refs[blocks], refs[blocks + 1 : -1], refs[-1]
-
-    @pl.when(pl.program_id(0) == 0)
-    def _():
-        a_buf[...] = jnp.concatenate([i[...] for i in ins], axis=0)
+    ins, w_ref, outs = refs[:blocks], refs[blocks], refs[blocks + 1 :]
+    a = jnp.concatenate([i[...] for i in ins], axis=0)
 
     _, cores, zs, _, _ = w_ref.shape
     w = jnp.concatenate([w_ref[0, c, z] for z in range(zs) for c in range(cores)], axis=0)
-    term = jnp.dot(a_buf[...], w, preferred_element_type=F32)
+    term = jnp.dot(a, w, preferred_element_type=F32)
     rows = outs[0].shape[0]
     for d, o in enumerate(outs):
         o[...] = term[d * rows : (d + 1) * rows, :].astype(BF16)
@@ -198,7 +195,6 @@
         + [pl.BlockSpec((1, cores, zs, part, cols), lambda j: (first + j, 0, 0, 0, 0))],
         out_specs=[pl.BlockSpec((rows, cols), lambda j: (0, j))] * len(blocks),
         out_shape=[jax.ShapeDtypeStruct((rows, count * cols), BF16)] * len(blocks),
-        scratch_shapes=[pltpu.VMEM((len(blocks) * rows, depth), BF16)],
         compiler_params=params(32),
         cost_estimate=pl.CostEstimate(
             flops=2 * len(blocks) * rows * depth * count * cols,

time: 176 us -> 176 us (level)
  no operation moved by 1% of the time
where the time goes in v13:
time: 176 us; the launch traced here: 175 us
  waiting for transfers between devices  91.8 us (52%)
  Pallas kernels  34.3 us (19%)
  starting transfers between devices  33.6 us (19%)
  between operations  13.7 us (8%)
    ppermute x6, waiting for transfers between devices, passed_along(): return lax.ppermute(block, axes, route)  53.4 us
    ppermute x9, waiting for transfers between devices, along_y(): lax.ppermute(block, ('y_lo', 'y_hi'), [(at(y), at(target(y))) for y in ra...  31.8 us
    ppermute x6, starting transfers between devices, passed_along(): return lax.ppermute(block, axes, route)  19.4 us
    pallas_call x3, Pallas kernels, project(): pl.pallas_call(functools.partial(project_kernel, len(blocks)), grid=(coun...  17.4 us
    ppermute x9, starting transfers between devices, along_y(): lax.ppermute(block, ('y_lo', 'y_hi'), [(at(y), at(target(y))) for y in ra...  14.1 us
    pallas_call x1, Pallas kernels, attend(): pl.pallas_call(functools.partial(attend_kernel, heads, HEAD ** (-0.5)), g...  8.64 us
    pallas_call x1, Pallas kernels, prepare(): pl.pallas_call(prepare_kernel, grid=(groups,), in_specs=[token_spec] * 3...  6.23 us
    all_gather x1, waiting for transfers between devices, shards(): weight = lax.all_gather(weight, ('x', 'core'), axis=0, tiled=False)  5.86 us
  transfers between devices with their start and end apart: 17, of which 12 were waited for; matrix products, arithmetic and copies ran while one was open for 1% of the time, Pallas kernels for 15%

profile of v13, /device:TPU:1, one launch (start us, length us, event | category | flops | bytes accessed | tf_op | source)
XLA Modules:
  0.0 174.9 jit_solution(5562608274106744838)
XLA Ops:
  7.3 6.2 %prepare.1 = (bf16[4,32,5120]{2,1,0:T(8,128)(2,1)}, bf16[2,2,32,5120]{3,2,1,0:T(8,128)(2,1)}, bf16[2,2,32,5120]{3,2,1,0:T(8,128)(2,1)}, bf16[2,2,32,5120]{3,2,1,0:T(8,128)(2,1)}, bf16[2,2,32,5120]{3,2,1,0:T(8,128)(2,1)}) custom-call(bf16[4,32,5120]{2,1,0:T(8,128)(2,1)} %bitcast.18, bf16[4,32,5120]{2,1,0:T(8,128)(2,1)} %bitcast.19, ...), custom_call_target="tpu_custom_call" | custom-call | bytes 12582912 | tf_op jit(solution)/shard_map/prepare/pallas_call | solution.py:79
  13.6 4.0 %collective-permute-start = (bf16[2,2,32,5120]{3,2,1,0:T(8,128)(2,1)}, bf16[2,2,32,5120]{3,2,1,0:T(8,128)(2,1)S(1)}, u32[]{:S(2)}, u32[]{:S(2)}) collective-permute-start(bf16[2,2,32,5120]{3,2,1,0:T(8,128)(2,1)} %get-tuple-element.32.f1), channel_id=1, source_target_pairs={{0,32},{32,64},{64,96},{96,128},{128,160},{160,192},{192,224},{1,3... | collective-permute-start | bytes 3932168 | tf_op jit(solution)/shard_map/ppermute | solution.py:28
  18.9 26.4 %collective-permute-done.hb = bf16[2,2,32,5120]{3,2,1,0:T(8,128)(2,1)S(1)} collective-permute-done((bf16[2,2,32,5120]{3,2,1,0:T(8,128)(2,1)}, bf16[2,2,32,5120]{3,2,1,0:T(8,128)(2,1)S(1)}, u32[]{:S(2)}, u32[]{:S(2)}) %collective-permute-start) | collective-permute-done | bytes 1310752 | tf_op jit(solution)/shard_map/ppermute | solution.py:28
  45.2 3.9 %collective-permute-done.1.ha = bf16[2,2,32,5120]{3,2,1,0:T(8,128)(2,1)S(1)} collective-permute-done((bf16[2,2,32,5120]{3,2,1,0:T(8,128)(2,1)}, bf16[2,2,32,5120]{3,2,1,0:T(8,128)(2,1)S(1)}, u32[]{:S(2)}, u32[]{:S(2)}) %collective-permute-start.1) | collective-permute-done | bytes 1310752 | tf_op jit(solution)/shard_map/ppermute | solution.py:28
  49.7 6.8 %collective-permute-start.5 = (bf16[2,2,32,5120]{3,2,1,0:T(8,128)(2,1)S(1)}, bf16[2,2,32,5120]{3,2,1,0:T(8,128)(2,1)S(1)}, u32[]{:S(2)}, u32[]{:S(2)}) collective-permute-start(bf16[2,2,32,5120]{3,2,1,0:T(8,128)(2,1)S(1)} %pad_maximum_fusion.1), channel_id=1, source_target_pairs={{1,0},{2,1},{3,2},{4,3},{5,4},{6,5},{7,6},{8,7},{9,8},{10,9},{11,1... | collective-permute-start | bytes 3932168 | tf_op jit(solution)/shard_map/ppermute | solution.py:28
  56.7 3.0 %collective-permute-start.4 = (bf16[2,2,32,5120]{3,2,1,0:T(8,128)(2,1)S(1)}, bf16[2,2,32,5120]{3,2,1,0:T(8,128)(2,1)S(1)}, u32[]{:S(2)}, u32[]{:S(2)}) collective-permute-start(bf16[2,2,32,5120]{3,2,1,0:T(8,128)(2,1)S(1)} %pad_maximum_fusion), channel_id=1, source_target_pairs={{0,1},{1,2},{2,3},{3,4},{4,5},{5,6},{6,7},{7,8},{8,9},{9,10},{10,1... | collective-permute-start | bytes 3932168 | tf_op jit(solution)/shard_map/ppermute | solution.py:28
  59.6 2.4 %collective-permute-start.2 = (bf16[2,2,32,5120]{3,2,1,0:T(8,128)(2,1)S(1)}, bf16[2,2,32,5120]{3,2,1,0:T(8,128)(2,1)S(1)}, u32[]{:S(2)}, u32[]{:S(2)}) collective-permute-start(bf16[2,2,32,5120]{3,2,1,0:T(8,128)(2,1)S(1)} %copy-done.10), channel_id=1, source_target_pairs={{0,1},{1,2},{2,3},{3,4},{4,5},{5,6},{6,7},{7,8},{8,9},{9,10},{10,1... | collective-permute-start | bytes 3932168 | tf_op jit(solution)/shard_map/ppermute | solution.py:28
  62.1 2.0 %collective-permute-start.3 = (bf16[2,2,32,5120]{3,2,1,0:T(8,128)(2,1)S(1)}, bf16[2,2,32,5120]{3,2,1,0:T(8,128)(2,1)S(1)}, u32[]{:S(2)}, u32[]{:S(2)}) collective-permute-start(bf16[2,2,32,5120]{3,2,1,0:T(8,128)(2,1)S(1)} %copy-done.9), channel_id=1, source_target_pairs={{1,0},{2,1},{3,2},{4,3},{5,4},{6,5},{7,6},{8,7},{9,8},{10,9},{11,1... | collective-permute-start | bytes 3932168 | tf_op jit(solution)/shard_map/ppermute | solution.py:28
  65.0 8.0 %collective-permute-done.5.ca = bf16[2,2,32,5120]{3,2,1,0:T(8,128)(2,1)S(1)} collective-permute-done((bf16[2,2,32,5120]{3,2,1,0:T(8,128)(2,1)S(1)}, bf16[2,2,32,5120]{3,2,1,0:T(8,128)(2,1)S(1)}, u32[]{:S(2)}, u32[]{:S(2)}) %collective-permute-start.5) | collective-permute-done | bytes 1310752 | tf_op jit(solution)/shard_map/ppermute | solution.py:28
  74.2 14.0 %collective-permute-done.2.rb = bf16[2,2,32,5120]{3,2,1,0:T(8,128)(2,1)S(1)} collective-permute-done((bf16[2,2,32,5120]{3,2,1,0:T(8,128)(2,1)S(1)}, bf16[2,2,32,5120]{3,2,1,0:T(8,128)(2,1)S(1)}, u32[]{:S(2)}, u32[]{:S(2)}) %collective-permute-start.2) | collective-permute-done | bytes 1310752 | tf_op jit(solution)/shard_map/ppermute | solution.py:28
  88.2 8.6 %attend.1 = (bf16[128,2560]{1,0:T(8,128)(2,1)}, bf16[128,2560]{1,0:T(8,128)(2,1)}) custom-call(s32[40]{0:T(128)S(1)} %add_add_fusion.combo_ref, s32[1]{0:T(128)} %bitcast.3.half_ref, bf16[4,32,5120]{2,1,0:T(8,128)(2,1)S(1)} %copy-done, bf16[2,2,32,5120]{3,2,1,0:T(8,128)(2,1)S(1)} %copy-done.1, bf16[2,2,32,5120]{3,2,1,0:T(8,128)(2,1)S(1)} %copy-done.2, ...), custom_call_target="tpu_custom_call" | custom-call | flops 1006632960 | bytes 33554432 | tf_op jit(solution)/shard_map/attend/pallas_call | solution.py:159
  98.0 1.9 %collective-permute-start.7 = (bf16[128,2560]{1,0:T(8,128)(2,1)}, bf16[128,2560]{1,0:T(8,128)(2,1)S(1)}, u32[]{:S(2)}, u32[]{:S(2)}) collective-permute-start(bf16[128,2560]{1,0:T(8,128)(2,1)} %get-tuple-element.40), channel_id=1, source_target_pairs={{0,144},{128,16},{16,128},{144,0},{1,145},{129,17},{17,129},{145,1... | collective-permute-start | bytes 1966088 | tf_op jit(solution)/shard_map/ppermute | solution.py:33
  100.4 9.2 %collective-permute-done.6.refs_0_ = bf16[128,2560]{1,0:T(8,128)(2,1)S(1)} collective-permute-done((bf16[128,2560]{1,0:T(8,128)(2,1)}, bf16[128,2560]{1,0:T(8,128)(2,1)S(1)}, u32[]{:S(2)}, u32[]{:S(2)}) %collective-permute-start.6) | collective-permute-done | bytes 655392 | tf_op jit(solution)/shard_map/ppermute | solution.py:33
  111.5 10.0 %collective-permute-done.8.refs_2_ = bf16[128,2560]{1,0:T(8,128)(2,1)S(1)} collective-permute-done((bf16[128,2560]{1,0:T(8,128)(2,1)}, bf16[128,2560]{1,0:T(8,128)(2,1)S(1)}, u32[]{:S(2)}, u32[]{:S(2)}) %collective-permute-start.8) | collective-permute-done | bytes 655392 | tf_op jit(solution)/shard_map/ppermute | solution.py:33
  121.5 5.9 %all-gather.7.cloned.1.call-done = bf16[64,160,640]{2,1,0:T(8,128)(2,1)} async-done(((bf16[8,160,640]{2,1,0:T(8,128)(2,1)}), bf16[64,160,640]{2,1,0:T(8,128)(2,1)}) %all-gather.7.cloned.1.call-update) | async-done | bytes 13107216 | tf_op jit(solution)/shard_map/all_gather | solution.py:254
  127.3 5.4 %project.3 = (bf16[128,1280]{1,0:T(8,128)(2,1)S(1)}, bf16[128,1280]{1,0:T(8,128)(2,1)S(1)}, bf16[128,1280]{1,0:T(8,128)(2,1)S(1)}) custom-call(bf16[128,2560]{1,0:T(8,128)(2,1)S(1)} %collective-permute-done.6.refs_0_, bf16[128,2560]{1,0:T(8,128)(2,1)S(1)} %collective-permute-done.7.refs_1_, bf16[128,2560]{1,0:T(8,128)(2,1)S(1)} %collective-permute-done.8.refs_2_, ...), custom_call_target="tpu_custom_call" | custom-call | flops 2516582400 | bytes 6553600 | tf_op jit(solution)/shard_map/project/pallas_call | solution.py:191
  132.7 2.8 %collective-permute-start.11 = (bf16[128,1280]{1,0:T(8,128)(2,1)S(1)}, bf16[128,1280]{1,0:T(8,128)(2,1)S(1)}, u32[]{:S(2)}, u32[]{:S(2)}) collective-permute-start(bf16[128,1280]{1,0:T(8,128)(2,1)S(1)} %get-tuple-element.42), channel_id=1, source_target_pairs={{0,16},{128,144},{16,0},{144,128},{1,17},{129,145},{17,1},{145,129... | collective-permute-start | bytes 983048 | tf_op jit(solution)/shard_map/ppermute | solution.py:33
  136.4 5.5 %project.4 = (bf16[128,1280]{1,0:T(8,128)(2,1)S(1)}, bf16[128,1280]{1,0:T(8,128)(2,1)S(1)}, bf16[128,1280]{1,0:T(8,128)(2,1)S(1)}) custom-call(bf16[128,2560]{1,0:T(8,128)(2,1)S(1)} %collective-permute-done.6.refs_0_, bf16[128,2560]{1,0:T(8,128)(2,1)S(1)} %collective-permute-done.7.refs_1_, bf16[128,2560]{1,0:T(8,128)(2,1)S(1)} %collective-permute-done.8.refs_2_, ...), custom_call_target="tpu_custom_call" | custom-call | flops 2516582400 | bytes 6553600 | tf_op jit(solution)/shard_map/project/pallas_call | solution.py:191
  141.9 3.0 %collective-permute-start.12 = (bf16[128,1280]{1,0:T(8,128)(2,1)S(1)}, bf16[128,1280]{1,0:T(8,128)(2,1)S(1)}, u32[]{:S(2)}, u32[]{:S(2)}) collective-permute-start(bf16[128,1280]{1,0:T(8,128)(2,1)S(1)} %get-tuple-element.52), channel_id=1, source_target_pairs={{0,16},{128,144},{16,0},{144,128},{1,17},{129,145},{17,1},{145,129... | collective-permute-start | bytes 983048 | tf_op jit(solution)/shard_map/ppermute | solution.py:33
  144.9 6.6 %project.5.mine = bf16[128,2560]{1,0:T(8,128)(2,1)S(1)} custom-call(bf16[128,2560]{1,0:T(8,128)(2,1)S(1)} %copy-done.4, bf16[4,2,8,160,640]{4,3,2,1,0:T(8,128)(2,1)} %bitcast.16), custom_call_target="tpu_custom_call" | custom-call | flops 1677721600 | bytes 13107200 | tf_op jit(solution)/shard_map/project/pallas_call | solution.py:191
  153.0 3.9 %collective-permute-start.14 = (bf16[128,1280]{1,0:T(8,128)(2,1)S(1)}, bf16[128,1280]{1,0:T(8,128)(2,1)S(1)}, u32[]{:S(2)}, u32[]{:S(2)}) collective-permute-start(bf16[128,1280]{1,0:T(8,128)(2,1)S(1)} %get-tuple-element.54), channel_id=1, source_target_pairs={{0,144},{128,16},{16,128},{144,0},{1,145},{129,17},{17,129},{145,1... | collective-permute-start | bytes 983048 | tf_op jit(solution)/shard_map/ppermute | solution.py:33
  156.9 4.6 %collective-permute-done.13.pair1 = bf16[128,1280]{1,0:T(8,128)(2,1)S(1)} collective-permute-done((bf16[128,1280]{1,0:T(8,128)(2,1)S(1)}, bf16[128,1280]{1,0:T(8,128)(2,1)S(1)}, u32[]{:S(2)}, u32[]{:S(2)}) %collective-permute-start.13) | collective-permute-done | bytes 327712 | tf_op jit(solution)/shard_map/ppermute | solution.py:33
  161.5 4.6 %collective-permute-done.14.across1 = bf16[128,1280]{1,0:T(8,128)(2,1)S(1)} collective-permute-done((bf16[128,1280]{1,0:T(8,128)(2,1)S(1)}, bf16[128,1280]{1,0:T(8,128)(2,1)S(1)}, u32[]{:S(2)}, u32[]{:S(2)}) %collective-permute-start.14) | collective-permute-done | bytes 327712 | tf_op jit(solution)/shard_map/ppermute | solution.py:33
  166.1 2.0 %finish.1 = bf16[128,5120]{1,0:T(8,128)(2,1)} custom-call(s32[1]{0:T(128)} %bitcast.y_ref, bf16[128,5120]{1,0:T(8,128)(2,1)S(1)} %bitcast.12, f32[1,5120]{1,0:T(1,128)S(1)} %bitcast.13, bf16[128,2560]{1,0:T(8,128)(2,1)S(1)} %project.5.mine, bf16[128,1280]{1,0:T(8,128)(2,1)S(1)} %collective-permute-done.11.far0, ...), custom_call_target="tpu_custom_call" | custom-call | tf_op jit(solution)/shard_map/finish/pallas_call | solution.py:222
  (59 shorter events, 10.6 us)
Async XLA Ops:
  6.5 42.6 %all-gather.5.cloned.1.call-start = ((), (), s32[]{:S(2)}) async-start(), calls=%async_computation | async-start | bytes 1843200 | tf_op jit(solution)/shard_map/all_gather | solution.py:240
  7.3 120.1 %all-gather.7.cloned.1.call-start = ((), (), s32[]{:S(2)}) async-start(), calls=%async_computation.1 | async-start | bytes 14745600 | tf_op jit(solution)/shard_map/all_gather | solution.py:254
  7.3 42.0 %copy-start.6 = (s32[40]{0:T(128)S(1)}, s32[40]{0:T(128)}, u32[]{:S(2)}) copy-start(s32[40]{0:T(128)} %param.19) | copy-start | bytes 484
  7.3 42.0 %copy-start.7 = (s32[40]{0:T(128)S(1)}, s32[40]{0:T(128)}, u32[]{:S(2)}) copy-start(s32[40]{0:T(128)} %param.18) | copy-start | bytes 484
  7.3 42.0 %copy-start.8 = (s32[40]{0:T(128)S(1)}, s32[40]{0:T(128)}, u32[]{:S(2)}) copy-start(s32[40]{0:T(128)} %param.17) | copy-start | bytes 484
  13.6 31.7 %collective-permute-start = (bf16[2,2,32,5120]{3,2,1,0:T(8,128)(2,1)}, bf16[2,2,32,5120]{3,2,1,0:T(8,128)(2,1)S(1)}, u32[]{:S(2)}, u32[]{:S(2)}) collective-permute-start(bf16[2,2,32,5120]{3,2,1,0:T(8,128)(2,1)} %get-tuple-element.32.f1), channel_id=1, source_target_pairs={{0,32},{32,64},{64,96},{96,128},{128,160},{160,192},{192,224},{1,3... | collective-permute-start | bytes 3932168 | tf_op jit(solution)/shard_map/ppermute | solution.py:28
  17.6 31.5 %collective-permute-start.1 = (bf16[2,2,32,5120]{3,2,1,0:T(8,128)(2,1)}, bf16[2,2,32,5120]{3,2,1,0:T(8,128)(2,1)S(1)}, u32[]{:S(2)}, u32[]{:S(2)}) collective-permute-start(bf16[2,2,32,5120]{3,2,1,0:T(8,128)(2,1)} %get-tuple-element.31.f0), channel_id=1, source_target_pairs={{32,0},{64,32},{96,64},{128,96},{160,128},{192,160},{224,192},{33,... | collective-permute-start | bytes 3932168 | tf_op jit(solution)/shard_map/ppermute | solution.py:28
  49.7 23.2 %collective-permute-start.5 = (bf16[2,2,32,5120]{3,2,1,0:T(8,128)(2,1)S(1)}, bf16[2,2,32,5120]{3,2,1,0:T(8,128)(2,1)S(1)}, u32[]{:S(2)}, u32[]{:S(2)}) collective-permute-start(bf16[2,2,32,5120]{3,2,1,0:T(8,128)(2,1)S(1)} %pad_maximum_fusion.1), channel_id=1, source_target_pairs={{1,0},{2,1},{3,2},{4,3},{5,4},{6,5},{7,6},{8,7},{9,8},{10,9},{11,1... | collective-permute-start | bytes 3932168 | tf_op jit(solution)/shard_map/ppermute | solution.py:28
  56.5 31.7 %copy-start = (bf16[4,32,5120]{2,1,0:T(8,128)(2,1)S(1)}, bf16[4,32,5120]{2,1,0:T(8,128)(2,1)}, u32[]{:S(2)}) copy-start(bf16[4,32,5120]{2,1,0:T(8,128)(2,1)} %get-tuple-element.30.q_ref) | copy-start | bytes 3932164
  56.5 31.7 %copy-start.1 = (bf16[2,2,32,5120]{3,2,1,0:T(8,128)(2,1)S(1)}, bf16[2,2,32,5120]{3,2,1,0:T(8,128)(2,1)}, u32[]{:S(2)}) copy-start(bf16[2,2,32,5120]{3,2,1,0:T(8,128)(2,1)} %get-tuple-element.31.f0) | copy-start | bytes 3932164
  56.5 31.7 %copy-start.2 = (bf16[2,2,32,5120]{3,2,1,0:T(8,128)(2,1)S(1)}, bf16[2,2,32,5120]{3,2,1,0:T(8,128)(2,1)}, u32[]{:S(2)}) copy-start(bf16[2,2,32,5120]{3,2,1,0:T(8,128)(2,1)} %get-tuple-element.32.f1) | copy-start | bytes 3932164
  56.7 17.5 %collective-permute-start.4 = (bf16[2,2,32,5120]{3,2,1,0:T(8,128)(2,1)S(1)}, bf16[2,2,32,5120]{3,2,1,0:T(8,128)(2,1)S(1)}, u32[]{:S(2)}, u32[]{:S(2)}) collective-permute-start(bf16[2,2,32,5120]{3,2,1,0:T(8,128)(2,1)S(1)} %pad_maximum_fusion), channel_id=1, source_target_pairs={{0,1},{1,2},{2,3},{3,4},{4,5},{5,6},{6,7},{7,8},{8,9},{9,10},{10,1... | collective-permute-start | bytes 3932168 | tf_op jit(solution)/shard_map/ppermute | solution.py:28
  59.6 28.6 %collective-permute-start.2 = (bf16[2,2,32,5120]{3,2,1,0:T(8,128)(2,1)S(1)}, bf16[2,2,32,5120]{3,2,1,0:T(8,128)(2,1)S(1)}, u32[]{:S(2)}, u32[]{:S(2)}) collective-permute-start(bf16[2,2,32,5120]{3,2,1,0:T(8,128)(2,1)S(1)} %copy-done.10), channel_id=1, source_target_pairs={{0,1},{1,2},{2,3},{3,4},{4,5},{5,6},{6,7},{7,8},{8,9},{9,10},{10,1... | collective-permute-start | bytes 3932168 | tf_op jit(solution)/shard_map/ppermute | solution.py:28
  62.1 26.1 %collective-permute-start.3 = (bf16[2,2,32,5120]{3,2,1,0:T(8,128)(2,1)S(1)}, bf16[2,2,32,5120]{3,2,1,0:T(8,128)(2,1)S(1)}, u32[]{:S(2)}, u32[]{:S(2)}) collective-permute-start(bf16[2,2,32,5120]{3,2,1,0:T(8,128)(2,1)S(1)} %copy-done.9), channel_id=1, source_target_pairs={{1,0},{2,1},{3,2},{4,3},{5,4},{6,5},{7,6},{8,7},{9,8},{10,9},{11,1... | collective-permute-start | bytes 3932168 | tf_op jit(solution)/shard_map/ppermute | solution.py:28
  96.9 12.7 %collective-permute-start.6 = (bf16[128,2560]{1,0:T(8,128)(2,1)}, bf16[128,2560]{1,0:T(8,128)(2,1)S(1)}, u32[]{:S(2)}, u32[]{:S(2)}) collective-permute-start(bf16[128,2560]{1,0:T(8,128)(2,1)} %get-tuple-element.48.refs_0_), channel_id=1, source_target_pairs={{0,128},{128,0},{16,144},{144,16},{1,129},{129,1},{17,145},{145,17... | collective-permute-start | bytes 1966088 | tf_op jit(solution)/shard_map/ppermute | solution.py:33
  98.0 13.5 %collective-permute-start.7 = (bf16[128,2560]{1,0:T(8,128)(2,1)}, bf16[128,2560]{1,0:T(8,128)(2,1)S(1)}, u32[]{:S(2)}, u32[]{:S(2)}) collective-permute-start(bf16[128,2560]{1,0:T(8,128)(2,1)} %get-tuple-element.40), channel_id=1, source_target_pairs={{0,144},{128,16},{16,128},{144,0},{1,145},{129,17},{17,129},{145,1... | collective-permute-start | bytes 1966088 | tf_op jit(solution)/shard_map/ppermute | solution.py:33
  99.9 21.6 %collective-permute-start.8 = (bf16[128,2560]{1,0:T(8,128)(2,1)}, bf16[128,2560]{1,0:T(8,128)(2,1)S(1)}, u32[]{:S(2)}, u32[]{:S(2)}) collective-permute-start(bf16[128,2560]{1,0:T(8,128)(2,1)} %get-tuple-element.40), channel_id=1, source_target_pairs={{0,16},{128,144},{16,0},{144,128},{1,17},{129,145},{17,1},{145,129... | collective-permute-start | bytes 1966088 | tf_op jit(solution)/shard_map/ppermute | solution.py:33
  132.7 28.7 %collective-permute-start.11 = (bf16[128,1280]{1,0:T(8,128)(2,1)S(1)}, bf16[128,1280]{1,0:T(8,128)(2,1)S(1)}, u32[]{:S(2)}, u32[]{:S(2)}) collective-permute-start(bf16[128,1280]{1,0:T(8,128)(2,1)S(1)} %get-tuple-element.42), channel_id=1, source_target_pairs={{0,16},{128,144},{16,0},{144,128},{1,17},{129,145},{17,1},{145,129... | collective-permute-start | bytes 983048 | tf_op jit(solution)/shard_map/ppermute | solution.py:33
  135.5 17.4 %collective-permute-start.10 = (bf16[128,1280]{1,0:T(8,128)(2,1)S(1)}, bf16[128,1280]{1,0:T(8,128)(2,1)S(1)}, u32[]{:S(2)}, u32[]{:S(2)}) collective-permute-start(bf16[128,1280]{1,0:T(8,128)(2,1)S(1)} %get-tuple-element.46), channel_id=1, source_target_pairs={{0,144},{128,16},{16,128},{144,0},{1,145},{129,17},{17,129},{145,1... | collective-permute-start | bytes 983048 | tf_op jit(solution)/shard_map/ppermute | solution.py:33
  136.4 16.6 %collective-permute-start.9 = (bf16[128,1280]{1,0:T(8,128)(2,1)S(1)}, bf16[128,1280]{1,0:T(8,128)(2,1)S(1)}, u32[]{:S(2)}, u32[]{:S(2)}) collective-permute-start(bf16[128,1280]{1,0:T(8,128)(2,1)S(1)} %get-tuple-element.45), channel_id=1, source_target_pairs={{0,128},{128,0},{16,144},{144,16},{1,129},{129,1},{17,145},{145,17... | collective-permute-start | bytes 983048 | tf_op jit(solution)/shard_map/ppermute | solution.py:33
  141.9 15.0 %collective-permute-start.12 = (bf16[128,1280]{1,0:T(8,128)(2,1)S(1)}, bf16[128,1280]{1,0:T(8,128)(2,1)S(1)}, u32[]{:S(2)}, u32[]{:S(2)}) collective-permute-start(bf16[128,1280]{1,0:T(8,128)(2,1)S(1)} %get-tuple-element.52), channel_id=1, source_target_pairs={{0,16},{128,144},{16,0},{144,128},{1,17},{129,145},{17,1},{145,129... | collective-permute-start | bytes 983048 | tf_op jit(solution)/shard_map/ppermute | solution.py:33
  144.9 21.2 %copy-start.5 = (f32[5120]{0:T(1024)S(1)}, f32[5120]{0:T(1024)}, u32[]{:S(2)}) copy-start(f32[5120]{0:T(1024)} %param.21) | copy-start | bytes 61444
  144.9 16.6 %collective-permute-start.13 = (bf16[128,1280]{1,0:T(8,128)(2,1)S(1)}, bf16[128,1280]{1,0:T(8,128)(2,1)S(1)}, u32[]{:S(2)}, u32[]{:S(2)}) collective-permute-start(bf16[128,1280]{1,0:T(8,128)(2,1)S(1)} %get-tuple-element.53), channel_id=1, source_target_pairs={{0,128},{128,0},{16,144},{144,16},{1,129},{129,1},{17,145},{145,17... | collective-permute-start | bytes 983048 | tf_op jit(solution)/shard_map/ppermute | solution.py:33
  153.0 13.1 %collective-permute-start.14 = (bf16[128,1280]{1,0:T(8,128)(2,1)S(1)}, bf16[128,1280]{1,0:T(8,128)(2,1)S(1)}, u32[]{:S(2)}, u32[]{:S(2)}) collective-permute-start(bf16[128,1280]{1,0:T(8,128)(2,1)S(1)} %get-tuple-element.54), channel_id=1, source_target_pairs={{0,144},{128,16},{16,128},{144,0},{1,145},{129,17},{17,129},{145,1... | collective-permute-start | bytes 983048 | tf_op jit(solution)/shard_map/ppermute | solution.py:33
  (4 other events, 52.2 us)
Sparse Core Ops, SparseCore 0:
  9.1 39.8 all-gather.4
  50.9 76.4 all-gather.6
